TPU v7x, 32 devices: a whole 2x2x4 slice. The times are simulated.
32 devices in a mesh: dp: 16 (over z, y, x), seq: 2 (over core).
Axes of the slice: x: 2, y: 2, z: 4, core: 2. Of those that a mesh axis runs over, the one named last changes fastest.
Arguments:
- tokens: bfloat16 [16, 2048, 1024], P('dp', 'seq'), may hold values from -6 to 6
- segments: int32 [16, 2048], P('dp'), may hold values from 0 to 3, never falling along the last dimension, each value on 1 to 768 neighbouring positions
- ln1_gain: bfloat16 [1024], P(('dp', 'seq')), may hold values from 0.5 to 1.5
- ln1_bias: bfloat16 [1024], P(('dp', 'seq')), may hold values from -1.75 to 1.75
- w_query: bfloat16 [1024, 1024], P(('dp', 'seq')), may hold values from -0.1875 to 0.1875
- w_key: bfloat16 [1024, 1024], P(('dp', 'seq')), may hold values from -0.1875 to 0.1875
- w_value: bfloat16 [1024, 1024], P(('dp', 'seq')), may hold values from -0.1875 to 0.1875
- w_out: bfloat16 [1024, 1024], P(('dp', 'seq')), may hold values from -3 to 3
- ln2_gain: bfloat16 [1024], P(('dp', 'seq')), may hold values from 0.5 to 1.5
- ln2_bias: bfloat16 [1024], P(('dp', 'seq')), may hold values from -1.75 to 1.75
- w_up: bfloat16 [1024, 4096], P(('dp', 'seq')), may hold values from -0.1875 to 0.1875
- w_down: bfloat16 [4096, 1024], P(('dp', 'seq')), may hold values from -0.09375 to 0.09375
- cotangent: bfloat16 [16, 2048, 1024], P('dp', 'seq'), may hold values from -6 to 6
Outputs:
- mixed: bfloat16 [16, 2048, 1024], P('dp', 'seq')
- token_grad: bfloat16 [16, 2048, 1024], P('dp', 'seq')
- grad_ln1_gain: float32 [1024], P(('dp', 'seq'))
- grad_ln1_bias: float32 [1024], P(('dp', 'seq'))
- grad_w_query: float32 [1024, 1024], P(('dp', 'seq'))
- grad_w_key: float32 [1024, 1024], P(('dp', 'seq'))
- grad_w_value: float32 [1024, 1024], P(('dp', 'seq'))
- grad_w_out: float32 [1024, 1024], P(('dp', 'seq'))
- grad_ln2_gain: float32 [1024], P(('dp', 'seq'))
- grad_ln2_bias: float32 [1024], P(('dp', 'seq'))
- grad_w_up: float32 [1024, 4096], P(('dp', 'seq'))
- grad_w_down: float32 [4096, 1024], P(('dp', 'seq'))
Inputs may be any that keep to these rules, and one draw needn't show every extreme that they name: `segments`: along each sequence the scene ids never fall; each of the 4 scenes has 1 to 768 tokens and one has exactly 768.
All inputs are finite; a program needn't handle non-finite values.
Results may differ from a plain program's by a relative error of at most 0.012.
Values may be sent and summed in bfloat16 or wider, within the bound.
No kernel may reach another device: no remote copies, remote signals or barrier semaphores. Data moves between devices by JAX's collectives and lax.ppermute only.
A program may use at most 256 MiB of HBM per device.

v0:
```python
from functools import partial

import jax
import jax.numpy as jnp
from jax import lax
from jax.sharding import PartitionSpec as P

HEAD_DIM = 64
GROUP = 4
QBLK = 512


def layer_norm(values, gain_vec, bias_vec):
    centre = values - jnp.mean(values, axis=-1, keepdims=True)
    spread = jnp.mean(centre * centre, axis=-1, keepdims=True)
    return centre * lax.rsqrt(spread + 1e-05) * gain_vec + bias_vec


def contract_rows(left, right):
    return lax.dot_general(
        left, right, (((0,), (0,)), ((), ())), preferred_element_type=jnp.float32
    )


def contract_cols(left, right):
    return lax.dot_general(
        left, right, (((1,), (1,)), ((), ())), preferred_element_type=jnp.float32
    )


def body(
    tokens,
    segments,
    ln1_gain,
    ln1_bias,
    w_query,
    w_key,
    w_value,
    w_out,
    ln2_gain,
    ln2_bias,
    w_up,
    w_down,
    cotangent,
):
    rows_here = tokens[0]
    n_rows = rows_here.shape[0]
    model_width = rows_here.shape[1]
    seg_full = segments[0]
    my_index = lax.axis_index("seq")
    seg_local = lax.dynamic_slice_in_dim(seg_full, my_index * n_rows, n_rows)
    gathered = (
        lax.all_gather(ln1_gain, ("dp", "seq"), axis=0, tiled=True),
        lax.all_gather(ln1_bias, ("dp", "seq"), axis=0, tiled=True),
        lax.all_gather(w_query, ("dp", "seq"), axis=0, tiled=True),
        lax.all_gather(w_key, ("dp", "seq"), axis=0, tiled=True),
        lax.all_gather(w_value, ("dp", "seq"), axis=0, tiled=True),
        lax.all_gather(w_out, ("dp", "seq"), axis=0, tiled=True),
        lax.all_gather(ln2_gain, ("dp", "seq"), axis=0, tiled=True),
        lax.all_gather(ln2_bias, ("dp", "seq"), axis=0, tiled=True),
        lax.all_gather(w_up, ("dp", "seq"), axis=0, tiled=True),
        lax.all_gather(w_down, ("dp", "seq"), axis=0, tiled=True),
    )
    gain_one, bias_one, query_w, key_w, value_w, out_w, gain_two, bias_two, up_w, down_w = gathered
    group_width = GROUP * HEAD_DIM
    groups = model_width // group_width
    blocks = n_rows // QBLK
    score_scale = HEAD_DIM ** (-0.5)
    inputs = rows_here.astype(jnp.float32)
    gain_one_f = gain_one.astype(jnp.float32)
    bias_one_f = bias_one.astype(jnp.float32)
    gain_two_f = gain_two.astype(jnp.float32)
    bias_two_f = bias_two.astype(jnp.float32)
    lowered_one = layer_norm(inputs, gain_one_f, bias_one_f).astype(jnp.bfloat16)
    queries = jnp.dot(lowered_one, query_w, preferred_element_type=jnp.float32).astype(jnp.bfloat16)
    keys_local = jnp.dot(lowered_one, key_w, preferred_element_type=jnp.float32).astype(
        jnp.bfloat16
    )
    values_local = jnp.dot(lowered_one, value_w, preferred_element_type=jnp.float32).astype(
        jnp.bfloat16
    )
    key_all, value_all = (
        lax.all_gather(keys_local, "seq", axis=0, tiled=True),
        lax.all_gather(values_local, "seq", axis=0, tiled=True),
    )
    kv_len = key_all.shape[0]
    key_groups = key_all.reshape(kv_len, groups, group_width).transpose(1, 0, 2)
    value_groups = value_all.reshape(kv_len, groups, group_width).transpose(1, 0, 2)
    seg_blocks = seg_local.reshape(blocks, QBLK)
    item_ids = jnp.arange(blocks * groups, dtype=jnp.int32)
    group_ids = item_ids % groups
    block_ids = item_ids // groups

    def to_items(matrix):
        return (
            matrix.reshape(blocks, QBLK, groups, group_width)
            .transpose(0, 2, 1, 3)
            .reshape(blocks * groups, QBLK, group_width)
        )

    def from_items(stacked):
        return (
            stacked.reshape(blocks, groups, QBLK, group_width)
            .transpose(0, 2, 1, 3)
            .reshape(n_rows, model_width)
        )

    def group_keys(group_id):
        return lax.dynamic_index_in_dim(key_groups, group_id, 0, keepdims=False).reshape(
            kv_len, GROUP, HEAD_DIM
        )

    def group_values(group_id):
        return lax.dynamic_index_in_dim(value_groups, group_id, 0, keepdims=False).reshape(
            kv_len, GROUP, HEAD_DIM
        )

    def item_scores(query_heads, key_item, block_id):
        seg_item = lax.dynamic_index_in_dim(seg_blocks, block_id, 0, keepdims=False)
        raw_scores = (
            jnp.einsum("qhd,khd->hqk", query_heads, key_item, preferred_element_type=jnp.float32)
            * score_scale
        )
        same_scene = seg_item[:, None] == seg_full[None, :]
        return jnp.where(same_scene[None], raw_scores, -1000000000.0)

    def attend(packed):
        query_item, group_id, block_id = packed
        query_heads = query_item.reshape(QBLK, GROUP, HEAD_DIM)
        scores = item_scores(query_heads, group_keys(group_id), block_id)
        top_score = jnp.max(scores, axis=-1, keepdims=True)
        expo = jnp.exp(scores - top_score)
        totals = jnp.sum(expo, axis=-1, keepdims=True)
        probs = (expo / totals).astype(jnp.bfloat16)
        result = jnp.einsum(
            "hqk,khd->qhd", probs, group_values(group_id), preferred_element_type=jnp.float32
        )
        return (result.reshape(QBLK, group_width), top_score + jnp.log(totals))

    query_items = to_items(queries)
    attended_items, log_totals = lax.map(attend, (query_items, group_ids, block_ids))
    attended = from_items(attended_items).astype(jnp.bfloat16)
    middle = inputs + jnp.dot(attended, out_w, preferred_element_type=jnp.float32)
    lowered_two = layer_norm(middle, gain_two_f, bias_two_f).astype(jnp.bfloat16)
    upward = jnp.dot(lowered_two, up_w, preferred_element_type=jnp.float32)
    activated = jax.nn.gelu(upward, approximate=False).astype(jnp.bfloat16)
    mixed = (middle + jnp.dot(activated, down_w, preferred_element_type=jnp.float32)).astype(
        jnp.bfloat16
    )
    again = (
        lax.all_gather(ln1_gain, ("dp", "seq"), axis=0, tiled=True),
        lax.all_gather(ln1_bias, ("dp", "seq"), axis=0, tiled=True),
        lax.all_gather(w_query, ("dp", "seq"), axis=0, tiled=True),
        lax.all_gather(w_key, ("dp", "seq"), axis=0, tiled=True),
        lax.all_gather(w_value, ("dp", "seq"), axis=0, tiled=True),
        lax.all_gather(w_out, ("dp", "seq"), axis=0, tiled=True),
        lax.all_gather(ln2_gain, ("dp", "seq"), axis=0, tiled=True),
        lax.all_gather(ln2_bias, ("dp", "seq"), axis=0, tiled=True),
        lax.all_gather(w_up, ("dp", "seq"), axis=0, tiled=True),
        lax.all_gather(w_down, ("dp", "seq"), axis=0, tiled=True),
    )
    gain_one, bias_one, query_w, key_w, value_w, out_w, gain_two, bias_two, up_w, down_w = again
    grad_out = cotangent[0]
    grad_down = contract_rows(activated, grad_out)
    grad_act = contract_cols(grad_out, down_w)
    unused_value, gelu_pull = jax.vjp(partial(jax.nn.gelu, approximate=False), upward)
    grad_upward = gelu_pull(grad_act)[0].astype(jnp.bfloat16)
    grad_up = contract_rows(lowered_two, grad_upward)
    grad_normed_two = contract_cols(grad_upward, up_w)
    unused_norm, norm_two_pull = jax.vjp(
        layer_norm, middle, gain_two.astype(jnp.float32), bias_two.astype(jnp.float32)
    )
    grad_middle_part, grad_gain_two, grad_bias_two = norm_two_pull(grad_normed_two)
    grad_middle = grad_out.astype(jnp.float32) + grad_middle_part
    grad_branch = grad_middle.astype(jnp.bfloat16)
    grad_outw = contract_rows(attended, grad_branch)
    grad_attended = contract_cols(grad_branch, out_w).astype(jnp.bfloat16)

    def attend_back(packed):
        query_item, grad_item, log_item, group_id, block_id = packed
        query_heads = query_item.reshape(QBLK, GROUP, HEAD_DIM)
        key_item = group_keys(group_id)
        value_item = group_values(group_id)
        scores = item_scores(query_heads, key_item, block_id)
        probs = jnp.exp(scores - log_item)
        lowered = probs.astype(jnp.bfloat16)
        grad_heads = grad_item.reshape(QBLK, GROUP, HEAD_DIM)
        grad_probs = jnp.einsum(
            "qhd,khd->hqk", grad_heads, value_item, preferred_element_type=jnp.float32
        )
        inner = jnp.sum(grad_probs * probs, axis=-1, keepdims=True)
        grad_scores = (probs * (grad_probs - inner)).astype(jnp.bfloat16)
        grad_query = (
            jnp.einsum("hqk,khd->qhd", grad_scores, key_item, preferred_element_type=jnp.float32)
            * score_scale
        )
        grad_key = (
            jnp.einsum("hqk,qhd->khd", grad_scores, query_heads, preferred_element_type=jnp.float32)
            * score_scale
        )
        grad_value = jnp.einsum(
            "hqk,qhd->khd", lowered, grad_heads, preferred_element_type=jnp.float32
        )
        return (
            grad_query.reshape(QBLK, group_width),
            grad_key.reshape(kv_len, group_width),
            grad_value.reshape(kv_len, group_width),
        )

    query_grad_items, key_grad_items, value_grad_items = lax.map(
        attend_back, (query_items, to_items(grad_attended), log_totals, group_ids, block_ids)
    )
    grad_queries = from_items(query_grad_items).astype(jnp.bfloat16)

    def key_layout(stacked):
        return (
            stacked.reshape(blocks, groups, kv_len, group_width)
            .sum(axis=0)
            .transpose(1, 0, 2)
            .reshape(kv_len, model_width)
        )

    key_terms = key_layout(key_grad_items)
    value_terms = key_layout(value_grad_items)
    grad_key_local, grad_value_local = (
        lax.psum_scatter(
            key_terms.astype(jnp.bfloat16), "seq", scatter_dimension=0, tiled=True
        ).astype(jnp.float32),
        lax.psum_scatter(
            value_terms.astype(jnp.bfloat16), "seq", scatter_dimension=0, tiled=True
        ).astype(jnp.float32),
    )
    grad_keys = grad_key_local.astype(jnp.bfloat16)
    grad_values = grad_value_local.astype(jnp.bfloat16)
    grad_qw = contract_rows(lowered_one, grad_queries)
    grad_kw = contract_rows(lowered_one, grad_keys)
    grad_vw = contract_rows(lowered_one, grad_values)
    grad_normed_one = (
        contract_cols(grad_queries, query_w)
        + contract_cols(grad_keys, key_w)
        + contract_cols(grad_values, value_w)
    )
    unused_first, norm_one_pull = jax.vjp(
        layer_norm, inputs, gain_one.astype(jnp.float32), bias_one.astype(jnp.float32)
    )
    grad_inputs_part, grad_gain_one, grad_bias_one = norm_one_pull(grad_normed_one)
    token_grad = (grad_middle + grad_inputs_part).astype(jnp.bfloat16)
    shares = (
        lax.psum_scatter(grad_gain_one, ("dp", "seq"), scatter_dimension=0, tiled=True),
        lax.psum_scatter(grad_bias_one, ("dp", "seq"), scatter_dimension=0, tiled=True),
        lax.psum_scatter(grad_qw, ("dp", "seq"), scatter_dimension=0, tiled=True),
        lax.psum_scatter(grad_kw, ("dp", "seq"), scatter_dimension=0, tiled=True),
        lax.psum_scatter(grad_vw, ("dp", "seq"), scatter_dimension=0, tiled=True),
        lax.psum_scatter(grad_outw, ("dp", "seq"), scatter_dimension=0, tiled=True),
        lax.psum_scatter(grad_gain_two, ("dp", "seq"), scatter_dimension=0, tiled=True),
        lax.psum_scatter(grad_bias_two, ("dp", "seq"), scatter_dimension=0, tiled=True),
        lax.psum_scatter(grad_up, ("dp", "seq"), scatter_dimension=0, tiled=True),
        lax.psum_scatter(grad_down, ("dp", "seq"), scatter_dimension=0, tiled=True),
    )
    return (
        mixed[None],
        token_grad[None],
        shares[0],
        shares[1],
        shares[2],
        shares[3],
        shares[4],
        shares[5],
        shares[6],
        shares[7],
        shares[8],
        shares[9],
    )


def solution(mesh):
    in_specs = (
        P("dp", "seq", None),
        P("dp", None),
        P(("dp", "seq")),
        P(("dp", "seq")),
        P(("dp", "seq"), None),
        P(("dp", "seq"), None),
        P(("dp", "seq"), None),
        P(("dp", "seq"), None),
        P(("dp", "seq")),
        P(("dp", "seq")),
        P(("dp", "seq"), None),
        P(("dp", "seq"), None),
        P("dp", "seq", None),
    )
    out_specs = (
        P("dp", "seq", None),
        P("dp", "seq", None),
        P(("dp", "seq")),
        P(("dp", "seq")),
        P(("dp", "seq"), None),
        P(("dp", "seq"), None),
        P(("dp", "seq"), None),
        P(("dp", "seq"), None),
        P(("dp", "seq")),
        P(("dp", "seq")),
        P(("dp", "seq"), None),
        P(("dp", "seq"), None),
    )
    return jax.shard_map(body, mesh=mesh, in_specs=in_specs, out_specs=out_specs, check_vma=False)
```

profile of v0, /device:TPU:0, one launch (start us, length us, event | category | flops | bytes accessed | tf_op | source)
XLA Modules:
  0.0 1901.4 jit_solution(16987439523870152397)
XLA Ops:
  12.8 42.2 %all-reduce.9 = (bf16[1024]{0:T(1024)(128)(2,1)S(1)}, bf16[1024]{0:T(1024)(128)(2,1)S(1)}, bf16[1024]{0:T(1024)(128)(2,1)S(1)}, bf16[1024]{0:T(1024)(128)(2,1)S(1)}) all-reduce(bf16[1024]{0:T(1024)(128)(2,1)S(1)} %dynamic-update-slice.1, bf16[1024]{0:T(1024)(128)(2,1)S(1)} %dynamic-update-slice, ...), channel_id=1, replica_groups=mesh['dp'=16,'seq'=2] {'dp','seq'}, use_global_device_ids=true, to_apply=%add.1 | all-reduce | flops 4096 | bytes 16384
  58.9 11.1 all-gather.15.cloned.1.call-done
  75.7 52.4 %all-gather.9.cloned.1.call-done = bf16[1024,1024]{1,0:T(8,128)(2,1)} async-done(((bf16[32,1024]{1,0:T(8,128)(2,1)}), bf16[1024,1024]{1,0:T(8,128)(2,1)}) %all-gather.9.cloned.1.call-update) | async-done | bytes 2097168 | tf_op jit(solution)/shard_map/all_gather | solution.py:57
  141.3 45.0 %all-gather.13.cloned.1.call-done = bf16[1024,1024]{1,0:T(8,128)(2,1)} async-done(((bf16[32,1024]{1,0:T(8,128)(2,1)}), bf16[1024,1024]{1,0:T(8,128)(2,1)}) %all-gather.13.cloned.1.call-update) | async-done | bytes 2097168 | tf_op jit(solution)/shard_map/all_gather | solution.py:55
  200.2 6.5 copy.76
  206.7 10.3 all-gather.11.cloned.1.call-done
  217.1 6.5 copy.75
  225.1 172.9 %while.26 = (s32[]{:T(128)}, bf16[8,512,256]{1,2,0:T(8,128)(2,1)}, f32[8,4,512,1]{2,1,3,0:T(4,128)}, s32[8]{0:T(128)S(1)}, bf16[4,2048,256]{1,2,0:T(8,128)(2,1)}...) while((s32[]{:T(128)}, bf16[8,512,256]{1,2,0:T(8,128)(2,1)}, ...), condition=%wide.region_5.6_spmd, body=%wide.region_2.5_spmd.sunk | while | flops 1125120000 | bytes 62470396 | solution.py:141
  415.2 47.2 %multiply_convert_fusion.1 = (bf16[1024,4096]{1,0:T(8,128)(2,1)}, f32[1024,4096]{1,0:T(8,128)}, f32[1024,4096]{1,0:T(8,128)}) fusion(bf16[1024,4096]{1,0:T(8,128)(2,1)} %all-gather.21.cloned.1.call-done, bf16[1024,1024]{0,1:T(8,128)(2,1)S(1)} %add_convert_fusion.5.clone.4), kind=kOutput, calls=%fused_computation.38 | convolution fusion | flops 8862564352 | bytes 52428800 | tf_op jit(solution)/shard_map/dot_general | solution.py:145
  462.3 23.4 %add_convert_fusion = bf16[1024,4096]{1,0:T(8,128)(2,1)} fusion(f32[1024,4096]{1,0:T(8,128)} %get-tuple-element.238, f32[1024,4096]{1,0:T(8,128)} %get-tuple-element.249, bf16[4096,1024]{1,0:T(8,128)(2,1)} %all-gather.23.cloned.1.call-done, bf16[1,1024,1024]{2,1,0:T(8,128)(2,1)} %param.29), kind=kOutput, calls=%fused_computation.37 | convolution fusion | flops 8648654848 | bytes 52428800 | tf_op jit(solution)/shard_map/dot_general | solution.py:26
  485.7 15.7 fusion.66
  528.8 393.5 %while.27 = (s32[]{:T(128)}, bf16[8,512,256]{1,2,0:T(8,128)(2,1)}, f32[8,2048,256]{1,2,0:T(8,128)}, f32[8,2048,256]{1,2,0:T(8,128)}, s32[8]{0:T(128)S(1)}, /*ind...) while((s32[]{:T(128)}, bf16[8,512,256]{1,2,0:T(8,128)(2,1)}, ...), condition=%wide.region_12.13_spmd, body=%wide.region_10.12_spmd.sunk | while | flops 2749102080 | bytes 168631056 | solution.py:210
  544.9 6.1 fusion.146
  551.0 11.6 multiply_reduce_fusion.5
  562.5 8.4 multiply_convert_fusion.3
  594.0 6.1 fusion.146
  600.1 11.6 multiply_reduce_fusion.5
  611.7 8.4 multiply_convert_fusion.3
  643.0 6.1 fusion.146
  649.2 11.6 multiply_reduce_fusion.5
  660.7 8.4 multiply_convert_fusion.3
  692.2 6.1 fusion.146
  698.3 11.6 multiply_reduce_fusion.5
  709.9 8.4 multiply_convert_fusion.3
  741.4 6.1 fusion.146
  747.5 11.6 multiply_reduce_fusion.5
  759.0 8.4 multiply_convert_fusion.3
  790.6 6.1 fusion.146
  796.7 11.6 multiply_reduce_fusion.5
  808.2 8.4 multiply_convert_fusion.3
  845.8 11.6 multiply_reduce_fusion.5
  857.4 8.4 multiply_convert_fusion.3
  888.8 6.1 fusion.146
  894.9 11.6 multiply_reduce_fusion.5
  906.4 8.4 multiply_convert_fusion.3
  922.3 10.9 reduce_sum.151
  933.3 11.3 reduce_sum.155
  977.9 16.7 fusion.53
  995.1 16.3 fusion.40
  1011.4 15.5 fusion.35
  1045.4 40.8 %all-reduce.8 = (f32[1024]{0:T(1024)S(1)}, f32[1024]{0:T(1024)S(1)}, f32[1024]{0:T(1024)S(1)}, f32[1024]{0:T(1024)S(1)}) all-reduce(f32[1024]{0:T(1024)S(1)} %get-tuple-element.177, f32[1024]{0:T(1024)S(1)} %get-tuple-element.179, f32[1024]{0:T(1024)S(1)} %copy-done.44, ...), channel_id=4, replica_groups=mesh['dp'=16,'seq'=2] {'dp','seq'}, use_global_device_ids=true, to_apply=%region_20.21.clone | all-reduce | flops 4096 | bytes 32768
  1088.5 6.3 fusion.36
  1098.7 8.6 reduce-scatter.19.cloned.1.call-done
  1107.3 139.4 %reduce-scatter.13.cloned.1.call-done = f32[32,1024]{1,0:T(8,128)} async-done(((f32[1024,1024]{1,0:T(8,128)}), f32[32,1024]{1,0:T(8,128)}) %reduce-scatter.13.cloned.1.call-update) | async-done | bytes 131088 | tf_op jit(solution)/shard_map/reduce_scatter | solution.py:251
  1246.8 139.6 %reduce-scatter.15.cloned.1.call-done = f32[32,1024]{1,0:T(8,128)} async-done(((f32[1024,1024]{1,0:T(8,128)}), f32[32,1024]{1,0:T(8,128)}) %reduce-scatter.15.cloned.1.call-update) | async-done | bytes 131088 | tf_op jit(solution)/shard_map/reduce_scatter | solution.py:252
  1386.3 139.4 %reduce-scatter.17.cloned.1.call-done = f32[32,1024]{1,0:T(8,128)} async-done(((f32[1024,1024]{1,0:T(8,128)}), f32[32,1024]{1,0:T(8,128)}) %reduce-scatter.17.cloned.1.call-update) | async-done | bytes 131088 | tf_op jit(solution)/shard_map/reduce_scatter | solution.py:253
  1525.8 181.4 %reduce-scatter.21.cloned.1.call-done = f32[32,4096]{1,0:T(8,128)} async-done(((f32[1024,4096]{1,0:T(8,128)}), f32[32,4096]{1,0:T(8,128)}) %reduce-scatter.21.cloned.1.call-update) | async-done | bytes 524304 | tf_op jit(solution)/shard_map/reduce_scatter | solution.py:257
  1707.2 187.4 %reduce-scatter.23.cloned.1.call-done = f32[128,1024]{1,0:T(8,128)} async-done(((f32[4096,1024]{1,0:T(8,128)}), f32[128,1024]{1,0:T(8,128)}) %reduce-scatter.23.cloned.1.call-update) | async-done | bytes 524304 | tf_op jit(solution)/shard_map/reduce_scatter | solution.py:258
  (520 shorter events, 445.4 us)
Async XLA Ops:
  7.2 62.9 %all-gather.15.cloned.1.call-start = ((), (), s32[]{:S(2)}) async-start(), calls=%async_computation.11 | async-start | bytes 2162688 | tf_op jit(solution)/shard_map/all_gather | solution.py:56
  7.9 120.2 %all-gather.9.cloned.1.call-start = ((), (), s32[]{:S(2)}) async-start(), calls=%async_computation.8 | async-start | bytes 2162688 | tf_op jit(solution)/shard_map/all_gather | solution.py:57
  8.7 177.6 %all-gather.13.cloned.1.call-start = ((), (), s32[]{:S(2)}) async-start(), calls=%async_computation.10 | async-start | bytes 2162688 | tf_op jit(solution)/shard_map/all_gather | solution.py:55
  9.4 190.8 %all-gather.17.cloned.1.call-start = ((), (), s32[]{:S(2)}) async-start(), calls=%async_computation.12 | async-start | bytes 6291456 | tf_op jit(solution)/shard_map/all_gather | solution.py:83
  55.0 131.3 %copy-start.45 = (f32[1024]{0:T(1024)}, f32[1024]{0:T(1024)S(1)}, u32[]{:S(2)}) copy-start(f32[1024]{0:T(1024)S(1)} %convert_element_type.123) | copy-start | bytes 12292
  55.0 131.3 %copy-start.36 = (f32[1024]{0:T(1024)}, f32[1024]{0:T(1024)S(1)}, u32[]{:S(2)}) copy-start(f32[1024]{0:T(1024)S(1)} %convert_element_type.122) | copy-start | bytes 12292
  57.9 128.4 %copy-start.5 = (bf16[1,1024,1024]{1,2,0:T(8,128)(2,1)}, bf16[1,1024,1024]{1,2,0:T(8,128)(2,1)S(1)}, u32[]{:S(2)}) copy-start(bf16[1,1024,1024]{1,2,0:T(8,128)(2,1)S(1)} %copy.55) | copy-start | bytes 6291460
  58.3 128.0 %copy-start.30 = (f32[1024]{0:T(1024)}, f32[1024]{0:T(1024)S(1)}, u32[]{:S(2)}) copy-start(f32[1024]{0:T(1024)S(1)} %broadcast_multiply_fusion.1) | copy-start | bytes 12292
  58.9 16.8 copy-start.32
  58.9 127.4 %copy-start.38 = (f32[1024]{0:T(1024)}, f32[1024]{0:T(1024)S(1)}, u32[]{:S(2)}) copy-start(f32[1024]{0:T(1024)S(1)} %fusion.51) | copy-start | bytes 12292
  75.7 60.2 %copy-start.18 = (s32[1,2048]{1,0:T(1,128)S(1)}, s32[1,2048]{1,0:T(1,128)}, u32[]{:S(2)}) copy-start(s32[1,2048]{1,0:T(1,128)} %param.18) | copy-start | bytes 24580
  75.7 141.4 %all-gather.11.cloned.1.call-start = ((), (), s32[]{:S(2)}) async-start(), calls=%async_computation.9 | async-start | bytes 6291456 | tf_op jit(solution)/shard_map/all_gather | solution.py:84
  133.8 273.5 %all-gather.19.cloned.1.call-start = ((), (), s32[]{:S(2)}) async-start(), calls=%async_computation.13 | async-start | bytes 2162688 | tf_op jit(solution)/shard_map/all_gather | solution.py:58
  134.3 280.8 %all-gather.21.cloned.1.call-start = ((), (), s32[]{:S(2)}) async-start(), calls=%async_computation.14 | async-start | bytes 8650752 | tf_op jit(solution)/shard_map/all_gather | solution.py:61
  135.1 327.2 %all-gather.23.cloned.1.call-start = ((), (), s32[]{:S(2)}) async-start(), calls=%async_computation.15 | async-start | bytes 8650752 | tf_op jit(solution)/shard_map/all_gather | solution.py:62
  135.8 829.2 %reduce-scatter.9.cloned.1.call-start = ((), (), s32[]{:S(2)}) async-start(), calls=%async_computation.16 | async-start | bytes 6291456 | tf_op jit(solution)/shard_map/reduce_scatter | solution.py:226
  398.0 9.1 copy-start.19
  398.1 9.1 copy-start.53
  398.1 9.1 copy-start.56
  399.4 7.8 copy-start.6
  536.0 8.9 copy-start.11
  537.1 7.8 copy-start.3
  585.1 8.9 copy-start.11
  586.2 7.8 copy-start.3
  634.2 8.9 copy-start.11
  635.2 7.8 copy-start.3
  683.3 8.9 copy-start.11
  684.4 7.8 copy-start.3
  732.5 8.9 copy-start.11
  781.7 8.9 copy-start.11
  782.8 7.8 copy-start.3
  830.8 8.9 copy-start.11
  831.9 7.8 copy-start.3
  879.9 8.9 copy-start.11
  881.0 7.8 copy-start.3
  933.2 37.9 %reduce-scatter.11.cloned.1.call-start = ((), (), s32[]{:S(2)}) async-start(), calls=%async_computation.17 | async-start | bytes 6291456 | tf_op jit(solution)/shard_map/reduce_scatter | solution.py:229
  944.7 162.7 %reduce-scatter.19.cloned.1.call-start = ((), (), s32[]{:S(2)}) async-start(), calls=%async_computation.21 | async-start | bytes 4325376 | tf_op jit(solution)/shard_map/reduce_scatter | solution.py:254
  952.4 294.4 %reduce-scatter.13.cloned.1.call-start = ((), (), s32[]{:S(2)}) async-start(), calls=%async_computation.18 | async-start | bytes 4325376 | tf_op jit(solution)/shard_map/reduce_scatter | solution.py:251
  952.4 7.9 copy-start.7
  952.4 7.9 copy-start.31
  952.4 7.9 copy-start.37
  952.4 7.8 copy-start.39
  952.4 7.8 copy-start.46
  964.8 421.5 %reduce-scatter.15.cloned.1.call-start = ((), (), s32[]{:S(2)}) async-start(), calls=%async_computation.19 | async-start | bytes 4325376 | tf_op jit(solution)/shard_map/reduce_scatter | solution.py:252
  971.1 554.7 %reduce-scatter.17.cloned.1.call-start = ((), (), s32[]{:S(2)}) async-start(), calls=%async_computation.20 | async-start | bytes 4325376 | tf_op jit(solution)/shard_map/reduce_scatter | solution.py:253
  977.3 729.9 %reduce-scatter.21.cloned.1.call-start = ((), (), s32[]{:S(2)}) async-start(), calls=%async_computation.22 | async-start | bytes 17301504 | tf_op jit(solution)/shard_map/reduce_scatter | solution.py:257
  994.7 900.0 %reduce-scatter.23.cloned.1.call-start = ((), (), s32[]{:S(2)}) async-start(), calls=%async_computation.23 | async-start | bytes 17301504 | tf_op jit(solution)/shard_map/reduce_scatter | solution.py:258
  1041.2 47.4 %copy-start.41 = (f32[1024]{0:T(1024)S(1)}, f32[1024]{0:T(1024)}, u32[]{:S(2)}) copy-start(f32[1024]{0:T(1024)} %copy-done.40) | copy-start | bytes 12292
  (76 other events, 238.3 us)
Sparse Core Ops, SparseCore 0:
  10.9 59.1 all-gather.14
  72.9 55.2 all-gather.8
  131.0 55.2 all-gather.12
  187.7 12.5 all-gather.16
  202.2 14.8 all-gather.10
  219.8 57.5 all-gather.18
  280.2 76.4 all-gather.20
  359.5 76.1 all-gather.22
  933.4 13.2 reduce-scatter.8
  948.9 13.3 reduce-scatter.10
  965.1 142.2 reduce-scatter.18
  1110.0 136.6 reduce-scatter.12
  1249.6 136.6 reduce-scatter.14
  1389.0 136.6 reduce-scatter.16
  1528.5 178.6 reduce-scatter.20
  1709.9 184.6 reduce-scatter.22
where the time goes:
time: 1910 us; the launch traced here: 1900 us
  waiting for transfers between devices  919 us (48%)
  matrix products  453 us (24%)
  local copies, waits for them, and re-layouts  200 us (10%)
  other arithmetic  165 us (9%)
  blocking collectives  83 us (4%)
  loops' own time  64.4 us (3%)
    reduce_scatter x1, waiting for transfers between devices, body(): lax.psum_scatter(grad_down, ('dp', 'seq'), scatter_dimension=0, tiled=True)  187 us
    reduce_scatter x1, waiting for transfers between devices, body(): lax.psum_scatter(grad_up, ('dp', 'seq'), scatter_dimension=0, tiled=True)  181 us
    reduce_scatter x1, waiting for transfers between devices, body(): lax.psum_scatter(grad_kw, ('dp', 'seq'), scatter_dimension=0, tiled=True)  140 us
    reduce_scatter x1, waiting for transfers between devices, body(): lax.psum_scatter(grad_vw, ('dp', 'seq'), scatter_dimension=0, tiled=True)  139 us
    reduce_scatter x1, waiting for transfers between devices, body(): lax.psum_scatter(grad_qw, ('dp', 'seq'), scatter_dimension=0, tiled=True)  139 us
    dot_general x8, matrix products, attend_back(): jnp.einsum('qhd,khd->hqk', grad_heads, value_item, preferred_element_type...  92.4 us
    unnamed x2, blocking collectives  83 us
    convert_element_type x8, other arithmetic, attend_back(): grad_scores = (probs * (grad_probs - inner)).astype(jnp.bfloat16)  67.5 us
  transfers between devices with their start and end apart: 16, of which 11 were waited for; matrix products, arithmetic and copies ran while one was open for 20% of the time, Pallas kernels for 0%

commit v1 on v0

v1 whole, which is shorter than its diff:
```python
from functools import partial

import jax
import jax.numpy as jnp
from jax import lax
from jax.experimental import pallas as pl
from jax.experimental.pallas import tpu as pltpu
from jax.sharding import PartitionSpec as P

BF16 = jnp.bfloat16
F32 = jnp.float32
HEAD_DIM = 64
GROUP = 4
GROUP_WIDTH = GROUP * HEAD_DIM
NEG = -1000000000.0
BOTH = ("dp", "seq")
LN_ROWS = 16
ATT_Q = 256
ATT_K = 512
ROWS = 256
FF_COLS = 512


def dot_nn(left, right):
    return lax.dot_general(left, right, (((1,), (0,)), ((), ())), preferred_element_type=F32)


def dot_nt(left, right):
    return lax.dot_general(left, right, (((1,), (1,)), ((), ())), preferred_element_type=F32)


def dot_tn(left, right):
    return lax.dot_general(left, right, (((0,), (0,)), ((), ())), preferred_element_type=F32)


def params(mib):
    return pltpu.CompilerParams(vmem_limit_bytes=mib << 20)


def cost(flops, nbytes):
    return pl.CostEstimate(flops=flops, bytes_accessed=nbytes, transcendentals=0)


def normed(values):
    centre = values - jnp.mean(values, axis=-1, keepdims=True)
    scale = lax.rsqrt(jnp.mean(centre * centre, axis=-1, keepdims=True) + 1e-05)
    return centre * scale, scale


def norm_back(grad, gain_vec, hat, scale):
    inner = grad * gain_vec
    return scale * (
        inner
        - jnp.mean(inner, axis=-1, keepdims=True)
        - hat * jnp.mean(inner * hat, axis=-1, keepdims=True)
    )


def flat(ref):
    value = ref[...]
    return value.reshape(-1, value.shape[-1])


def resident(shape):
    zeros = (0,) * len(shape)
    return pl.BlockSpec(shape, lambda *_: zeros, pipeline_mode=pl.Buffered(1))


def tile_spec(gathered, rows, t):
    devices, _, width = gathered.shape
    return pl.BlockSpec((devices, rows, width), lambda *_: (0, t, 0), pipeline_mode=pl.Buffered(1))


def kv_kernel(x_ref, gain_ref, bias_ref, wk_ref, wv_ref, h_ref, kv_ref):
    hat, _ = normed(x_ref[...].astype(F32))
    low = (hat * gain_ref[...] + bias_ref[...]).astype(BF16)
    h_ref[...] = low
    kv_ref[0] = dot_nn(low, flat(wk_ref)).astype(BF16)
    kv_ref[1] = dot_nn(low, flat(wv_ref)).astype(BF16)


def kv_call(x, gain, bias, gathered, rows):
    n, d = x.shape
    return pl.pallas_call(
        kv_kernel,
        grid=(n // ROWS,),
        in_specs=[
            pl.BlockSpec((ROWS, d), lambda i: (i, 0)),
            resident((1, d)),
            resident((1, d)),
            tile_spec(gathered, rows, 1),
            tile_spec(gathered, rows, 2),
        ],
        out_specs=[
            pl.BlockSpec((ROWS, d), lambda i: (i, 0)),
            pl.BlockSpec((2, ROWS, d), lambda i: (0, i, 0)),
        ],
        out_shape=[jax.ShapeDtypeStruct((n, d), BF16), jax.ShapeDtypeStruct((2, n, d), BF16)],
        compiler_params=params(40),
        cost_estimate=cost(4 * n * d * d, 4 * d * d + 8 * n * d),
        name="kv_proj",
    )(x, gain, bias, gathered, gathered)


def q_kernel(h_ref, wq_ref, q_ref):
    q_ref[...] = (dot_nn(h_ref[...], flat(wq_ref)).astype(BF16).astype(F32) * 0.125).astype(BF16)


def q_call(h, gathered, rows):
    n, d = h.shape
    return pl.pallas_call(
        q_kernel,
        grid=(n // ROWS,),
        in_specs=[pl.BlockSpec((ROWS, d), lambda i: (i, 0)), tile_spec(gathered, rows, 0)],
        out_specs=pl.BlockSpec((ROWS, d), lambda i: (i, 0)),
        out_shape=jax.ShapeDtypeStruct((n, d), BF16),
        compiler_params=params(32),
        cost_estimate=cost(2 * n * d * d, 2 * d * d + 4 * n * d),
        name="q_proj",
    )(h, gathered)


def stack_heads(block):
    lane = lax.broadcasted_iota(jnp.int32, block.shape, 1) // HEAD_DIM
    zero = jnp.zeros_like(block)
    return jnp.concatenate([jnp.where(lane == h, block, zero) for h in range(GROUP)], axis=0)


def head_cols(value, h, width):
    return value[:, h * width : (h + 1) * width]


def head_rows(value, h):
    return value[h * HEAD_DIM : (h + 1) * HEAD_DIM, :]


def attend_kernel(bq, bk, tab, q_ref, ko_ref, vo_ref, kp_ref, vp_ref, sq_ref, so_ref, sp_ref, o_ref, lse_ref):
    i = pl.program_id(1)
    stacked = stack_heads(q_ref[...])
    seg_q = jnp.concatenate([sq_ref[0]] * GROUP, axis=1)

    def over(k_ref, v_ref, s_ref, first, count, state):
        def step(j, carry):
            top, total, acc = carry
            at = pl.multiple_of((first + j) * bk, bk)
            scores = dot_nt(k_ref[0, pl.ds(at, bk), :], stacked)
            scores = jnp.where(s_ref[pl.ds(at, bk), :] == seg_q, scores, NEG)
            new_top = jnp.maximum(top, jnp.max(scores, axis=0, keepdims=True))
            decay = jnp.exp(top - new_top)
            probs = jnp.exp(scores - new_top)
            total = total * decay + jnp.sum(probs, axis=0, keepdims=True)
            low = probs.astype(BF16)
            values = v_ref[0, pl.ds(at, bk), :].T
            acc = tuple(
                acc[h] * head_cols(decay, h, bq) + dot_nn(head_rows(values, h), head_cols(low, h, bq))
                for h in range(GROUP)
            )
            return new_top, total, acc

        return lax.fori_loop(0, count, step, state)

    state = (
        jnp.full((1, GROUP * bq), -jnp.inf, F32),
        jnp.zeros((1, GROUP * bq), F32),
        tuple(jnp.zeros((HEAD_DIM, bq), F32) for _ in range(GROUP)),
    )
    state = over(ko_ref, vo_ref, so_ref, tab[4 * i], tab[4 * i + 1], state)
    top, total, acc = over(kp_ref, vp_ref, sp_ref, tab[4 * i + 2], tab[4 * i + 3], state)
    out = jnp.concatenate([acc[h] / head_cols(total, h, bq) for h in range(GROUP)], axis=0)
    o_ref[...] = out.T.astype(BF16)
    lse_ref[0, 0] = top + jnp.log(total)


def attend_call(tab, q, own, other, seg_q, seg_own, seg_other, bq, bk):
    n, d = q.shape
    groups, blocks = d // GROUP_WIDTH, n // bq
    query = pl.BlockSpec((bq, GROUP_WIDTH), lambda g, i, *_: (i, g))

    def half(which):
        return pl.BlockSpec((1, n, GROUP_WIDTH), lambda g, i, *_: (which, 0, g))

    column = pl.BlockSpec((n, 1), lambda g, i, *_: (0, 0))
    spec = pltpu.PrefetchScalarGridSpec(
        num_scalar_prefetch=1,
        grid=(groups, blocks),
        in_specs=[
            query,
            half(0),
            half(1),
            half(0),
            half(1),
            pl.BlockSpec((1, 1, bq), lambda g, i, *_: (i, 0, 0)),
            column,
            column,
        ],
        out_specs=[query, pl.BlockSpec((1, 1, 1, GROUP * bq), lambda g, i, *_: (g, i, 0, 0))],
    )
    return pl.pallas_call(
        partial(attend_kernel, bq, bk),
        grid_spec=spec,
        out_shape=[
            jax.ShapeDtypeStruct((n, d), BF16),
            jax.ShapeDtypeStruct((groups, blocks, 1, GROUP * bq), F32),
        ],
        compiler_params=params(56),
        cost_estimate=cost(30_000_000_000, 12 * n * d),
        name="attend",
    )(tab, q, own, own, other, other, seg_q, seg_own, seg_other)


def attend_back_kernel(
    bq, bk, tab, q_ref, go_ref, o_ref, ko_ref, vo_ref, kp_ref, vp_ref, sq_ref, so_ref, sp_ref, lse_ref,
    dq_ref, down_ref, dpart_ref, dko, dvo, dkp, dvp,
):
    i = pl.program_id(1)

    @pl.when(i == 0)
    def _():
        for ref in (dko, dvo, dkp, dvp):
            ref[...] = jnp.zeros_like(ref)

    stacked = stack_heads(q_ref[...])
    grad = go_ref[...]
    stacked_grad = stack_heads(grad)
    product = (grad.astype(F32) * o_ref[...].astype(F32)).T
    inner = jnp.concatenate(
        [jnp.sum(head_rows(product, h), axis=0, keepdims=True) for h in range(GROUP)], axis=1
    )
    seg_q = jnp.concatenate([sq_ref[0]] * GROUP, axis=1)
    lse = lse_ref[0, 0]

    def over(k_ref, v_ref, s_ref, dk, dv, first, count, state):
        def step(j, acc):
            at = pl.multiple_of((first + j) * bk, bk)
            keys = k_ref[0, pl.ds(at, bk), :]
            scores = dot_nt(keys, stacked)
            scores = jnp.where(s_ref[pl.ds(at, bk), :] == seg_q, scores, NEG)
            probs = jnp.exp(scores - lse)
            grad_probs = dot_nt(v_ref[0, pl.ds(at, bk), :], stacked_grad)
            grad_scores = (probs * (grad_probs - inner)).astype(BF16)
            dv[pl.ds(at, bk), :] += dot_nn(probs.astype(BF16), stacked_grad)
            dk[pl.ds(at, bk), :] += dot_nn(grad_scores, stacked)
            keys_t = keys.T
            return tuple(
                acc[h] + dot_nn(head_rows(keys_t, h), head_cols(grad_scores, h, bq)) for h in range(GROUP)
            )

        return lax.fori_loop(0, count, step, state)

    state = tuple(jnp.zeros((HEAD_DIM, bq), F32) for _ in range(GROUP))
    state = over(ko_ref, vo_ref, so_ref, dko, dvo, tab[4 * i], tab[4 * i + 1], state)
    state = over(kp_ref, vp_ref, sp_ref, dkp, dvp, tab[4 * i + 2], tab[4 * i + 3], state)
    dq_ref[...] = (jnp.concatenate(state, axis=0).T * 0.125).astype(BF16)

    @pl.when(i == pl.num_programs(1) - 1)
    def _():
        down_ref[0] = dko[...].astype(BF16)
        down_ref[1] = dvo[...].astype(BF16)
        dpart_ref[0] = dkp[...].astype(BF16)
        dpart_ref[1] = dvp[...].astype(BF16)


def attend_back_call(tab, q, grad, out, own, other, seg_q, seg_own, seg_other, lse, bq, bk):
    n, d = q.shape
    groups, blocks = d // GROUP_WIDTH, n // bq
    query = pl.BlockSpec((bq, GROUP_WIDTH), lambda g, i, *_: (i, g))

    def half(which):
        return pl.BlockSpec((1, n, GROUP_WIDTH), lambda g, i, *_: (which, 0, g))

    column = pl.BlockSpec((n, 1), lambda g, i, *_: (0, 0))
    pair = pl.BlockSpec((2, n, GROUP_WIDTH), lambda g, i, *_: (0, 0, g))
    spec = pltpu.PrefetchScalarGridSpec(
        num_scalar_prefetch=1,
        grid=(groups, blocks),
        in_specs=[
            query,
            query,
            query,
            half(0),
            half(1),
            half(0),
            half(1),
            pl.BlockSpec((1, 1, bq), lambda g, i, *_: (i, 0, 0)),
            column,
            column,
            pl.BlockSpec((1, 1, 1, GROUP * bq), lambda g, i, *_: (g, i, 0, 0)),
        ],
        out_specs=[query, pair, pair],
        scratch_shapes=[pltpu.VMEM((n, GROUP_WIDTH), F32)] * 4,
    )
    return pl.pallas_call(
        partial(attend_back_kernel, bq, bk),
        grid_spec=spec,
        out_shape=[
            jax.ShapeDtypeStruct((n, d), BF16),
            jax.ShapeDtypeStruct((2, n, d), BF16),
            jax.ShapeDtypeStruct((2, n, d), BF16),
        ],
        compiler_params=params(56),
        cost_estimate=cost(45_000_000_000, 24 * n * d),
        name="attend_back",
    )(tab, q, grad, out, own, own, other, other, seg_q, seg_own, seg_other, lse)


def mid_kernel(x_ref, o_ref, wo_ref, gain_ref, bias_ref, r_ref, h_ref):
    mid = x_ref[...].astype(F32) + dot_nn(o_ref[...], flat(wo_ref))
    r_ref[...] = mid
    hat, _ = normed(mid)
    h_ref[...] = (hat * gain_ref[...] + bias_ref[...]).astype(BF16)


def mid_call(x, o, gathered, rows, t, gain, bias):
    n, d = x.shape
    row = pl.BlockSpec((ROWS, d), lambda i: (i, 0))
    return pl.pallas_call(
        mid_kernel,
        grid=(n // ROWS,),
        in_specs=[row, row, tile_spec(gathered, rows, t), resident((1, d)), resident((1, d))],
        out_specs=[row, row],
        out_shape=[jax.ShapeDtypeStruct((n, d), F32), jax.ShapeDtypeStruct((n, d), BF16)],
        compiler_params=params(32),
        cost_estimate=cost(2 * n * d * d, 2 * d * d + 10 * n * d),
        name="out_proj",
    )(x, o, gathered, gain, bias)


def mid_back_kernel(gh_ref, r_ref, g_ref, o_ref, wo_ref, gain_ref, gr_ref, go_ref, dwo_ref, dln_ref, acc):
    i = pl.program_id(0)
    hat, scale = normed(r_ref[...])
    grad = gh_ref[...]
    total = g_ref[...].astype(F32) + norm_back(grad, gain_ref[...], hat, scale)
    gr_ref[...] = total
    low = total.astype(BF16)
    go_ref[...] = dot_nt(low, flat(wo_ref)).astype(BF16)
    part = dot_tn(o_ref[...], low)
    dgain = jnp.sum(grad * hat, axis=0, keepdims=True)
    dbias = jnp.sum(grad, axis=0, keepdims=True)

    @pl.when(i == 0)
    def _():
        acc[...] = part
        dln_ref[0:1, :] = dgain
        dln_ref[1:2, :] = dbias

    @pl.when(i > 0)
    def _():
        acc[...] += part
        dln_ref[0:1, :] += dgain
        dln_ref[1:2, :] += dbias

    @pl.when(i == pl.num_programs(0) - 1)
    def _():
        dwo_ref[...] = acc[...].astype(BF16)


def mid_back_call(grad, mid, cot, o, gathered, rows, t, gain):
    n, d = mid.shape
    row = pl.BlockSpec((ROWS, d), lambda i: (i, 0))
    return pl.pallas_call(
        mid_back_kernel,
        grid=(n // ROWS,),
        in_specs=[row, row, row, row, tile_spec(gathered, rows, t), resident((1, d))],
        out_specs=[
            row,
            row,
            pl.BlockSpec((d, d), lambda i: (0, 0)),
            pl.BlockSpec((2, d), lambda i: (0, 0)),
        ],
        out_shape=[
            jax.ShapeDtypeStruct((n, d), F32),
            jax.ShapeDtypeStruct((n, d), BF16),
            jax.ShapeDtypeStruct((d, d), BF16),
            jax.ShapeDtypeStruct((2, d), F32),
        ],
        scratch_shapes=[pltpu.VMEM((d, d), F32)],
        compiler_params=params(48),
        cost_estimate=cost(4 * n * d * d, 4 * d * d + 18 * n * d),
        name="out_proj_back",
    )(grad, mid, cot, o, gathered, gain)


def ffn_kernel(last, h_ref, g_ref, wu_ref, wd_ref, mi_ref, gi_ref, mo_ref, go_ref, dwu_ref, dwd_ref, *rest):
    j = pl.program_id(0)
    h, grad = h_ref[...], g_ref[...]
    wu, wd = flat(wu_ref), flat(wd_ref)
    up = dot_nn(h, wu)
    cdf = 0.5 * (1.0 + lax.erf(up * 0.7071067811865476))
    act = (up * cdf).astype(BF16)
    slope = cdf + up * (jnp.exp(-0.5 * up * up) * 0.3989422804014327)
    gu = (dot_nt(grad, wd) * slope).astype(BF16)
    dwd_ref[...] = dot_tn(act, grad).astype(BF16).reshape(dwd_ref.shape)
    dwu_ref[...] = dot_tn(h, gu).astype(BF16).reshape(dwu_ref.shape)
    mo = rest[0] if last else mo_ref

    @pl.when(j == 0)
    def _():
        mo[...] = mi_ref[...] + dot_nn(act, wd)
        if gi_ref is None:
            go_ref[...] = dot_nt(gu, wu)
        else:
            go_ref[...] = gi_ref[...] + dot_nt(gu, wu)

    @pl.when(j > 0)
    def _():
        mo[...] += dot_nn(act, wd)
        go_ref[...] += dot_nt(gu, wu)

    if last:

        @pl.when(j == pl.num_programs(0) - 1)
        def _():
            mo_ref[...] = mo[...].astype(BF16)


def ffn_call(h, cot, wu, wu_specs, wd, wd_specs, mid, gmid, width, last):
    n, d = h.shape
    steps = width // FF_COLS
    full = resident((n, d))
    const = pl.BlockSpec((n, d), lambda j: (0, 0))
    in_specs = [full, full, wu_specs[0], wd_specs[0], full]
    args = [h, cot, wu, wd, mid]
    aliases = {} if last else {4: 0}
    body = partial(ffn_kernel, last)
    if gmid is None:
        def body(h_ref, g_ref, wu_ref, wd_ref, mi_ref, *refs):
            ffn_kernel(last, h_ref, g_ref, wu_ref, wd_ref, mi_ref, None, *refs)
    else:
        in_specs.append(full)
        args.append(gmid)
        aliases[5] = 1
    return pl.pallas_call(
        body,
        grid=(steps,),
        in_specs=in_specs,
        out_specs=[const, const, wu_specs[1], wd_specs[1]],
        out_shape=[
            jax.ShapeDtypeStruct((n, d), BF16 if last else F32),
            jax.ShapeDtypeStruct((n, d), F32),
            wu_specs[2],
            wd_specs[2],
        ],
        scratch_shapes=[pltpu.VMEM((n, d), F32)] if last else [],
        input_output_aliases=aliases,
        compiler_params=params(60),
        cost_estimate=cost(12 * n * d * width, 8 * d * width + 20 * n * d),
        name="ffn",
    )(*args)


def head_back_kernel(dq_ref, dk_ref, rk_ref, dv_ref, rv_ref, x_ref, gr_ref, wq_ref, wk_ref, wv_ref, gain_ref, tg_ref, dkv_ref, dln_ref):
    i = pl.program_id(0)
    dk = (dk_ref[0].astype(F32) + rk_ref[0].astype(F32)).astype(BF16)
    dv = (dv_ref[0].astype(F32) + rv_ref[0].astype(F32)).astype(BF16)
    dkv_ref[0] = dk
    dkv_ref[1] = dv
    grad = dot_nt(dq_ref[...], flat(wq_ref)) + dot_nt(dk, flat(wk_ref)) + dot_nt(dv, flat(wv_ref))
    hat, scale = normed(x_ref[...].astype(F32))
    tg_ref[...] = (gr_ref[...] + norm_back(grad, gain_ref[...], hat, scale)).astype(BF16)
    dgain = jnp.sum(grad * hat, axis=0, keepdims=True)
    dbias = jnp.sum(grad, axis=0, keepdims=True)

    @pl.when(i == 0)
    def _():
        dln_ref[0:1, :] = dgain
        dln_ref[1:2, :] = dbias

    @pl.when(i > 0)
    def _():
        dln_ref[0:1, :] += dgain
        dln_ref[1:2, :] += dbias


def head_back_call(dq, dkv, rkv, x, gr, gathered, rows, gain):
    n, d = x.shape
    row = pl.BlockSpec((ROWS, d), lambda i: (i, 0))

    def half(which):
        return pl.BlockSpec((1, ROWS, d), lambda i: (which, i, 0))

    return pl.pallas_call(
        head_back_kernel,
        grid=(n // ROWS,),
        in_specs=[
            row,
            half(0),
            half(0),
            half(1),
            half(1),
            row,
            row,
            tile_spec(gathered, rows, 0),
            tile_spec(gathered, rows, 1),
            tile_spec(gathered, rows, 2),
            resident((1, d)),
        ],
        out_specs=[
            row,
            pl.BlockSpec((2, ROWS, d), lambda i: (0, i, 0)),
            pl.BlockSpec((2, d), lambda i: (0, 0)),
        ],
        out_shape=[
            jax.ShapeDtypeStruct((n, d), BF16),
            jax.ShapeDtypeStruct((2, n, d), BF16),
            jax.ShapeDtypeStruct((2, d), F32),
        ],
        compiler_params=params(48),
        cost_estimate=cost(6 * n * d * d, 6 * d * d + 18 * n * d),
        name="qkv_back",
    )(dq, dkv, rkv, dkv, rkv, x, gr, gathered, gathered, gathered, gain)


def qkv_grad_kernel(h_ref, dq_ref, dk_ref, dv_ref, out_ref):
    h = h_ref[...]
    out_ref[0] = dot_tn(h, dq_ref[...]).astype(BF16)
    out_ref[1] = dot_tn(h, dk_ref[0]).astype(BF16)
    out_ref[2] = dot_tn(h, dv_ref[0]).astype(BF16)


def qkv_grad_call(h, dq, dkv):
    n, d = h.shape
    width = 256
    return pl.pallas_call(
        qkv_grad_kernel,
        grid=(d // width,),
        in_specs=[
            resident((n, d)),
            pl.BlockSpec((n, width), lambda j: (0, j)),
            pl.BlockSpec((1, n, width), lambda j: (0, 0, j)),
            pl.BlockSpec((1, n, width), lambda j: (1, 0, j)),
        ],
        out_specs=pl.BlockSpec((3, d, width), lambda j: (0, 0, j)),
        out_shape=jax.ShapeDtypeStruct((3, d, d), BF16),
        compiler_params=params(40),
        cost_estimate=cost(6 * n * d * d, 6 * d * d + 8 * n * d),
        name="qkv_grad",
    )(h, dq, dkv, dkv)


def block_table(seg_full, seg_local, my_index, n, bq, bk):
    first, last = seg_local[::bq], seg_local[bq - 1 :: bq]
    low = jnp.sum((seg_full[None, :] < first[:, None]).astype(jnp.int32), axis=1)
    high = jnp.sum((seg_full[None, :] <= last[:, None]).astype(jnp.int32), axis=1)
    columns = []
    for index in (my_index, 1 - my_index):
        start = jnp.clip(low - index * n, 0, n)
        stop = jnp.clip(high - index * n, 0, n)
        block = start // bk
        columns += [block, jnp.where(stop > start, (stop + bk - 1) // bk - block, 0)]
    return jnp.stack(columns, axis=1).reshape(-1).astype(jnp.int32)


def body(
    tokens,
    segments,
    ln1_gain,
    ln1_bias,
    w_query,
    w_key,
    w_value,
    w_out,
    ln2_gain,
    ln2_bias,
    w_up,
    w_down,
    cotangent,
):
    x = tokens[0]
    n, d = x.shape
    cot = cotangent[0]
    rows = w_query.shape[0]
    devices = d // rows
    hidden = w_up.shape[1]
    per_device = hidden // devices
    parts = 2
    sub = per_device // parts
    width = hidden // parts
    my_index = lax.axis_index("seq")
    seg_full = segments[0]
    seg_local = lax.dynamic_slice_in_dim(seg_full, my_index * n, n)
    seg_other = lax.dynamic_slice_in_dim(seg_full, (1 - my_index) * n, n)
    tab = block_table(seg_full, seg_local, my_index, n, ATT_Q, ATT_K)
    seg_q = seg_local.reshape(n // ATT_Q, 1, ATT_Q)
    seg_own_col, seg_other_col = seg_local[:, None], seg_other[:, None]

    vectors = jnp.concatenate([ln1_gain, ln1_bias, ln2_gain, ln2_bias]).reshape(1, 4 * rows)
    ln_block = jnp.pad(vectors, ((0, LN_ROWS - 1), (0, d - 4 * rows)))
    first_local = jnp.concatenate([w_query, w_key, w_value, ln_block], axis=0)
    up_parts = w_up.reshape(rows, devices, parts, sub).transpose(2, 0, 1, 3).reshape(parts, rows, width // d, d)
    up_parts = up_parts.transpose(0, 2, 1, 3).reshape(parts, (width // d) * rows, d)
    part_local = [
        jnp.concatenate([up_parts[p], w_down[p * sub : (p + 1) * sub]], axis=0) for p in range(parts)
    ]
    part_local[0] = jnp.concatenate([part_local[0], w_out], axis=0)

    def gather(local):
        out = lax.all_gather(local, BOTH, axis=0, tiled=True)
        return out.reshape(devices, local.shape[0], d)

    first = gather(first_local)
    second = [gather(p) for p in part_local]

    aligned = rows % 16 == 0
    if aligned:
        qkv_w, qkv_rows = first, rows
        out_w, out_t, out_rows = second[0], second[0].shape[1] // rows - 1, rows
    else:
        qkv_w = first[:, : 3 * rows].reshape(devices, 3, rows, d).transpose(1, 0, 2, 3).reshape(1, 3 * d, d)
        qkv_rows = d
        out_w, out_t, out_rows = second[0][:, -rows:].reshape(1, d, d), 0, d
    ln = first[:, 3 * rows, : 4 * rows].reshape(devices, 4, rows).transpose(1, 0, 2).reshape(4, 1, d).astype(F32)

    h1, own = kv_call(x, ln[0], ln[1], qkv_w, qkv_rows)
    swap = [(0, 1), (1, 0)]
    other = lax.ppermute(own, "seq", swap)
    q = q_call(h1, qkv_w, qkv_rows)
    attended, lse = attend_call(tab, q, own, other, seg_q, seg_own_col, seg_other_col, ATT_Q, ATT_K)
    mid, h2 = mid_call(x, attended, out_w, out_rows, out_t, ln[2], ln[3])

    up_rows = (width // d) * rows
    group = FF_COLS // sub
    carry, gmid, shares = mid, None, []
    for p in range(parts):
        if aligned:
            per_tile = d // FF_COLS
            wu = wd = second[p]
            wu_specs = (
                pl.BlockSpec((devices, rows, FF_COLS), lambda j: (0, j // per_tile, j % per_tile)),
                pl.BlockSpec((devices, rows, FF_COLS), lambda j: (0, j // per_tile, j % per_tile)),
                jax.ShapeDtypeStruct((devices, up_rows, d), BF16),
            )
            tile = up_rows // sub
            wd_specs = (
                pl.BlockSpec((group, sub, d), lambda j: (j, tile, 0)),
                pl.BlockSpec((group, sub, d), lambda j: (j, 0, 0)),
                jax.ShapeDtypeStruct((devices, sub, d), BF16),
            )
        else:
            wu = second[p][:, :up_rows].reshape(devices, width // d, rows, d).transpose(0, 2, 1, 3).reshape(d, width)
            wd = second[p][:, up_rows : up_rows + sub].reshape(width, d)
            wu_block = pl.BlockSpec((d, FF_COLS), lambda j: (0, j))
            wd_block = pl.BlockSpec((FF_COLS, d), lambda j: (j, 0))
            wu_specs = (wu_block, wu_block, jax.ShapeDtypeStruct((d, width), BF16))
            wd_specs = (wd_block, wd_block, jax.ShapeDtypeStruct((width, d), BF16))
        carry, gmid, dwu, dwd = ffn_call(
            h2, cot, wu, wu_specs, wd, wd_specs, carry, gmid, width, p == parts - 1
        )
        if not aligned:
            dwu = dwu.reshape(devices, rows, width // d, d).transpose(0, 2, 1, 3)
        packed = jnp.concatenate(
            [dwu.reshape(devices, up_rows, d), dwd.reshape(devices, sub, d)], axis=1
        ).reshape(devices * (up_rows + sub), d)
        shares.append(lax.psum_scatter(packed, BOTH, scatter_dimension=0, tiled=True))
    mixed = carry

    grad_mid, grad_att, dwo, dln2 = mid_back_call(gmid, mid, cot, attended, out_w, out_rows, out_t, ln[2])
    dq, dkv, sent = attend_back_call(
        tab, q, grad_att, attended, own, other, seg_q, seg_own_col, seg_other_col, lse, ATT_Q, ATT_K
    )
    received = lax.ppermute(sent, "seq", swap)
    token_grad, dkv, dln1 = head_back_call(dq, dkv, received, x, grad_mid, qkv_w, qkv_rows, ln[0])
    dqkv = qkv_grad_call(h1, dq, dkv)

    dln = jnp.concatenate([dln1, dln2], axis=0).astype(BF16)
    dln = dln.reshape(4, devices, rows).transpose(1, 0, 2).reshape(devices, 1, 4 * rows)
    dln = jnp.pad(dln, ((0, 0), (0, LN_ROWS - 1), (0, d - 4 * rows)))
    dqkv = dqkv.reshape(3, devices, rows, d).transpose(1, 0, 2, 3).reshape(devices, 3 * rows, d)
    packed = jnp.concatenate([dqkv, dwo.reshape(devices, rows, d), dln], axis=1)
    packed = packed.reshape(devices * packed.shape[1], d)
    tail = lax.psum_scatter(packed, BOTH, scatter_dimension=0, tiled=True).astype(F32)
    dln = tail[4 * rows, : 4 * rows].reshape(4, rows)

    up_share = jnp.stack([s[:up_rows] for s in shares]).astype(F32)
    up_share = up_share.reshape(parts, width // d, rows, d).transpose(0, 2, 1, 3).reshape(parts, rows, devices, sub)
    up_share = up_share.transpose(1, 2, 0, 3).reshape(rows, hidden)
    down_share = jnp.concatenate([s[up_rows:] for s in shares], axis=0).astype(F32)
    return (
        mixed[None],
        token_grad[None],
        dln[0],
        dln[1],
        tail[:rows],
        tail[rows : 2 * rows],
        tail[2 * rows : 3 * rows],
        tail[3 * rows : 4 * rows],
        dln[2],
        dln[3],
        up_share,
        down_share,
    )


def solution(mesh):
    row, act, vec = P(BOTH, None), P("dp", "seq", None), P(BOTH)
    in_specs = (act, P("dp", None), vec, vec, row, row, row, row, vec, vec, row, row, act)
    out_specs = (act, act, vec, vec, row, row, row, row, vec, vec, row, row)
    return jax.shard_map(body, mesh=mesh, in_specs=in_specs, out_specs=out_specs, check_vma=False)
```

time: 1910 us -> 759 us (0.40)
  waiting for transfers between devices: 919 us -> 411 us
  matrix products: 453 us -> 0 us
  Pallas kernels: 0 us -> 255 us
  local copies, waits for them, and re-layouts: 200 us -> 43.7 us
  other arithmetic: 165 us -> 29.2 us
  blocking collectives: 83 us -> 0 us
  loops' own time: 64.4 us -> 0 us
    reduce_scatter x8 -> x3, waiting for transfers between devices: 796 us -> 291 us  [the longest x2 151 us: body(): lax.psum_scatter(packed, BOTH, scatter_dimension=0, tiled=True)]
    dot_general x74 -> x0, matrix products: 453 us -> none  [the longest x8 92.4 us: attend_back(): jnp.einsum('qhd,khd->hqk', grad_heads, value_item, preferred_element_type...]
    pallas_call x0 -> x10, Pallas kernels: none -> 255 us  [the longest x2 76.9 us: ffn_call(): pl.pallas_call(body, grid=(steps,), in_specs=in_specs, out_specs=[const,...]
    unnamed x2 -> x0, blocking collectives: 83 us -> none
    dynamic_slice x97 -> x0, local copies, waits for them, and re-layouts: 81.2 us -> none  [the longest x56 35.2 us: body(): lax.map(attend, (query_items, group_ids, block_ids))]
    convert_element_type x14 -> x3, other arithmetic: 70.2 us -> 2.8 us  [the longest x1 1.08 us: body(): lax.psum_scatter(packed, BOTH, scatter_dimension=0, tiled=True).astype(F32)]
    reduce_sum x16 -> x1, other arithmetic: 67.5 us -> 0.23 us  [block_table(): jnp.sum((seg_full[None, :] < first[:, None]).astype(jnp.int32), axis=1)]
    another operation x2 -> x0, loops' own time: 64.4 us -> none  [the longest x1 32.6 us: body(): lax.map(attend_back, (query_items, to_items(grad_attended), log_totals, g...]
  transfers between devices with their start and end apart: 16 -> 8, of which waited for: 11 -> 7; matrix products, arithmetic and copies ran while one was open for 20% -> 4% of each run, Pallas kernels for 0% -> 29%
where the time goes in v1:
time: 759 us; the launch traced here: 755 us
  waiting for transfers between devices  411 us (54%)
  Pallas kernels  255 us (34%)
  local copies, waits for them, and re-layouts  43.7 us (6%)
  other arithmetic  29.2 us (4%)
  between operations  14.6 us (2%)
    reduce_scatter x2, waiting for transfers between devices, body(): lax.psum_scatter(packed, BOTH, scatter_dimension=0, tiled=True)  151 us
    reduce_scatter x1, waiting for transfers between devices, body(): lax.psum_scatter(packed, BOTH, scatter_dimension=0, tiled=True).astype(F32)  140 us
    all_gather x3, waiting for transfers between devices, gather(): out = lax.all_gather(local, BOTH, axis=0, tiled=True)  113 us
    pallas_call x2, Pallas kernels, ffn_call(): pl.pallas_call(body, grid=(steps,), in_specs=in_specs, out_specs=[const,...  76.9 us
    pallas_call x1, Pallas kernels, attend_back_call(): pl.pallas_call(partial(attend_back_kernel, bq, bk), grid_spec=spec, out_s...  72.8 us
    pallas_call x1, Pallas kernels, attend_call(): pl.pallas_call(partial(attend_kernel, bq, bk), grid_spec=spec, out_shape=...  50.4 us
    unnamed x43, local copies, waits for them, and re-layouts  26.5 us
    concatenate x2, other arithmetic, body(): jnp.concatenate([dwu.reshape(devices, up_rows, d), dwd.reshape(devices, s...  16.9 us
  transfers between devices with their start and end apart: 8, of which 7 were waited for; matrix products, arithmetic and copies ran while one was open for 4% of the time, Pallas kernels for 29%

profile of v1, /device:TPU:0, one launch (start us, length us, event | category | flops | bytes accessed | tf_op | source)
XLA Modules:
  0.0 754.7 jit_solution(2235505250380594492)
XLA Ops:
  7.2 0.9 maximum_bitcast_fusion.1
  8.2 1.6 fusion.3
  9.8 1.5 reshape.409
  11.9 1.0 fusion.11
  12.9 1.6 pad_maximum_fusion.2
  15.4 72.3 %all-gather.4.cloned.1.call-done = bf16[3584,1024]{1,0:T(8,128)(2,1)} async-done(((bf16[112,1024]{1,0:T(8,128)(2,1)}), bf16[3584,1024]{1,0:T(8,128)(2,1)}) %all-gather.4.cloned.1.call-update) | async-done | bytes 7340048 | tf_op jit(solution)/shard_map/all_gather | solution.py:597
  87.7 0.9 fusion.4
  88.8 9.5 %kv_proj.1 = (bf16[1024,1024]{1,0:T(8,128)(2,1)S(1)}, bf16[2,1024,1024]{2,1,0:T(8,128)(2,1)}) custom-call(bf16[1024,1024]{1,0:T(8,128)(2,1)S(1)} %bitcast.100, f32[1,1024]{1,0:T(1,128)S(1)} %squeeze.40.gain_ref, f32[1,1024]{1,0:T(1,128)S(1)} %squeeze.41.bias_ref, bf16[32,112,1024]{2,1,0:T(8,128)(2,1)} %bitcast.90, bf16[32,112,1024]{2,1,0:T(8,128)(2,1)} %bitcast.91), custom_call_target="tpu_custom_call" | custom-call | flops 4294967296 | bytes 12582912 | tf_op jit(solution)/shard_map/kv_proj/pallas_call | solution.py:84
  98.4 1.3 copy-done.9
  101.1 1.0 copy.61.sp_ref
  102.1 1.0 copy.60.so_ref
  103.3 3.1 copy-done
  106.4 1.6 copy-done.10
  108.0 3.0 q_proj.1.q_ref
  111.1 1.3 copy-done.12
  112.4 50.4 %attend.1 = (bf16[1024,1024]{1,0:T(8,128)(2,1)}, f32[4,4,1,1024]{3,2,1,0:T(1,128)}) custom-call(s32[16]{0:T(128)} %reshape.405.tab, bf16[1024,1024]{1,0:T(8,128)(2,1)} %copy-done.12, bf16[2,1024,1024]{2,1,0:T(8,128)(2,1)} %get-tuple-element.37.ko_ref.vo_ref, bf16[2,1024,1024]{2,1,0:T(8,128)(2,1)} %get-tuple-element.37.ko_ref.vo_ref, ...), custom_call_target="tpu_custom_call" | custom-call | flops 30000001024 | bytes 12582912 | tf_op jit(solution)/shard_map/attend/pallas_call | solution.py:198
  162.8 13.7 %all-gather.6.cloned.1.call-done = bf16[5120,1024]{1,0:T(8,128)(2,1)} async-done(((bf16[160,1024]{1,0:T(8,128)(2,1)}), bf16[5120,1024]{1,0:T(8,128)(2,1)}) %all-gather.6.cloned.1.call-update) | async-done | bytes 10485776 | tf_op jit(solution)/shard_map/all_gather | solution.py:597
  176.5 4.0 copy-done.1
  180.5 1.6 copy-done.4
  182.1 4.2 out_proj.1
  186.3 1.9 copy-done.3
  188.2 2.0 copy.78.mi_ref
  190.2 38.5 %ffn.2 = (f32[1024,1024]{1,0:T(8,128)}, f32[1024,1024]{1,0:T(8,128)}, bf16[32,64,1024]{2,1,0:T(8,128)(2,1)}, bf16[32,64,1024]{2,1,0:T(8,128)(2,1)}) custom-call(bf16[1024,1024]{1,0:T(8,128)(2,1)} %copy-done.17, bf16[1024,1024]{1,0:T(8,128)(2,1)} %bitcast.110, bf16[32,160,1024]{2,1,0:T(8,128)(2,1)} %bitcast.96, ...), custom_call_target="tpu_custom_call", output_to_operand_aliasing={{0}: (4, {})} | custom-call | flops 25769803776 | bytes 37748736 | tf_op jit(solution)/shard_map/ffn/pallas_call | solution.py:432
  228.6 26.8 %all-gather.8.cloned.1.call-done = bf16[4096,1024]{1,0:T(8,128)(2,1)} async-done(((bf16[128,1024]{1,0:T(8,128)(2,1)}), bf16[4096,1024]{1,0:T(8,128)(2,1)}) %all-gather.8.cloned.1.call-update) | async-done | bytes 8388624 | tf_op jit(solution)/shard_map/all_gather | solution.py:597
  255.5 38.4 %ffn.3 = (bf16[1024,1024]{1,0:T(8,128)(2,1)}, f32[1024,1024]{1,0:T(8,128)}, bf16[32,64,1024]{2,1,0:T(8,128)(2,1)}, bf16[32,64,1024]{2,1,0:T(8,128)(2,1)}) custom-call(bf16[1024,1024]{1,0:T(8,128)(2,1)} %copy-done.17, bf16[1024,1024]{1,0:T(8,128)(2,1)} %bitcast.111, bf16[32,128,1024]{2,1,0:T(8,128)(2,1)} %bitcast.126, ...), custom_call_target="tpu_custom_call", output_to_operand_aliasing={{1}: (5, {})} | custom-call | flops 25769803776 | bytes 37748736 | tf_op jit(solution)/shard_map/ffn/pallas_call | solution.py:432
  293.9 8.4 %pad_maximum_fusion.1 = bf16[32,128,1024]{2,1,0:T(8,128)(2,1)} fusion(bf16[32,64,1024]{2,1,0:T(8,128)(2,1)} %get-tuple-element.59, bf16[32,64,1024]{2,1,0:T(8,128)(2,1)} %get-tuple-element.58), kind=kLoop, calls=%fused_computation.4 | loop fusion | flops 16777216 | bytes 16777216 | tf_op jit(solution)/shard_map/concatenate | solution.py:650
  302.4 13.5 %out_proj_back.1 = (f32[1024,1024]{1,0:T(8,128)}, bf16[1024,1024]{1,0:T(8,128)(2,1)S(1)}, bf16[1024,1024]{1,0:T(8,128)(2,1)S(1)}, f32[2,1024]{1,0:T(2,128)S(1)}) custom-call(f32[1024,1024]{1,0:T(8,128)} %get-tuple-element.44.gh_ref, f32[1024,1024]{1,0:T(8,128)} %copy-done.3, bf16[1024,1024]{1,0:T(8,128)(2,1)} %bitcast.112, ...), custom_call_target="tpu_custom_call" | custom-call | flops 4294967296 | bytes 23068672 | tf_op jit(solution)/shard_map/out_proj_back/pallas_call | solution.py:360
  315.9 1.3 copy-done.5
  317.2 1.3 copy-done.16
  318.5 72.8 %attend_back.1 = (bf16[1024,1024]{1,0:T(8,128)(2,1)}, bf16[2,1024,1024]{2,1,0:T(8,128)(2,1)}, bf16[2,1024,1024]{2,1,0:T(8,128)(2,1)}) custom-call(s32[16]{0:T(128)} %reshape.405.tab, bf16[1024,1024]{1,0:T(8,128)(2,1)} %copy-done.12, bf16[1024,1024]{1,0:T(8,128)(2,1)} %copy-done.16, bf16[1024,1024]{1,0:T(8,128)(2,1)} %get-tuple-element.38.o_ref, ...), custom_call_target="tpu_custom_call" | custom-call | flops 44999999488 | bytes 25165824 | tf_op jit(solution)/shard_map/attend_back/pallas_call | solution.py:292
  391.7 7.3 collective-permute-done.1.rk_ref.rv_ref
  398.9 1.6 copy-done.7
  400.5 14.8 %qkv_back.1 = (bf16[1024,1024]{1,0:T(8,128)(2,1)}, bf16[2,1024,1024]{2,1,0:T(8,128)(2,1)}, f32[2,1024]{1,0:T(2,128)S(1)}) custom-call(bf16[1024,1024]{1,0:T(8,128)(2,1)S(1)} %copy-done.7, bf16[2,1024,1024]{2,1,0:T(8,128)(2,1)} %get-tuple-element.48.dk_ref.dv_ref, bf16[2,1024,1024]{2,1,0:T(8,128)(2,1)} %collective-permute-done.1.rk_ref.rv_ref, ...), custom_call_target="tpu_custom_call" | custom-call | flops 6442450944 | bytes 25165824 | tf_op jit(solution)/shard_map/qkv_back/pallas_call | solution.py:481
  415.5 1.6 copy-done.8
  417.1 1.6 copy-done.11
  418.7 2.3 copy-done.15
  421.0 9.6 %qkv_grad.1 = bf16[3,1024,1024]{2,1,0:T(8,128)(2,1)} custom-call(bf16[1024,1024]{1,0:T(8,128)(2,1)S(1)} %copy-done.11, bf16[1024,1024]{1,0:T(8,128)(2,1)S(1)} %copy-done.8, bf16[2,1024,1024]{2,1,0:T(8,128)(2,1)S(1)} %copy-done.15, bf16[2,1024,1024]{2,1,0:T(8,128)(2,1)S(1)} %copy-done.15), custom_call_target="tpu_custom_call" | custom-call | flops 6442450944 | bytes 14680064 | tf_op jit(solution)/shard_map/qkv_grad/pallas_call | solution.py:523
  430.6 3.7 copy.67
  434.3 4.1 fusion.1
  438.7 8.5 %pad_maximum_fusion = bf16[32,128,1024]{2,1,0:T(8,128)(2,1)} fusion(bf16[32,64,1024]{2,1,0:T(8,128)(2,1)} %get-tuple-element.57, bf16[32,64,1024]{2,1,0:T(8,128)(2,1)} %get-tuple-element.56), kind=kLoop, calls=%fused_computation.3 | loop fusion | flops 16777216 | bytes 16777216 | tf_op jit(solution)/shard_map/concatenate | solution.py:650
  447.2 3.1 reduce-scatter.8.cloned.1.call-done
  450.4 1.0 fusion.9
  451.5 139.9 %reduce-scatter.4.cloned.1.call-done = bf16[144,1024]{1,0:T(8,128)(2,1)} async-done(((bf16[4608,1024]{1,0:T(8,128)(2,1)}), bf16[144,1024]{1,0:T(8,128)(2,1)}) %reduce-scatter.4.cloned.1.call-update) | async-done | bytes 294928 | tf_op jit(solution)/shard_map/reduce_scatter | solution.py:670
  591.4 1.1 convert_element_type.43
  593.1 148.2 %reduce-scatter.6.cloned.1.call-done = bf16[128,1024]{1,0:T(8,128)(2,1)} async-done(((bf16[4096,1024]{1,0:T(8,128)(2,1)}), bf16[128,1024]{1,0:T(8,128)(2,1)}) %reduce-scatter.6.cloned.1.call-update) | async-done | bytes 262160 | tf_op jit(solution)/shard_map/reduce_scatter | solution.py:653
  741.3 1.0 fusion.8
  744.2 1.8 reshape.424
  746.0 0.8 maximum_convert_fusion
  (80 shorter events, 7.8 us)
Async XLA Ops:
  7.2 81.7 %copy-start.2 = (bf16[1,1024,1024]{2,1,0:T(8,128)(2,1)S(1)}, bf16[1,1024,1024]{2,1,0:T(8,128)(2,1)}, u32[]{:S(2)}) copy-start(bf16[1,1024,1024]{2,1,0:T(8,128)(2,1)} %param.13) | copy-start | bytes 6291460
  7.2 80.5 %all-gather.4.cloned.1.call-start = ((), (), s32[]{:S(2)}) async-start(), calls=%async_computation.3 | async-start | bytes 7569408 | tf_op jit(solution)/shard_map/all_gather | solution.py:597
  9.8 166.7 %all-gather.6.cloned.1.call-start = ((), (), s32[]{:S(2)}) async-start(), calls=%async_computation.4 | async-start | bytes 10813440 | tf_op jit(solution)/shard_map/all_gather | solution.py:597
  14.5 240.9 %all-gather.8.cloned.1.call-start = ((), (), s32[]{:S(2)}) async-start(), calls=%async_computation.5 | async-start | bytes 8650752 | tf_op jit(solution)/shard_map/all_gather | solution.py:597
  15.4 435.0 %reduce-scatter.8.cloned.1.call-start = ((), (), s32[]{:S(2)}) async-start(), calls=%async_computation.8 | async-start | bytes 8650752 | tf_op jit(solution)/shard_map/reduce_scatter | solution.py:653
  88.8 9.6 %copy-start.13 = (f32[1,1024]{1,0:T(1,128)}, f32[1,1024]{1,0:T(1,128)S(1)}, u32[]{:S(2)}) copy-start(f32[1,1024]{1,0:T(1,128)S(1)} %squeeze.40.gain_ref) | copy-start | bytes 12292
  88.8 11.1 %copy-start.19 = (s32[1,2048]{1,0:T(1,128)S(1)}, s32[1,2048]{1,0:T(1,128)}, u32[]{:S(2)}) copy-start(s32[1,2048]{1,0:T(1,128)} %param.14) | copy-start | bytes 24580
  98.4 1.3 copy-start.9
  99.7 12.7 %collective-permute-start = (bf16[2,1024,1024]{2,1,0:T(8,128)(2,1)}, bf16[2,1024,1024]{2,1,0:T(8,128)(2,1)}, u32[]{:S(2)}, u32[]{:S(2)}) collective-permute-start(bf16[2,1024,1024]{2,1,0:T(8,128)(2,1)} %get-tuple-element.37.ko_ref.vo_ref), channel_id=1, source_target_pairs={{0,1},{1,0},{2,3},{3,2},{4,5},{5,4},{6,7},{7,6},{8,9},{9,8},{10,11... | collective-permute-start | bytes 12582920 | tf_op jit(solution)/shard_map/ppermute | solution.py:615
  99.9 11.1 %copy-start.20 = (s32[1,1024]{1,0:T(1,128)}, s32[1,1024]{1,0:T(1,128)S(1)}, u32[]{:S(2)}) copy-start(s32[1,1024]{1,0:T(1,128)S(1)} %get-tuple-element.83) | copy-start | bytes 12292
  103.3 3.1 copy-start
  106.4 1.6 copy-start.10
  111.1 1.3 copy-start.12
  176.5 4.0 copy-start.1
  180.5 1.6 copy-start.4
  186.3 1.9 copy-start.3
  186.3 3.9 copy-start.17
  302.3 289.1 %reduce-scatter.4.cloned.1.call-start = ((), (), s32[]{:S(2)}) async-start(), calls=%async_computation.6 | async-start | bytes 9732096 | tf_op jit(solution)/shard_map/reduce_scatter | solution.py:670
  315.9 1.3 copy-start.5
  317.2 1.3 copy-start.16
  318.5 80.4 %copy-start.14 = (f32[1,1024]{1,0:T(1,128)S(1)}, f32[1,1024]{1,0:T(1,128)}, u32[]{:S(2)}) copy-start(f32[1,1024]{1,0:T(1,128)} %copy-done.13) | copy-start | bytes 12292
  391.4 7.6 %collective-permute-start.1 = (bf16[2,1024,1024]{2,1,0:T(8,128)(2,1)}, bf16[2,1024,1024]{2,1,0:T(8,128)(2,1)}, u32[]{:S(2)}, u32[]{:S(2)}) collective-permute-start(bf16[2,1024,1024]{2,1,0:T(8,128)(2,1)} %get-tuple-element.49), channel_id=1, source_target_pairs={{0,1},{1,0},{2,3},{3,2},{4,5},{5,4},{6,7},{7,6},{8,9},{9,8},{10,11... | collective-permute-start | bytes 12582920 | tf_op jit(solution)/shard_map/ppermute | solution.py:660
  398.9 1.6 copy-start.7
  415.5 1.6 copy-start.8
  417.1 1.6 copy-start.11
  418.7 2.3 copy-start.15
  430.6 3.7 copy-start.6
  438.4 302.9 %reduce-scatter.6.cloned.1.call-start = ((), (), s32[]{:S(2)}) async-start(), calls=%async_computation.7 | async-start | bytes 8650752 | tf_op jit(solution)/shard_map/reduce_scatter | solution.py:653
  591.4 155.4 %copy-start.18 = (bf16[144,1024]{1,0:T(8,128)(2,1)S(1)}, bf16[144,1024]{1,0:T(8,128)(2,1)}, u32[]{:S(2)}) copy-start(bf16[144,1024]{1,0:T(8,128)(2,1)} %reduce-scatter.4.cloned.1.call-done) | copy-start | bytes 884740
Sparse Core Ops, SparseCore 0:
  11.4 76.1 all-gather.3
  91.1 85.4 all-gather.5
  179.4 76.0 all-gather.7
  302.4 147.8 reduce-scatter.7
  456.1 135.2 reduce-scatter.3
  593.6 147.6 reduce-scatter.5

commit v2 on v1

--- a/solution.py
+++ b/solution.py
@@ -260,19 +260,19 @@
         dpart_ref[1] = dvp[...].astype(BF16)
 
 
-def attend_back_call(tab, q, grad, out, own, other, seg_q, seg_own, seg_other, lse, bq, bk):
+def attend_back_call(tab, q, grad, out, own, other, seg_q, seg_own, seg_other, lse, bq, bk, g):
     n, d = q.shape
-    groups, blocks = d // GROUP_WIDTH, n // bq
-    query = pl.BlockSpec((bq, GROUP_WIDTH), lambda g, i, *_: (i, g))
+    blocks = n // bq
+    query = pl.BlockSpec((bq, GROUP_WIDTH), lambda _, i, *__: (i, g))
 
     def half(which):
-        return pl.BlockSpec((1, n, GROUP_WIDTH), lambda g, i, *_: (which, 0, g))
-
-    column = pl.BlockSpec((n, 1), lambda g, i, *_: (0, 0))
-    pair = pl.BlockSpec((2, n, GROUP_WIDTH), lambda g, i, *_: (0, 0, g))
+        return pl.BlockSpec((1, n, GROUP_WIDTH), lambda *_: (which, 0, g))
+
+    column = pl.BlockSpec((n, 1), lambda *_: (0, 0))
+    pair = pl.BlockSpec((2, n, GROUP_WIDTH), lambda *_: (0, 0, 0))
     spec = pltpu.PrefetchScalarGridSpec(
         num_scalar_prefetch=1,
-        grid=(groups, blocks),
+        grid=(1, blocks),
         in_specs=[
             query,
             query,
@@ -281,24 +281,24 @@
             half(1),
             half(0),
             half(1),
-            pl.BlockSpec((1, 1, bq), lambda g, i, *_: (i, 0, 0)),
+            pl.BlockSpec((1, 1, bq), lambda _, i, *__: (i, 0, 0)),
             column,
             column,
-            pl.BlockSpec((1, 1, 1, GROUP * bq), lambda g, i, *_: (g, i, 0, 0)),
+            pl.BlockSpec((1, 1, 1, GROUP * bq), lambda _, i, *__: (g, i, 0, 0)),
         ],
-        out_specs=[query, pair, pair],
+        out_specs=[pl.BlockSpec((bq, GROUP_WIDTH), lambda _, i, *__: (i, 0)), pair, pair],
         scratch_shapes=[pltpu.VMEM((n, GROUP_WIDTH), F32)] * 4,
     )
     return pl.pallas_call(
         partial(attend_back_kernel, bq, bk),
         grid_spec=spec,
         out_shape=[
-            jax.ShapeDtypeStruct((n, d), BF16),
-            jax.ShapeDtypeStruct((2, n, d), BF16),
-            jax.ShapeDtypeStruct((2, n, d), BF16),
+            jax.ShapeDtypeStruct((n, GROUP_WIDTH), BF16),
+            jax.ShapeDtypeStruct((2, n, GROUP_WIDTH), BF16),
+            jax.ShapeDtypeStruct((2, n, GROUP_WIDTH), BF16),
         ],
         compiler_params=params(56),
-        cost_estimate=cost(45_000_000_000, 24 * n * d),
+        cost_estimate=cost(12_000_000_000, 6 * n * d),
         name="attend_back",
     )(tab, q, grad, out, own, own, other, other, seg_q, seg_own, seg_other, lse)
 
@@ -325,7 +325,7 @@
     )(x, o, gathered, gain, bias)
 
 
-def mid_back_kernel(gh_ref, r_ref, g_ref, o_ref, wo_ref, gain_ref, gr_ref, go_ref, dwo_ref, dln_ref, acc):
+def mid_back_kernel(me, gh_ref, r_ref, g_ref, o_ref, wo_ref, gain_ref, gr_ref, go_ref, keep_ref, send_ref, dln_ref, acc):
     i = pl.program_id(0)
     hat, scale = normed(r_ref[...])
     grad = gh_ref[...]
@@ -351,36 +351,64 @@
 
     @pl.when(i == pl.num_programs(0) - 1)
     def _():
-        dwo_ref[...] = acc[...].astype(BF16)
-
-
-def mid_back_call(grad, mid, cot, o, gathered, rows, t, gain):
+        lanes = keep_ref.shape[3]
+        for ref, value in zip(
+            (keep_ref, send_ref), split_pairs(acc[...].astype(BF16), keep_ref.shape[1], me[0]), strict=True
+        ):
+            for t in range(ref.shape[0]):
+                ref[t] = value[:, :, t * lanes : (t + 1) * lanes]
+
+
+def mid_back_call(me, grad, mid, cot, o, gathered, rows, t, gain, groups):
     n, d = mid.shape
-    row = pl.BlockSpec((ROWS, d), lambda i: (i, 0))
-    return pl.pallas_call(
-        mid_back_kernel,
+    row = pl.BlockSpec((ROWS, d), lambda i, *_: (i, 0))
+    share = (d // GROUP_WIDTH, groups, d // (2 * groups), GROUP_WIDTH)
+    spec = pltpu.PrefetchScalarGridSpec(
+        num_scalar_prefetch=1,
         grid=(n // ROWS,),
         in_specs=[row, row, row, row, tile_spec(gathered, rows, t), resident((1, d))],
         out_specs=[
             row,
             row,
-            pl.BlockSpec((d, d), lambda i: (0, 0)),
-            pl.BlockSpec((2, d), lambda i: (0, 0)),
+            pl.BlockSpec(share, lambda *_: (0, 0, 0, 0)),
+            pl.BlockSpec(share, lambda *_: (0, 0, 0, 0)),
+            pl.BlockSpec((2, d), lambda *_: (0, 0)),
         ],
+        scratch_shapes=[pltpu.VMEM((d, d), F32)],
+    )
+    return pl.pallas_call(
+        mid_back_kernel,
+        grid_spec=spec,
         out_shape=[
             jax.ShapeDtypeStruct((n, d), F32),
             jax.ShapeDtypeStruct((n, d), BF16),
-            jax.ShapeDtypeStruct((d, d), BF16),
+            jax.ShapeDtypeStruct(share, BF16),
+            jax.ShapeDtypeStruct(share, BF16),
             jax.ShapeDtypeStruct((2, d), F32),
         ],
-        scratch_shapes=[pltpu.VMEM((d, d), F32)],
         compiler_params=params(48),
         cost_estimate=cost(4 * n * d * d, 4 * d * d + 18 * n * d),
         name="out_proj_back",
-    )(grad, mid, cot, o, gathered, gain)
-
-
-def ffn_kernel(last, h_ref, g_ref, wu_ref, wd_ref, mi_ref, gi_ref, mo_ref, go_ref, dwu_ref, dwd_ref, *rest):
+    )(me, grad, mid, cot, o, gathered, gain)
+
+
+def split_pairs(value, groups, my_index):
+    rows = value.shape[0] // (2 * groups)
+    pairs = value.reshape(groups, 2, rows, value.shape[1])
+    even, odd = pairs[:, 0], pairs[:, 1]
+    first = my_index == 0
+    return jnp.where(first, even, odd), jnp.where(first, odd, even)
+
+
+def ffn_kernel(last, first, aligned, me, *refs):
+    h_ref, g_ref, wu_ref, wd_ref, mi_ref = refs[:5]
+    refs = refs[5:]
+    gi_ref = None
+    if not first:
+        gi_ref, refs = refs[0], refs[1:]
+    mo_ref, go_ref = refs[:2]
+    refs = refs[2:]
+    grads, rest = (refs[:4], refs[4:]) if aligned else (refs[:2], refs[2:])
     j = pl.program_id(0)
     h, grad = h_ref[...], g_ref[...]
     wu, wd = flat(wu_ref), flat(wd_ref)
@@ -389,14 +417,23 @@
     act = (up * cdf).astype(BF16)
     slope = cdf + up * (jnp.exp(-0.5 * up * up) * 0.3989422804014327)
     gu = (dot_nt(grad, wd) * slope).astype(BF16)
-    dwd_ref[...] = dot_tn(act, grad).astype(BF16).reshape(dwd_ref.shape)
-    dwu_ref[...] = dot_tn(h, gu).astype(BF16).reshape(dwu_ref.shape)
+    dwd = dot_tn(act, grad).astype(BF16)
+    dwu = dot_tn(h, gu).astype(BF16)
+    if aligned:
+        my_index = me[0]
+        grads[0][...], grads[1][...] = split_pairs(dwu, grads[0].shape[0], my_index)
+        for ref, value in zip(grads[2:], split_pairs(dwd, grads[2].shape[1], my_index), strict=True):
+            for t in range(ref.shape[0]):
+                ref[t] = value[:, t * ref.shape[2] : (t + 1) * ref.shape[2]]
+    else:
+        grads[0][...] = dwu
+        grads[1][...] = dwd
     mo = rest[0] if last else mo_ref
 
     @pl.when(j == 0)
     def _():
         mo[...] = mi_ref[...] + dot_nn(act, wd)
-        if gi_ref is None:
+        if first:
             go_ref[...] = dot_nt(gu, wu)
         else:
             go_ref[...] = gi_ref[...] + dot_nt(gu, wu)
@@ -413,48 +450,74 @@
             mo_ref[...] = mo[...].astype(BF16)
 
 
-def ffn_call(h, cot, wu, wu_specs, wd, wd_specs, mid, gmid, width, last):
+def ffn_call(me, h, cot, wu, wd, mid, gmid, grad_specs, width, last, aligned):
     n, d = h.shape
-    steps = width // FF_COLS
     full = resident((n, d))
-    const = pl.BlockSpec((n, d), lambda j: (0, 0))
-    in_specs = [full, full, wu_specs[0], wd_specs[0], full]
-    args = [h, cot, wu, wd, mid]
-    aliases = {} if last else {4: 0}
-    body = partial(ffn_kernel, last)
-    if gmid is None:
-        def body(h_ref, g_ref, wu_ref, wd_ref, mi_ref, *refs):
-            ffn_kernel(last, h_ref, g_ref, wu_ref, wd_ref, mi_ref, None, *refs)
-    else:
+    const = pl.BlockSpec((n, d), lambda j, *_: (0, 0))
+    in_specs = [full, full, wu[1], wd[1], full]
+    args = [h, cot, wu[0], wd[0], mid]
+    aliases = {} if last else {5: 0}
+    if gmid is not None:
         in_specs.append(full)
         args.append(gmid)
-        aliases[5] = 1
+        aliases[6] = 1
+    spec = pltpu.PrefetchScalarGridSpec(
+        num_scalar_prefetch=1,
+        grid=(width // FF_COLS,),
+        in_specs=in_specs,
+        out_specs=[const, const] + [g[0] for g in grad_specs],
+        scratch_shapes=[pltpu.VMEM((n, d), F32)] if last else [],
+    )
     return pl.pallas_call(
-        body,
-        grid=(steps,),
-        in_specs=in_specs,
-        out_specs=[const, const, wu_specs[1], wd_specs[1]],
+        partial(ffn_kernel, last, gmid is None, aligned),
+        grid_spec=spec,
         out_shape=[
             jax.ShapeDtypeStruct((n, d), BF16 if last else F32),
             jax.ShapeDtypeStruct((n, d), F32),
-            wu_specs[2],
-            wd_specs[2],
-        ],
-        scratch_shapes=[pltpu.VMEM((n, d), F32)] if last else [],
+        ]
+        + [g[1] for g in grad_specs],
         input_output_aliases=aliases,
         compiler_params=params(60),
         cost_estimate=cost(12 * n * d * width, 8 * d * width + 20 * n * d),
         name="ffn",
-    )(*args)
-
-
-def head_back_kernel(dq_ref, dk_ref, rk_ref, dv_ref, rv_ref, x_ref, gr_ref, wq_ref, wk_ref, wv_ref, gain_ref, tg_ref, dkv_ref, dln_ref):
+    )(me, *args)
+
+
+def qkv_grad_kernel(groups, me, h_ref, dq_ref, dkv_ref, rkv_ref, keep_ref, send_ref, sum_ref):
+    h = h_ref[...]
+    my_index = me[0]
+    keep_ref[0], send_ref[0] = split_pairs(dot_tn(h, dq_ref[...]).astype(BF16), groups, my_index)
+    for t in range(2):
+        grad = (dkv_ref[t].astype(F32) + rkv_ref[t].astype(F32)).astype(BF16)
+        sum_ref[t] = grad
+        keep_ref[t + 1], send_ref[t + 1] = split_pairs(dot_tn(h, grad).astype(BF16), groups, my_index)
+
+
+def qkv_grad_call(me, h, dq, dkv, rkv, groups):
+    n, d = h.shape
+    width = dq.shape[1]
+    rows = d // (2 * groups)
+    whole = pl.BlockSpec(memory_space=pltpu.VMEM)
+    out = jax.ShapeDtypeStruct((3, groups, rows, width), BF16)
+    return pl.pallas_call(
+        partial(qkv_grad_kernel, groups),
+        in_specs=[pl.BlockSpec(memory_space=pltpu.SMEM)] + [whole] * 4,
+        out_specs=[whole] * 3,
+        out_shape=[out, out, jax.ShapeDtypeStruct((2, n, width), BF16)],
+        compiler_params=params(40),
+        cost_estimate=cost(6 * n * d * width, 6 * d * width + 2 * n * d + 8 * n * width),
+        name="qkv_grad",
+    )(me, h, dq, dkv, rkv)
+
+
+def head_back_kernel(count, *refs):
+    dqs, dkvs = refs[:count], refs[count : 2 * count]
+    x_ref, gr_ref, wq_ref, wk_ref, wv_ref, gain_ref, tg_ref, dln_ref = refs[2 * count :]
     i = pl.program_id(0)
-    dk = (dk_ref[0].astype(F32) + rk_ref[0].astype(F32)).astype(BF16)
-    dv = (dv_ref[0].astype(F32) + rv_ref[0].astype(F32)).astype(BF16)
-    dkv_ref[0] = dk
-    dkv_ref[1] = dv
-    grad = dot_nt(dq_ref[...], flat(wq_ref)) + dot_nt(dk, flat(wk_ref)) + dot_nt(dv, flat(wv_ref))
+    dq = jnp.concatenate([r[...] for r in dqs], axis=1)
+    dk = jnp.concatenate([r[0] for r in dkvs], axis=1)
+    dv = jnp.concatenate([r[1] for r in dkvs], axis=1)
+    grad = dot_nt(dq, flat(wq_ref)) + dot_nt(dk, flat(wk_ref)) + dot_nt(dv, flat(wv_ref))
     hat, scale = normed(x_ref[...].astype(F32))
     tg_ref[...] = (gr_ref[...] + norm_back(grad, gain_ref[...], hat, scale)).astype(BF16)
     dgain = jnp.sum(grad * hat, axis=0, keepdims=True)
@@ -471,22 +534,16 @@
         dln_ref[1:2, :] += dbias
 
 
-def head_back_call(dq, dkv, rkv, x, gr, gathered, rows, gain):
+def head_back_call(dqs, dkvs, x, gr, gathered, rows, gain):
     n, d = x.shape
     row = pl.BlockSpec((ROWS, d), lambda i: (i, 0))
-
-    def half(which):
-        return pl.BlockSpec((1, ROWS, d), lambda i: (which, i, 0))
-
+    width = dqs[0].shape[1]
     return pl.pallas_call(
-        head_back_kernel,
+        partial(head_back_kernel, len(dqs)),
         grid=(n // ROWS,),
-        in_specs=[
-            row,
-            half(0),
-            half(0),
-            half(1),
-            half(1),
+        in_specs=[pl.BlockSpec((ROWS, width), lambda i: (i, 0))] * len(dqs)
+        + [pl.BlockSpec((2, ROWS, width), lambda i: (0, i, 0))] * len(dkvs)
+        + [
             row,
             row,
             tile_spec(gathered, rows, 0),
@@ -494,47 +551,91 @@
             tile_spec(gathered, rows, 2),
             resident((1, d)),
         ],
-        out_specs=[
-            row,
-            pl.BlockSpec((2, ROWS, d), lambda i: (0, i, 0)),
-            pl.BlockSpec((2, d), lambda i: (0, 0)),
-        ],
-        out_shape=[
-            jax.ShapeDtypeStruct((n, d), BF16),
-            jax.ShapeDtypeStruct((2, n, d), BF16),
-            jax.ShapeDtypeStruct((2, d), F32),
-        ],
+        out_specs=[row, pl.BlockSpec((2, d), lambda i: (0, 0))],
+        out_shape=[jax.ShapeDtypeStruct((n, d), BF16), jax.ShapeDtypeStruct((2, d), F32)],
         compiler_params=params(48),
-        cost_estimate=cost(6 * n * d * d, 6 * d * d + 18 * n * d),
+        cost_estimate=cost(6 * n * d * d, 6 * d * d + 14 * n * d),
         name="qkv_back",
-    )(dq, dkv, rkv, dkv, rkv, x, gr, gathered, gathered, gathered, gain)
-
-
-def qkv_grad_kernel(h_ref, dq_ref, dk_ref, dv_ref, out_ref):
-    h = h_ref[...]
-    out_ref[0] = dot_tn(h, dq_ref[...]).astype(BF16)
-    out_ref[1] = dot_tn(h, dk_ref[0]).astype(BF16)
-    out_ref[2] = dot_tn(h, dv_ref[0]).astype(BF16)
-
-
-def qkv_grad_call(h, dq, dkv):
-    n, d = h.shape
-    width = 256
-    return pl.pallas_call(
-        qkv_grad_kernel,
-        grid=(d // width,),
-        in_specs=[
-            resident((n, d)),
-            pl.BlockSpec((n, width), lambda j: (0, j)),
-            pl.BlockSpec((1, n, width), lambda j: (0, 0, j)),
-            pl.BlockSpec((1, n, width), lambda j: (1, 0, j)),
-        ],
-        out_specs=pl.BlockSpec((3, d, width), lambda j: (0, 0, j)),
-        out_shape=jax.ShapeDtypeStruct((3, d, d), BF16),
-        compiler_params=params(40),
-        cost_estimate=cost(6 * n * d * d, 6 * d * d + 8 * n * d),
-        name="qkv_grad",
-    )(h, dq, dkv, dkv)
+    )(*dqs, *dkvs, x, gr, gathered, gathered, gathered, gain)
+
+
+class Term:
+    def __init__(self, array, axes, first=0, count=None):
+        self.array, self.axes, self.first = array, axes, first
+        self.count = array.shape[0] if count is None else count
+
+    def pick(self, mine, settled, flipped):
+        starts, sizes = [self.first], [self.count]
+        for b in self.axes:
+            fixed = b in settled or b == flipped
+            starts.append((1 - mine[b] if b == flipped else mine[b]) if fixed else 0)
+            sizes.append(1 if fixed else 2)
+        shape = self.array.shape[-2:]
+        piece = lax.dynamic_slice(self.array, starts + [0, 0], sizes + list(shape))
+        return piece.reshape((self.count,) + (2,) * sizes[1:].count(2) + shape).astype(F32)
+
+
+class Cube:
+    def __init__(self, dp, index):
+        self.bits = dp.bit_length() - 1
+        self.dp = dp
+        self.mine = [(index >> b) & 1 for b in range(self.bits)]
+
+    def swap(self, array, bit):
+        return lax.ppermute(array, "dp", [(i, i ^ (1 << bit)) for i in range(self.dp)])
+
+    def terms(self, arrays, first=0, count=None):
+        made = []
+        for array in arrays:
+            lead, _, rows, width = array.shape
+            shape = (lead,) + (2,) * self.bits + (rows, width)
+            made.append(Term(array.reshape(shape), list(range(self.bits))[::-1], first, count))
+        return made
+
+    def total(self, terms, settled, flipped=None):
+        out = terms[0].pick(self.mine, settled, flipped)
+        for term in terms[1:]:
+            out = out + term.pick(self.mine, settled, flipped)
+        return out
+
+
+class Scatter:
+    def __init__(self, cube, one, two):
+        self.cube, self.sides, self.step = cube, (one, two), 0
+        self.settled = [[], []]
+        self.last = []
+
+    def advance(self):
+        bit = self.step
+        if self.step < 2:
+            plan = [((0,), bit), ((1,), 1 - bit)]
+        else:
+            plan = [((0, 1), bit)]
+        self.last = []
+        for sides, bit in plan:
+            streams = [(s, stream) for s in sides for stream in self.sides[s]]
+            sent = [self.cube.total(stream, self.settled[s], bit).astype(BF16) for s, stream in streams]
+            got = self.cube.swap(sent[0] if len(sent) == 1 else jnp.concatenate(sent, axis=0), bit)
+            self.last.append(got)
+            at = 0
+            for s, stream in streams:
+                count = stream[0].count
+                axes = [b for b in stream[0].axes if b not in self.settled[s] and b != bit]
+                stream.append(Term(got, axes, at, count))
+                at += count
+            for s in sides:
+                self.settled[s].append(bit)
+        self.step += 1
+        return self
+
+    def finish(self):
+        while self.step < self.cube.bits:
+            self.advance()
+        return [[self.cube.total(stream, self.settled[s]) for stream in self.sides[s]] for s in range(2)]
+
+
+def gate(value, *others):
+    return lax.optimization_barrier((value, others))[0]
 
 
 def block_table(seg_full, seg_local, my_index, n, bq, bk):
@@ -617,72 +718,140 @@
     attended, lse = attend_call(tab, q, own, other, seg_q, seg_own_col, seg_other_col, ATT_Q, ATT_K)
     mid, h2 = mid_call(x, attended, out_w, out_rows, out_t, ln[2], ln[3])
 
+    dp = devices // 2
+    cube = Cube(dp, lax.axis_index("dp"))
+    me = my_index.reshape(1).astype(jnp.int32)
+
+    def exchange(value):
+        return lax.ppermute(value, "seq", swap)
+
+    def halves(value, axis):
+        keep = lax.dynamic_index_in_dim(value, my_index, axis, keepdims=False)
+        send = lax.dynamic_index_in_dim(value, 1 - my_index, axis, keepdims=False)
+        return keep, send
+
     up_rows = (width // d) * rows
+    tiles = width // d
     group = FF_COLS // sub
-    carry, gmid, shares = mid, None, []
+    carry, gmid, ffn, crossed = mid, None, [], []
     for p in range(parts):
         if aligned:
             per_tile = d // FF_COLS
-            wu = wd = second[p]
-            wu_specs = (
-                pl.BlockSpec((devices, rows, FF_COLS), lambda j: (0, j // per_tile, j % per_tile)),
-                pl.BlockSpec((devices, rows, FF_COLS), lambda j: (0, j // per_tile, j % per_tile)),
-                jax.ShapeDtypeStruct((devices, up_rows, d), BF16),
+            tile = up_rows // sub
+            wu = (second[p], pl.BlockSpec((devices, rows, FF_COLS), lambda j, *_: (0, j // per_tile, j % per_tile)))
+            wd = (second[p], pl.BlockSpec((group, sub, d), lambda j, *_: (j, tile, 0)))
+            up_out = (
+                pl.BlockSpec((None, dp, rows, FF_COLS), lambda j, *_: (j // per_tile, 0, 0, j % per_tile)),
+                jax.ShapeDtypeStruct((tiles, dp, rows, d), BF16),
             )
-            tile = up_rows // sub
-            wd_specs = (
-                pl.BlockSpec((group, sub, d), lambda j: (j, tile, 0)),
-                pl.BlockSpec((group, sub, d), lambda j: (j, 0, 0)),
-                jax.ShapeDtypeStruct((devices, sub, d), BF16),
+            down_out = (
+                pl.BlockSpec((tiles, group // 2, rows, d), lambda j, *_: (0, j, 0, 0)),
+                jax.ShapeDtypeStruct((tiles, dp, rows, d), BF16),
             )
+            grad_specs = [up_out, up_out, down_out, down_out]
         else:
-            wu = second[p][:, :up_rows].reshape(devices, width // d, rows, d).transpose(0, 2, 1, 3).reshape(d, width)
-            wd = second[p][:, up_rows : up_rows + sub].reshape(width, d)
-            wu_block = pl.BlockSpec((d, FF_COLS), lambda j: (0, j))
-            wd_block = pl.BlockSpec((FF_COLS, d), lambda j: (j, 0))
-            wu_specs = (wu_block, wu_block, jax.ShapeDtypeStruct((d, width), BF16))
-            wd_specs = (wd_block, wd_block, jax.ShapeDtypeStruct((width, d), BF16))
-        carry, gmid, dwu, dwd = ffn_call(
-            h2, cot, wu, wu_specs, wd, wd_specs, carry, gmid, width, p == parts - 1
+            up_w = second[p][:, :up_rows].reshape(devices, tiles, rows, d).transpose(0, 2, 1, 3).reshape(d, width)
+            down_w = second[p][:, up_rows : up_rows + sub].reshape(width, d)
+            up_block = pl.BlockSpec((d, FF_COLS), lambda j, *_: (0, j))
+            down_block = pl.BlockSpec((FF_COLS, d), lambda j, *_: (j, 0))
+            wu, wd = (up_w, up_block), (down_w, down_block)
+            grad_specs = [
+                (up_block, jax.ShapeDtypeStruct((d, width), BF16)),
+                (down_block, jax.ShapeDtypeStruct((width, d), BF16)),
+            ]
+        carry, gmid, *grads = ffn_call(
+            me, h2, cot, wu, wd, carry, gmid, grad_specs, width, p == parts - 1, aligned
         )
         if not aligned:
-            dwu = dwu.reshape(devices, rows, width // d, d).transpose(0, 2, 1, 3)
-        packed = jnp.concatenate(
-            [dwu.reshape(devices, up_rows, d), dwd.reshape(devices, sub, d)], axis=1
-        ).reshape(devices * (up_rows + sub), d)
-        shares.append(lax.psum_scatter(packed, BOTH, scatter_dimension=0, tiled=True))
+            dwu = grads[0].reshape(dp, 2, rows, tiles, d).transpose(3, 0, 1, 2, 4)
+            dwd = grads[1].reshape(dp, 2, tiles, rows, d).transpose(2, 0, 1, 3, 4)
+            grads = [*halves(dwu, 2), *halves(dwd, 2)]
+        keep_up, send_up, keep_down, send_down = grads
+        crossed.append((exchange(send_up), exchange(send_down)))
+        ffn.append(
+            Scatter(cube, [cube.terms([keep_up, crossed[p][0]])], [cube.terms([keep_down, crossed[p][1]])])
+        )
     mixed = carry
 
-    grad_mid, grad_att, dwo, dln2 = mid_back_call(gmid, mid, cot, attended, out_w, out_rows, out_t, ln[2])
-    dq, dkv, sent = attend_back_call(
-        tab, q, grad_att, attended, own, other, seg_q, seg_own_col, seg_other_col, lse, ATT_Q, ATT_K
-    )
-    received = lax.ppermute(sent, "seq", swap)
-    token_grad, dkv, dln1 = head_back_call(dq, dkv, received, x, grad_mid, qkv_w, qkv_rows, ln[0])
-    dqkv = qkv_grad_call(h1, dq, dkv)
-
-    dln = jnp.concatenate([dln1, dln2], axis=0).astype(BF16)
-    dln = dln.reshape(4, devices, rows).transpose(1, 0, 2).reshape(devices, 1, 4 * rows)
-    dln = jnp.pad(dln, ((0, 0), (0, LN_ROWS - 1), (0, d - 4 * rows)))
-    dqkv = dqkv.reshape(3, devices, rows, d).transpose(1, 0, 2, 3).reshape(devices, 3 * rows, d)
-    packed = jnp.concatenate([dqkv, dwo.reshape(devices, rows, d), dln], axis=1)
-    packed = packed.reshape(devices * packed.shape[1], d)
-    tail = lax.psum_scatter(packed, BOTH, scatter_dimension=0, tiled=True).astype(F32)
-    dln = tail[4 * rows, : 4 * rows].reshape(4, rows)
-
-    up_share = jnp.stack([s[:up_rows] for s in shares]).astype(F32)
-    up_share = up_share.reshape(parts, width // d, rows, d).transpose(0, 2, 1, 3).reshape(parts, rows, devices, sub)
-    up_share = up_share.transpose(1, 2, 0, 3).reshape(rows, hidden)
-    down_share = jnp.concatenate([s[up_rows:] for s in shares], axis=0).astype(F32)
+    early, late = ffn
+    gmid = gate(gmid, crossed[0])
+    early.advance()
+    grad_mid, grad_att, keep_out, send_out, dln2 = mid_back_call(
+        me, gmid, mid, cot, attended, out_w, out_rows, out_t, ln[2], dp
+    )
+    got_out = exchange(send_out)
+    late.advance()
+    dqs, dkvs, qkv_terms, raw = [], [], [], []
+
+    def finish_group(g):
+        dq, dkv, got = raw[g]
+        keep, send, dkv = qkv_grad_call(me, h1, dq, dkv, got, dp)
+        dqs.append(dq)
+        dkvs.append(dkv)
+        qkv_terms.append([keep, exchange(send)])
+        return dkv
+
+    def attend_group(g, *waited):
+        dq, dkv, sent = attend_back_call(
+            gate(tab, *waited), q, grad_att, attended, own, other, seg_q, seg_own_col, seg_other_col, lse,
+            ATT_Q, ATT_K, g,
+        )
+        raw.append((dq, dkv, exchange(sent)))
+
+    attend_group(0, crossed[1])
+    waited = early.last
+    early.advance()
+    attend_group(1, waited)
+    done = finish_group(0)
+    waited = early.last + late.last + [done]
+    early.advance()
+    late.advance()
+    attend_group(2, waited)
+    done = finish_group(1)
+    tail_one = Scatter(
+        cube,
+        [cube.terms(qkv_terms[0]), cube.terms([keep_out, got_out], 0, 2)],
+        [cube.terms(qkv_terms[1]), cube.terms([keep_out, got_out], 2, 2)],
+    )
+    waited = early.last + late.last + [done]
+    early.advance()
+    late.advance()
+    tail_one.advance()
+    attend_group(3, waited)
+    finish_group(2)
+    finish_group(3)
+    tail_two = Scatter(cube, [cube.terms(qkv_terms[2])], [cube.terms(qkv_terms[3])])
+    waited = early.last + late.last + tail_one.last
+    late.advance()
+    tail_one.advance()
+    tail_two.advance()
+    token_grad, dln1 = head_back_call(dqs, dkvs, x, gate(grad_mid, *waited), qkv_w, qkv_rows, ln[0])
+
+    dln = jnp.concatenate([dln1, dln2], axis=0).reshape(4, dp, 2, rows).transpose(2, 1, 0, 3)
+    keep, send = halves(dln.reshape(2, dp, 4 * rows), 0)
+    dln = keep + exchange(send)
+    for b in range(cube.bits)[::-1]:
+        pair = dln.reshape(2, -1, 4 * rows)
+        sent = lax.dynamic_index_in_dim(pair, 1 - cube.mine[b], 0, keepdims=False)
+        dln = lax.dynamic_index_in_dim(pair, cube.mine[b], 0, keepdims=False) + cube.swap(sent, b)
+    dln = dln.reshape(4, rows)
+
+    ffn_sums = [f.finish() for f in ffn]
+    (one_a, one_b), (two_a, two_b) = tail_one.finish(), tail_two.finish()
+    up_share = jnp.stack([s[0][0] for s in ffn_sums]).reshape(parts, tiles, rows, devices // tiles, sub)
+    up_share = up_share.transpose(2, 1, 3, 0, 4).reshape(rows, hidden)
+    down_share = jnp.concatenate([s[1][0].reshape(sub, d) for s in ffn_sums], axis=0)
+    qkv_share = jnp.concatenate([one_a[0], one_b[0], two_a[0], two_b[0]], axis=-1)
+    out_share = jnp.concatenate([one_a[1], one_b[1]], axis=0).transpose(1, 0, 2).reshape(rows, d)
     return (
         mixed[None],
         token_grad[None],
         dln[0],
         dln[1],
-        tail[:rows],
-        tail[rows : 2 * rows],
-        tail[2 * rows : 3 * rows],
-        tail[3 * rows : 4 * rows],
+        qkv_share[0],
+        qkv_share[1],
+        qkv_share[2],
+        out_share,
         dln[2],
         dln[3],
         up_share,

time: 759 us -> 631 us (0.83)
  waiting for transfers between devices: 411 us -> 201 us
  starting transfers between devices: 0.92 us -> 41.1 us
  other arithmetic: 29.2 us -> 65.7 us
  local copies, waits for them, and re-layouts: 43.7 us -> 51.5 us
    reduce_scatter x3 -> x0, waiting for transfers between devices: 291 us -> none  [the longest x2 151 us: body(): lax.psum_scatter(packed, BOTH, scatter_dimension=0, tiled=True)]
    ppermute x1 -> x42, waiting for transfers between devices: 7.26 us -> 78 us  [the longest x28 68.4 us: swap(): lax.ppermute(array, 'dp', [(i, i ^ 1 << bit) for i in range(self.dp)])]
    convert_element_type x2 -> x35, other arithmetic: 1.92 us -> 46.2 us  [advance(): self.cube.total(stream, self.settled[s], bit).astype(BF16)]
    ppermute x1 -> x42, starting transfers between devices: 0.19 us -> 40.7 us  [the longest x28 34.6 us: swap(): lax.ppermute(array, 'dp', [(i, i ^ 1 << bit) for i in range(self.dp)])]
    concatenate x3 -> x15, other arithmetic: 20.9 us -> 3.74 us  [the longest x12 2.86 us: advance(): jnp.concatenate(sent, axis=0)]
    all_gather x3, waiting for transfers between devices: 113 us -> 123 us  [gather(): out = lax.all_gather(local, BOTH, axis=0, tiled=True)]
    pallas_call x1, Pallas kernels: 50.4 us -> 41.7 us  [attend_call(): pl.pallas_call(partial(attend_kernel, bq, bk), grid_spec=spec, out_shape=...]
    dynamic_slice x0 -> x7, local copies, waits for them, and re-layouts: none -> 8.17 us  [pick(): piece = lax.dynamic_slice(self.array, starts + [0, 0], sizes + list(shape))]
  transfers between devices with their start and end apart: 8 -> 46, of which waited for: 7 -> 23; matrix products, arithmetic and copies ran while one was open for 4% -> 14% of each run, Pallas kernels for 29% -> 31%
where the time goes in v2:
time: 631 us; the launch traced here: 623 us
  Pallas kernels  249 us (39%)
  waiting for transfers between devices  201 us (32%)
  other arithmetic  65.7 us (10%)
  local copies, waits for them, and re-layouts  51.5 us (8%)
  starting transfers between devices  41.1 us (7%)
  between operations  14.9 us (2%)
    all_gather x3, waiting for transfers between devices, gather(): out = lax.all_gather(local, BOTH, axis=0, tiled=True)  123 us
    pallas_call x2, Pallas kernels, ffn_call(): pl.pallas_call(partial(ffn_kernel, last, gmid is None, aligned), grid_spe...  77.1 us
    pallas_call x4, Pallas kernels, attend_back_call(): pl.pallas_call(partial(attend_back_kernel, bq, bk), grid_spec=spec, out_s...  73.4 us
    ppermute x28, waiting for transfers between devices, swap(): lax.ppermute(array, 'dp', [(i, i ^ 1 << bit) for i in range(self.dp)])  68.4 us
    convert_element_type x35, other arithmetic, advance(): self.cube.total(stream, self.settled[s], bit).astype(BF16)  46.2 us
    pallas_call x1, Pallas kernels, attend_call(): pl.pallas_call(partial(attend_kernel, bq, bk), grid_spec=spec, out_shape=...  41.7 us
    ppermute x28, starting transfers between devices, swap(): lax.ppermute(array, 'dp', [(i, i ^ 1 << bit) for i in range(self.dp)])  34.6 us
    unnamed x121, local copies, waits for them, and re-layouts  24 us
  transfers between devices with their start and end apart: 46, of which 23 were waited for; matrix products, arithmetic and copies ran while one was open for 14% of the time, Pallas kernels for 31%

profile of v2, /device:TPU:0, one launch (start us, length us, event | category | flops | bytes accessed | tf_op | source)
XLA Modules:
  0.0 623.4 jit_solution(16153030296136098878)
XLA Ops:
  13.5 74.2 %all-gather.4.cloned.1.call-done = bf16[3584,1024]{1,0:T(8,128)(2,1)} async-done(((bf16[112,1024]{1,0:T(8,128)(2,1)}), bf16[3584,1024]{1,0:T(8,128)(2,1)}) %all-gather.4.cloned.1.call-update) | async-done | bytes 7340048 | tf_op jit(solution)/shard_map/all_gather | solution.py:698
  88.8 9.5 %kv_proj.1 = (bf16[1024,1024]{1,0:T(8,128)(2,1)S(1)}, bf16[2,1024,1024]{2,1,0:T(8,128)(2,1)}) custom-call(bf16[1024,1024]{1,0:T(8,128)(2,1)S(1)} %bitcast.732, f32[1,1024]{1,0:T(1,128)S(1)} %squeeze.84.gain_ref.refs_13_, f32[1,1024]{1,0:T(1,128)S(1)} %squeeze.85.bias_ref, bf16[32,112,1024]{2,1,0:T(8,128)(2,1)} %bitcast.721, bf16[32,112,1024]{2,1,0:T(8,128)(2,1)} %bitcast.722), custom_call_target="tpu_custom_call" | custom-call | flops 4294967296 | bytes 12582912 | tf_op jit(solution)/shard_map/kv_proj/pallas_call | solution.py:84
  103.3 3.1 copy-done
  108.0 3.0 q_proj.1.q_ref
  112.5 41.7 %attend.1 = (bf16[1024,1024]{1,0:T(8,128)(2,1)}, f32[4,4,1,1024]{3,2,1,0:T(1,128)}) custom-call(s32[16]{0:T(128)} %reshape.992.tab, bf16[1024,1024]{1,0:T(8,128)(2,1)} %copy-done.8, bf16[2,1024,1024]{2,1,0:T(8,128)(2,1)} %get-tuple-element.68.ko_ref.vo_ref, bf16[2,1024,1024]{2,1,0:T(8,128)(2,1)} %get-tuple-element.68.ko_ref.vo_ref, ...), custom_call_target="tpu_custom_call" | custom-call | flops 30000001024 | bytes 12582912 | tf_op jit(solution)/shard_map/attend/pallas_call | solution.py:198
  154.2 22.1 %all-gather.6.cloned.1.call-done = bf16[5120,1024]{1,0:T(8,128)(2,1)} async-done(((bf16[160,1024]{1,0:T(8,128)(2,1)}), bf16[5120,1024]{1,0:T(8,128)(2,1)}) %all-gather.6.cloned.1.call-update) | async-done | bytes 10485776 | tf_op jit(solution)/shard_map/all_gather | solution.py:698
  176.3 4.0 copy-done.1
  181.8 4.2 out_proj.1
  190.0 38.3 %ffn.2 = (f32[1024,1024]{1,0:T(8,128)}, f32[1024,1024]{1,0:T(8,128)}, bf16[2,16,32,1024]{3,2,1,0:T(8,128)(2,1)}, bf16[2,16,32,1024]{3,2,1,0:T(8,128)(2,1)}, bf16...) custom-call(s32[1]{0:T(128)} %bitcast.me, ...), custom_call_target="tpu_custom_call", output_to_operand_aliasing={{0}: (5, {})} | custom-call | flops 25769803776 | bytes 37748736 | tf_op jit(solution)/shard_map/ffn/pallas_call | solution.py:471
  228.2 27.0 %all-gather.8.cloned.1.call-done = bf16[4096,1024]{1,0:T(8,128)(2,1)} async-done(((bf16[128,1024]{1,0:T(8,128)(2,1)}), bf16[4096,1024]{1,0:T(8,128)(2,1)}) %all-gather.8.cloned.1.call-update) | async-done | bytes 8388624 | tf_op jit(solution)/shard_map/all_gather | solution.py:698
  255.2 38.8 %ffn.3 = (bf16[1024,1024]{1,0:T(8,128)(2,1)}, f32[1024,1024]{1,0:T(8,128)}, bf16[2,16,32,1024]{3,2,1,0:T(8,128)(2,1)}, bf16[2,16,32,1024]{3,2,1,0:T(8,128)(2,1)}...) custom-call(s32[1]{0:T(128)} %bitcast.me, ...), custom_call_target="tpu_custom_call", output_to_operand_aliasing={{1}: (6, {})} | custom-call | flops 25769803776 | bytes 37748736 | tf_op jit(solution)/shard_map/ffn/pallas_call | solution.py:471
  298.6 6.0 collective-permute-done.2
  304.6 3.0 collective-permute-done.4
  307.6 13.8 %out_proj_back.1 = (f32[1024,1024]{1,0:T(8,128)}, bf16[1024,1024]{1,0:T(8,128)(2,1)S(1)}, bf16[4,16,32,256]{3,2,1,0:T(8,128)(2,1)S(1)}, bf16[4,16,32,256]{3,2,1,0:T(8,128)(2,1)S(1)}, f32[2,1024]{1,0:T(2,128)S(1)}) custom-call(s32[1]{0:T(128)} %bitcast.me, f32[1024,1024]{1,0:T(8,128)} %get-tuple-element.81.gh_ref, f32[1024,1024]{1,0:T(8,128)} %copy-done.3, ...), custom_call_target="tpu_custom_call" | custom-call | flops 4294967296 | bytes 23068672 | tf_op jit(solution)/shard_map/out_proj_back/pallas_call | solution.py:379
  324.5 2.6 fusion.1
  328.6 2.6 fusion.2
  331.8 2.6 fusion.3
  335.8 18.2 %attend_back.4 = (bf16[1024,256]{1,0:T(8,128)(2,1)}, bf16[2,1024,256]{2,1,0:T(8,128)(2,1)}, bf16[2,1024,256]{2,1,0:T(8,128)(2,1)}) custom-call(s32[16]{0:T(128)} %reshape.992.tab, bf16[1024,1024]{1,0:T(8,128)(2,1)} %copy-done.8, bf16[1024,1024]{1,0:T(8,128)(2,1)} %copy-done.28, bf16[1024,1024]{1,0:T(8,128)(2,1)} %get-tuple-element.69.o_ref, ...), custom_call_target="tpu_custom_call" | custom-call | flops 12000000000 | bytes 6291456 | tf_op jit(solution)/shard_map/attend_back/pallas_call | solution.py:292
  356.3 2.6 fusion.7
  359.0 2.9 collective-permute-start.7
  364.2 6.7 %collective-permute-done.9 = bf16[2,2,2,2,32,1024]{5,4,0,3,2,1:T(8,128)(2,1)} collective-permute-done((bf16[2,2,2,2,32,1024]{5,4,0,3,2,1:T(8,128)(2,1)}, bf16[2,2,2,2,32,1024]{5,4,0,3,2,1:T(8,128)(2,1)}, u32[]{:S(2)}, u32[]{:S(2)}) %collective-permute-start.9) | collective-permute-done | bytes 1048608 | tf_op jit(solution)/shard_map/ppermute | solution.py:585
  372.4 2.5 fusion.5
  379.9 18.5 %attend_back.5 = (bf16[1024,256]{1,0:T(8,128)(2,1)}, bf16[2,1024,256]{2,1,0:T(8,128)(2,1)}, bf16[2,1024,256]{2,1,0:T(8,128)(2,1)}) custom-call(s32[16]{0:T(128)} %reshape.992.tab, bf16[1024,1024]{1,0:T(8,128)(2,1)} %copy-done.8, bf16[1024,1024]{1,0:T(8,128)(2,1)} %copy-done.28, bf16[1024,1024]{1,0:T(8,128)(2,1)} %get-tuple-element.69.o_ref, ...), custom_call_target="tpu_custom_call" | custom-call | flops 12000000000 | bytes 6291456 | tf_op jit(solution)/shard_map/attend_back/pallas_call | solution.py:292
  414.4 3.1 collective-permute-start.12
  417.5 18.2 %attend_back.6 = (bf16[1024,256]{1,0:T(8,128)(2,1)}, bf16[2,1024,256]{2,1,0:T(8,128)(2,1)}, bf16[2,1024,256]{2,1,0:T(8,128)(2,1)}) custom-call(s32[16]{0:T(128)} %reshape.992.tab, bf16[1024,1024]{1,0:T(8,128)(2,1)} %copy-done.8, bf16[1024,1024]{1,0:T(8,128)(2,1)} %copy-done.28, bf16[1024,1024]{1,0:T(8,128)(2,1)} %get-tuple-element.69.o_ref, ...), custom_call_target="tpu_custom_call" | custom-call | flops 12000000000 | bytes 6291456 | tf_op jit(solution)/shard_map/attend_back/pallas_call | solution.py:292
  444.4 2.8 qkv_grad.5
  448.3 18.6 %attend_back.7 = (bf16[1024,256]{1,0:T(8,128)(2,1)}, bf16[2,1024,256]{2,1,0:T(8,128)(2,1)}, bf16[2,1024,256]{2,1,0:T(8,128)(2,1)}) custom-call(s32[16]{0:T(128)} %reshape.992.tab, bf16[1024,1024]{1,0:T(8,128)(2,1)} %copy-done.8, bf16[1024,1024]{1,0:T(8,128)(2,1)} %copy-done.28, bf16[1024,1024]{1,0:T(8,128)(2,1)} %get-tuple-element.69.o_ref, ...), custom_call_target="tpu_custom_call" | custom-call | flops 12000000000 | bytes 6291456 | tf_op jit(solution)/shard_map/attend_back/pallas_call | solution.py:292
  471.6 3.0 collective-permute-start.18
  475.2 15.6 %collective-permute-done.42 = bf16[4,32,1024]{2,1,0:T(8,128)(2,1)S(1)} collective-permute-done((bf16[4,32,1024]{2,1,0:T(8,128)(2,1)S(1)}, bf16[4,32,1024]{2,1,0:T(8,128)(2,1)S(1)}, u32[]{:S(2)}, u32[]{:S(2)}) %collective-permute-start.42) | collective-permute-done | bytes 262176 | tf_op jit(solution)/shard_map/ppermute | solution.py:585
  490.8 2.2 fusion.23
  493.0 2.9 collective-permute-done.18
  495.9 2.4 fusion.24
  499.3 2.4 copy.522
  505.2 3.2 maximum_bitcast_fusion
  508.4 3.0 reshape.1024
  513.9 3.9 collective-permute-start.30
  520.1 4.2 qkv_grad.6
  527.6 3.3 qkv_grad.7
  533.7 5.7 collective-permute-done.24
  540.3 14.0 %qkv_back.1 = (bf16[1024,1024]{1,0:T(8,128)(2,1)}, f32[2,1024]{1,0:T(2,128)S(1)}) custom-call(bf16[1024,256]{1,0:T(8,128)(2,1)S(1)} %copy-done.21, bf16[1024,256]{1,0:T(8,128)(2,1)S(1)} %copy-done.23, bf16[1024,256]{1,0:T(8,128)(2,1)S(1)} %copy-done.24, bf16[1024,256]{1,0:T(8,128)(2,1)S(1)} %copy-done.25, ...), custom_call_target="tpu_custom_call" | custom-call | flops 6442450944 | bytes 20971520 | tf_op jit(solution)/shard_map/qkv_back/pallas_call | solution.py:541
  557.3 3.5 collective-permute-done.26
  562.1 2.4 collective-permute-done.27
  571.3 5.7 collective-permute-done.29
  588.2 2.3 collective-permute-done.36
  591.5 3.3 collective-permute-done.38
  596.5 4.1 collective-permute-done.39
  602.8 4.6 collective-permute-done.40
  610.4 4.5 collective-permute-done.41
  (302 shorter events, 121.7 us)
Async XLA Ops:
  7.2 80.5 %all-gather.4.cloned.1.call-start = ((), (), s32[]{:S(2)}) async-start(), calls=%async_computation | async-start | bytes 7569408 | tf_op jit(solution)/shard_map/all_gather | solution.py:698
  9.7 166.6 %all-gather.6.cloned.1.call-start = ((), (), s32[]{:S(2)}) async-start(), calls=%async_computation.1 | async-start | bytes 10813440 | tf_op jit(solution)/shard_map/all_gather | solution.py:698
  11.3 77.5 %copy-start.2 = (bf16[1,1024,1024]{2,1,0:T(8,128)(2,1)S(1)}, bf16[1,1024,1024]{2,1,0:T(8,128)(2,1)}, u32[]{:S(2)}) copy-start(bf16[1,1024,1024]{2,1,0:T(8,128)(2,1)} %param.13) | copy-start | bytes 6291460
  12.7 242.6 %all-gather.8.cloned.1.call-start = ((), (), s32[]{:S(2)}) async-start(), calls=%async_computation.2 | async-start | bytes 8650752 | tf_op jit(solution)/shard_map/all_gather | solution.py:698
  99.7 12.8 %collective-permute-start = (bf16[2,1024,1024]{2,1,0:T(8,128)(2,1)}, bf16[2,1024,1024]{2,1,0:T(8,128)(2,1)}, u32[]{:S(2)}, u32[]{:S(2)}) collective-permute-start(bf16[2,1024,1024]{2,1,0:T(8,128)(2,1)} %get-tuple-element.68.ko_ref.vo_ref), channel_id=1, source_target_pairs={{0,1},{1,0},{2,3},{3,2},{4,5},{5,4},{6,7},{7,6},{8,9},{9,8},{10,11... | collective-permute-start | bytes 12582920 | tf_op jit(solution)/shard_map/ppermute | solution.py:716
  294.1 4.5 collective-permute-start.1
  294.3 10.2 %collective-permute-start.2 = (bf16[2,16,32,1024]{3,2,1,0:T(8,128)(2,1)}, bf16[2,16,32,1024]{3,2,1,0:T(8,128)(2,1)}, u32[]{:S(2)}, u32[]{:S(2)}) collective-permute-start(bf16[2,16,32,1024]{3,2,1,0:T(8,128)(2,1)} %get-tuple-element.76), channel_id=1, source_target_pairs={{0,1},{1,0},{2,3},{3,2},{4,5},{5,4},{6,7},{7,6},{8,9},{9,8},{10,11... | collective-permute-start | bytes 6291464 | tf_op jit(solution)/shard_map/ppermute | solution.py:726
  294.6 10.0 %collective-permute-start.3 = (bf16[2,16,32,1024]{3,2,1,0:T(8,128)(2,1)}, bf16[2,16,32,1024]{3,2,1,0:T(8,128)(2,1)S(1)}, u32[]{:S(2)}, u32[]{:S(2)}) collective-permute-start(bf16[2,16,32,1024]{3,2,1,0:T(8,128)(2,1)} %get-tuple-element.79), channel_id=1, source_target_pairs={{0,1},{1,0},{2,3},{3,2},{4,5},{5,4},{6,7},{7,6},{8,9},{9,8},{10,11... | collective-permute-start | bytes 6291464 | tf_op jit(solution)/shard_map/ppermute | solution.py:726
  294.9 12.7 %collective-permute-start.4 = (bf16[2,16,32,1024]{3,2,1,0:T(8,128)(2,1)}, bf16[2,16,32,1024]{3,2,1,0:T(8,128)(2,1)}, u32[]{:S(2)}, u32[]{:S(2)}) collective-permute-start(bf16[2,16,32,1024]{3,2,1,0:T(8,128)(2,1)} %get-tuple-element.80), channel_id=1, source_target_pairs={{0,1},{1,0},{2,3},{3,2},{4,5},{5,4},{6,7},{7,6},{8,9},{9,8},{10,11... | collective-permute-start | bytes 6291464 | tf_op jit(solution)/shard_map/ppermute | solution.py:726
  321.4 82.4 %copy-start.12 = (bf16[4,16,32,256]{3,2,1,0:T(8,128)(2,1)}, bf16[4,16,32,256]{3,2,1,0:T(8,128)(2,1)S(1)}, u32[]{:S(2)}) copy-start(bf16[4,16,32,256]{3,2,1,0:T(8,128)(2,1)S(1)} %get-tuple-element.110) | copy-start | bytes 3145732
  322.8 33.5 %collective-permute-start.5 = (bf16[2,2,2,2,32,1024]{5,4,0,3,2,1:T(8,128)(2,1)}, bf16[2,2,2,2,32,1024]{5,4,0,3,2,1:T(8,128)(2,1)S(1)}, u32[]{:S(2)}, u32[]{:S(2)}) collective-permute-start(bf16[2,2,2,2,32,1024]{5,4,0,3,2,1:T(8,128)(2,1)} %fusion), channel_id=1, source_target_pairs={{0,2},{2,0},{4,6},{6,4},{8,10},{10,8},{12,14},{14,12},{16,18},{18,... | collective-permute-start | bytes 3145736 | tf_op jit(solution)/shard_map/ppermute | solution.py:585
  327.1 29.2 %collective-permute-start.6 = (bf16[2,2,2,2,32,1024]{5,4,0,3,2,1:T(8,128)(2,1)}, bf16[2,2,2,2,32,1024]{5,4,0,3,2,1:T(8,128)(2,1)}, u32[]{:S(2)}, u32[]{:S(2)}) collective-permute-start(bf16[2,2,2,2,32,1024]{5,4,0,3,2,1:T(8,128)(2,1)} %fusion.1), channel_id=1, source_target_pairs={{0,4},{2,6},{4,0},{6,2},{8,12},{10,14},{12,8},{14,10},{16,20},{18,... | collective-permute-start | bytes 3145736 | tf_op jit(solution)/shard_map/ppermute | solution.py:585
  331.3 39.7 %collective-permute-start.9 = (bf16[2,2,2,2,32,1024]{5,4,0,3,2,1:T(8,128)(2,1)}, bf16[2,2,2,2,32,1024]{5,4,0,3,2,1:T(8,128)(2,1)}, u32[]{:S(2)}, u32[]{:S(2)}) collective-permute-start(bf16[2,2,2,2,32,1024]{5,4,0,3,2,1:T(8,128)(2,1)} %fusion.2), channel_id=1, source_target_pairs={{0,2},{2,0},{4,6},{6,4},{8,10},{10,8},{12,14},{14,12},{16,18},{18,... | collective-permute-start | bytes 3145736 | tf_op jit(solution)/shard_map/ppermute | solution.py:585
  334.4 41.5 %collective-permute-start.10 = (bf16[2,2,2,2,32,1024]{5,4,0,3,2,1:T(8,128)(2,1)}, bf16[2,2,2,2,32,1024]{5,4,0,3,2,1:T(8,128)(2,1)}, u32[]{:S(2)}, u32[]{:S(2)}) collective-permute-start(bf16[2,2,2,2,32,1024]{5,4,0,3,2,1:T(8,128)(2,1)} %fusion.3), channel_id=1, source_target_pairs={{0,4},{2,6},{4,0},{6,2},{8,12},{10,14},{12,8},{14,10},{16,20},{18,... | collective-permute-start | bytes 3145736 | tf_op jit(solution)/shard_map/ppermute | solution.py:585
  354.0 53.2 %collective-permute-start.11 = (bf16[2,1024,256]{2,1,0:T(8,128)(2,1)}, bf16[2,1024,256]{2,1,0:T(8,128)(2,1)S(1)}, u32[]{:S(2)}, u32[]{:S(2)}) collective-permute-start(bf16[2,1024,256]{2,1,0:T(8,128)(2,1)} %get-tuple-element.92), channel_id=1, source_target_pairs={{0,1},{1,0},{2,3},{3,2},{4,5},{5,4},{6,7},{7,6},{8,9},{9,8},{10,11... | collective-permute-start | bytes 3145736 | tf_op jit(solution)/shard_map/ppermute | solution.py:726
  356.3 42.1 %collective-permute-start.21 = (bf16[4,16,32,256]{3,2,1,0:T(8,128)(2,1)S(1)}, bf16[4,16,32,256]{3,2,1,0:T(8,128)(2,1)}, u32[]{:S(2)}, u32[]{:S(2)}) collective-permute-start(bf16[4,16,32,256]{3,2,1,0:T(8,128)(2,1)S(1)} %get-tuple-element.111), channel_id=1, source_target_pairs={{0,1},{1,0},{2,3},{3,2},{4,5},{5,4},{6,7},{7,6},{8,9},{9,8},{10,11... | collective-permute-start | bytes 3145736 | tf_op jit(solution)/shard_map/ppermute | solution.py:726
  359.0 51.4 %collective-permute-start.7 = (bf16[2,2,2,32,1024]{4,3,0,2,1:T(8,128)(2,1)}, bf16[2,2,2,32,1024]{4,3,0,2,1:T(8,128)(2,1)}, u32[]{:S(2)}, u32[]{:S(2)}) collective-permute-start(bf16[2,2,2,32,1024]{4,3,0,2,1:T(8,128)(2,1)} %fusion.7), channel_id=1, source_target_pairs={{0,4},{2,6},{4,0},{6,2},{8,12},{10,14},{12,8},{14,10},{16,20},{18,... | collective-permute-start | bytes 1572872 | tf_op jit(solution)/shard_map/ppermute | solution.py:585
  371.0 40.0 %collective-permute-start.8 = (bf16[2,2,2,32,1024]{4,3,0,1,2:T(8,128)(2,1)}, bf16[2,2,2,32,1024]{4,3,0,1,2:T(8,128)(2,1)}, u32[]{:S(2)}, u32[]{:S(2)}) collective-permute-start(bf16[2,2,2,32,1024]{4,3,0,1,2:T(8,128)(2,1)} %copy.414), channel_id=1, source_target_pairs={{0,2},{2,0},{4,6},{6,4},{8,10},{10,8},{12,14},{14,12},{16,18},{18,... | collective-permute-start | bytes 1572872 | tf_op jit(solution)/shard_map/ppermute | solution.py:585
  375.9 62.5 %collective-permute-start.13 = (bf16[2,2,2,32,1024]{4,3,0,2,1:T(8,128)(2,1)}, bf16[2,2,2,32,1024]{4,3,0,2,1:T(8,128)(2,1)}, u32[]{:S(2)}, u32[]{:S(2)}) collective-permute-start(bf16[2,2,2,32,1024]{4,3,0,2,1:T(8,128)(2,1)} %fusion.5), channel_id=1, source_target_pairs={{0,4},{2,6},{4,0},{6,2},{8,12},{10,14},{12,8},{14,10},{16,20},{18,... | collective-permute-start | bytes 1572872 | tf_op jit(solution)/shard_map/ppermute | solution.py:585
  398.4 37.2 %collective-permute-start.14 = (bf16[2,2,2,32,1024]{4,3,0,1,2:T(8,128)(2,1)}, bf16[2,2,2,32,1024]{4,3,0,1,2:T(8,128)(2,1)}, u32[]{:S(2)}, u32[]{:S(2)}) collective-permute-start(bf16[2,2,2,32,1024]{4,3,0,1,2:T(8,128)(2,1)} %copy.430), channel_id=1, source_target_pairs={{0,2},{2,0},{4,6},{6,4},{8,10},{10,8},{12,14},{14,12},{16,18},{18,... | collective-permute-start | bytes 1572872 | tf_op jit(solution)/shard_map/ppermute | solution.py:585
  407.2 37.2 %collective-permute-start.15 = (bf16[2,1024,256]{2,1,0:T(8,128)(2,1)}, bf16[2,1024,256]{2,1,0:T(8,128)(2,1)S(1)}, u32[]{:S(2)}, u32[]{:S(2)}) collective-permute-start(bf16[2,1024,256]{2,1,0:T(8,128)(2,1)} %get-tuple-element.97), channel_id=1, source_target_pairs={{0,1},{1,0},{2,3},{3,2},{4,5},{5,4},{6,7},{7,6},{8,9},{9,8},{10,11... | collective-permute-start | bytes 3145736 | tf_op jit(solution)/shard_map/ppermute | solution.py:726
  410.4 30.2 %collective-permute-start.20 = (bf16[3,16,32,256]{3,2,1,0:T(8,128)(2,1)S(1)}, bf16[3,16,32,256]{3,2,1,0:T(8,128)(2,1)}, u32[]{:S(2)}, u32[]{:S(2)}) collective-permute-start(bf16[3,16,32,256]{3,2,1,0:T(8,128)(2,1)S(1)} %get-tuple-element.109), channel_id=1, source_target_pairs={{0,1},{1,0},{2,3},{3,2},{4,5},{5,4},{6,7},{7,6},{8,9},{9,8},{10,11... | collective-permute-start | bytes 2359304 | tf_op jit(solution)/shard_map/ppermute | solution.py:726
  414.4 33.8 %collective-permute-start.12 = (bf16[4,2,32,1024]{3,2,0,1:T(8,128)(2,1)}, bf16[4,2,32,1024]{3,2,0,1:T(8,128)(2,1)}, u32[]{:S(2)}, u32[]{:S(2)}) collective-permute-start(bf16[4,2,32,1024]{3,2,0,1:T(8,128)(2,1)} %pad_maximum_fusion.2), channel_id=1, source_target_pairs={{0,8},{2,10},{4,12},{6,14},{8,0},{10,2},{12,4},{14,6},{16,24},{18,... | collective-permute-start | bytes 1572872 | tf_op jit(solution)/shard_map/ppermute | solution.py:585
  435.7 84.4 %collective-permute-start.16 = (bf16[2,1024,256]{2,1,0:T(8,128)(2,1)}, bf16[2,1024,256]{2,1,0:T(8,128)(2,1)}, u32[]{:S(2)}, u32[]{:S(2)}) collective-permute-start(bf16[2,1024,256]{2,1,0:T(8,128)(2,1)} %get-tuple-element.102), channel_id=1, source_target_pairs={{0,1},{1,0},{2,3},{3,2},{4,5},{5,4},{6,7},{7,6},{8,9},{9,8},{10,11... | collective-permute-start | bytes 3145736 | tf_op jit(solution)/shard_map/ppermute | solution.py:726
  440.6 27.7 %collective-permute-start.19 = (bf16[4,2,32,1024]{3,2,0,1:T(8,128)(2,1)}, bf16[4,2,32,1024]{3,2,0,1:T(8,128)(2,1)S(1)}, u32[]{:S(2)}, u32[]{:S(2)}) collective-permute-start(bf16[4,2,32,1024]{3,2,0,1:T(8,128)(2,1)} %pad_maximum_fusion.3), channel_id=1, source_target_pairs={{0,8},{2,10},{4,12},{6,14},{8,0},{10,2},{12,4},{14,6},{16,24},{18,... | collective-permute-start | bytes 1572872 | tf_op jit(solution)/shard_map/ppermute | solution.py:585
  442.7 68.8 %collective-permute-start.22 = (bf16[5,2,2,2,32,256]{5,4,0,3,2,1:T(8,128)(2,1)}, bf16[5,2,2,2,32,256]{5,4,0,3,2,1:T(8,128)(2,1)}, u32[]{:S(2)}, u32[]{:S(2)}) collective-permute-start(bf16[5,2,2,2,32,256]{5,4,0,3,2,1:T(8,128)(2,1)} %pad_maximum_fusion), channel_id=1, source_target_pairs={{0,2},{2,0},{4,6},{6,4},{8,10},{10,8},{12,14},{14,12},{16,18},{18,... | collective-permute-start | bytes 1966088 | tf_op jit(solution)/shard_map/ppermute | solution.py:585
  466.8 60.7 %collective-permute-start.17 = (bf16[2,1024,256]{2,1,0:T(8,128)(2,1)}, bf16[2,1024,256]{2,1,0:T(8,128)(2,1)}, u32[]{:S(2)}, u32[]{:S(2)}) collective-permute-start(bf16[2,1024,256]{2,1,0:T(8,128)(2,1)} %get-tuple-element.105), channel_id=1, source_target_pairs={{0,1},{1,0},{2,3},{3,2},{4,5},{5,4},{6,7},{7,6},{8,9},{9,8},{10,11... | collective-permute-start | bytes 3145736 | tf_op jit(solution)/shard_map/ppermute | solution.py:726
  469.8 21.0 %collective-permute-start.42 = (bf16[4,32,1024]{2,1,0:T(8,128)(2,1)S(1)}, bf16[4,32,1024]{2,1,0:T(8,128)(2,1)S(1)}, u32[]{:S(2)}, u32[]{:S(2)}) collective-permute-start(bf16[4,32,1024]{2,1,0:T(8,128)(2,1)S(1)} %pad_maximum_fusion.12), channel_id=1, source_target_pairs={{0,16},{2,18},{4,20},{6,22},{8,24},{10,26},{12,28},{14,30},{16,0},... | collective-permute-start | bytes 786440 | tf_op jit(solution)/shard_map/ppermute | solution.py:585
  471.6 24.4 %collective-permute-start.18 = (bf16[4,32,1024]{2,1,0:T(8,128)(2,1)S(1)}, bf16[4,32,1024]{2,1,0:T(8,128)(2,1)S(1)}, u32[]{:S(2)}, u32[]{:S(2)}) collective-permute-start(bf16[4,32,1024]{2,1,0:T(8,128)(2,1)S(1)} %pad_maximum_fusion.11), channel_id=1, source_target_pairs={{0,16},{2,18},{4,20},{6,22},{8,24},{10,26},{12,28},{14,30},{16,0},... | collective-permute-start | bytes 786440 | tf_op jit(solution)/shard_map/ppermute | solution.py:585
  490.8 27.1 %collective-permute-start.23 = (bf16[3,16,32,256]{3,2,1,0:T(8,128)(2,1)}, bf16[3,16,32,256]{3,2,1,0:T(8,128)(2,1)}, u32[]{:S(2)}, u32[]{:S(2)}) collective-permute-start(bf16[3,16,32,256]{3,2,1,0:T(8,128)(2,1)} %get-tuple-element.113), channel_id=1, source_target_pairs={{0,1},{1,0},{2,3},{3,2},{4,5},{5,4},{6,7},{7,6},{8,9},{9,8},{10,11... | collective-permute-start | bytes 2359304 | tf_op jit(solution)/shard_map/ppermute | solution.py:726
  513.9 12.5 %collective-permute-start.30 = (bf16[5,2,2,32,256]{4,3,0,2,1:T(8,128)(2,1)S(1)}, bf16[5,2,2,32,256]{4,3,0,2,1:T(8,128)(2,1)S(1)}, u32[]{:S(2)}, u32[]{:S(2)}) collective-permute-start(bf16[5,2,2,32,256]{4,3,0,2,1:T(8,128)(2,1)S(1)} %pad_maximum_fusion.7), channel_id=1, source_target_pairs={{0,4},{2,6},{4,0},{6,2},{8,12},{10,14},{12,8},{14,10},{16,20},{18,... | collective-permute-start | bytes 983048 | tf_op jit(solution)/shard_map/ppermute | solution.py:585
  519.1 20.4 %collective-permute-start.24 = (bf16[5,2,2,2,32,256]{5,4,0,3,2,1:T(8,128)(2,1)S(1)}, bf16[5,2,2,2,32,256]{5,4,0,3,2,1:T(8,128)(2,1)S(1)}, u32[]{:S(2)}, u32[]{:S(2)}) collective-permute-start(bf16[5,2,2,2,32,256]{5,4,0,3,2,1:T(8,128)(2,1)S(1)} %pad_maximum_fusion.1), channel_id=1, source_target_pairs={{0,4},{2,6},{4,0},{6,2},{8,12},{10,14},{12,8},{14,10},{16,20},{18,... | collective-permute-start | bytes 1966088 | tf_op jit(solution)/shard_map/ppermute | solution.py:585
  525.2 43.2 %collective-permute-start.34 = (bf16[3,16,32,256]{3,2,1,0:T(8,128)(2,1)}, bf16[3,16,32,256]{3,2,1,0:T(8,128)(2,1)}, u32[]{:S(2)}, u32[]{:S(2)}) collective-permute-start(bf16[3,16,32,256]{3,2,1,0:T(8,128)(2,1)} %get-tuple-element.119), channel_id=1, source_target_pairs={{0,1},{1,0},{2,3},{3,2},{4,5},{5,4},{6,7},{7,6},{8,9},{9,8},{10,11... | collective-permute-start | bytes 2359304 | tf_op jit(solution)/shard_map/ppermute | solution.py:726
  554.6 1.6 collective-permute-start.25
  555.7 27.5 %collective-permute-start.37 = (bf16[3,16,32,256]{3,2,1,0:T(8,128)(2,1)S(1)}, bf16[3,16,32,256]{3,2,1,0:T(8,128)(2,1)S(1)}, u32[]{:S(2)}, u32[]{:S(2)}) collective-permute-start(bf16[3,16,32,256]{3,2,1,0:T(8,128)(2,1)S(1)} %copy-done.31), channel_id=1, source_target_pairs={{0,1},{1,0},{2,3},{3,2},{4,5},{5,4},{6,7},{7,6},{8,9},{9,8},{10,11... | collective-permute-start | bytes 2359304 | tf_op jit(solution)/shard_map/ppermute | solution.py:726
  556.3 4.6 collective-permute-start.26
  560.9 3.6 collective-permute-start.27
  564.4 3.6 collective-permute-start.28
  566.2 10.8 %collective-permute-start.31 = (bf16[5,2,2,32,256]{4,3,0,2,1:T(8,128)(2,1)S(1)}, bf16[5,2,2,32,256]{4,3,0,2,1:T(8,128)(2,1)S(1)}, u32[]{:S(2)}, u32[]{:S(2)}) collective-permute-start(bf16[5,2,2,32,256]{4,3,0,2,1:T(8,128)(2,1)S(1)} %pad_maximum_fusion.8), channel_id=1, source_target_pairs={{0,2},{2,0},{4,6},{6,4},{8,10},{10,8},{12,14},{14,12},{16,18},{18,... | collective-permute-start | bytes 983048 | tf_op jit(solution)/shard_map/ppermute | solution.py:585
  568.0 9.0 %collective-permute-start.29 = (f32[1,128]{1,0:T(1,128)S(1)}, f32[1,128]{1,0:T(1,128)S(1)}, u32[]{:S(2)}, u32[]{:S(2)}) collective-permute-start(f32[1,128]{1,0:T(1,128)S(1)} %constant_dynamic-slice_fusion.86), channel_id=1, source_target_pairs={{0,2},{2,0},{4,6},{6,4},{8,10},{10,8},{12,14},{14,12},{16,18},{18,... | collective-permute-start | bytes 1544 | tf_op jit(solution)/shard_map/ppermute | solution.py:585
  569.5 12.3 %collective-permute-start.35 = (bf16[3,2,2,2,32,256]{5,4,0,1,3,2:T(8,128)(2,1)S(1)}, bf16[3,2,2,2,32,256]{5,4,0,1,3,2:T(8,128)(2,1)S(1)}, u32[]{:S(2)}, u32[]{:S(2)}) collective-permute-start(bf16[3,2,2,2,32,256]{5,4,0,1,3,2:T(8,128)(2,1)S(1)} %fusion.15), channel_id=1, source_target_pairs={{0,2},{2,0},{4,6},{6,4},{8,10},{10,8},{12,14},{14,12},{16,18},{18,... | collective-permute-start | bytes 1179656 | tf_op jit(solution)/shard_map/ppermute | solution.py:585
  579.0 7.1 %collective-permute-start.32 = (bf16[10,2,32,256]{3,2,0,1:T(8,128)(2,1)S(1)}, bf16[10,2,32,256]{3,2,0,1:T(8,128)(2,1)S(1)}, u32[]{:S(2)}, u32[]{:S(2)}) collective-permute-start(bf16[10,2,32,256]{3,2,0,1:T(8,128)(2,1)S(1)} %pad_maximum_fusion.9), channel_id=1, source_target_pairs={{0,8},{2,10},{4,12},{6,14},{8,0},{10,2},{12,4},{14,6},{16,24},{18,... | collective-permute-start | bytes 983048 | tf_op jit(solution)/shard_map/ppermute | solution.py:585
  582.9 7.6 %collective-permute-start.36 = (bf16[3,2,2,32,256]{4,3,0,2,1:T(8,128)(2,1)S(1)}, bf16[3,2,2,32,256]{4,3,0,2,1:T(8,128)(2,1)S(1)}, u32[]{:S(2)}, u32[]{:S(2)}) collective-permute-start(bf16[3,2,2,32,256]{4,3,0,2,1:T(8,128)(2,1)S(1)} %copy.491), channel_id=1, source_target_pairs={{0,4},{2,6},{4,0},{6,2},{8,12},{10,14},{12,8},{14,10},{16,20},{18,... | collective-permute-start | bytes 589832 | tf_op jit(solution)/shard_map/ppermute | solution.py:585
  583.4 11.4 %collective-permute-start.38 = (bf16[3,2,2,2,32,256]{5,4,0,1,3,2:T(8,128)(2,1)S(1)}, bf16[3,2,2,2,32,256]{5,4,0,1,3,2:T(8,128)(2,1)S(1)}, u32[]{:S(2)}, u32[]{:S(2)}) collective-permute-start(bf16[3,2,2,2,32,256]{5,4,0,1,3,2:T(8,128)(2,1)S(1)} %fusion.16), channel_id=1, source_target_pairs={{0,4},{2,6},{4,0},{6,2},{8,12},{10,14},{12,8},{14,10},{16,20},{18,... | collective-permute-start | bytes 1179656 | tf_op jit(solution)/shard_map/ppermute | solution.py:585
  588.0 7.5 %collective-permute-start.33 = (bf16[10,32,256]{2,1,0:T(8,128)(2,1)S(1)}, bf16[10,32,256]{2,1,0:T(8,128)(2,1)S(1)}, u32[]{:S(2)}, u32[]{:S(2)}) collective-permute-start(bf16[10,32,256]{2,1,0:T(8,128)(2,1)S(1)} %pad_maximum_fusion.14), channel_id=1, source_target_pairs={{0,16},{2,18},{4,20},{6,22},{8,24},{10,26},{12,28},{14,30},{16,0},... | collective-permute-start | bytes 491528 | tf_op jit(solution)/shard_map/ppermute | solution.py:585
  594.8 5.7 collective-permute-start.39
  600.7 6.8 %collective-permute-start.40 = (bf16[6,2,32,256]{3,2,0,1:T(8,128)(2,1)S(1)}, bf16[6,2,32,256]{3,2,0,1:T(8,128)(2,1)S(1)}, u32[]{:S(2)}, u32[]{:S(2)}) collective-permute-start(bf16[6,2,32,256]{3,2,0,1:T(8,128)(2,1)S(1)} %pad_maximum_fusion.13), channel_id=1, source_target_pairs={{0,8},{2,10},{4,12},{6,14},{8,0},{10,2},{12,4},{14,6},{16,24},{18,... | collective-permute-start | bytes 589832 | tf_op jit(solution)/shard_map/ppermute | solution.py:585
  608.3 6.6 %collective-permute-start.41 = (bf16[6,32,256]{2,1,0:T(8,128)(2,1)S(1)}, bf16[6,32,256]{2,1,0:T(8,128)(2,1)S(1)}, u32[]{:S(2)}, u32[]{:S(2)}) collective-permute-start(bf16[6,32,256]{2,1,0:T(8,128)(2,1)S(1)} %pad_maximum_fusion.15), channel_id=1, source_target_pairs={{0,16},{2,18},{4,20},{6,22},{8,24},{10,26},{12,28},{14,30},{16,0},... | collective-permute-start | bytes 294920 | tf_op jit(solution)/shard_map/ppermute | solution.py:585
  (58 other events, 512.2 us)
Sparse Core Ops, SparseCore 0:
  11.4 76.1 all-gather.3
  91.1 85.1 all-gather.5
  179.1 76.0 all-gather.7

commit v3 on v2

--- a/solution.py
+++ b/solution.py
@@ -1,3 +1,4 @@
+import math
 from functools import partial
 
 import jax
@@ -19,6 +20,7 @@
 ATT_K = 512
 ROWS = 256
 FF_COLS = 512
+COST_SCALE = 100
 
 
 def dot_nn(left, right):
@@ -38,7 +40,7 @@
 
 
 def cost(flops, nbytes):
-    return pl.CostEstimate(flops=flops, bytes_accessed=nbytes, transcendentals=0)
+    return pl.CostEstimate(flops=flops // COST_SCALE, bytes_accessed=nbytes // COST_SCALE, transcendentals=0)
 
 
 def normed(values):
@@ -400,15 +402,8 @@
     return jnp.where(first, even, odd), jnp.where(first, odd, even)
 
 
-def ffn_kernel(last, first, aligned, me, *refs):
-    h_ref, g_ref, wu_ref, wd_ref, mi_ref = refs[:5]
-    refs = refs[5:]
-    gi_ref = None
-    if not first:
-        gi_ref, refs = refs[0], refs[1:]
-    mo_ref, go_ref = refs[:2]
-    refs = refs[2:]
-    grads, rest = (refs[:4], refs[4:]) if aligned else (refs[:2], refs[2:])
+def ffn_kernel(aligned, me, h_ref, g_ref, wu_ref, wd_ref, mid_ref, mixed_ref, gh_ref, *refs):
+    grads, acc = refs[:-1], refs[-1]
     j = pl.program_id(0)
     h, grad = h_ref[...], g_ref[...]
     wu, wd = flat(wu_ref), flat(wd_ref)
@@ -428,59 +423,42 @@
     else:
         grads[0][...] = dwu
         grads[1][...] = dwd
-    mo = rest[0] if last else mo_ref
 
     @pl.when(j == 0)
     def _():
-        mo[...] = mi_ref[...] + dot_nn(act, wd)
-        if first:
-            go_ref[...] = dot_nt(gu, wu)
-        else:
-            go_ref[...] = gi_ref[...] + dot_nt(gu, wu)
+        acc[...] = mid_ref[...] + dot_nn(act, wd)
+        gh_ref[...] = dot_nt(gu, wu)
 
     @pl.when(j > 0)
     def _():
-        mo[...] += dot_nn(act, wd)
-        go_ref[...] += dot_nt(gu, wu)
-
-    if last:
-
-        @pl.when(j == pl.num_programs(0) - 1)
-        def _():
-            mo_ref[...] = mo[...].astype(BF16)
-
-
-def ffn_call(me, h, cot, wu, wd, mid, gmid, grad_specs, width, last, aligned):
+        acc[...] += dot_nn(act, wd)
+        gh_ref[...] += dot_nt(gu, wu)
+
+    @pl.when(j == pl.num_programs(0) - 1)
+    def _():
+        mixed_ref[...] = acc[...].astype(BF16)
+
+
+def ffn_call(me, h, cot, wu, wd, mid, grad_specs, hidden, aligned):
     n, d = h.shape
     full = resident((n, d))
     const = pl.BlockSpec((n, d), lambda j, *_: (0, 0))
-    in_specs = [full, full, wu[1], wd[1], full]
-    args = [h, cot, wu[0], wd[0], mid]
-    aliases = {} if last else {5: 0}
-    if gmid is not None:
-        in_specs.append(full)
-        args.append(gmid)
-        aliases[6] = 1
     spec = pltpu.PrefetchScalarGridSpec(
         num_scalar_prefetch=1,
-        grid=(width // FF_COLS,),
-        in_specs=in_specs,
+        grid=(hidden // FF_COLS,),
+        in_specs=[full, full, wu[1], wd[1], full],
         out_specs=[const, const] + [g[0] for g in grad_specs],
-        scratch_shapes=[pltpu.VMEM((n, d), F32)] if last else [],
+        scratch_shapes=[pltpu.VMEM((n, d), F32)],
     )
     return pl.pallas_call(
-        partial(ffn_kernel, last, gmid is None, aligned),
+        partial(ffn_kernel, aligned),
         grid_spec=spec,
-        out_shape=[
-            jax.ShapeDtypeStruct((n, d), BF16 if last else F32),
-            jax.ShapeDtypeStruct((n, d), F32),
-        ]
+        out_shape=[jax.ShapeDtypeStruct((n, d), BF16), jax.ShapeDtypeStruct((n, d), F32)]
         + [g[1] for g in grad_specs],
-        input_output_aliases=aliases,
         compiler_params=params(60),
-        cost_estimate=cost(12 * n * d * width, 8 * d * width + 20 * n * d),
+        cost_estimate=cost(12 * n * d * hidden, 8 * d * hidden + 14 * n * d),
         name="ffn",
-    )(me, *args)
+    )(me, h, cot, wu[0], wd[0], mid)
 
 
 def qkv_grad_kernel(groups, me, h_ref, dq_ref, dkv_ref, rkv_ref, keep_ref, send_ref, sum_ref):
@@ -563,23 +541,33 @@
     def __init__(self, array, axes, first=0, count=None):
         self.array, self.axes, self.first = array, axes, first
         self.count = array.shape[0] if count is None else count
-
-    def pick(self, mine, settled, flipped):
-        starts, sizes = [self.first], [self.count]
-        for b in self.axes:
-            fixed = b in settled or b == flipped
-            starts.append((1 - mine[b] if b == flipped else mine[b]) if fixed else 0)
-            sizes.append(1 if fixed else 2)
-        shape = self.array.shape[-2:]
-        piece = lax.dynamic_slice(self.array, starts + [0, 0], sizes + list(shape))
-        return piece.reshape((self.count,) + (2,) * sizes[1:].count(2) + shape).astype(F32)
+        self.whole = first % self.count != 0
+
+    def spec(self, settled, flipped, open_bits):
+        def index_map(step, mine):
+            at = [0 if self.whole else self.first // self.count]
+            for b in self.axes:
+                if b == flipped:
+                    at.append(1 - mine[b])
+                elif b in settled:
+                    at.append(mine[b])
+                else:
+                    at.append((step >> (len(open_bits) - 1 - open_bits.index(b))) & 1)
+            return (*at, 0, 0)
+
+        lead = self.array.shape[0] if self.whole else self.count
+        return pl.BlockSpec((lead,) + (None,) * len(self.axes) + self.array.shape[-2:], index_map)
+
+    def read(self, ref):
+        start = self.first if self.whole else 0
+        return ref[start : start + self.count].astype(F32)
 
 
 class Cube:
     def __init__(self, dp, index):
         self.bits = dp.bit_length() - 1
         self.dp = dp
-        self.mine = [(index >> b) & 1 for b in range(self.bits)]
+        self.mine = ((index >> jnp.arange(self.bits, dtype=jnp.int32)) & 1).astype(jnp.int32)
 
     def swap(self, array, bit):
         return lax.ppermute(array, "dp", [(i, i ^ (1 << bit)) for i in range(self.dp)])
@@ -592,46 +580,92 @@
             made.append(Term(array.reshape(shape), list(range(self.bits))[::-1], first, count))
         return made
 
-    def total(self, terms, settled, flipped=None):
-        out = terms[0].pick(self.mine, settled, flipped)
-        for term in terms[1:]:
-            out = out + term.pick(self.mine, settled, flipped)
-        return out
+    def add(self, outputs, dtype):
+        in_specs, args, plan, out_specs, out_shape = [], [], [], [], []
+        steps = 1
+        for output in outputs:
+            lead = 0
+            for stream, settled, flipped in output:
+                open_bits = [b for b in range(self.bits)[::-1] if b not in settled and b != flipped]
+                steps = 2 ** len(open_bits)
+                for term in stream:
+                    in_specs.append(term.spec(settled, flipped, open_bits))
+                    args.append(term.array)
+                plan.append((len(out_specs), lead, list(stream)))
+                lead += stream[0].count
+            count = len(open_bits)
+
+            def out_map(step, mine, count=count):
+                return (0, *[(step >> (count - 1 - k)) & 1 for k in range(count)], 0, 0)
+
+            shape = output[0][0][0].array.shape[-2:]
+            out_specs.append(pl.BlockSpec((lead,) + (None,) * count + shape, out_map))
+            out_shape.append(jax.ShapeDtypeStruct((lead,) + (2,) * count + shape, dtype))
+
+        def kernel(mine, *refs):
+            ins, outs = refs[: len(args)], refs[len(args) :]
+            at = 0
+            for out, first, stream in plan:
+                total = stream[0].read(ins[at])
+                for k in range(1, len(stream)):
+                    total = total + stream[k].read(ins[at + k])
+                outs[out][first : first + stream[0].count] = total.astype(dtype)
+                at += len(stream)
+
+        spec = pltpu.PrefetchScalarGridSpec(
+            num_scalar_prefetch=1, grid=(steps,), in_specs=in_specs, out_specs=out_specs
+        )
+        size = sum(math.prod(o.shape) for o in out_shape)
+        return pl.pallas_call(
+            kernel,
+            grid_spec=spec,
+            out_shape=out_shape,
+            compiler_params=params(40),
+            cost_estimate=cost(4 * size, 8 * size),
+            name="add_terms",
+        )(self.mine, *args)
 
 
 class Scatter:
     def __init__(self, cube, one, two):
         self.cube, self.sides, self.step = cube, (one, two), 0
-        self.settled = [[], []]
+        self.settled = []
+        self.sent, self.last = [], []
+
+    def advance(self):
+        step = self.step
+        done = (self.settled, self.settled)
+        if step == 0:
+            flips, groups = (0, 1), ((0,), (1,))
+            done = ([], [])
+        elif step == 1:
+            flips, groups = (1, 0), ((0,), (1,))
+            done = ([0], [1])
+        else:
+            flips, groups = (step, step), ((0, 1),)
+            done = (list(range(step)),) * 2
+        self.sent = self.cube.add(
+            [[(stream, done[s], flips[s]) for s in group for stream in self.sides[s]] for group in groups], BF16
+        )
         self.last = []
-
-    def advance(self):
-        bit = self.step
-        if self.step < 2:
-            plan = [((0,), bit), ((1,), 1 - bit)]
-        else:
-            plan = [((0, 1), bit)]
-        self.last = []
-        for sides, bit in plan:
-            streams = [(s, stream) for s in sides for stream in self.sides[s]]
-            sent = [self.cube.total(stream, self.settled[s], bit).astype(BF16) for s, stream in streams]
-            got = self.cube.swap(sent[0] if len(sent) == 1 else jnp.concatenate(sent, axis=0), bit)
+        for group, sent in zip(groups, self.sent, strict=True):
+            got = self.cube.swap(sent, flips[group[0]])
             self.last.append(got)
             at = 0
-            for s, stream in streams:
-                count = stream[0].count
-                axes = [b for b in stream[0].axes if b not in self.settled[s] and b != bit]
-                stream.append(Term(got, axes, at, count))
-                at += count
-            for s in sides:
-                self.settled[s].append(bit)
+            for s in group:
+                axes = [b for b in range(self.cube.bits)[::-1] if b not in done[s] and b != flips[s]]
+                for stream in self.sides[s]:
+                    stream.append(Term(got, axes, at, stream[0].count))
+                    at += stream[0].count
         self.step += 1
         return self
 
     def finish(self):
         while self.step < self.cube.bits:
             self.advance()
-        return [[self.cube.total(stream, self.settled[s]) for stream in self.sides[s]] for s in range(2)]
+        done = list(range(self.cube.bits))
+        outs = self.cube.add([[(stream, done, None)] for side in self.sides for stream in side], F32)
+        return outs
 
 
 def gate(value, *others):
@@ -673,9 +707,6 @@
     devices = d // rows
     hidden = w_up.shape[1]
     per_device = hidden // devices
-    parts = 2
-    sub = per_device // parts
-    width = hidden // parts
     my_index = lax.axis_index("seq")
     seg_full = segments[0]
     seg_local = lax.dynamic_slice_in_dim(seg_full, my_index * n, n)
@@ -687,28 +718,25 @@
     vectors = jnp.concatenate([ln1_gain, ln1_bias, ln2_gain, ln2_bias]).reshape(1, 4 * rows)
     ln_block = jnp.pad(vectors, ((0, LN_ROWS - 1), (0, d - 4 * rows)))
     first_local = jnp.concatenate([w_query, w_key, w_value, ln_block], axis=0)
-    up_parts = w_up.reshape(rows, devices, parts, sub).transpose(2, 0, 1, 3).reshape(parts, rows, width // d, d)
-    up_parts = up_parts.transpose(0, 2, 1, 3).reshape(parts, (width // d) * rows, d)
-    part_local = [
-        jnp.concatenate([up_parts[p], w_down[p * sub : (p + 1) * sub]], axis=0) for p in range(parts)
-    ]
-    part_local[0] = jnp.concatenate([part_local[0], w_out], axis=0)
+    tiles = hidden // d
+    up_local = w_up.reshape(rows, tiles, d).transpose(1, 0, 2).reshape(tiles * rows, d)
+    second_local = jnp.concatenate([up_local, w_down, w_out], axis=0)
 
     def gather(local):
         out = lax.all_gather(local, BOTH, axis=0, tiled=True)
         return out.reshape(devices, local.shape[0], d)
 
     first = gather(first_local)
-    second = [gather(p) for p in part_local]
+    second = gather(second_local)
 
     aligned = rows % 16 == 0
     if aligned:
         qkv_w, qkv_rows = first, rows
-        out_w, out_t, out_rows = second[0], second[0].shape[1] // rows - 1, rows
+        out_w, out_t, out_rows = second, second.shape[1] // rows - 1, rows
     else:
         qkv_w = first[:, : 3 * rows].reshape(devices, 3, rows, d).transpose(1, 0, 2, 3).reshape(1, 3 * d, d)
         qkv_rows = d
-        out_w, out_t, out_rows = second[0][:, -rows:].reshape(1, d, d), 0, d
+        out_w, out_t, out_rows = second[:, -rows:].reshape(1, d, d), 0, d
     ln = first[:, 3 * rows, : 4 * rows].reshape(devices, 4, rows).transpose(1, 0, 2).reshape(4, 1, d).astype(F32)
 
     h1, own = kv_call(x, ln[0], ln[1], qkv_w, qkv_rows)
@@ -730,119 +758,103 @@
         send = lax.dynamic_index_in_dim(value, 1 - my_index, axis, keepdims=False)
         return keep, send
 
-    up_rows = (width // d) * rows
-    tiles = width // d
-    group = FF_COLS // sub
-    carry, gmid, ffn, crossed = mid, None, [], []
-    for p in range(parts):
-        if aligned:
-            per_tile = d // FF_COLS
-            tile = up_rows // sub
-            wu = (second[p], pl.BlockSpec((devices, rows, FF_COLS), lambda j, *_: (0, j // per_tile, j % per_tile)))
-            wd = (second[p], pl.BlockSpec((group, sub, d), lambda j, *_: (j, tile, 0)))
-            up_out = (
-                pl.BlockSpec((None, dp, rows, FF_COLS), lambda j, *_: (j // per_tile, 0, 0, j % per_tile)),
-                jax.ShapeDtypeStruct((tiles, dp, rows, d), BF16),
-            )
-            down_out = (
-                pl.BlockSpec((tiles, group // 2, rows, d), lambda j, *_: (0, j, 0, 0)),
-                jax.ShapeDtypeStruct((tiles, dp, rows, d), BF16),
-            )
-            grad_specs = [up_out, up_out, down_out, down_out]
-        else:
-            up_w = second[p][:, :up_rows].reshape(devices, tiles, rows, d).transpose(0, 2, 1, 3).reshape(d, width)
-            down_w = second[p][:, up_rows : up_rows + sub].reshape(width, d)
-            up_block = pl.BlockSpec((d, FF_COLS), lambda j, *_: (0, j))
-            down_block = pl.BlockSpec((FF_COLS, d), lambda j, *_: (j, 0))
-            wu, wd = (up_w, up_block), (down_w, down_block)
-            grad_specs = [
-                (up_block, jax.ShapeDtypeStruct((d, width), BF16)),
-                (down_block, jax.ShapeDtypeStruct((width, d), BF16)),
-            ]
-        carry, gmid, *grads = ffn_call(
-            me, h2, cot, wu, wd, carry, gmid, grad_specs, width, p == parts - 1, aligned
+    up_rows = tiles * rows
+    group = FF_COLS // per_device
+    if aligned:
+        per_tile = d // FF_COLS
+        wu = (second, pl.BlockSpec((devices, rows, FF_COLS), lambda j, *_: (0, j // per_tile, j % per_tile)))
+        wd = (second, pl.BlockSpec((group, per_device, d), lambda j, *_: (j, up_rows // per_device, 0)))
+        up_out = (
+            pl.BlockSpec((None, dp, rows, FF_COLS), lambda j, *_: (j // per_tile, 0, 0, j % per_tile)),
+            jax.ShapeDtypeStruct((tiles, dp, rows, d), BF16),
         )
-        if not aligned:
-            dwu = grads[0].reshape(dp, 2, rows, tiles, d).transpose(3, 0, 1, 2, 4)
-            dwd = grads[1].reshape(dp, 2, tiles, rows, d).transpose(2, 0, 1, 3, 4)
-            grads = [*halves(dwu, 2), *halves(dwd, 2)]
-        keep_up, send_up, keep_down, send_down = grads
-        crossed.append((exchange(send_up), exchange(send_down)))
-        ffn.append(
-            Scatter(cube, [cube.terms([keep_up, crossed[p][0]])], [cube.terms([keep_down, crossed[p][1]])])
+        down_out = (
+            pl.BlockSpec((tiles, group // 2, rows, d), lambda j, *_: (0, j, 0, 0)),
+            jax.ShapeDtypeStruct((tiles, dp, rows, d), BF16),
         )
-    mixed = carry
-
-    early, late = ffn
-    gmid = gate(gmid, crossed[0])
-    early.advance()
+        grad_specs = [up_out, up_out, down_out, down_out]
+    else:
+        up_w = second[:, :up_rows].reshape(devices, tiles, rows, d).transpose(0, 2, 1, 3).reshape(d, hidden)
+        down_w = second[:, up_rows : up_rows + per_device].reshape(hidden, d)
+        up_block = pl.BlockSpec((d, FF_COLS), lambda j, *_: (0, j))
+        down_block = pl.BlockSpec((FF_COLS, d), lambda j, *_: (j, 0))
+        wu, wd = (up_w, up_block), (down_w, down_block)
+        grad_specs = [
+            (up_block, jax.ShapeDtypeStruct((d, hidden), BF16)),
+            (down_block, jax.ShapeDtypeStruct((hidden, d), BF16)),
+        ]
+    mixed, gmid, *grads = ffn_call(me, h2, cot, wu, wd, mid, grad_specs, hidden, aligned)
+    if not aligned:
+        dwu = grads[0].reshape(dp, 2, rows, tiles, d).transpose(3, 0, 1, 2, 4)
+        dwd = grads[1].reshape(dp, 2, tiles, rows, d).transpose(2, 0, 1, 3, 4)
+        grads = [*halves(dwu, 2), *halves(dwd, 2)]
+    keep_up, send_up, keep_down, send_down = grads
+    got_up, got_down = exchange(send_up), exchange(send_down)
+    big = Scatter(cube, [cube.terms([keep_up, got_up])], [cube.terms([keep_down, got_down])])
+    big.advance()
     grad_mid, grad_att, keep_out, send_out, dln2 = mid_back_call(
-        me, gmid, mid, cot, attended, out_w, out_rows, out_t, ln[2], dp
+        me, gate(gmid, big.sent), mid, cot, attended, out_w, out_rows, out_t, ln[2], dp
     )
     got_out = exchange(send_out)
-    late.advance()
     dqs, dkvs, qkv_terms, raw = [], [], [], []
 
-    def finish_group(g):
+    def finish_group(g, *waited):
         dq, dkv, got = raw[g]
-        keep, send, dkv = qkv_grad_call(me, h1, dq, dkv, got, dp)
+        keep, send, dkv = qkv_grad_call(me, h1, gate(dq, *waited), dkv, got, dp)
         dqs.append(dq)
         dkvs.append(dkv)
         qkv_terms.append([keep, exchange(send)])
         return dkv
 
     def attend_group(g, *waited):
+        if raw:
+            waited += (raw[-1][0],)
         dq, dkv, sent = attend_back_call(
             gate(tab, *waited), q, grad_att, attended, own, other, seg_q, seg_own_col, seg_other_col, lse,
             ATT_Q, ATT_K, g,
         )
         raw.append((dq, dkv, exchange(sent)))
 
-    attend_group(0, crossed[1])
-    waited = early.last
-    early.advance()
-    attend_group(1, waited)
-    done = finish_group(0)
-    waited = early.last + late.last + [done]
-    early.advance()
-    late.advance()
-    attend_group(2, waited)
+    attend_group(0)
+    attend_group(1)
+    first_done = big.last
+    big.advance()
+    finish_group(0, first_done, big.sent)
     done = finish_group(1)
     tail_one = Scatter(
         cube,
         [cube.terms(qkv_terms[0]), cube.terms([keep_out, got_out], 0, 2)],
         [cube.terms(qkv_terms[1]), cube.terms([keep_out, got_out], 2, 2)],
     )
-    waited = early.last + late.last + [done]
-    early.advance()
-    late.advance()
     tail_one.advance()
-    attend_group(3, waited)
-    finish_group(2)
-    finish_group(3)
+    attend_group(2, tail_one.sent, done)
+    waited = [big.last, tail_one.last]
+    big.advance()
+    tail_one.advance()
+    attend_group(3, *waited, big.sent, tail_one.sent)
+    waited = [big.last, tail_one.last]
+    big.advance()
+    tail_one.advance()
+    finish_group(2, big.sent)
+    finish_group(3, dkvs[-1], tail_one.sent)
     tail_two = Scatter(cube, [cube.terms(qkv_terms[2])], [cube.terms(qkv_terms[3])])
-    waited = early.last + late.last + tail_one.last
-    late.advance()
+    tail_two.advance()
+    waited = [big.last, tail_one.last]
     tail_one.advance()
-    tail_two.advance()
+    waited += [tail_one.sent, tail_two.sent]
     token_grad, dln1 = head_back_call(dqs, dkvs, x, gate(grad_mid, *waited), qkv_w, qkv_rows, ln[0])
 
-    dln = jnp.concatenate([dln1, dln2], axis=0).reshape(4, dp, 2, rows).transpose(2, 1, 0, 3)
-    keep, send = halves(dln.reshape(2, dp, 4 * rows), 0)
-    dln = keep + exchange(send)
-    for b in range(cube.bits)[::-1]:
-        pair = dln.reshape(2, -1, 4 * rows)
-        sent = lax.dynamic_index_in_dim(pair, 1 - cube.mine[b], 0, keepdims=False)
-        dln = lax.dynamic_index_in_dim(pair, cube.mine[b], 0, keepdims=False) + cube.swap(sent, b)
-    dln = dln.reshape(4, rows)
-
-    ffn_sums = [f.finish() for f in ffn]
-    (one_a, one_b), (two_a, two_b) = tail_one.finish(), tail_two.finish()
-    up_share = jnp.stack([s[0][0] for s in ffn_sums]).reshape(parts, tiles, rows, devices // tiles, sub)
-    up_share = up_share.transpose(2, 1, 3, 0, 4).reshape(rows, hidden)
-    down_share = jnp.concatenate([s[1][0].reshape(sub, d) for s in ffn_sums], axis=0)
-    qkv_share = jnp.concatenate([one_a[0], one_b[0], two_a[0], two_b[0]], axis=-1)
-    out_share = jnp.concatenate([one_a[1], one_b[1]], axis=0).transpose(1, 0, 2).reshape(rows, d)
+    dln = jnp.concatenate([dln1, dln2], axis=0).reshape(4, devices, rows).transpose(1, 0, 2)
+    dln = lax.all_to_all(dln.reshape(devices, 4 * rows), BOTH, 0, 0, tiled=True)
+    dln = jnp.sum(dln.reshape(devices, 4, rows), axis=0)
+
+    up_share, down_share = big.finish()
+    one_a, out_a, one_b, out_b = tail_one.finish()
+    two_a, two_b = tail_two.finish()
+    up_share = up_share.transpose(1, 0, 2).reshape(rows, hidden)
+    down_share = down_share.reshape(per_device, d)
+    qkv_share = jnp.concatenate([one_a, one_b, two_a, two_b], axis=-1)
+    out_share = jnp.concatenate([out_a, out_b], axis=0).transpose(1, 0, 2).reshape(rows, d)
     return (
         mixed[None],
         token_grad[None],

time: 631 us -> 586 us (0.929)
  other arithmetic: 65.7 us -> 6.22 us
  Pallas kernels: 249 us -> 290 us
  starting transfers between devices: 41.1 us -> 26.3 us
  local copies, waits for them, and re-layouts: 51.5 us -> 40.9 us
    convert_element_type x35 -> x0, other arithmetic: 46.2 us -> none  [advance(): self.cube.total(stream, self.settled[s], bit).astype(BF16)]
    pallas_call x2 -> x16, Pallas kernels: 77.1 us -> 106 us  [the longest x1 66.8 us: ffn_call(): pl.pallas_call(partial(ffn_kernel, aligned), grid_spec=spec, out_shape=[j...]
    ppermute x28 -> x18, starting transfers between devices: 34.6 us -> 14.1 us  [swap(): lax.ppermute(array, 'dp', [(i, i ^ 1 << bit) for i in range(self.dp)])]
    ppermute x28 -> x18, waiting for transfers between devices: 68.4 us -> 50.9 us  [swap(): lax.ppermute(array, 'dp', [(i, i ^ 1 << bit) for i in range(self.dp)])]
    unnamed x121 -> x131, local copies, waits for them, and re-layouts: 24 us -> 32.9 us
    ppermute x14 -> x11, waiting for transfers between devices: 9.53 us -> 18.4 us  [exchange(): return lax.ppermute(value, 'seq', swap)]
    pallas_call x4, Pallas kernels: 73.4 us -> 81.8 us  [attend_back_call(): pl.pallas_call(partial(attend_back_kernel, bq, bk), grid_spec=spec, out_s...]
    all_gather x3 -> x2, waiting for transfers between devices: 123 us -> 132 us  [gather(): out = lax.all_gather(local, BOTH, axis=0, tiled=True)]
  transfers between devices with their start and end apart: 46 -> 33, of which waited for: 23 -> 13; matrix products, arithmetic and copies ran while one was open for 14% -> 2% of each run, Pallas kernels for 31% -> 35%
where the time goes in v3:
time: 586 us; the launch traced here: 580 us
  Pallas kernels  290 us (49%)
  waiting for transfers between devices  201 us (34%)
  local copies, waits for them, and re-layouts  40.9 us (7%)
  starting transfers between devices  26.3 us (4%)
  between operations  15 us (3%)
  other arithmetic  6.22 us (1%)
    all_gather x2, waiting for transfers between devices, gather(): out = lax.all_gather(local, BOTH, axis=0, tiled=True)  132 us
    pallas_call x4, Pallas kernels, attend_back_call(): pl.pallas_call(partial(attend_back_kernel, bq, bk), grid_spec=spec, out_s...  81.8 us
    pallas_call x1, Pallas kernels, ffn_call(): pl.pallas_call(partial(ffn_kernel, aligned), grid_spec=spec, out_shape=[j...  66.8 us
    ppermute x18, waiting for transfers between devices, swap(): lax.ppermute(array, 'dp', [(i, i ^ 1 << bit) for i in range(self.dp)])  50.9 us
    pallas_call x1, Pallas kernels, attend_call(): pl.pallas_call(partial(attend_kernel, bq, bk), grid_spec=spec, out_shape=...  47 us
    pallas_call x15, Pallas kernels, add(): pl.pallas_call(kernel, grid_spec=spec, out_shape=out_shape, compiler_para...  39.1 us
    unnamed x131, local copies, waits for them, and re-layouts  32.9 us
    ppermute x11, waiting for transfers between devices, exchange(): return lax.ppermute(value, 'seq', swap)  18.4 us
  transfers between devices with their start and end apart: 33, of which 13 were waited for; matrix products, arithmetic and copies ran while one was open for 2% of the time, Pallas kernels for 35%

profile of v3, /device:TPU:0, one launch (start us, length us, event | category | flops | bytes accessed | tf_op | source)
XLA Modules:
  0.0 579.9 jit_solution(17726853661717186294)
XLA Ops:
  8.0 1.6 fusion.1
  10.7 1.9 pad_maximum_fusion
  12.6 75.1 %all-gather.3.cloned.1.call-done = bf16[3584,1024]{1,0:T(8,128)(2,1)} async-done(((bf16[112,1024]{1,0:T(8,128)(2,1)}), bf16[3584,1024]{1,0:T(8,128)(2,1)}) %all-gather.3.cloned.1.call-update) | async-done | bytes 7340048 | tf_op jit(solution)/shard_map/all_gather | solution.py:726
  88.8 1.6 copy-done.32
  90.4 9.5 %kv_proj.1 = (bf16[1024,1024]{1,0:T(8,128)(2,1)S(1)}, bf16[2,1024,1024]{2,1,0:T(8,128)(2,1)}) custom-call(bf16[1024,1024]{1,0:T(8,128)(2,1)S(1)} %bitcast.170, f32[1,1024]{1,0:T(1,128)S(1)} %squeeze.35.gain_ref.refs_13_, f32[1,1024]{1,0:T(1,128)S(1)} %squeeze.36.bias_ref, bf16[32,112,1024]{2,1,0:T(8,128)(2,1)} %bitcast.98, bf16[32,112,1024]{2,1,0:T(8,128)(2,1)} %bitcast.99), custom_call_target="tpu_custom_call" | custom-call | flops 42949672 | bytes 125829 | tf_op jit(solution)/shard_map/kv_proj/pallas_call | solution.py:86
  103.5 3.1 copy-done
  106.7 3.1 q_proj.1.q_ref
  111.1 47.0 %attend.1 = (bf16[1024,1024]{1,0:T(8,128)(2,1)}, f32[4,4,1,1024]{3,2,1,0:T(1,128)}) custom-call(s32[16]{0:T(128)} %reshape.422.tab, bf16[1024,1024]{1,0:T(8,128)(2,1)} %copy-done.4, bf16[2,1024,1024]{2,1,0:T(8,128)(2,1)} %get-tuple-element.84.ko_ref.vo_ref, bf16[2,1024,1024]{2,1,0:T(8,128)(2,1)} %get-tuple-element.84.ko_ref.vo_ref, ...), custom_call_target="tpu_custom_call" | custom-call | flops 300000000 | bytes 125829 | tf_op jit(solution)/shard_map/attend/pallas_call | solution.py:200
  158.1 56.5 %all-gather.5.cloned.1.call-done = bf16[9216,1024]{1,0:T(8,128)(2,1)} async-done(((bf16[288,1024]{1,0:T(8,128)(2,1)}), bf16[9216,1024]{1,0:T(8,128)(2,1)}) %all-gather.5.cloned.1.call-update) | async-done | bytes 18874384 | tf_op jit(solution)/shard_map/all_gather | solution.py:726
  216.2 5.7 out_proj.1
  221.9 2.0 copy-done.34
  225.3 66.8 %ffn.1 = (bf16[1024,1024]{1,0:T(8,128)(2,1)}, f32[1024,1024]{1,0:T(8,128)}, bf16[4,16,32,1024]{3,2,1,0:T(8,128)(2,1)}, bf16[4,16,32,1024]{3,2,1,0:T(8,128)(2,1)}...) custom-call(s32[1]{0:T(128)} %bitcast.me, bf16[1024,1024]{1,0:T(8,128)(2,1)} %copy-done.44, ...), custom_call_target="tpu_custom_call" | custom-call | flops 515396064 | bytes 482344 | tf_op jit(solution)/shard_map/ffn/pallas_call | solution.py:453
  292.6 7.0 %collective-permute-done.1 = bf16[4,16,32,1024]{3,2,1,0:T(8,128)(2,1)} collective-permute-done((bf16[4,16,32,1024]{3,2,1,0:T(8,128)(2,1)}, bf16[4,16,32,1024]{3,2,1,0:T(8,128)(2,1)}, u32[]{:S(2)}, u32[]{:S(2)}) %collective-permute-start.1) | collective-permute-done | bytes 4194336 | tf_op jit(solution)/shard_map/ppermute | solution.py:754
  299.5 6.0 %collective-permute-done.2 = bf16[4,16,32,1024]{3,2,1,0:T(8,128)(2,1)} collective-permute-done((bf16[4,16,32,1024]{3,2,1,0:T(8,128)(2,1)}, bf16[4,16,32,1024]{3,2,1,0:T(8,128)(2,1)}, u32[]{:S(2)}, u32[]{:S(2)}) %collective-permute-start.2) | collective-permute-done | bytes 4194336 | tf_op jit(solution)/shard_map/ppermute | solution.py:754
  305.5 2.2 copy-done.1
  307.7 7.9 %add_terms.15 = (bf16[4,2,2,2,32,1024]{5,4,3,2,1,0:T(8,128)(2,1)}, bf16[4,2,2,2,32,1024]{5,4,3,2,1,0:T(8,128)(2,1)}) custom-call(s32[4]{0:T(128)S(1)} %shift-right-arithmetic_and_fusion.mine, bf16[4,2,2,2,2,32,1024]{6,5,4,3,2,1,0:T(8,128)(2,1)S(1)} %bitcast.124, bf16[4,2,2,2,2,32,1024]{6,5,4,3,2,1,0:T(8,128)(2,1)} %bitcast.20.refs_1_, ...), custom_call_target="tpu_custom_call" | custom-call | flops 83886 | bytes 167772 | tf_op jit(solution)/shard_map/add_terms/pallas_call | solution.py:619
  317.7 13.5 %out_proj_back.1 = (f32[1024,1024]{1,0:T(8,128)}, bf16[1024,1024]{1,0:T(8,128)(2,1)S(1)}, bf16[4,16,32,256]{3,2,1,0:T(8,128)(2,1)S(1)}, bf16[4,16,32,256]{3,2,1,0:T(8,128)(2,1)S(1)}, f32[2,1024]{1,0:T(2,128)S(1)}) custom-call(s32[1]{0:T(128)} %bitcast.me, f32[1024,1024]{1,0:T(8,128)} %get-tuple-element.96.gh_ref, f32[1024,1024]{1,0:T(8,128)} %copy-done.34, ...), custom_call_target="tpu_custom_call" | custom-call | flops 42949672 | bytes 230686 | tf_op jit(solution)/shard_map/out_proj_back/pallas_call | solution.py:381
  332.5 20.5 %attend_back.4 = (bf16[1024,256]{1,0:T(8,128)(2,1)}, bf16[2,1024,256]{2,1,0:T(8,128)(2,1)}, bf16[2,1024,256]{2,1,0:T(8,128)(2,1)}) custom-call(s32[16]{0:T(128)} %reshape.422.tab, bf16[1024,1024]{1,0:T(8,128)(2,1)} %copy-done.4, bf16[1024,1024]{1,0:T(8,128)(2,1)} %copy-done.9, bf16[1024,1024]{1,0:T(8,128)(2,1)} %get-tuple-element.85.o_ref, ...), custom_call_target="tpu_custom_call" | custom-call | flops 120000000 | bytes 62914 | tf_op jit(solution)/shard_map/attend_back/pallas_call | solution.py:294
  353.0 20.3 %attend_back.5 = (bf16[1024,256]{1,0:T(8,128)(2,1)}, bf16[2,1024,256]{2,1,0:T(8,128)(2,1)}, bf16[2,1024,256]{2,1,0:T(8,128)(2,1)}) custom-call(s32[16]{0:T(128)} %reshape.422.tab, bf16[1024,1024]{1,0:T(8,128)(2,1)} %copy-done.4, bf16[1024,1024]{1,0:T(8,128)(2,1)} %copy-done.9, bf16[1024,1024]{1,0:T(8,128)(2,1)} %get-tuple-element.85.o_ref, ...), custom_call_target="tpu_custom_call" | custom-call | flops 120000000 | bytes 62914 | tf_op jit(solution)/shard_map/attend_back/pallas_call | solution.py:294
  373.3 2.9 collective-permute-start.8
  376.7 2.0 collective-permute-done.8.rkv_ref
  382.6 1.9 qkv_grad.5
  385.9 5.3 add_terms.16
  391.2 1.9 qkv_grad.4
  394.3 2.1 collective-permute-done.6
  396.5 4.0 add_terms.17
  400.6 2.0 collective-permute-start.13
  402.5 20.7 %attend_back.6 = (bf16[1024,256]{1,0:T(8,128)(2,1)}, bf16[2,1024,256]{2,1,0:T(8,128)(2,1)}, bf16[2,1024,256]{2,1,0:T(8,128)(2,1)}) custom-call(s32[16]{0:T(128)} %reshape.422.tab, bf16[1024,1024]{1,0:T(8,128)(2,1)} %copy-done.4, bf16[1024,1024]{1,0:T(8,128)(2,1)} %copy-done.9, bf16[1024,1024]{1,0:T(8,128)(2,1)} %get-tuple-element.85.o_ref, ...), custom_call_target="tpu_custom_call" | custom-call | flops 120000000 | bytes 62914 | tf_op jit(solution)/shard_map/attend_back/pallas_call | solution.py:294
  424.2 3.7 add_terms.18
  427.9 6.1 %collective-permute-done.12.refs_2_.refs_5_.refs_6_.refs_7_.refs_8_ = bf16[5,2,2,2,32,256]{5,4,3,2,1,0:T(8,128)(2,1)S(1)} collective-permute-done((bf16[5,2,2,2,32,256]{5,4,3,2,1,0:T(8,128)(2,1)}, bf16[5,2,2,2,32,256]{5,4,3,2,1,0:T(8,128)(2,1)S(1)}, u32[]{:S(2)}, u32[]{:S(2)}) %collective-permute-start.12) | collective-permute-done | bytes 655392 | tf_op jit(solution)/shard_map/ppermute | solution.py:573
  434.0 1.8 add_terms.19
  435.9 20.3 %attend_back.7 = (bf16[1024,256]{1,0:T(8,128)(2,1)}, bf16[2,1024,256]{2,1,0:T(8,128)(2,1)}, bf16[2,1024,256]{2,1,0:T(8,128)(2,1)}) custom-call(s32[16]{0:T(128)} %reshape.422.tab, bf16[1024,1024]{1,0:T(8,128)(2,1)} %copy-done.4, bf16[1024,1024]{1,0:T(8,128)(2,1)} %copy-done.9, bf16[1024,1024]{1,0:T(8,128)(2,1)} %get-tuple-element.85.o_ref, ...), custom_call_target="tpu_custom_call" | custom-call | flops 120000000 | bytes 62914 | tf_op jit(solution)/shard_map/attend_back/pallas_call | solution.py:294
  458.1 9.0 %collective-permute-done.16.refs_3_.refs_7_.refs_8_.refs_9_ = bf16[5,2,2,32,256]{4,3,2,1,0:T(8,128)(2,1)S(1)} collective-permute-done((bf16[5,2,2,32,256]{4,3,2,1,0:T(8,128)(2,1)S(1)}, bf16[5,2,2,32,256]{4,3,2,1,0:T(8,128)(2,1)S(1)}, u32[]{:S(2)}, u32[]{:S(2)}) %collective-permute-start.16) | collective-permute-done | bytes 327712 | tf_op jit(solution)/shard_map/ppermute | solution.py:573
  472.4 1.7 add_terms.21
  474.1 2.8 add_terms.20
  477.0 3.3 qkv_grad.6
  480.4 3.2 qkv_grad.7
  489.0 1.7 collective-permute-start.25
  491.9 5.6 collective-permute-done.20.refs_4_.refs_9_.refs_14_.refs_19_.refs_10_.refs_16_.refs_22_
  498.3 24.6 %collective-permute-done.23.refs_5_.refs_11_.refs_17_.refs_23_ = bf16[10,32,256]{2,1,0:T(8,128)(2,1)S(1)} collective-permute-done((bf16[10,32,256]{2,1,0:T(8,128)(2,1)S(1)}, bf16[10,32,256]{2,1,0:T(8,128)(2,1)S(1)}, u32[]{:S(2)}, u32[]{:S(2)}) %collective-permute-start.23) | collective-permute-done | bytes 163872 | tf_op jit(solution)/shard_map/ppermute | solution.py:573
  525.9 1.7 collective-permute-start.27
  527.6 13.8 %qkv_back.1 = (bf16[1024,1024]{1,0:T(8,128)(2,1)}, f32[2,1024]{1,0:T(2,128)S(1)}) custom-call(bf16[1024,256]{1,0:T(8,128)(2,1)S(1)} %copy-done.38, bf16[1024,256]{1,0:T(8,128)(2,1)S(1)} %copy-done.40, bf16[1024,256]{1,0:T(8,128)(2,1)S(1)} %copy-done.42, bf16[1024,256]{1,0:T(8,128)(2,1)S(1)} %copy-done.43, bf16[2,1024,256]{2,1,0:T(8,128)(2,1)S(1)} %copy-done.54, ...), custom_call_target="tpu_custom_call" | custom-call | flops 64424508 | bytes 209715 | tf_op jit(solution)/shard_map/qkv_back/pallas_call | solution.py:519
  541.5 1.6 add_terms.26
  544.0 4.7 all-to-all-start
  550.1 2.2 copy-done.3
  553.4 3.3 add_terms.29
  562.6 2.7 collective-permute-start.29
  565.9 4.7 collective-permute-done.29.refs_5_.refs_11_
  (215 shorter events, 52.4 us)
Async XLA Ops:
  7.2 80.5 %all-gather.3.cloned.1.call-start = ((), (), s32[]{:S(2)}) async-start(), calls=%async_computation.1 | async-start | bytes 7569408 | tf_op jit(solution)/shard_map/all_gather | solution.py:726
  9.6 205.0 %all-gather.5.cloned.1.call-start = ((), (), s32[]{:S(2)}) async-start(), calls=%async_computation.2 | async-start | bytes 19464192 | tf_op jit(solution)/shard_map/all_gather | solution.py:726
  99.9 11.2 %collective-permute-start = (bf16[2,1024,1024]{2,1,0:T(8,128)(2,1)}, bf16[2,1024,1024]{2,1,0:T(8,128)(2,1)}, u32[]{:S(2)}, u32[]{:S(2)}) collective-permute-start(bf16[2,1024,1024]{2,1,0:T(8,128)(2,1)} %get-tuple-element.84.ko_ref.vo_ref), channel_id=1, source_target_pairs={{0,1},{1,0},{2,3},{3,2},{4,5},{5,4},{6,7},{7,6},{8,9},{9,8},{10,11... | collective-permute-start | bytes 12582920 | tf_op jit(solution)/shard_map/ppermute | solution.py:744
  111.1 103.5 %copy-start.33 = (bf16[1,1024,1024]{2,1,0:T(8,128)(2,1)S(1)}, bf16[1,1024,1024]{2,1,0:T(8,128)(2,1)}, u32[]{:S(2)}) copy-start(bf16[1,1024,1024]{2,1,0:T(8,128)(2,1)} %param.13) | copy-start | bytes 6291460
  292.0 7.5 %collective-permute-start.1 = (bf16[4,16,32,1024]{3,2,1,0:T(8,128)(2,1)}, bf16[4,16,32,1024]{3,2,1,0:T(8,128)(2,1)}, u32[]{:S(2)}, u32[]{:S(2)}) collective-permute-start(bf16[4,16,32,1024]{3,2,1,0:T(8,128)(2,1)} %get-tuple-element.91), channel_id=1, source_target_pairs={{0,1},{1,0},{2,3},{3,2},{4,5},{5,4},{6,7},{7,6},{8,9},{9,8},{10,11... | collective-permute-start | bytes 12582920 | tf_op jit(solution)/shard_map/ppermute | solution.py:754
  292.3 13.2 %collective-permute-start.2 = (bf16[4,16,32,1024]{3,2,1,0:T(8,128)(2,1)}, bf16[4,16,32,1024]{3,2,1,0:T(8,128)(2,1)}, u32[]{:S(2)}, u32[]{:S(2)}) collective-permute-start(bf16[4,16,32,1024]{3,2,1,0:T(8,128)(2,1)} %get-tuple-element.93), channel_id=1, source_target_pairs={{0,1},{1,0},{2,3},{3,2},{4,5},{5,4},{6,7},{7,6},{8,9},{9,8},{10,11... | collective-permute-start | bytes 12582920 | tf_op jit(solution)/shard_map/ppermute | solution.py:754
  315.6 70.3 %collective-permute-start.3 = (bf16[4,2,2,2,32,1024]{5,4,3,2,1,0:T(8,128)(2,1)}, bf16[4,2,2,2,32,1024]{5,4,3,2,1,0:T(8,128)(2,1)}, u32[]{:S(2)}, u32[]{:S(2)}) collective-permute-start(bf16[4,2,2,2,32,1024]{5,4,3,2,1,0:T(8,128)(2,1)} %get-tuple-element.94), channel_id=1, source_target_pairs={{0,2},{2,0},{4,6},{6,4},{8,10},{10,8},{12,14},{14,12},{16,18},{18,... | collective-permute-start | bytes 6291464 | tf_op jit(solution)/shard_map/ppermute | solution.py:573
  317.0 68.9 %collective-permute-start.4 = (bf16[4,2,2,2,32,1024]{5,4,3,2,1,0:T(8,128)(2,1)}, bf16[4,2,2,2,32,1024]{5,4,3,2,1,0:T(8,128)(2,1)}, u32[]{:S(2)}, u32[]{:S(2)}) collective-permute-start(bf16[4,2,2,2,32,1024]{5,4,3,2,1,0:T(8,128)(2,1)} %get-tuple-element.95), channel_id=1, source_target_pairs={{0,4},{2,6},{4,0},{6,2},{8,12},{10,14},{12,8},{14,10},{16,20},{18,... | collective-permute-start | bytes 6291464 | tf_op jit(solution)/shard_map/ppermute | solution.py:573
  373.3 5.4 collective-permute-start.8
  376.2 15.0 %collective-permute-start.5 = (bf16[2,1024,256]{2,1,0:T(8,128)(2,1)}, bf16[2,1024,256]{2,1,0:T(8,128)(2,1)S(1)}, u32[]{:S(2)}, u32[]{:S(2)}) collective-permute-start(bf16[2,1024,256]{2,1,0:T(8,128)(2,1)} %get-tuple-element.106), channel_id=1, source_target_pairs={{0,1},{1,0},{2,3},{3,2},{4,5},{5,4},{6,7},{7,6},{8,9},{9,8},{10,11... | collective-permute-start | bytes 3145736 | tf_op jit(solution)/shard_map/ppermute | solution.py:754
  376.3 18.0 %collective-permute-start.7 = (bf16[4,16,32,256]{3,2,1,0:T(8,128)(2,1)S(1)}, bf16[4,16,32,256]{3,2,1,0:T(8,128)(2,1)S(1)}, u32[]{:S(2)}, u32[]{:S(2)}) collective-permute-start(bf16[4,16,32,256]{3,2,1,0:T(8,128)(2,1)S(1)} %get-tuple-element.110), channel_id=1, source_target_pairs={{0,1},{1,0},{2,3},{3,2},{4,5},{5,4},{6,7},{7,6},{8,9},{9,8},{10,11... | collective-permute-start | bytes 3145736 | tf_op jit(solution)/shard_map/ppermute | solution.py:754
  385.5 10.9 %copy-start.10 = (bf16[3,16,32,256]{3,2,1,0:T(8,128)(2,1)}, bf16[3,16,32,256]{3,2,1,0:T(8,128)(2,1)S(1)}, u32[]{:S(2)}) copy-start(bf16[3,16,32,256]{3,2,1,0:T(8,128)(2,1)S(1)} %get-tuple-element.113) | copy-start | bytes 2359300
  385.5 8.8 %collective-permute-start.9 = (bf16[3,16,32,256]{3,2,1,0:T(8,128)(2,1)S(1)}, bf16[3,16,32,256]{3,2,1,0:T(8,128)(2,1)S(1)}, u32[]{:S(2)}, u32[]{:S(2)}) collective-permute-start(bf16[3,16,32,256]{3,2,1,0:T(8,128)(2,1)S(1)} %get-tuple-element.114), channel_id=1, source_target_pairs={{0,1},{1,0},{2,3},{3,2},{4,5},{5,4},{6,7},{7,6},{8,9},{9,8},{10,11... | collective-permute-start | bytes 2359304 | tf_op jit(solution)/shard_map/ppermute | solution.py:754
  394.2 2.3 collective-permute-start.6
  394.3 29.9 %collective-permute-start.10 = (bf16[4,2,2,32,1024]{4,3,2,1,0:T(8,128)(2,1)}, bf16[4,2,2,32,1024]{4,3,2,1,0:T(8,128)(2,1)}, u32[]{:S(2)}, u32[]{:S(2)}) collective-permute-start(bf16[4,2,2,32,1024]{4,3,2,1,0:T(8,128)(2,1)} %get-tuple-element.102), channel_id=1, source_target_pairs={{0,4},{2,6},{4,0},{6,2},{8,12},{10,14},{12,8},{14,10},{16,20},{18,... | collective-permute-start | bytes 3145736 | tf_op jit(solution)/shard_map/ppermute | solution.py:573
  394.3 29.9 %collective-permute-start.11 = (bf16[4,2,2,32,1024]{4,3,2,1,0:T(8,128)(2,1)}, bf16[4,2,2,32,1024]{4,3,2,1,0:T(8,128)(2,1)}, u32[]{:S(2)}, u32[]{:S(2)}) collective-permute-start(bf16[4,2,2,32,1024]{4,3,2,1,0:T(8,128)(2,1)} %get-tuple-element.103), channel_id=1, source_target_pairs={{0,2},{2,0},{4,6},{6,4},{8,10},{10,8},{12,14},{14,12},{16,18},{18,... | collective-permute-start | bytes 3145736 | tf_op jit(solution)/shard_map/ppermute | solution.py:573
  400.5 33.5 %collective-permute-start.12 = (bf16[5,2,2,2,32,256]{5,4,3,2,1,0:T(8,128)(2,1)}, bf16[5,2,2,2,32,256]{5,4,3,2,1,0:T(8,128)(2,1)S(1)}, u32[]{:S(2)}, u32[]{:S(2)}) collective-permute-start(bf16[5,2,2,2,32,256]{5,4,3,2,1,0:T(8,128)(2,1)} %get-tuple-element.115), channel_id=1, source_target_pairs={{0,2},{2,0},{4,6},{6,4},{8,10},{10,8},{12,14},{14,12},{16,18},{18,... | collective-permute-start | bytes 1966088 | tf_op jit(solution)/shard_map/ppermute | solution.py:573
  400.6 33.4 %collective-permute-start.13 = (bf16[5,2,2,2,32,256]{5,4,3,2,1,0:T(8,128)(2,1)}, bf16[5,2,2,2,32,256]{5,4,3,2,1,0:T(8,128)(2,1)S(1)}, u32[]{:S(2)}, u32[]{:S(2)}) collective-permute-start(bf16[5,2,2,2,32,256]{5,4,3,2,1,0:T(8,128)(2,1)} %get-tuple-element.116), channel_id=1, source_target_pairs={{0,4},{2,6},{4,0},{6,2},{8,12},{10,14},{12,8},{14,10},{16,20},{18,... | collective-permute-start | bytes 1966088 | tf_op jit(solution)/shard_map/ppermute | solution.py:573
  423.2 10.8 %copy-start.11 = (bf16[3,16,32,256]{3,2,1,0:T(8,128)(2,1)S(1)}, bf16[3,16,32,256]{3,2,1,0:T(8,128)(2,1)}, u32[]{:S(2)}) copy-start(bf16[3,16,32,256]{3,2,1,0:T(8,128)(2,1)} %copy-done.10) | copy-start | bytes 2359300
  423.3 10.7 %copy-start.15 = (bf16[3,16,32,256]{3,2,1,0:T(8,128)(2,1)S(1)}, bf16[3,16,32,256]{3,2,1,0:T(8,128)(2,1)}, u32[]{:S(2)}) copy-start(bf16[3,16,32,256]{3,2,1,0:T(8,128)(2,1)} %copy-done.14) | copy-start | bytes 2359300
  423.3 10.7 %copy-start.19 = (bf16[3,16,32,256]{3,2,1,0:T(8,128)(2,1)S(1)}, bf16[3,16,32,256]{3,2,1,0:T(8,128)(2,1)}, u32[]{:S(2)}) copy-start(bf16[3,16,32,256]{3,2,1,0:T(8,128)(2,1)} %copy-done.18) | copy-start | bytes 2359300
  423.3 10.7 %copy-start.23 = (bf16[3,16,32,256]{3,2,1,0:T(8,128)(2,1)S(1)}, bf16[3,16,32,256]{3,2,1,0:T(8,128)(2,1)}, u32[]{:S(2)}) copy-start(bf16[3,16,32,256]{3,2,1,0:T(8,128)(2,1)} %copy-done.22) | copy-start | bytes 2359300
  423.3 53.6 %collective-permute-start.15 = (bf16[2,1024,256]{2,1,0:T(8,128)(2,1)}, bf16[2,1024,256]{2,1,0:T(8,128)(2,1)}, u32[]{:S(2)}, u32[]{:S(2)}) collective-permute-start(bf16[2,1024,256]{2,1,0:T(8,128)(2,1)} %get-tuple-element.127), channel_id=1, source_target_pairs={{0,1},{1,0},{2,3},{3,2},{4,5},{5,4},{6,7},{7,6},{8,9},{9,8},{10,11... | collective-permute-start | bytes 3145736 | tf_op jit(solution)/shard_map/ppermute | solution.py:754
  427.9 46.2 %collective-permute-start.14 = (bf16[8,2,32,1024]{3,2,1,0:T(8,128)(2,1)}, bf16[8,2,32,1024]{3,2,1,0:T(8,128)(2,1)}, u32[]{:S(2)}, u32[]{:S(2)}) collective-permute-start(bf16[8,2,32,1024]{3,2,1,0:T(8,128)(2,1)} %add_terms.18), channel_id=1, source_target_pairs={{0,8},{2,10},{4,12},{6,14},{8,0},{10,2},{12,4},{14,6},{16,24},{18,... | collective-permute-start | bytes 3145736 | tf_op jit(solution)/shard_map/ppermute | solution.py:573
  456.2 24.2 %collective-permute-start.18 = (bf16[2,1024,256]{2,1,0:T(8,128)(2,1)}, bf16[2,1024,256]{2,1,0:T(8,128)(2,1)}, u32[]{:S(2)}, u32[]{:S(2)}) collective-permute-start(bf16[2,1024,256]{2,1,0:T(8,128)(2,1)} %get-tuple-element.131), channel_id=1, source_target_pairs={{0,1},{1,0},{2,3},{3,2},{4,5},{5,4},{6,7},{7,6},{8,9},{9,8},{10,11... | collective-permute-start | bytes 3145736 | tf_op jit(solution)/shard_map/ppermute | solution.py:754
  457.4 9.7 %collective-permute-start.16 = (bf16[5,2,2,32,256]{4,3,2,1,0:T(8,128)(2,1)S(1)}, bf16[5,2,2,32,256]{4,3,2,1,0:T(8,128)(2,1)S(1)}, u32[]{:S(2)}, u32[]{:S(2)}) collective-permute-start(bf16[5,2,2,32,256]{4,3,2,1,0:T(8,128)(2,1)S(1)} %get-tuple-element.120), channel_id=1, source_target_pairs={{0,4},{2,6},{4,0},{6,2},{8,12},{10,14},{12,8},{14,10},{16,20},{18,... | collective-permute-start | bytes 983048 | tf_op jit(solution)/shard_map/ppermute | solution.py:573
  458.1 9.8 %collective-permute-start.17 = (bf16[5,2,2,32,256]{4,3,2,1,0:T(8,128)(2,1)S(1)}, bf16[5,2,2,32,256]{4,3,2,1,0:T(8,128)(2,1)S(1)}, u32[]{:S(2)}, u32[]{:S(2)}) collective-permute-start(bf16[5,2,2,32,256]{4,3,2,1,0:T(8,128)(2,1)S(1)} %get-tuple-element.121), channel_id=1, source_target_pairs={{0,2},{2,0},{4,6},{6,4},{8,10},{10,8},{12,14},{14,12},{16,18},{18,... | collective-permute-start | bytes 983048 | tf_op jit(solution)/shard_map/ppermute | solution.py:573
  480.3 5.4 collective-permute-start.21
  484.5 56.9 %copy-start.28 = (bf16[3,16,32,256]{3,2,1,0:T(8,128)(2,1)}, bf16[3,16,32,256]{3,2,1,0:T(8,128)(2,1)S(1)}, u32[]{:S(2)}) copy-start(bf16[3,16,32,256]{3,2,1,0:T(8,128)(2,1)S(1)} %get-tuple-element.136) | copy-start | bytes 2359300
  484.5 13.1 %copy-start.13 = (bf16[3,16,32,256]{3,2,1,0:T(8,128)(2,1)S(1)}, bf16[3,16,32,256]{3,2,1,0:T(8,128)(2,1)}, u32[]{:S(2)}) copy-start(bf16[3,16,32,256]{3,2,1,0:T(8,128)(2,1)} %copy-done.10) | copy-start | bytes 2359300
  484.5 13.1 %copy-start.17 = (bf16[3,16,32,256]{3,2,1,0:T(8,128)(2,1)S(1)}, bf16[3,16,32,256]{3,2,1,0:T(8,128)(2,1)}, u32[]{:S(2)}) copy-start(bf16[3,16,32,256]{3,2,1,0:T(8,128)(2,1)} %copy-done.14) | copy-start | bytes 2359300
  484.5 13.1 %copy-start.21 = (bf16[3,16,32,256]{3,2,1,0:T(8,128)(2,1)S(1)}, bf16[3,16,32,256]{3,2,1,0:T(8,128)(2,1)}, u32[]{:S(2)}) copy-start(bf16[3,16,32,256]{3,2,1,0:T(8,128)(2,1)} %copy-done.18) | copy-start | bytes 2359300
  484.5 13.1 %copy-start.25 = (bf16[3,16,32,256]{3,2,1,0:T(8,128)(2,1)S(1)}, bf16[3,16,32,256]{3,2,1,0:T(8,128)(2,1)}, u32[]{:S(2)}) copy-start(bf16[3,16,32,256]{3,2,1,0:T(8,128)(2,1)} %copy-done.22) | copy-start | bytes 2359300
  484.5 2.5 collective-permute-start.22
  485.1 12.5 %collective-permute-start.20 = (bf16[10,2,32,256]{3,2,1,0:T(8,128)(2,1)S(1)}, bf16[10,2,32,256]{3,2,1,0:T(8,128)(2,1)S(1)}, u32[]{:S(2)}, u32[]{:S(2)}) collective-permute-start(bf16[10,2,32,256]{3,2,1,0:T(8,128)(2,1)S(1)} %add_terms.21), channel_id=1, source_target_pairs={{0,8},{2,10},{4,12},{6,14},{8,0},{10,2},{12,4},{14,6},{16,24},{18,... | collective-permute-start | bytes 983048 | tf_op jit(solution)/shard_map/ppermute | solution.py:573
  485.7 55.7 %copy-start.26 = (bf16[3,16,32,256]{3,2,1,0:T(8,128)(2,1)}, bf16[3,16,32,256]{3,2,1,0:T(8,128)(2,1)S(1)}, u32[]{:S(2)}) copy-start(bf16[3,16,32,256]{3,2,1,0:T(8,128)(2,1)S(1)} %collective-permute-done.21) | copy-start | bytes 2359300
  487.0 54.5 %copy-start.30 = (bf16[3,16,32,256]{3,2,1,0:T(8,128)(2,1)}, bf16[3,16,32,256]{3,2,1,0:T(8,128)(2,1)S(1)}, u32[]{:S(2)}) copy-start(bf16[3,16,32,256]{3,2,1,0:T(8,128)(2,1)S(1)} %collective-permute-done.22) | copy-start | bytes 2359300
  488.5 35.2 %collective-permute-start.24 = (bf16[3,2,2,2,32,256]{5,4,3,2,1,0:T(8,128)(2,1)S(1)}, bf16[3,2,2,2,32,256]{5,4,3,2,1,0:T(8,128)(2,1)S(1)}, u32[]{:S(2)}, u32[]{:S(2)}) collective-permute-start(bf16[3,2,2,2,32,256]{5,4,3,2,1,0:T(8,128)(2,1)S(1)} %get-tuple-element.138), channel_id=1, source_target_pairs={{0,2},{2,0},{4,6},{6,4},{8,10},{10,8},{12,14},{14,12},{16,18},{18,... | collective-permute-start | bytes 1179656 | tf_op jit(solution)/shard_map/ppermute | solution.py:573
  489.0 34.7 %collective-permute-start.25 = (bf16[3,2,2,2,32,256]{5,4,3,2,1,0:T(8,128)(2,1)S(1)}, bf16[3,2,2,2,32,256]{5,4,3,2,1,0:T(8,128)(2,1)S(1)}, u32[]{:S(2)}, u32[]{:S(2)}) collective-permute-start(bf16[3,2,2,2,32,256]{5,4,3,2,1,0:T(8,128)(2,1)S(1)} %get-tuple-element.139), channel_id=1, source_target_pairs={{0,4},{2,6},{4,0},{6,2},{8,12},{10,14},{12,8},{14,10},{16,20},{18,... | collective-permute-start | bytes 1179656 | tf_op jit(solution)/shard_map/ppermute | solution.py:573
  490.7 36.8 %collective-permute-start.19 = (bf16[8,32,1024]{2,1,0:T(8,128)(2,1)S(1)}, bf16[8,32,1024]{2,1,0:T(8,128)(2,1)S(1)}, u32[]{:S(2)}, u32[]{:S(2)}) collective-permute-start(bf16[8,32,1024]{2,1,0:T(8,128)(2,1)S(1)} %add_terms.20), channel_id=1, source_target_pairs={{0,16},{2,18},{4,20},{6,22},{8,24},{10,26},{12,28},{14,30},{16,0},... | collective-permute-start | bytes 1572872 | tf_op jit(solution)/shard_map/ppermute | solution.py:573
  498.3 24.7 %collective-permute-start.23 = (bf16[10,32,256]{2,1,0:T(8,128)(2,1)S(1)}, bf16[10,32,256]{2,1,0:T(8,128)(2,1)S(1)}, u32[]{:S(2)}, u32[]{:S(2)}) collective-permute-start(bf16[10,32,256]{2,1,0:T(8,128)(2,1)S(1)} %add_terms.22), channel_id=1, source_target_pairs={{0,16},{2,18},{4,20},{6,22},{8,24},{10,26},{12,28},{14,30},{16,0},... | collective-permute-start | bytes 491528 | tf_op jit(solution)/shard_map/ppermute | solution.py:573
  523.7 17.8 %copy-start.35 = (bf16[3,2,2,2,32,256]{5,4,3,2,1,0:T(8,128)(2,1)}, bf16[3,2,2,2,32,256]{5,4,3,2,1,0:T(8,128)(2,1)S(1)}, u32[]{:S(2)}) copy-start(bf16[3,2,2,2,32,256]{5,4,3,2,1,0:T(8,128)(2,1)S(1)} %collective-permute-done.25.refs_5_.refs_6_.refs_7_.refs_8_) | copy-start | bytes 1179652
  525.0 16.5 %collective-permute-start.26 = (bf16[3,2,2,32,256]{4,3,2,1,0:T(8,128)(2,1)S(1)}, bf16[3,2,2,32,256]{4,3,2,1,0:T(8,128)(2,1)S(1)}, u32[]{:S(2)}, u32[]{:S(2)}) collective-permute-start(bf16[3,2,2,32,256]{4,3,2,1,0:T(8,128)(2,1)S(1)} %get-tuple-element.146), channel_id=1, source_target_pairs={{0,4},{2,6},{4,0},{6,2},{8,12},{10,14},{12,8},{14,10},{16,20},{18,... | collective-permute-start | bytes 589832 | tf_op jit(solution)/shard_map/ppermute | solution.py:573
  525.9 15.6 %collective-permute-start.27 = (bf16[3,2,2,32,256]{4,3,2,1,0:T(8,128)(2,1)S(1)}, bf16[3,2,2,32,256]{4,3,2,1,0:T(8,128)(2,1)S(1)}, u32[]{:S(2)}, u32[]{:S(2)}) collective-permute-start(bf16[3,2,2,32,256]{4,3,2,1,0:T(8,128)(2,1)S(1)} %get-tuple-element.147), channel_id=1, source_target_pairs={{0,2},{2,0},{4,6},{6,4},{8,10},{10,8},{12,14},{14,12},{16,18},{18,... | collective-permute-start | bytes 589832 | tf_op jit(solution)/shard_map/ppermute | solution.py:573
  527.6 13.9 %copy-start.45 = (bf16[8,32,1024]{2,1,0:T(8,128)(2,1)}, bf16[8,32,1024]{2,1,0:T(8,128)(2,1)S(1)}, u32[]{:S(2)}) copy-start(bf16[8,32,1024]{2,1,0:T(8,128)(2,1)S(1)} %collective-permute-done.19.refs_5_.refs_11_) | copy-start | bytes 1572868
  543.1 15.2 %collective-permute-start.28 = (bf16[6,2,32,256]{3,2,1,0:T(8,128)(2,1)}, bf16[6,2,32,256]{3,2,1,0:T(8,128)(2,1)}, u32[]{:S(2)}, u32[]{:S(2)}) collective-permute-start(bf16[6,2,32,256]{3,2,1,0:T(8,128)(2,1)} %add_terms.26), channel_id=1, source_target_pairs={{0,8},{2,10},{4,12},{6,14},{8,0},{10,2},{12,4},{14,6},{16,24},{18,... | collective-permute-start | bytes 589832 | tf_op jit(solution)/shard_map/ppermute | solution.py:573
  544.0 13.5 %all-to-all-start = ((f32[32,1,128]{2,1,0:T(1,128)}), f32[32,1,128]{2,1,0:T(1,128)}, u32[]{:S(2)}, u32[]{:S(2)}) async-start(f32[32,1,128]{2,1,0:T(1,128)} %bitcast.35), calls=%async_computation | async-start | bytes 32768 | tf_op jit(solution)/shard_map/all_to_all | solution.py:848
  562.6 7.9 %collective-permute-start.29 = (bf16[6,32,256]{2,1,0:T(8,128)(2,1)S(1)}, bf16[6,32,256]{2,1,0:T(8,128)(2,1)S(1)}, u32[]{:S(2)}, u32[]{:S(2)}) collective-permute-start(bf16[6,32,256]{2,1,0:T(8,128)(2,1)S(1)} %add_terms.27), channel_id=1, source_target_pairs={{0,16},{2,18},{4,20},{6,22},{8,24},{10,26},{12,28},{14,30},{16,0},... | collective-permute-start | bytes 294920 | tf_op jit(solution)/shard_map/ppermute | solution.py:573
  (49 other events, 152.4 us)
Sparse Core Ops, SparseCore 0:
  11.4 76.1 all-gather.2
  91.1 123.4 all-gather.4

commit v4 on v3

v4 whole, which is shorter than its diff:
```python
import math
from functools import partial

import jax
import jax.numpy as jnp
from jax import lax
from jax.experimental import pallas as pl
from jax.experimental.pallas import tpu as pltpu
from jax.sharding import PartitionSpec as P

BF16 = jnp.bfloat16
F32 = jnp.float32
HEAD_DIM = 64
GROUP = 4
GROUP_WIDTH = GROUP * HEAD_DIM
NEG = -1000000000.0
BOTH = ("dp", "seq")
ATT_Q = 256
ATT_K = 512
ROWS = 256
FF_COLS = 512
COST_SCALE = 100000
STEP_BITS = 1


def dot_nn(left, right):
    return lax.dot_general(left, right, (((1,), (0,)), ((), ())), preferred_element_type=F32)


def dot_nt(left, right):
    return lax.dot_general(left, right, (((1,), (1,)), ((), ())), preferred_element_type=F32)


def dot_tn(left, right):
    return lax.dot_general(left, right, (((0,), (0,)), ((), ())), preferred_element_type=F32)


def params(mib):
    return pltpu.CompilerParams(vmem_limit_bytes=mib << 20)


def cost(flops, nbytes, scale=None):
    if scale:
        return pl.CostEstimate(flops=scale * flops, bytes_accessed=scale * nbytes, transcendentals=0)
    return pl.CostEstimate(flops=flops // COST_SCALE, bytes_accessed=nbytes // COST_SCALE, transcendentals=0)


def normed(values):
    centre = values - jnp.mean(values, axis=-1, keepdims=True)
    scale = lax.rsqrt(jnp.mean(centre * centre, axis=-1, keepdims=True) + 1e-05)
    return centre * scale, scale


def norm_back(grad, gain_vec, hat, scale):
    inner = grad * gain_vec
    return scale * (
        inner
        - jnp.mean(inner, axis=-1, keepdims=True)
        - hat * jnp.mean(inner * hat, axis=-1, keepdims=True)
    )


def flat(ref):
    value = ref[...]
    return value.reshape(-1, value.shape[-1])


def resident(shape):
    zeros = (0,) * len(shape)
    return pl.BlockSpec(shape, lambda *_: zeros, pipeline_mode=pl.Buffered(1))


class Spread:
    def __init__(self, block, pieces):
        self.block, self.pieces = block, pieces
        self.args = [b for rounds, *_ in pieces for b in rounds.buffers]

    def start(self, refs, place, target, sem, columns=None):
        for i, (rounds, first, count, at) in enumerate(self.pieces):
            for ref, (flips, core) in zip(refs[4 * i : 4 * i + 4], rounds.parts, strict=True):
                for e, flip in enumerate(flips):
                    device = (place[0] ^ flip) * 2 + (place[1] ^ core)
                    row = pl.multiple_of(device * self.block + at, count)
                    source = ref.at[e, pl.ds(first, count)]
                    if columns is not None:
                        source = ref.at[e, pl.ds(first, count), columns]
                    pltpu.make_async_copy(source, target.at[pl.ds(row, count), :], sem).start()

    def start_rows(self, refs, place, target, sem, first, group):
        ((rounds, begin, count, _),) = self.pieces
        for k in range(group):
            device = first + k
            flip = (device // 2) ^ place[0]
            at, last = rounds.index(flip)
            core = (device % 2) ^ place[1]
            for i, ref in enumerate(refs):

                @pl.when((last == i % 2) & (core == i // 2))
                def _(ref=ref, at=at, k=k):
                    pltpu.make_async_copy(
                        ref.at[at, pl.ds(begin, count)], target.at[pl.ds(k * count, count), :], sem
                    ).start()


class Plain:
    def __init__(self, array, block):
        self.args, self.block = [array], block

    def start(self, refs, place, target, sem, columns=None):
        source = refs[0] if columns is None else refs[0].at[:, columns]
        pltpu.make_async_copy(source, target, sem).start()

    def start_rows(self, refs, place, target, sem, first, group):
        pltpu.make_async_copy(refs[0].at[pl.ds(first * self.block, group * self.block), :], target, sem).start()


def arrived(target, sem):
    pltpu.make_async_copy(target, target, sem).wait()


def cut(refs, weights):
    parts = []
    for weight in weights:
        parts.append(refs[: len(weight.args)])
        refs = refs[len(weight.args) :]
    return parts, refs


def load_all(weights, parts, place, targets, sem):
    @pl.when(pl.program_id(0) == 0)
    def _():
        for i, weight in enumerate(weights):
            weight.start(parts[i], place, targets[i], sem.at[i])
        for i in range(len(weights)):
            arrived(targets[i], sem.at[i])


HBM = pl.BlockSpec(memory_space=pl.ANY)


def weight_args(weights):
    args = [a for w in weights for a in w.args]
    return [HBM] * len(args), args


def kv_kernel(weights, place, x_ref, gain_ref, bias_ref, *refs):
    parts, refs = cut(refs, weights)
    h_ref, kv_ref, wk, wv, sem = refs
    load_all(weights, parts, place, (wk, wv), sem)
    hat, _ = normed(x_ref[...].astype(F32))
    low = (hat * gain_ref[...] + bias_ref[...]).astype(BF16)
    h_ref[...] = low
    kv_ref[0] = dot_nn(low, wk[...]).astype(BF16)
    kv_ref[1] = dot_nn(low, wv[...]).astype(BF16)


def kv_call(place, x, gain, bias, weights):
    n, d = x.shape
    row = pl.BlockSpec((ROWS, d), lambda i, *_: (i, 0))
    specs, args = weight_args(weights)
    spec = pltpu.PrefetchScalarGridSpec(
        num_scalar_prefetch=1,
        grid=(n // ROWS,),
        in_specs=[row, resident((1, d)), resident((1, d))] + specs,
        out_specs=[row, pl.BlockSpec((2, ROWS, d), lambda i, *_: (0, i, 0))],
        scratch_shapes=[pltpu.VMEM((d, d), BF16)] * 2 + [pltpu.SemaphoreType.DMA((2,))],
    )
    return pl.pallas_call(
        partial(kv_kernel, weights),
        grid_spec=spec,
        out_shape=[jax.ShapeDtypeStruct((n, d), BF16), jax.ShapeDtypeStruct((2, n, d), BF16)],
        compiler_params=params(40),
        cost_estimate=cost(4 * n * d * d, 4 * d * d + 8 * n * d),
        name="kv_proj",
    )(place, x, gain, bias, *args)


def q_kernel(weights, place, h_ref, *refs):
    parts, refs = cut(refs, weights)
    q_ref, wq, sem = refs
    load_all(weights, parts, place, (wq,), sem)
    q_ref[...] = (dot_nn(h_ref[...], wq[...]).astype(BF16).astype(F32) * 0.125).astype(BF16)


def q_call(place, h, weights):
    n, d = h.shape
    row = pl.BlockSpec((ROWS, d), lambda i, *_: (i, 0))
    specs, args = weight_args(weights)
    spec = pltpu.PrefetchScalarGridSpec(
        num_scalar_prefetch=1,
        grid=(n // ROWS,),
        in_specs=[row] + specs,
        out_specs=row,
        scratch_shapes=[pltpu.VMEM((d, d), BF16), pltpu.SemaphoreType.DMA((1,))],
    )
    return pl.pallas_call(
        partial(q_kernel, weights),
        grid_spec=spec,
        out_shape=jax.ShapeDtypeStruct((n, d), BF16),
        compiler_params=params(32),
        cost_estimate=cost(2 * n * d * d, 2 * d * d + 4 * n * d),
        name="q_proj",
    )(place, h, *args)


def stack_heads(block):
    lane = lax.broadcasted_iota(jnp.int32, block.shape, 1) // HEAD_DIM
    zero = jnp.zeros_like(block)
    return jnp.concatenate([jnp.where(lane == h, block, zero) for h in range(GROUP)], axis=0)


def head_cols(value, h, width):
    return value[:, h * width : (h + 1) * width]


def head_rows(value, h):
    return value[h * HEAD_DIM : (h + 1) * HEAD_DIM, :]


def attend_kernel(bq, bk, tab, q_ref, ko_ref, vo_ref, kp_ref, vp_ref, sq_ref, so_ref, sp_ref, o_ref, lse_ref):
    i = pl.program_id(1)
    stacked = stack_heads(q_ref[...])
    seg_q = jnp.concatenate([sq_ref[0]] * GROUP, axis=1)

    def over(k_ref, v_ref, s_ref, first, count, state):
        def step(j, carry):
            top, total, acc = carry
            at = pl.multiple_of((first + j) * bk, bk)
            scores = dot_nt(k_ref[0, pl.ds(at, bk), :], stacked)
            scores = jnp.where(s_ref[pl.ds(at, bk), :] == seg_q, scores, NEG)
            new_top = jnp.maximum(top, jnp.max(scores, axis=0, keepdims=True))
            decay = jnp.exp(top - new_top)
            probs = jnp.exp(scores - new_top)
            total = total * decay + jnp.sum(probs, axis=0, keepdims=True)
            low = probs.astype(BF16)
            values = v_ref[0, pl.ds(at, bk), :].T
            acc = tuple(
                acc[h] * head_cols(decay, h, bq) + dot_nn(head_rows(values, h), head_cols(low, h, bq))
                for h in range(GROUP)
            )
            return new_top, total, acc

        return lax.fori_loop(0, count, step, state)

    state = (
        jnp.full((1, GROUP * bq), -jnp.inf, F32),
        jnp.zeros((1, GROUP * bq), F32),
        tuple(jnp.zeros((HEAD_DIM, bq), F32) for _ in range(GROUP)),
    )
    state = over(ko_ref, vo_ref, so_ref, tab[4 * i], tab[4 * i + 1], state)
    top, total, acc = over(kp_ref, vp_ref, sp_ref, tab[4 * i + 2], tab[4 * i + 3], state)
    out = jnp.concatenate([acc[h] / head_cols(total, h, bq) for h in range(GROUP)], axis=0)
    o_ref[...] = out.T.astype(BF16)
    lse_ref[0, 0] = top + jnp.log(total)


def attend_call(tab, q, own, other, seg_q, seg_own, seg_other, bq, bk, first, groups):
    n, d = q.shape
    blocks = n // bq
    query = pl.BlockSpec((bq, GROUP_WIDTH), lambda g, i, *_: (i, g + first))

    def half(which):
        return pl.BlockSpec((1, n, GROUP_WIDTH), lambda g, i, *_: (which, 0, g + first))

    column = pl.BlockSpec((n, 1), lambda g, i, *_: (0, 0))
    spec = pltpu.PrefetchScalarGridSpec(
        num_scalar_prefetch=1,
        grid=(groups, blocks),
        in_specs=[
            query,
            half(0),
            half(1),
            half(0),
            half(1),
            pl.BlockSpec((1, 1, bq), lambda g, i, *_: (i, 0, 0)),
            column,
            column,
        ],
        out_specs=[
            pl.BlockSpec((bq, GROUP_WIDTH), lambda g, i, *_: (i, g)),
            pl.BlockSpec((1, 1, 1, GROUP * bq), lambda g, i, *_: (g, i, 0, 0)),
        ],
    )
    return pl.pallas_call(
        partial(attend_kernel, bq, bk),
        grid_spec=spec,
        out_shape=[
            jax.ShapeDtypeStruct((n, groups * GROUP_WIDTH), BF16),
            jax.ShapeDtypeStruct((groups, blocks, 1, GROUP * bq), F32),
        ],
        compiler_params=params(56),
        cost_estimate=cost(8_000_000_000 * groups, 3 * groups * n * d),
        name="attend",
    )(tab, q, own, own, other, other, seg_q, seg_own, seg_other)


def attend_back_kernel(
    bq, bk, tab, q_ref, go_ref, o_ref, ko_ref, vo_ref, kp_ref, vp_ref, sq_ref, so_ref, sp_ref, lse_ref,
    dq_ref, down_ref, dpart_ref, dko, dvo, dkp, dvp,
):
    i = pl.program_id(1)

    @pl.when(i == 0)
    def _():
        for ref in (dko, dvo, dkp, dvp):
            ref[...] = jnp.zeros_like(ref)

    stacked = stack_heads(q_ref[...])
    grad = go_ref[...]
    stacked_grad = stack_heads(grad)
    product = (grad.astype(F32) * o_ref[...].astype(F32)).T
    inner = jnp.concatenate(
        [jnp.sum(head_rows(product, h), axis=0, keepdims=True) for h in range(GROUP)], axis=1
    )
    seg_q = jnp.concatenate([sq_ref[0]] * GROUP, axis=1)
    lse = lse_ref[0, 0]

    def over(k_ref, v_ref, s_ref, dk, dv, first, count, state):
        def step(j, acc):
            at = pl.multiple_of((first + j) * bk, bk)
            keys = k_ref[0, pl.ds(at, bk), :]
            scores = dot_nt(keys, stacked)
            scores = jnp.where(s_ref[pl.ds(at, bk), :] == seg_q, scores, NEG)
            probs = jnp.exp(scores - lse)
            grad_probs = dot_nt(v_ref[0, pl.ds(at, bk), :], stacked_grad)
            grad_scores = (probs * (grad_probs - inner)).astype(BF16)
            dv[pl.ds(at, bk), :] += dot_nn(probs.astype(BF16), stacked_grad)
            dk[pl.ds(at, bk), :] += dot_nn(grad_scores, stacked)
            keys_t = keys.T
            return tuple(
                acc[h] + dot_nn(head_rows(keys_t, h), head_cols(grad_scores, h, bq)) for h in range(GROUP)
            )

        return lax.fori_loop(0, count, step, state)

    state = tuple(jnp.zeros((HEAD_DIM, bq), F32) for _ in range(GROUP))
    state = over(ko_ref, vo_ref, so_ref, dko, dvo, tab[4 * i], tab[4 * i + 1], state)
    state = over(kp_ref, vp_ref, sp_ref, dkp, dvp, tab[4 * i + 2], tab[4 * i + 3], state)
    dq_ref[...] = (jnp.concatenate(state, axis=0).T * 0.125).astype(BF16)

    @pl.when(i == pl.num_programs(1) - 1)
    def _():
        down_ref[0] = dko[...].astype(BF16)
        down_ref[1] = dvo[...].astype(BF16)
        dpart_ref[0] = dkp[...].astype(BF16)
        dpart_ref[1] = dvp[...].astype(BF16)


def attend_back_call(tab, q, grad, out, own, other, seg_q, seg_own, seg_other, lse, bq, bk, first, groups, out_first):
    n, d = q.shape
    blocks = n // bq
    query = pl.BlockSpec((bq, GROUP_WIDTH), lambda g, i, *_: (i, g + first))

    def half(which):
        return pl.BlockSpec((1, n, GROUP_WIDTH), lambda g, i, *_: (which, 0, g + first))

    column = pl.BlockSpec((n, 1), lambda *_: (0, 0))
    pair = pl.BlockSpec((2, n, GROUP_WIDTH), lambda g, i, *_: (0, 0, g))
    spec = pltpu.PrefetchScalarGridSpec(
        num_scalar_prefetch=1,
        grid=(groups, blocks),
        in_specs=[
            query,
            query,
            pl.BlockSpec((bq, GROUP_WIDTH), lambda g, i, *_: (i, g + out_first)),
            half(0),
            half(1),
            half(0),
            half(1),
            pl.BlockSpec((1, 1, bq), lambda g, i, *_: (i, 0, 0)),
            column,
            column,
            pl.BlockSpec((1, 1, 1, GROUP * bq), lambda g, i, *_: (g + out_first, i, 0, 0)),
        ],
        out_specs=[pl.BlockSpec((bq, GROUP_WIDTH), lambda g, i, *_: (i, g)), pair, pair],
        scratch_shapes=[pltpu.VMEM((n, GROUP_WIDTH), F32)] * 4,
    )
    width = groups * GROUP_WIDTH
    return pl.pallas_call(
        partial(attend_back_kernel, bq, bk),
        grid_spec=spec,
        out_shape=[
            jax.ShapeDtypeStruct((n, width), BF16),
            jax.ShapeDtypeStruct((2, n, width), BF16),
            jax.ShapeDtypeStruct((2, n, width), BF16),
        ],
        compiler_params=params(56),
        cost_estimate=cost(12_000_000_000 * groups, 6 * groups * n * d),
        name="attend_back",
    )(tab, q, grad, out, own, own, other, other, seg_q, seg_own, seg_other, lse)


def mid_kernel(weights, count, place, x_ref, gain_ref, bias_ref, *refs):
    outs, refs = refs[:count], refs[count:]
    parts, refs = cut(refs, weights)
    r_ref, h_ref, wo, sem = refs
    load_all(weights, parts, place, (wo,), sem)
    mid = x_ref[...].astype(F32) + dot_nn(jnp.concatenate([o[...] for o in outs], axis=1), wo[...])
    r_ref[...] = mid
    hat, _ = normed(mid)
    h_ref[...] = (hat * gain_ref[...] + bias_ref[...]).astype(BF16)


def mid_call(place, x, outs, weights, gain, bias):
    n, d = x.shape
    row = pl.BlockSpec((ROWS, d), lambda i, *_: (i, 0))
    specs, args = weight_args(weights)
    spec = pltpu.PrefetchScalarGridSpec(
        num_scalar_prefetch=1,
        grid=(n // ROWS,),
        in_specs=[row, resident((1, d)), resident((1, d))]
        + [pl.BlockSpec((ROWS, o.shape[1]), lambda i, *_: (i, 0)) for o in outs]
        + specs,
        out_specs=[row, row],
        scratch_shapes=[pltpu.VMEM((d, d), BF16), pltpu.SemaphoreType.DMA((1,))],
    )
    return pl.pallas_call(
        partial(mid_kernel, weights, len(outs)),
        grid_spec=spec,
        out_shape=[jax.ShapeDtypeStruct((n, d), F32), jax.ShapeDtypeStruct((n, d), BF16)],
        compiler_params=params(32),
        cost_estimate=cost(2 * n * d * d, 2 * d * d + 10 * n * d),
        name="out_proj",
    )(place, x, gain, bias, *outs, *args)


def mid_back_kernel(weights, count, place, gh_ref, r_ref, g_ref, gain_ref, *refs):
    outs, refs = refs[:count], refs[count:]
    parts, refs = cut(refs, weights)
    gr_ref, go_ref, keep_ref, send_ref, dln_ref, acc, wo, sem = refs
    load_all(weights, parts, place, (wo,), sem)
    i = pl.program_id(0)
    hat, scale = normed(r_ref[...])
    grad = gh_ref[...]
    total = g_ref[...].astype(F32) + norm_back(grad, gain_ref[...], hat, scale)
    gr_ref[...] = total
    low = total.astype(BF16)
    go_ref[...] = dot_nt(low, wo[...]).astype(BF16)
    part = dot_tn(jnp.concatenate([o[...] for o in outs], axis=1), low)
    dgain = jnp.sum(grad * hat, axis=0, keepdims=True)
    dbias = jnp.sum(grad, axis=0, keepdims=True)

    @pl.when(i == 0)
    def _():
        acc[...] = part
        dln_ref[0:1, :] = dgain
        dln_ref[1:2, :] = dbias

    @pl.when(i > 0)
    def _():
        acc[...] += part
        dln_ref[0:1, :] += dgain
        dln_ref[1:2, :] += dbias

    @pl.when(i == pl.num_programs(0) - 1)
    def _():
        lanes = keep_ref.shape[3]
        for ref, value in zip(
            (keep_ref, send_ref), split_pairs(acc[...].astype(BF16), keep_ref.shape[1], place[1]), strict=True
        ):
            for t in range(ref.shape[0]):
                ref[t] = value[:, :, t * lanes : (t + 1) * lanes]


def mid_back_call(place, grad, mid, cot, outs, weights, gain, groups):
    n, d = mid.shape
    row = pl.BlockSpec((ROWS, d), lambda i, *_: (i, 0))
    share = (d // GROUP_WIDTH, groups, d // (2 * groups), GROUP_WIDTH)
    specs, args = weight_args(weights)
    spec = pltpu.PrefetchScalarGridSpec(
        num_scalar_prefetch=1,
        grid=(n // ROWS,),
        in_specs=[row, row, row, resident((1, d))]
        + [pl.BlockSpec((ROWS, o.shape[1]), lambda i, *_: (i, 0)) for o in outs]
        + specs,
        out_specs=[
            row,
            row,
            pl.BlockSpec(share, lambda *_: (0, 0, 0, 0)),
            pl.BlockSpec(share, lambda *_: (0, 0, 0, 0)),
            pl.BlockSpec((2, d), lambda *_: (0, 0)),
        ],
        scratch_shapes=[
            pltpu.VMEM((d, d), F32),
            pltpu.VMEM((d, d), BF16),
            pltpu.SemaphoreType.DMA((1,)),
        ],
    )
    return pl.pallas_call(
        partial(mid_back_kernel, weights, len(outs)),
        grid_spec=spec,
        out_shape=[
            jax.ShapeDtypeStruct((n, d), F32),
            jax.ShapeDtypeStruct((n, d), BF16),
            jax.ShapeDtypeStruct(share, BF16),
            jax.ShapeDtypeStruct(share, BF16),
            jax.ShapeDtypeStruct((2, d), F32),
        ],
        compiler_params=params(48),
        cost_estimate=cost(4 * n * d * d, 4 * d * d + 18 * n * d),
        name="out_proj_back",
    )(place, grad, mid, cot, gain, *outs, *args)


def split_pairs(value, groups, my_index):
    rows = value.shape[0] // (2 * groups)
    pairs = value.reshape(groups, 2, rows, value.shape[1])
    even, odd = pairs[:, 0], pairs[:, 1]
    first = my_index == 0
    return jnp.where(first, even, odd), jnp.where(first, odd, even)


def ffn_grads(h, grad, wu, wd):
    up = dot_nn(h, wu)
    cdf = 0.5 * (1.0 + lax.erf(up * 0.7071067811865476))
    act = (up * cdf).astype(BF16)
    slope = cdf + up * (jnp.exp(-0.5 * up * up) * 0.3989422804014327)
    gu = (dot_nt(grad, wd) * slope).astype(BF16)
    return act, gu, dot_tn(h, gu).astype(BF16), dot_tn(act, grad).astype(BF16)


def ffn_sums(j, act, gu, wu, wd, mid_ref, mixed_ref, gh_ref, acc):
    @pl.when(j == 0)
    def _():
        acc[...] = mid_ref[...] + dot_nn(act, wd)
        gh_ref[...] = dot_nt(gu, wu)

    @pl.when(j > 0)
    def _():
        acc[...] += dot_nn(act, wd)
        gh_ref[...] += dot_nt(gu, wu)

    @pl.when(j == pl.num_programs(0) - 1)
    def _():
        mixed_ref[...] = acc[...].astype(BF16)


def ffn_kernel(ups, downs, aligned, place, h_ref, g_ref, mid_ref, *refs):
    parts, refs = cut(refs, ups + downs)
    mixed_ref, gh_ref = refs[:2]
    grads = refs[2:6] if aligned else refs[2:4]
    wu_s, wd_s, acc, sem = refs[-4:]
    j, steps = pl.program_id(0), pl.num_programs(0)
    per_tile = h_ref.shape[1] // FF_COLS
    group = FF_COLS // sum(w.block for w in downs)

    def fetch(step, slot):
        column = pl.ds(pl.multiple_of((step % per_tile) * FF_COLS, FF_COLS), FF_COLS)
        for t, up in enumerate(ups):

            @pl.when(step // per_tile == t)
            def _(t=t, up=up):
                up.start(parts[t], place, wu_s.at[slot], sem.at[slot, 0], column)

        at = 0
        for i, down in enumerate(downs):
            count = group * down.block
            down.start_rows(
                parts[len(ups) + i], place, wd_s.at[slot, pl.ds(at, count), :], sem.at[slot, 1], step * group, group
            )
            at += count

    @pl.when(j == 0)
    def _():
        fetch(j, 0)

    @pl.when(j + 1 < steps)
    def _():
        fetch(j + 1, (j + 1) % 2)

    slot = j % 2
    arrived(wu_s.at[slot], sem.at[slot, 0])
    arrived(wd_s.at[slot], sem.at[slot, 1])
    wu, wd = wu_s[slot], wd_s[slot]
    if len(downs) > 1:
        width = wd.shape[1]
        stack, at = [], 0
        for down in downs:
            count = group * down.block
            stack.append(wd[at : at + count].reshape(group, down.block, width))
            at += count
        wd = jnp.concatenate(stack, axis=1).reshape(FF_COLS, width)
    act, gu, dwu, dwd = ffn_grads(h_ref[...], g_ref[...], wu, wd)
    if aligned:
        grads[0][...], grads[1][...] = split_pairs(dwu, grads[0].shape[0], place[1])
        for ref, value in zip(grads[2:], split_pairs(dwd, grads[2].shape[1], place[1]), strict=True):
            for t in range(ref.shape[0]):
                ref[t] = value[:, t * ref.shape[2] : (t + 1) * ref.shape[2]]
    else:
        grads[0][...] = dwu
        grads[1][...] = dwd
    ffn_sums(j, act, gu, wu, wd, mid_ref, mixed_ref, gh_ref, acc)


def ffn_call(place, h, cot, ups, downs, mid, grad_specs, hidden, aligned):
    n, d = h.shape
    full = resident((n, d))
    const = pl.BlockSpec((n, d), lambda j, *_: (0, 0))
    specs, args = weight_args(ups + downs)
    spec = pltpu.PrefetchScalarGridSpec(
        num_scalar_prefetch=1,
        grid=(hidden // FF_COLS,),
        in_specs=[full, full, full] + specs,
        out_specs=[const, const] + [g[0] for g in grad_specs],
        scratch_shapes=[
            pltpu.VMEM((2, d, FF_COLS), BF16),
            pltpu.VMEM((2, FF_COLS, d), BF16),
            pltpu.VMEM((n, d), F32),
            pltpu.SemaphoreType.DMA((2, 2)),
        ],
    )
    return pl.pallas_call(
        partial(ffn_kernel, ups, downs, aligned),
        grid_spec=spec,
        out_shape=[jax.ShapeDtypeStruct((n, d), BF16), jax.ShapeDtypeStruct((n, d), F32)]
        + [g[1] for g in grad_specs],
        compiler_params=params(60),
        cost_estimate=cost(12 * n * d * hidden, 8 * d * hidden + 14 * n * d),
        name="ffn",
    )(place, h, cot, mid, *args)


def qkv_grad_kernel(groups, place, h_ref, dq_ref, dkv_ref, rkv_ref, keep_ref, send_ref, sum_ref):
    h = h_ref[...]
    my_index = place[1]
    keep_ref[0], send_ref[0] = split_pairs(dot_tn(h, dq_ref[...]).astype(BF16), groups, my_index)
    for t in range(2):
        grad = (dkv_ref[t].astype(F32) + rkv_ref[t].astype(F32)).astype(BF16)
        sum_ref[t] = grad
        keep_ref[t + 1], send_ref[t + 1] = split_pairs(dot_tn(h, grad).astype(BF16), groups, my_index)


def qkv_grad_call(place, h, dq, dkv, rkv, groups):
    n, d = h.shape
    width = dq.shape[1]
    rows = d // (2 * groups)
    heads = width // GROUP_WIDTH
    pair = pl.BlockSpec((2, n, GROUP_WIDTH), lambda g, *_: (0, 0, g))
    share = pl.BlockSpec((3, groups, rows, GROUP_WIDTH), lambda g, *_: (g, 0, 0, 0))
    out = jax.ShapeDtypeStruct((3 * heads, groups, rows, GROUP_WIDTH), BF16)
    spec = pltpu.PrefetchScalarGridSpec(
        num_scalar_prefetch=1,
        grid=(heads,),
        in_specs=[resident((n, d)), pl.BlockSpec((n, GROUP_WIDTH), lambda g, *_: (0, g)), pair, pair],
        out_specs=[share, share, pair],
    )
    return pl.pallas_call(
        partial(qkv_grad_kernel, groups),
        grid_spec=spec,
        out_shape=[out, out, jax.ShapeDtypeStruct((2, n, width), BF16)],
        compiler_params=params(40),
        cost_estimate=cost(6 * n * d * width, 6 * d * width + 2 * n * d + 8 * n * width),
        name="qkv_grad",
    )(place, h, dq, dkv, rkv)


def head_back_kernel(weights, count, place, *refs):
    dqs, dkvs = refs[:count], refs[count : 2 * count]
    x_ref, gr_ref, gain_ref = refs[2 * count : 2 * count + 3]
    parts, refs = cut(refs[2 * count + 3 :], weights)
    tg_ref, dln_ref, wq, wk, wv, sem = refs
    load_all(weights, parts, place, (wq, wk, wv), sem)
    i = pl.program_id(0)
    dq = jnp.concatenate([r[...] for r in dqs], axis=1)
    dk = jnp.concatenate([r[0] for r in dkvs], axis=1)
    dv = jnp.concatenate([r[1] for r in dkvs], axis=1)
    grad = dot_nt(dq, wq[...]) + dot_nt(dk, wk[...]) + dot_nt(dv, wv[...])
    hat, scale = normed(x_ref[...].astype(F32))
    tg_ref[...] = (gr_ref[...] + norm_back(grad, gain_ref[...], hat, scale)).astype(BF16)
    dgain = jnp.sum(grad * hat, axis=0, keepdims=True)
    dbias = jnp.sum(grad, axis=0, keepdims=True)

    @pl.when(i == 0)
    def _():
        dln_ref[0:1, :] = dgain
        dln_ref[1:2, :] = dbias

    @pl.when(i > 0)
    def _():
        dln_ref[0:1, :] += dgain
        dln_ref[1:2, :] += dbias


def head_back_call(place, dqs, dkvs, x, gr, weights, gain):
    n, d = x.shape
    row = pl.BlockSpec((ROWS, d), lambda i, *_: (i, 0))
    specs, args = weight_args(weights)
    spec = pltpu.PrefetchScalarGridSpec(
        num_scalar_prefetch=1,
        grid=(n // ROWS,),
        in_specs=[pl.BlockSpec((ROWS, a.shape[1]), lambda i, *_: (i, 0)) for a in dqs]
        + [pl.BlockSpec((2, ROWS, a.shape[2]), lambda i, *_: (0, i, 0)) for a in dkvs]
        + [row, row, resident((1, d))]
        + specs,
        out_specs=[row, pl.BlockSpec((2, d), lambda *_: (0, 0))],
        scratch_shapes=[pltpu.VMEM((d, d), BF16)] * 3 + [pltpu.SemaphoreType.DMA((3,))],
    )
    return pl.pallas_call(
        partial(head_back_kernel, weights, len(dqs)),
        grid_spec=spec,
        out_shape=[jax.ShapeDtypeStruct((n, d), BF16), jax.ShapeDtypeStruct((2, d), F32)],
        compiler_params=params(48),
        cost_estimate=cost(6 * n * d * d, 6 * d * d + 14 * n * d),
        name="qkv_back",
    )(place, *dqs, *dkvs, x, gr, gain, *args)


class Term:
    def __init__(self, array, axes, first=0, count=None):
        self.array, self.axes, self.first = array, axes, first
        self.count = array.shape[0] if count is None else count
        self.whole = first % self.count != 0

    def spec(self, settled, flipped, open_bits, steps_bits):
        def index_map(step, mine):
            at = [0 if self.whole else self.first // self.count]
            for b in self.axes:
                if (flipped >> b) & 1:
                    at.append(1 - mine[b])
                elif b in settled:
                    at.append(mine[b])
                elif b in steps_bits:
                    at.append((step >> (len(steps_bits) - 1 - steps_bits.index(b))) & 1)
                else:
                    at.append(0)
            return (*at, 0, 0)

        lead = self.array.shape[0] if self.whole else self.count
        inner = tuple(2 if b in open_bits and b not in steps_bits else None for b in self.axes)
        return pl.BlockSpec((lead,) + inner + self.array.shape[-2:], index_map)

    def read(self, ref):
        start = self.first if self.whole else 0
        return ref[start : start + self.count].astype(F32)


class Cube:
    def __init__(self, dp, index, order):
        self.bits = dp.bit_length() - 1
        self.dp, self.order = dp, order
        self.mine = ((index >> jnp.arange(self.bits, dtype=jnp.int32)) & 1).astype(jnp.int32)

    def send(self, array, flip):
        return lax.ppermute(array, "dp", [(i, i ^ flip) for i in range(self.dp)])

    def far(self, low=2):
        return [f << low for f in range(1, 1 << (self.bits - low))]

    def terms(self, arrays, first=0, count=None):
        made = []
        for array in arrays:
            lead, _, rows, width = array.shape
            shape = (lead,) + (2,) * self.bits + (rows, width)
            made.append(Term(array.reshape(shape), list(range(self.bits))[::-1], first, count))
        return made

    def add(self, outputs, dtype):
        in_specs, args, plan, out_specs, out_shape = [], [], [], [], []
        for output in outputs:
            lead = 0
            for stream, settled, flipped in output:
                open_bits = [b for b in range(self.bits)[::-1] if b not in settled and not (flipped >> b) & 1]
                steps_bits = open_bits[:STEP_BITS]
                for term in stream:
                    in_specs.append(term.spec(settled, flipped, open_bits, steps_bits))
                    args.append(term.array)
                plan.append((len(out_specs), lead, list(stream)))
                lead += stream[0].count
            outer, inner = len(steps_bits), len(open_bits) - len(steps_bits)

            def out_map(step, mine, outer=outer, inner=inner):
                return (0, *[(step >> (outer - 1 - k)) & 1 for k in range(outer)], *[0] * inner, 0, 0)

            shape = output[0][0][0].array.shape[-2:]
            out_specs.append(pl.BlockSpec((lead,) + (None,) * outer + (2,) * inner + shape, out_map))
            out_shape.append(jax.ShapeDtypeStruct((lead,) + (2,) * (outer + inner) + shape, dtype))

        def kernel(mine, *refs):
            ins, outs = refs[: len(args)], refs[len(args) :]
            at = 0
            for out, first, stream in plan:
                total = stream[0].read(ins[at])
                for k in range(1, len(stream)):
                    total = total + stream[k].read(ins[at + k])
                outs[out][first : first + stream[0].count] = total.astype(dtype)
                at += len(stream)

        spec = pltpu.PrefetchScalarGridSpec(
            num_scalar_prefetch=1, grid=(2**outer,), in_specs=in_specs, out_specs=out_specs
        )
        size = sum(math.prod(o.shape) for o in out_shape)
        call = pl.pallas_call(
            kernel,
            grid_spec=spec,
            out_shape=out_shape,
            compiler_params=params(40),
            cost_estimate=cost(4 * size, 8 * size),
            name="add_terms",
        )
        return self.order.run(call, self.mine, *args)


def merge(arrays, outputs, *awaited):
    d = arrays[0].shape[-1]
    shapes = []
    for output in outputs:
        blocks = sum(arrays[i].shape[0] for i, _, _ in output)
        shapes.append(jax.ShapeDtypeStruct((blocks, output[0][2], d), BF16))

    def kernel(*refs):
        ins, outs = refs[: len(arrays)], refs[len(arrays) + len(awaited) :]
        for out, output in zip(outs, outputs, strict=True):
            at = 0
            for i, first, count in output:
                blocks = ins[i].shape[0]
                out[at : at + blocks] = ins[i][:, first : first + count]
                at += blocks

    whole = pl.BlockSpec(memory_space=pltpu.VMEM)
    size = sum(math.prod(shape.shape) for shape in shapes)
    return pl.pallas_call(
        kernel,
        in_specs=[whole] * len(arrays) + [HBM] * len(awaited),
        out_specs=[whole] * len(outputs),
        out_shape=shapes,
        compiler_params=params(40),
        cost_estimate=cost(size, 4 * size),
        name="merge",
    )(*arrays, *awaited)


class Side:
    def __init__(self, cube, order):
        self.cube, self.order = cube, order

    def hold(self, held, bit):
        self.held = held
        self.got = self.cube.send(held, 1 << bit)

    def parts_of(self):
        last = 1 << self.order[1]
        flips = [0] + self.cube.far()
        flips = flips + [f ^ (1 << self.order[0]) for f in flips]
        moved = [f ^ last for f in flips]
        return [(flips, 0), (moved, 0), (flips, 1), (moved, 1)]

    def index(self, flip):
        first, last = self.order
        return (flip >> 2) + (((flip >> first) & 1) << (self.cube.bits - 2)), (flip >> last) & 1


class Gather:
    def __init__(self, cube, order, exchange, one, two):
        self.cube, self.order, self.exchange = cube, order, exchange
        self.rows = one.shape[0]
        self.local = jnp.concatenate([one, two], axis=0)[None]
        self.sides = (Side(cube, (1, 0)), Side(cube, (0, 1)))

    def far(self):
        local = self.order.after(self.local)
        self.pieces = [local] + [self.cube.send(local, f) for f in self.cube.far()]
        self.order.note(local)

    def near(self, *awaited):
        total = self.local.shape[1]
        outputs = [
            [(i, first, count) for i in range(len(self.pieces))]
            for first, count in ((0, self.rows), (self.rows, total - self.rows))
        ]
        held = self.order.run(lambda first, *rest: merge((first, *rest), outputs, *awaited), *self.pieces)
        for s, array in zip(self.sides, held, strict=True):
            s.hold(array, s.order[0])

    def last(self, *awaited):
        arrays = [a for s in self.sides for a in (s.held, s.got)]
        outputs = [[(i, 0, arrays[i].shape[1]), (i + 1, 0, arrays[i].shape[1])] for i in (0, 2)]
        held = self.order.run(lambda first, *rest: merge((first, *rest), outputs, *awaited), *arrays)
        for s, array in zip(self.sides, held, strict=True):
            s.hold(array, s.order[1])
            s.other = self.exchange(s.held)

    def finish(self):
        for s in self.sides:
            s.buffers = [s.held, s.got, s.other, self.exchange(self.order.after(s.got))]
            s.parts = s.parts_of()


class Order:
    def __init__(self):
        self.token = ()

    def after(self, *values):
        if self.token:
            values = lax.optimization_barrier((values, self.token))[0]
        return values if len(values) > 1 else values[0]

    def note(self, *token):
        self.token = token

    def run(self, call, first, *rest):
        out = call(self.after(first), *rest)
        self.note(jax.tree.leaves(out)[0])
        return out


class Scatter:
    def __init__(self, cube, one, two):
        self.cube, self.sides, self.step = cube, (one, two), 0
        self.sent, self.last = [], []

    def advance(self):
        step, cube = self.step, self.cube
        if step < 2:
            flips = (1 << step, 1 << (1 - step))
            done = ([], []) if step == 0 else ([0], [1])
            self.sent = cube.add(
                [[(stream, done[s], flips[s]) for stream in self.sides[s]] for s in range(2)], BF16
            )
            self.last = []
            for s in range(2):
                got = cube.send(self.sent[s], flips[s])
                self.last.append(got)
                axes = [b for b in range(cube.bits)[::-1] if b not in done[s] and not (flips[s] >> b) & 1]
                at = 0
                for stream in self.sides[s]:
                    stream.append(Term(got, axes, at, stream[0].count))
                    at += stream[0].count
        else:
            streams = [stream for side in self.sides for stream in side]
            done = list(range(cube.bits))
            self.sent = cube.add([[(stream, done, f) for stream in streams] for f in cube.far()], BF16)
            self.last = [cube.send(sent, f) for sent, f in zip(self.sent, cube.far(), strict=True)]
            for got in self.last:
                at = 0
                for stream in streams:
                    stream.append(Term(got, [], at, stream[0].count))
                    at += stream[0].count
        self.step += 1
        return self

    def finish(self):
        while self.step < 3:
            self.advance()
        done = list(range(self.cube.bits))
        return self.cube.add([[(stream, done, 0)] for side in self.sides for stream in side], F32)


def gate(value, *others):
    return lax.optimization_barrier((value, others))[0]


def block_table(seg_full, seg_local, my_index, n, bq, bk):
    first, last = seg_local[::bq], seg_local[bq - 1 :: bq]
    low = jnp.sum((seg_full[None, :] < first[:, None]).astype(jnp.int32), axis=1)
    high = jnp.sum((seg_full[None, :] <= last[:, None]).astype(jnp.int32), axis=1)
    columns = []
    for index in (my_index, 1 - my_index):
        start = jnp.clip(low - index * n, 0, n)
        stop = jnp.clip(high - index * n, 0, n)
        block = start // bk
        columns += [block, jnp.where(stop > start, (stop + bk - 1) // bk - block, 0)]
    return jnp.stack(columns, axis=1).reshape(-1).astype(jnp.int32)


def body(
    tokens,
    segments,
    ln1_gain,
    ln1_bias,
    w_query,
    w_key,
    w_value,
    w_out,
    ln2_gain,
    ln2_bias,
    w_up,
    w_down,
    cotangent,
):
    x = tokens[0]
    n, d = x.shape
    cot = cotangent[0]
    rows = w_query.shape[0]
    devices = d // rows
    hidden = w_up.shape[1]
    per_device = hidden // devices
    my_index = lax.axis_index("seq")
    seg_full = segments[0]
    seg_local = lax.dynamic_slice_in_dim(seg_full, my_index * n, n)
    seg_other = lax.dynamic_slice_in_dim(seg_full, (1 - my_index) * n, n)
    tab = block_table(seg_full, seg_local, my_index, n, ATT_Q, ATT_K)
    seg_q = seg_local.reshape(n // ATT_Q, 1, ATT_Q)
    seg_own_col, seg_other_col = seg_local[:, None], seg_other[:, None]

    dp = devices // 2
    dp_index = lax.axis_index("dp")
    order = Order()
    cube = Cube(dp, dp_index, order)
    place = jnp.stack([dp_index, my_index]).astype(jnp.int32)
    swap = [(0, 1), (1, 0)]
    tiles = hidden // d

    def exchange(value):
        return lax.ppermute(value, "seq", swap)

    def halves(value, axis):
        keep = lax.dynamic_index_in_dim(value, my_index, axis, keepdims=False)
        send = lax.dynamic_index_in_dim(value, 1 - my_index, axis, keepdims=False)
        return keep, send

    vectors = jnp.concatenate([ln1_gain, ln1_bias, ln2_gain, ln2_bias]).astype(F32)
    vectors = jnp.broadcast_to(vectors[None], (devices, 4 * rows))
    vectors = lax.all_to_all(vectors, BOTH, 0, 0, tiled=True)
    ln = vectors.reshape(devices, 4, rows).transpose(1, 0, 2).reshape(4, 1, d)

    aligned = rows % 32 == 0
    groups = d // GROUP_WIDTH
    if aligned:
        cut_row, half_down = rows // 2, per_device // 2
        up_tiles = w_up.reshape(rows, tiles, d).transpose(1, 0, 2)
        half_up = tiles // 2 * rows
        low_up, high_up = (u.reshape(half_up, d) for u in (up_tiles[: tiles // 2], up_tiles[tiles // 2 :]))
        head = Gather(
            cube, order, exchange,
            jnp.concatenate([w_key, w_query[:cut_row]]), jnp.concatenate([w_value, w_query[cut_row:]]),
        )
        low = Gather(
            cube, order, exchange,
            jnp.concatenate([low_up, w_out[:cut_row]]), jnp.concatenate([w_down[:half_down], w_out[cut_row:]]),
        )
        high = Gather(cube, order, exchange, high_up, w_down[half_down:])
        head.far()
        head.near(vectors)
        low.far()
        head.last()
        order.note(*[side.got for side in head.sides])
        head.finish()
        low.near()
        high.far()
        key_w = Spread(rows, [(head.sides[0], 0, rows, 0)])
        value_w = Spread(rows, [(head.sides[1], 0, rows, 0)])
        query_w = Spread(rows, [(head.sides[0], rows, cut_row, 0), (head.sides[1], rows, cut_row, cut_row)])
    else:
        every = jnp.concatenate([w_query, w_key, w_value, w_out], axis=0).reshape(4, rows, d)
        every = lax.all_gather(every, BOTH, axis=1, tiled=True)
        query_w, key_w, value_w, out_w = (Plain(every[t], rows) for t in range(4))
        up_all = lax.all_gather(w_up, BOTH, axis=0, tiled=True)
        ups = [Plain(up_all[:, t * d : (t + 1) * d], rows) for t in range(tiles)]
        downs = [Plain(lax.all_gather(w_down, BOTH, axis=0, tiled=True), per_device)]

    h1, own = order.run(kv_call, place, x, ln[0], ln[1], [key_w, value_w])
    if aligned:
        low.last()
    other = exchange(order.after(own))
    q = order.run(q_call, place, h1, [query_w])
    outs, lses = [], []
    plan = [(0, 1), (1, 1), (2, 2)] if groups == 4 else [(g, 1) for g in range(groups)]
    for i, (start, count) in enumerate(plan):
        if aligned and i == 1:
            high.near(*[side.other for side in low.sides])
        if aligned and i == 2:
            high.last()
            low.finish()
        out, lse = order.run(
            attend_call, tab, q, own, other, seg_q, seg_own_col, seg_other_col, ATT_Q, ATT_K, start, count
        )
        outs.append(out)
        lses.append(lse)
    if aligned:
        out_w = Spread(
            rows, [(low.sides[0], half_up, cut_row, 0), (low.sides[1], half_down, cut_row, cut_row)]
        )
    mid, h2 = order.run(mid_call, place, x, outs, [out_w], ln[2], ln[3])
    if aligned:
        high.finish()

    up_rows = tiles * rows
    if aligned:
        ups = [
            Spread(rows, [((low, high)[t // (tiles // 2)].sides[0], t % (tiles // 2) * rows, rows, 0)])
            for t in range(tiles)
        ]
        downs = [Spread(half_down, [(r.sides[1], 0, half_down, 0)]) for r in (low, high)]
        per_tile = d // FF_COLS
        group = FF_COLS // per_device
        up_out = (
            pl.BlockSpec((None, dp, rows, FF_COLS), lambda j, *_: (j // per_tile, 0, 0, j % per_tile)),
            jax.ShapeDtypeStruct((tiles, dp, rows, d), BF16),
        )
        down_out = (
            pl.BlockSpec((tiles, group // 2, rows, d), lambda j, *_: (0, j, 0, 0)),
            jax.ShapeDtypeStruct((tiles, dp, rows, d), BF16),
        )
        grad_specs = [up_out, up_out, down_out, down_out]
    else:
        grad_specs = [
            (pl.BlockSpec((d, FF_COLS), lambda j, *_: (0, j)), jax.ShapeDtypeStruct((d, hidden), BF16)),
            (pl.BlockSpec((FF_COLS, d), lambda j, *_: (j, 0)), jax.ShapeDtypeStruct((hidden, d), BF16)),
        ]
    mixed, gmid, *grads = order.run(ffn_call, place, h2, cot, ups, downs, mid, grad_specs, hidden, aligned)
    if not aligned:
        dwu = grads[0].reshape(dp, 2, rows, tiles, d).transpose(3, 0, 1, 2, 4)
        dwd = grads[1].reshape(dp, 2, tiles, rows, d).transpose(2, 0, 1, 3, 4)
        grads = [*halves(dwu, 2), *halves(dwd, 2)]
    keep_up, send_up, keep_down, send_down = grads
    got_up, got_down = exchange(send_up), exchange(send_down)
    big = Scatter(cube, [cube.terms([keep_up, got_up])], [cube.terms([keep_down, got_down])])

    grad_mid, grad_att, keep_out, send_out, dln2 = order.run(
        mid_back_call, place, gmid, mid, cot, outs, [out_w], ln[2], dp
    )
    big.advance()
    got_out = exchange(order.after(send_out))
    dqs, dkvs = [], []

    def attend_back(g):
        which = [i for i, (start, _) in enumerate(plan) if start <= g][-1]
        return order.run(
            attend_back_call, tab, q, grad_att, outs[which], own, other, seg_q, seg_own_col, seg_other_col,
            lses[which], ATT_Q, ATT_K, g, 1, g - plan[which][0],
        )

    def finish_group(dq, dkv, got):
        keep, send, dkv = order.run(qkv_grad_call, place, h1, dq, dkv, got, dp)
        dqs.append(dq)
        dkvs.append(dkv)
        return keep, send

    dq_0, dkv_0, sent_0 = attend_back(0)
    dq_1, dkv_1, sent_1 = attend_back(1)
    got_0 = exchange(order.after(sent_0))
    big.advance()
    got_1 = exchange(order.after(sent_1))
    keep_0, send_0 = finish_group(dq_0, dkv_0, got_0)
    keep_1, send_1 = finish_group(dq_1, dkv_1, got_1)
    terms_0, terms_1 = [keep_0, exchange(order.after(send_0))], [keep_1, exchange(order.after(send_1))]
    dq_2, dkv_2, sent_2 = attend_back(2)
    big.advance()
    tail_one = Scatter(
        cube,
        [cube.terms(terms_0), cube.terms([keep_out, got_out], 0, 2)],
        [cube.terms(terms_1), cube.terms([keep_out, got_out], 2, 2)],
    )
    tail_one.advance()
    got_2 = exchange(order.after(sent_2))
    dq_3, dkv_3, sent_3 = attend_back(3)
    up_share, down_share = big.finish()
    tail_one.advance()
    got_3 = exchange(order.after(sent_3))
    keep_2, send_2 = finish_group(dq_2, dkv_2, got_2)
    keep_3, send_3 = finish_group(dq_3, dkv_3, got_3)
    tail_one.advance()
    terms_2, terms_3 = [keep_2, exchange(order.after(send_2))], [keep_3, exchange(order.after(send_3))]
    tail_two = Scatter(cube, [cube.terms(terms_2)], [cube.terms(terms_3)])
    tail_two.advance()
    token_grad, dln1 = order.run(
        head_back_call, place, dqs, dkvs, x, grad_mid, [query_w, key_w, value_w], ln[0]
    )
    tail_two.advance()
    one_a, out_a, one_b, out_b = tail_one.finish()
    dln = jnp.concatenate([dln1, order.after(dln2)], axis=0).reshape(4, devices, rows).transpose(1, 0, 2)
    dln = lax.all_to_all(dln.reshape(devices, 4 * rows), BOTH, 0, 0, tiled=True)
    dln = jnp.sum(dln.reshape(devices, 4, rows), axis=0)
    tail_two.advance()
    two_a, two_b = tail_two.finish()

    up_share = up_share.transpose(1, 0, 2).reshape(rows, hidden)
    down_share = down_share.reshape(per_device, d)
    qkv_share = jnp.concatenate([one_a, one_b, two_a, two_b], axis=-1)
    out_share = jnp.concatenate([out_a, out_b], axis=0).transpose(1, 0, 2).reshape(rows, d)
    return (
        mixed[None],
        token_grad[None],
        dln[0],
        dln[1],
        qkv_share[0],
        qkv_share[1],
        qkv_share[2],
        out_share,
        dln[2],
        dln[3],
        up_share,
        down_share,
    )


def solution(mesh):
    row, act, vec = P(BOTH, None), P("dp", "seq", None), P(BOTH)
    in_specs = (act, P("dp", None), vec, vec, row, row, row, row, vec, vec, row, row, act)
    out_specs = (act, act, vec, vec, row, row, row, row, vec, vec, row, row)
    return jax.shard_map(body, mesh=mesh, in_specs=in_specs, out_specs=out_specs, check_vma=False)
```

time: 586 us -> 558 us (0.952)
  waiting for transfers between devices: 201 us -> 111 us
  starting transfers between devices: 26.3 us -> 79 us
  between operations: 15 us -> 2.04 us
  Pallas kernels: 290 us -> 302 us
  local copies, waits for them, and re-layouts: 40.9 us -> 47.9 us
    all_gather x2 -> x0, waiting for transfers between devices: 132 us -> none  [gather(): out = lax.all_gather(local, BOTH, axis=0, tiled=True)]
    ppermute x19 -> x42, starting transfers between devices: 14.4 us -> 65 us  [send(): return lax.ppermute(array, 'dp', [(i, i ^ flip) for i in range(self.dp)])]
    ppermute x19 -> x42, waiting for transfers between devices: 50.9 us -> 92.3 us  [send(): return lax.ppermute(array, 'dp', [(i, i ^ flip) for i in range(self.dp)])]
    pallas_call x25 -> x28, Pallas kernels: 162 us -> 180 us  [the longest x1 69.7 us: ffn_call(): pl.pallas_call(partial(ffn_kernel, ups, downs, aligned), grid_spec=spec,...]
    ppermute x11 -> x24, waiting for transfers between devices: 18.4 us -> 6.8 us  [exchange(): return lax.ppermute(value, 'seq', swap)]
    all_to_all x0 -> x1, waiting for transfers between devices: none -> 9.18 us  [body(): vectors = lax.all_to_all(vectors, BOTH, 0, 0, tiled=True)]
    pallas_call x4, Pallas kernels: 81.8 us -> 72.9 us  [attend_back_call(): pl.pallas_call(partial(attend_back_kernel, bq, bk), grid_spec=spec, out_s...]
    all_to_all x0 -> x1, starting transfers between devices: none -> 5.99 us  [body(): vectors = lax.all_to_all(vectors, BOTH, 0, 0, tiled=True)]
  transfers between devices with their start and end apart: 33 -> 68, of which waited for: 13 -> 22; matrix products, arithmetic and copies ran while one was open for 2% -> 3% of each run, Pallas kernels for 35% -> 39%
where the time goes in v4:
time: 558 us; the launch traced here: 547 us
  Pallas kernels  302 us (54%)
  waiting for transfers between devices  111 us (20%)
  starting transfers between devices  79 us (14%)
  local copies, waits for them, and re-layouts  47.9 us (9%)
    ppermute x42, waiting for transfers between devices, send(): return lax.ppermute(array, 'dp', [(i, i ^ flip) for i in range(self.dp)])  92.3 us
    pallas_call x4, Pallas kernels, attend_back_call(): pl.pallas_call(partial(attend_back_kernel, bq, bk), grid_spec=spec, out_s...  72.9 us
    pallas_call x1, Pallas kernels, ffn_call(): pl.pallas_call(partial(ffn_kernel, ups, downs, aligned), grid_spec=spec,...  69.7 us
    ppermute x42, starting transfers between devices, send(): return lax.ppermute(array, 'dp', [(i, i ^ flip) for i in range(self.dp)])  65 us
    pallas_call x3, Pallas kernels, attend_call(): pl.pallas_call(partial(attend_kernel, bq, bk), grid_spec=spec, out_shape=...  48.6 us
    unnamed x183, local copies, waits for them, and re-layouts  36 us
    pallas_call x12, Pallas kernels, run(): out = call(self.after(first), *rest)  30.6 us
    pallas_call x1, Pallas kernels, head_back_call(): pl.pallas_call(partial(head_back_kernel, weights, len(dqs)), grid_spec=sp...  19.2 us
  transfers between devices with their start and end apart: 68, of which 22 were waited for; matrix products, arithmetic and copies ran while one was open for 3% of the time, Pallas kernels for 39%

profile of v4, /device:TPU:0, one launch (start us, length us, event | category | flops | bytes accessed | tf_op | source)
XLA Modules:
  0.0 547.1 jit_solution(18374258610382270296)
XLA Ops:
  2.4 5.1 collective-permute-start.2
  9.5 6.0 %all-to-all-start = ((f32[32,1,128]{2,1,0:T(1,128)}), f32[32,1,128]{2,1,0:T(1,128)S(1)}, u32[]{:S(2)}, u32[]{:S(2)}) async-start(f32[32,1,128]{2,1,0:T(1,128)} %broadcast_in_dim.35), calls=%async_computation | async-start | bytes 32768 | tf_op jit(solution)/shard_map/all_to_all | solution.py:1013
  17.2 9.2 %all-to-all-done = f32[32,1,128]{2,1,0:T(1,128)S(1)} async-done(((f32[32,1,128]{2,1,0:T(1,128)}), f32[32,1,128]{2,1,0:T(1,128)S(1)}, u32[]{:S(2)}, u32[]{:S(2)}) %all-to-all-start) | async-done | bytes 16416 | tf_op jit(solution)/shard_map/all_to_all | solution.py:1013
  28.5 8.8 %collective-permute-done.4.refs_3_ = bf16[4,48,1024]{2,1,0:T(8,128)(2,1)S(1)} collective-permute-done((bf16[4,48,1024]{2,1,0:T(8,128)(2,1)S(1)}, bf16[4,48,1024]{2,1,0:T(8,128)(2,1)S(1)}, u32[]{:S(2)}, u32[]{:S(2)}) %collective-permute-start.4) | collective-permute-done | bytes 393248 | tf_op jit(solution)/shard_map/ppermute | solution.py:744
  39.8 2.5 collective-permute-start.9
  42.3 13.6 %collective-permute-done.5.refs_1_.refs_12_.refs_20_ = bf16[8,48,1024]{2,1,0:T(8,128)(2,1)S(1)} collective-permute-done((bf16[8,48,1024]{2,1,0:T(8,128)(2,1)S(1)}, bf16[8,48,1024]{2,1,0:T(8,128)(2,1)S(1)}, u32[]{:S(2)}, u32[]{:S(2)}) %collective-permute-start.5) | collective-permute-done | bytes 786464 | tf_op jit(solution)/shard_map/ppermute | solution.py:744
  58.5 12.6 %collective-permute-done.8.refs_2_ = bf16[1,160,1024]{2,1,0:T(8,128)(2,1)S(1)} collective-permute-done((bf16[1,160,1024]{2,1,0:T(8,128)(2,1)S(1)}, bf16[1,160,1024]{2,1,0:T(8,128)(2,1)S(1)}, u32[]{:S(2)}, u32[]{:S(2)}) %collective-permute-start.8) | collective-permute-done | bytes 327712 | tf_op jit(solution)/shard_map/ppermute | solution.py:744
  83.7 12.6 %kv_proj.1 = (bf16[1024,1024]{1,0:T(8,128)(2,1)S(1)}, bf16[2,1024,1024]{2,1,0:T(8,128)(2,1)}) custom-call(s32[2]{0:T(128)S(1)} %pad_add_fusion.1.place, bf16[1024,1024]{1,0:T(8,128)(2,1)S(1)} %bitcast.170, f32[1,1024]{1,0:T(1,128)S(1)} %squeeze.35.gain_ref.refs_10_, f32[1,1024]{1,0:T(1,128)S(1)} %squeeze.36.bias_ref, ...), custom_call_target="tpu_custom_call" | custom-call | flops 42949 | bytes 125 | tf_op jit(solution)/shard_map/kv_proj/pallas_call | solution.py:168
  96.4 3.8 merge.9
  100.8 2.5 collective-permute-start.19
  103.3 8.5 %collective-permute-done.19.refs_3_ = bf16[1,128,1024]{2,1,0:T(8,128)(2,1)S(1)} collective-permute-done((bf16[1,128,1024]{2,1,0:T(8,128)(2,1)S(1)}, bf16[1,128,1024]{2,1,0:T(8,128)(2,1)S(1)}, u32[]{:S(2)}, u32[]{:S(2)}) %collective-permute-start.19) | collective-permute-done | bytes 262176 | tf_op jit(solution)/shard_map/ppermute | solution.py:744
  113.0 12.4 %collective-permute-done.18.refs_2_ = bf16[1,128,1024]{2,1,0:T(8,128)(2,1)S(1)} collective-permute-done((bf16[1,128,1024]{2,1,0:T(8,128)(2,1)S(1)}, bf16[1,128,1024]{2,1,0:T(8,128)(2,1)S(1)}, u32[]{:S(2)}, u32[]{:S(2)}) %collective-permute-start.18) | collective-permute-done | bytes 262176 | tf_op jit(solution)/shard_map/ppermute | solution.py:744
  135.5 6.4 %q_proj.1.q_ref = bf16[1024,1024]{1,0:T(8,128)(2,1)S(1)} custom-call(s32[2]{0:T(128)S(1)} %pad_add_fusion.1.place, bf16[1024,1024]{1,0:T(8,128)(2,1)S(1)} %get-tuple-element.167.h_ref, bf16[8,48,1024]{2,1,0:T(8,128)(2,1)S(1)} %copy-done.30, bf16[8,48,1024]{2,1,0:T(8,128)(2,1)S(1)} %copy-done.38, bf16[8,48,1024]{2,1,0:T(8,128)(2,1)S(1)} %copy-done.42, ...), custom_call_target="tpu_custom_call" | custom-call | flops 21474 | bytes 62 | tf_op jit(solution)/shard_map/q_proj/pallas_call | solution.py:196
  143.2 12.9 %attend.3 = (bf16[1024,256]{1,0:T(8,128)(2,1)}, f32[1,4,1,1024]{3,2,1,0:T(1,128)}) custom-call(s32[16]{0:T(128)} %reshape.436.tab, bf16[1024,1024]{1,0:T(8,128)(2,1)} %copy-done.1, bf16[2,1024,1024]{2,1,0:T(8,128)(2,1)} %get-tuple-element.174.ko_ref.vo_ref, bf16[2,1024,1024]{2,1,0:T(8,128)(2,1)} %get-tuple-element.174.ko_ref.vo_ref, ...), custom_call_target="tpu_custom_call" | custom-call | flops 80000 | bytes 31 | tf_op jit(solution)/shard_map/attend/pallas_call | solution.py:284
  159.6 12.8 %attend.4 = (bf16[1024,256]{1,0:T(8,128)(2,1)}, f32[1,4,1,1024]{3,2,1,0:T(1,128)}) custom-call(s32[16]{0:T(128)} %reshape.436.tab, bf16[1024,1024]{1,0:T(8,128)(2,1)} %copy-done.1, bf16[2,1024,1024]{2,1,0:T(8,128)(2,1)} %get-tuple-element.174.ko_ref.vo_ref, bf16[2,1024,1024]{2,1,0:T(8,128)(2,1)} %get-tuple-element.174.ko_ref.vo_ref, ...), custom_call_target="tpu_custom_call" | custom-call | flops 80000 | bytes 31 | tf_op jit(solution)/shard_map/attend/pallas_call | solution.py:284
  177.7 22.9 %attend.5 = (bf16[1024,512]{1,0:T(8,128)(2,1)}, f32[2,4,1,1024]{3,2,1,0:T(1,128)}) custom-call(s32[16]{0:T(128)} %reshape.436.tab, bf16[1024,1024]{1,0:T(8,128)(2,1)} %copy-done.1, bf16[2,1024,1024]{2,1,0:T(8,128)(2,1)} %get-tuple-element.174.ko_ref.vo_ref, bf16[2,1024,1024]{2,1,0:T(8,128)(2,1)} %get-tuple-element.174.ko_ref.vo_ref, ...), custom_call_target="tpu_custom_call" | custom-call | flops 160000 | bytes 62 | tf_op jit(solution)/shard_map/attend/pallas_call | solution.py:284
  202.3 6.8 %out_proj.1 = (f32[1024,1024]{1,0:T(8,128)S(1)}, bf16[1024,1024]{1,0:T(8,128)(2,1)S(1)}) custom-call(s32[2]{0:T(128)S(1)} %pad_add_fusion.1.place, bf16[1024,1024]{1,0:T(8,128)(2,1)S(1)} %bitcast.171, f32[1,1024]{1,0:T(1,128)S(1)} %squeeze.37.gain_ref, f32[1,1024]{1,0:T(1,128)S(1)} %squeeze.38.bias_ref, bf16[1024,256]{1,0:T(8,128)(2,1)S(1)} %copy-done.46, ...), custom_call_target="tpu_custom_call" | custom-call | flops 21474 | bytes 125 | tf_op jit(solution)/shard_map/out_proj/pallas_call | solution.py:417
  209.1 2.0 copy-done.26
  213.1 2.3 collective-permute-done.30.refs_11_.refs_15_
  218.0 69.7 %ffn.1 = (bf16[1024,1024]{1,0:T(8,128)(2,1)}, f32[1024,1024]{1,0:T(8,128)}, bf16[4,16,32,1024]{3,2,1,0:T(8,128)(2,1)}, bf16[4,16,32,1024]{3,2,1,0:T(8,128)(2,1)}...) custom-call(s32[2]{0:T(128)} %copy-done.74, bf16[1024,1024]{1,0:T(8,128)(2,1)} %copy-done.50, ...), custom_call_target="tpu_custom_call" | custom-call | flops 515396 | bytes 482 | tf_op jit(solution)/shard_map/ffn/pallas_call | solution.py:612
  288.3 15.7 %out_proj_back.1 = (f32[1024,1024]{1,0:T(8,128)}, bf16[1024,1024]{1,0:T(8,128)(2,1)}, bf16[4,16,32,256]{3,2,1,0:T(8,128)(2,1)S(1)}, bf16[4,16,32,256]{3,2,1,0:T(8,128)(2,1)}, f32[2,1024]{1,0:T(2,128)S(1)}) custom-call(s32[2]{0:T(128)S(1)} %copy-done.75, f32[1024,1024]{1,0:T(8,128)} %get-tuple-element.197.gh_ref, f32[1024,1024]{1,0:T(8,128)} %copy-done.26, ...), custom_call_target="tpu_custom_call" | custom-call | flops 42949 | bytes 230 | tf_op jit(solution)/shard_map/out_proj_back/pallas_call | solution.py:489
  304.0 5.3 add_terms.12
  309.4 5.4 collective-permute-start.36
  314.8 18.2 %attend_back.4 = (bf16[1024,256]{1,0:T(8,128)(2,1)}, bf16[2,1024,256]{2,1,0:T(8,128)(2,1)}, bf16[2,1024,256]{2,1,0:T(8,128)(2,1)}) custom-call(s32[16]{0:T(128)} %reshape.436.tab, bf16[1024,1024]{1,0:T(8,128)(2,1)} %copy-done.1, bf16[1024,1024]{1,0:T(8,128)(2,1)} %get-tuple-element.206.go_ref, bf16[1024,256]{1,0:T(8,128)(2,1)} %get-tuple-element.175.refs_0_.o_ref, ...), custom_call_target="tpu_custom_call" | custom-call | flops 120000 | bytes 62 | tf_op jit(solution)/shard_map/attend_back/pallas_call | solution.py:379
  333.1 18.2 %attend_back.5 = (bf16[1024,256]{1,0:T(8,128)(2,1)}, bf16[2,1024,256]{2,1,0:T(8,128)(2,1)}, bf16[2,1024,256]{2,1,0:T(8,128)(2,1)}) custom-call(s32[16]{0:T(128)} %reshape.436.tab, bf16[1024,1024]{1,0:T(8,128)(2,1)} %copy-done.1, bf16[1024,1024]{1,0:T(8,128)(2,1)} %get-tuple-element.206.go_ref, bf16[1024,256]{1,0:T(8,128)(2,1)} %get-tuple-element.180.refs_1_.o_ref, ...), custom_call_target="tpu_custom_call" | custom-call | flops 120000 | bytes 62 | tf_op jit(solution)/shard_map/attend_back/pallas_call | solution.py:379
  351.3 6.0 %collective-permute-done.37.refs_5_.refs_6_.refs_14_.refs_22_.refs_9_ = bf16[4,2,2,2,32,1024]{5,4,3,2,1,0:T(8,128)(2,1)S(1)} collective-permute-done((bf16[4,2,2,2,32,1024]{5,4,3,2,1,0:T(8,128)(2,1)}, bf16[4,2,2,2,32,1024]{5,4,3,2,1,0:T(8,128)(2,1)S(1)}, u32[]{:S(2)}, u32[]{:S(2)}) %collective-permute-start.37) | collective-permute-done | bytes 2097184 | tf_op jit(solution)/shard_map/ppermute | solution.py:744
  357.3 3.7 collective-permute-done.36.refs_2_.refs_10_.refs_18_
  361.0 4.6 add_terms.13
  367.8 3.4 qkv_grad.4
  372.3 3.4 qkv_grad.5
  377.1 18.2 %attend_back.6 = (bf16[1024,256]{1,0:T(8,128)(2,1)}, bf16[2,1024,256]{2,1,0:T(8,128)(2,1)}, bf16[2,1024,256]{2,1,0:T(8,128)(2,1)}) custom-call(s32[16]{0:T(128)} %reshape.436.tab, bf16[1024,1024]{1,0:T(8,128)(2,1)} %copy-done.1, bf16[1024,1024]{1,0:T(8,128)(2,1)} %get-tuple-element.206.go_ref, bf16[1024,512]{1,0:T(8,128)(2,1)} %get-tuple-element.185.refs_2_.o_ref, ...), custom_call_target="tpu_custom_call" | custom-call | flops 120000 | bytes 62 | tf_op jit(solution)/shard_map/attend_back/pallas_call | solution.py:379
  396.9 4.5 add_terms.14
  401.4 2.9 add_terms.15
  407.8 6.4 %collective-permute-start.46 = (bf16[8,32,1024]{2,1,0:T(8,128)(2,1)}, bf16[8,32,1024]{2,1,0:T(8,128)(2,1)S(1)}, u32[]{:S(2)}, u32[]{:S(2)}) collective-permute-start(bf16[8,32,1024]{2,1,0:T(8,128)(2,1)} %get-tuple-element.243), channel_id=1, source_target_pairs={{0,16},{2,18},{4,20},{6,22},{8,24},{10,26},{12,28},{14,30},{16,0},... | collective-permute-start | bytes 1572872 | tf_op jit(solution)/shard_map/ppermute | solution.py:744
  414.8 18.3 %attend_back.7 = (bf16[1024,256]{1,0:T(8,128)(2,1)}, bf16[2,1024,256]{2,1,0:T(8,128)(2,1)}, bf16[2,1024,256]{2,1,0:T(8,128)(2,1)}) custom-call(s32[16]{0:T(128)} %reshape.436.tab, bf16[1024,1024]{1,0:T(8,128)(2,1)} %copy-done.1, bf16[1024,1024]{1,0:T(8,128)(2,1)} %get-tuple-element.206.go_ref, bf16[1024,512]{1,0:T(8,128)(2,1)} %get-tuple-element.185.refs_2_.o_ref, ...), custom_call_target="tpu_custom_call" | custom-call | flops 120000 | bytes 62 | tf_op jit(solution)/shard_map/attend_back/pallas_call | solution.py:379
  433.1 15.1 %collective-permute-done.46.refs_5_.refs_12_ = bf16[8,32,1024]{2,1,0:T(8,128)(2,1)S(1)} collective-permute-done((bf16[8,32,1024]{2,1,0:T(8,128)(2,1)}, bf16[8,32,1024]{2,1,0:T(8,128)(2,1)S(1)}, u32[]{:S(2)}, u32[]{:S(2)}) %collective-permute-start.46) | collective-permute-done | bytes 524320 | tf_op jit(solution)/shard_map/ppermute | solution.py:744
  448.2 2.3 collective-permute-done.45.refs_4_.refs_11_
  452.1 3.5 add_terms.16
  455.7 2.5 add_terms.17
  460.0 2.5 qkv_grad.6
  463.5 2.5 qkv_grad.7
  477.2 9.5 %collective-permute-start.59 = (bf16[10,32,256]{2,1,0:T(8,128)(2,1)S(1)}, bf16[10,32,256]{2,1,0:T(8,128)(2,1)S(1)}, u32[]{:S(2)}, u32[]{:S(2)}) collective-permute-start(bf16[10,32,256]{2,1,0:T(8,128)(2,1)S(1)} %get-tuple-element.280), channel_id=1, source_target_pairs={{0,16},{2,18},{4,20},{6,22},{8,24},{10,26},{12,28},{14,30},{16,0},... | collective-permute-start | bytes 491528 | tf_op jit(solution)/shard_map/ppermute | solution.py:744
  486.8 3.0 collective-permute-start.60
  490.6 19.2 %qkv_back.1 = (bf16[1024,1024]{1,0:T(8,128)(2,1)}, f32[2,1024]{1,0:T(2,128)S(1)}) custom-call(s32[2]{0:T(128)S(1)} %copy-done.75, bf16[1024,256]{1,0:T(8,128)(2,1)S(1)} %copy-done.52, bf16[1024,256]{1,0:T(8,128)(2,1)S(1)} %copy-done.54, bf16[1024,256]{1,0:T(8,128)(2,1)S(1)} %copy-done.55, bf16[1024,256]{1,0:T(8,128)(2,1)S(1)} %copy-done.56, ...), custom_call_target="tpu_custom_call" | custom-call | flops 64424 | bytes 209 | tf_op jit(solution)/shard_map/qkv_back/pallas_call | solution.py:698
  517.5 3.5 all-to-all-start.1
  525.3 2.8 all-to-all-done.1
  534.7 2.6 collective-permute-start.64
  539.4 5.8 %collective-permute-done.64.refs_5_.refs_12_ = bf16[6,32,256]{2,1,0:T(8,128)(2,1)S(1)} collective-permute-done((bf16[6,32,256]{2,1,0:T(8,128)(2,1)S(1)}, bf16[6,32,256]{2,1,0:T(8,128)(2,1)S(1)}, u32[]{:S(2)}, u32[]{:S(2)}) %collective-permute-start.64) | collective-permute-done | bytes 98336 | tf_op jit(solution)/shard_map/ppermute | solution.py:744
  (348 shorter events, 102.7 us)
Async XLA Ops:
  2.4 24.0 %collective-permute-start.2 = (bf16[1,96,1024]{2,1,0:T(8,128)(2,1)S(1)}, bf16[1,96,1024]{2,1,0:T(8,128)(2,1)S(1)}, u32[]{:S(2)}, u32[]{:S(2)}) collective-permute-start(bf16[1,96,1024]{2,1,0:T(8,128)(2,1)S(1)} %maximum_bitcast_fusion.2.refs_0_), channel_id=1, source_target_pairs={{0,24},{2,26},{4,28},{6,30},{8,16},{10,18},{12,20},{14,22},{16,8},... | collective-permute-start | bytes 589832 | tf_op jit(solution)/shard_map/ppermute | solution.py:744
  7.5 18.9 %collective-permute-start.1 = (bf16[1,96,1024]{2,1,0:T(8,128)(2,1)S(1)}, bf16[1,96,1024]{2,1,0:T(8,128)(2,1)S(1)}, u32[]{:S(2)}, u32[]{:S(2)}) collective-permute-start(bf16[1,96,1024]{2,1,0:T(8,128)(2,1)S(1)} %maximum_bitcast_fusion.2.refs_0_), channel_id=1, source_target_pairs={{0,16},{2,18},{4,20},{6,22},{8,24},{10,26},{12,28},{14,30},{16,0},... | collective-permute-start | bytes 589832 | tf_op jit(solution)/shard_map/ppermute | solution.py:744
  7.5 18.9 %collective-permute-start = (bf16[1,96,1024]{2,1,0:T(8,128)(2,1)S(1)}, bf16[1,96,1024]{2,1,0:T(8,128)(2,1)S(1)}, u32[]{:S(2)}, u32[]{:S(2)}) collective-permute-start(bf16[1,96,1024]{2,1,0:T(8,128)(2,1)S(1)} %maximum_bitcast_fusion.2.refs_0_), channel_id=1, source_target_pairs={{0,8},{2,10},{4,12},{6,14},{8,0},{10,2},{12,4},{14,6},{16,24},{18,... | collective-permute-start | bytes 589832 | tf_op jit(solution)/shard_map/ppermute | solution.py:744
  9.5 16.8 %all-to-all-start = ((f32[32,1,128]{2,1,0:T(1,128)}), f32[32,1,128]{2,1,0:T(1,128)S(1)}, u32[]{:S(2)}, u32[]{:S(2)}) async-start(f32[32,1,128]{2,1,0:T(1,128)} %broadcast_in_dim.35), calls=%async_computation | async-start | bytes 32768 | tf_op jit(solution)/shard_map/all_to_all | solution.py:1013
  37.8 18.2 %collective-permute-start.5 = (bf16[8,48,1024]{2,1,0:T(8,128)(2,1)S(1)}, bf16[8,48,1024]{2,1,0:T(8,128)(2,1)S(1)}, u32[]{:S(2)}, u32[]{:S(2)}) collective-permute-start(bf16[8,48,1024]{2,1,0:T(8,128)(2,1)S(1)} %get-tuple-element.159.refs_0_.refs_11_.refs_19_), channel_id=1, source_target_pairs={{0,2},{2,0},{4,6},{6,4},{8,10},{10,8},{12,14},{14,12},{16,18},{18,... | collective-permute-start | bytes 2359304 | tf_op jit(solution)/shard_map/ppermute | solution.py:744
  39.2 17.8 %collective-permute-start.6 = (bf16[8,48,1024]{2,1,0:T(8,128)(2,1)S(1)}, bf16[8,48,1024]{2,1,0:T(8,128)(2,1)}, u32[]{:S(2)}, u32[]{:S(2)}) collective-permute-start(bf16[8,48,1024]{2,1,0:T(8,128)(2,1)S(1)} %get-tuple-element.160.refs_4_.refs_15_.refs_23_), channel_id=1, source_target_pairs={{0,4},{2,6},{4,0},{6,2},{8,12},{10,14},{12,8},{14,10},{16,20},{18,... | collective-permute-start | bytes 2359304 | tf_op jit(solution)/shard_map/ppermute | solution.py:744
  39.8 32.7 %collective-permute-start.10 = (bf16[8,48,1024]{2,1,0:T(8,128)(2,1)S(1)}, bf16[8,48,1024]{2,1,0:T(8,128)(2,1)S(1)}, u32[]{:S(2)}, u32[]{:S(2)}) collective-permute-start(bf16[8,48,1024]{2,1,0:T(8,128)(2,1)S(1)} %get-tuple-element.159.refs_0_.refs_11_.refs_19_), channel_id=1, source_target_pairs={{0,1},{1,0},{2,3},{3,2},{4,5},{5,4},{6,7},{7,6},{8,9},{9,8},{10,11... | collective-permute-start | bytes 2359304 | tf_op jit(solution)/shard_map/ppermute | solution.py:1004
  39.8 17.2 %collective-permute-start.9 = (bf16[1,160,1024]{2,1,0:T(8,128)(2,1)S(1)}, bf16[1,160,1024]{2,1,0:T(8,128)(2,1)S(1)}, u32[]{:S(2)}, u32[]{:S(2)}) collective-permute-start(bf16[1,160,1024]{2,1,0:T(8,128)(2,1)S(1)} %maximum_bitcast_fusion.refs_0_), channel_id=1, source_target_pairs={{0,24},{2,26},{4,28},{6,30},{8,16},{10,18},{12,20},{14,22},{16,8},... | collective-permute-start | bytes 983048 | tf_op jit(solution)/shard_map/ppermute | solution.py:744
  42.3 28.7 %collective-permute-start.8 = (bf16[1,160,1024]{2,1,0:T(8,128)(2,1)S(1)}, bf16[1,160,1024]{2,1,0:T(8,128)(2,1)S(1)}, u32[]{:S(2)}, u32[]{:S(2)}) collective-permute-start(bf16[1,160,1024]{2,1,0:T(8,128)(2,1)S(1)} %maximum_bitcast_fusion.refs_0_), channel_id=1, source_target_pairs={{0,16},{2,18},{4,20},{6,22},{8,24},{10,26},{12,28},{14,30},{16,0},... | collective-permute-start | bytes 983048 | tf_op jit(solution)/shard_map/ppermute | solution.py:744
  56.0 15.1 %collective-permute-start.7 = (bf16[1,160,1024]{2,1,0:T(8,128)(2,1)S(1)}, bf16[1,160,1024]{2,1,0:T(8,128)(2,1)S(1)}, u32[]{:S(2)}, u32[]{:S(2)}) collective-permute-start(bf16[1,160,1024]{2,1,0:T(8,128)(2,1)S(1)} %maximum_bitcast_fusion.refs_0_), channel_id=1, source_target_pairs={{0,8},{2,10},{4,12},{6,14},{8,0},{10,2},{12,4},{14,6},{16,24},{18,... | collective-permute-start | bytes 983048 | tf_op jit(solution)/shard_map/ppermute | solution.py:744
  57.1 21.7 %collective-permute-start.12 = (bf16[8,48,1024]{2,1,0:T(8,128)(2,1)S(1)}, bf16[8,48,1024]{2,1,0:T(8,128)(2,1)}, u32[]{:S(2)}, u32[]{:S(2)}) collective-permute-start(bf16[8,48,1024]{2,1,0:T(8,128)(2,1)S(1)} %get-tuple-element.160.refs_4_.refs_15_.refs_23_), channel_id=1, source_target_pairs={{0,1},{1,0},{2,3},{3,2},{4,5},{5,4},{6,7},{7,6},{8,9},{9,8},{10,11... | collective-permute-start | bytes 2359304 | tf_op jit(solution)/shard_map/ppermute | solution.py:1004
  57.1 21.7 %collective-permute-start.11 = (bf16[8,48,1024]{2,1,0:T(8,128)(2,1)S(1)}, bf16[8,48,1024]{2,1,0:T(8,128)(2,1)}, u32[]{:S(2)}, u32[]{:S(2)}) collective-permute-start(bf16[8,48,1024]{2,1,0:T(8,128)(2,1)S(1)} %collective-permute-done.5.refs_1_.refs_12_.refs_20_), channel_id=1, source_target_pairs={{0,1},{1,0},{2,3},{3,2},{4,5},{5,4},{6,7},{7,6},{8,9},{9,8},{10,11... | collective-permute-start | bytes 2359304 | tf_op jit(solution)/shard_map/ppermute | solution.py:1004
  72.0 24.5 %collective-permute-start.15 = (bf16[4,80,1024]{2,1,0:T(8,128)(2,1)}, bf16[4,80,1024]{2,1,0:T(8,128)(2,1)}, u32[]{:S(2)}, u32[]{:S(2)}) collective-permute-start(bf16[4,80,1024]{2,1,0:T(8,128)(2,1)} %get-tuple-element.169.refs_2_), channel_id=1, source_target_pairs={{0,2},{2,0},{4,6},{6,4},{8,10},{10,8},{12,14},{14,12},{16,18},{18,... | collective-permute-start | bytes 1966088 | tf_op jit(solution)/shard_map/ppermute | solution.py:744
  73.5 23.0 %collective-permute-start.14 = (bf16[4,80,1024]{2,1,0:T(8,128)(2,1)S(1)}, bf16[4,80,1024]{2,1,0:T(8,128)(2,1)}, u32[]{:S(2)}, u32[]{:S(2)}) collective-permute-start(bf16[4,80,1024]{2,1,0:T(8,128)(2,1)S(1)} %get-tuple-element.168.refs_0_), channel_id=1, source_target_pairs={{0,4},{2,6},{4,0},{6,2},{8,12},{10,14},{12,8},{14,10},{16,20},{18,... | collective-permute-start | bytes 1966088 | tf_op jit(solution)/shard_map/ppermute | solution.py:744
  100.3 27.8 %collective-permute-start.16 = (bf16[2,1024,1024]{2,1,0:T(8,128)(2,1)}, bf16[2,1024,1024]{2,1,0:T(8,128)(2,1)}, u32[]{:S(2)}, u32[]{:S(2)}) collective-permute-start(bf16[2,1024,1024]{2,1,0:T(8,128)(2,1)} %get-tuple-element.174.ko_ref.vo_ref), channel_id=1, source_target_pairs={{0,1},{1,0},{2,3},{3,2},{4,5},{5,4},{6,7},{7,6},{8,9},{9,8},{10,11... | collective-permute-start | bytes 12582920 | tf_op jit(solution)/shard_map/ppermute | solution.py:1004
  100.3 55.9 %collective-permute-start.21 = (bf16[8,80,1024]{2,1,0:T(8,128)(2,1)}, bf16[8,80,1024]{2,1,0:T(8,128)(2,1)}, u32[]{:S(2)}, u32[]{:S(2)}) collective-permute-start(bf16[8,80,1024]{2,1,0:T(8,128)(2,1)} %get-tuple-element.177.refs_7_.refs_16_), channel_id=1, source_target_pairs={{0,1},{1,0},{2,3},{3,2},{4,5},{5,4},{6,7},{7,6},{8,9},{9,8},{10,11... | collective-permute-start | bytes 3932168 | tf_op jit(solution)/shard_map/ppermute | solution.py:1004
  100.8 55.4 %collective-permute-start.20 = (bf16[8,80,1024]{2,1,0:T(8,128)(2,1)}, bf16[8,80,1024]{2,1,0:T(8,128)(2,1)S(1)}, u32[]{:S(2)}, u32[]{:S(2)}) collective-permute-start(bf16[8,80,1024]{2,1,0:T(8,128)(2,1)} %get-tuple-element.170.refs_3_.refs_0_.refs_4_), channel_id=1, source_target_pairs={{0,1},{1,0},{2,3},{3,2},{4,5},{5,4},{6,7},{7,6},{8,9},{9,8},{10,11... | collective-permute-start | bytes 3932168 | tf_op jit(solution)/shard_map/ppermute | solution.py:1004
  103.3 22.2 %collective-permute-start.18 = (bf16[1,128,1024]{2,1,0:T(8,128)(2,1)S(1)}, bf16[1,128,1024]{2,1,0:T(8,128)(2,1)S(1)}, u32[]{:S(2)}, u32[]{:S(2)}) collective-permute-start(bf16[1,128,1024]{2,1,0:T(8,128)(2,1)S(1)} %copy-done.57), channel_id=1, source_target_pairs={{0,16},{2,18},{4,20},{6,22},{8,24},{10,26},{12,28},{14,30},{16,0},... | collective-permute-start | bytes 786440 | tf_op jit(solution)/shard_map/ppermute | solution.py:744
  112.5 61.4 %collective-permute-start.26 = (bf16[8,80,1024]{2,1,0:T(8,128)(2,1)}, bf16[8,80,1024]{2,1,0:T(8,128)(2,1)}, u32[]{:S(2)}, u32[]{:S(2)}) collective-permute-start(bf16[8,80,1024]{2,1,0:T(8,128)(2,1)} %get-tuple-element.177.refs_7_.refs_16_), channel_id=1, source_target_pairs={{0,4},{2,6},{4,0},{6,2},{8,12},{10,14},{12,8},{14,10},{16,20},{18,... | collective-permute-start | bytes 3932168 | tf_op jit(solution)/shard_map/ppermute | solution.py:744
  126.2 47.7 %collective-permute-start.24 = (bf16[8,80,1024]{2,1,0:T(8,128)(2,1)}, bf16[8,80,1024]{2,1,0:T(8,128)(2,1)}, u32[]{:S(2)}, u32[]{:S(2)}) collective-permute-start(bf16[8,80,1024]{2,1,0:T(8,128)(2,1)} %get-tuple-element.170.refs_3_.refs_0_.refs_4_), channel_id=1, source_target_pairs={{0,2},{2,0},{4,6},{6,4},{8,10},{10,8},{12,14},{14,12},{16,18},{18,... | collective-permute-start | bytes 3932168 | tf_op jit(solution)/shard_map/ppermute | solution.py:744
  128.1 28.1 %collective-permute-start.17 = (bf16[1,128,1024]{2,1,0:T(8,128)(2,1)}, bf16[1,128,1024]{2,1,0:T(8,128)(2,1)}, u32[]{:S(2)}, u32[]{:S(2)}) collective-permute-start(bf16[1,128,1024]{2,1,0:T(8,128)(2,1)} %maximum_bitcast_fusion.1.refs_0_), channel_id=1, source_target_pairs={{0,8},{2,10},{4,12},{6,14},{8,0},{10,2},{12,4},{14,6},{16,24},{18,... | collective-permute-start | bytes 786440 | tf_op jit(solution)/shard_map/ppermute | solution.py:744
  157.4 15.0 %collective-permute-start.23 = (bf16[4,64,1024]{2,1,0:T(8,128)(2,1)S(1)}, bf16[4,64,1024]{2,1,0:T(8,128)(2,1)S(1)}, u32[]{:S(2)}, u32[]{:S(2)}) collective-permute-start(bf16[4,64,1024]{2,1,0:T(8,128)(2,1)S(1)} %get-tuple-element.182.refs_2_), channel_id=1, source_target_pairs={{0,2},{2,0},{4,6},{6,4},{8,10},{10,8},{12,14},{14,12},{16,18},{18,... | collective-permute-start | bytes 1572872 | tf_op jit(solution)/shard_map/ppermute | solution.py:744
  173.9 26.7 %collective-permute-start.25 = (bf16[8,80,1024]{2,1,0:T(8,128)(2,1)}, bf16[8,80,1024]{2,1,0:T(8,128)(2,1)S(1)}, u32[]{:S(2)}, u32[]{:S(2)}) collective-permute-start(bf16[8,80,1024]{2,1,0:T(8,128)(2,1)} %collective-permute-done.24.refs_4_.refs_1_.refs_5_), channel_id=1, source_target_pairs={{0,1},{1,0},{2,3},{3,2},{4,5},{5,4},{6,7},{7,6},{8,9},{9,8},{10,11... | collective-permute-start | bytes 3932168 | tf_op jit(solution)/shard_map/ppermute | solution.py:1004
  173.9 27.1 %collective-permute-start.27 = (bf16[8,80,1024]{2,1,0:T(8,128)(2,1)}, bf16[8,80,1024]{2,1,0:T(8,128)(2,1)}, u32[]{:S(2)}, u32[]{:S(2)}) collective-permute-start(bf16[8,80,1024]{2,1,0:T(8,128)(2,1)} %collective-permute-done.26.refs_8_.refs_17_), channel_id=1, source_target_pairs={{0,1},{1,0},{2,3},{3,2},{4,5},{5,4},{6,7},{7,6},{8,9},{9,8},{10,11... | collective-permute-start | bytes 3932168 | tf_op jit(solution)/shard_map/ppermute | solution.py:1004
  174.4 38.2 %collective-permute-start.31 = (bf16[8,64,1024]{2,1,0:T(8,128)(2,1)}, bf16[8,64,1024]{2,1,0:T(8,128)(2,1)}, u32[]{:S(2)}, u32[]{:S(2)}) collective-permute-start(bf16[8,64,1024]{2,1,0:T(8,128)(2,1)} %get-tuple-element.193.refs_20_), channel_id=1, source_target_pairs={{0,4},{2,6},{4,0},{6,2},{8,12},{10,14},{12,8},{14,10},{16,20},{18,... | collective-permute-start | bytes 3145736 | tf_op jit(solution)/shard_map/ppermute | solution.py:744
  175.7 36.9 %collective-permute-start.28 = (bf16[8,64,1024]{2,1,0:T(8,128)(2,1)}, bf16[8,64,1024]{2,1,0:T(8,128)(2,1)}, u32[]{:S(2)}, u32[]{:S(2)}) collective-permute-start(bf16[8,64,1024]{2,1,0:T(8,128)(2,1)} %get-tuple-element.183.refs_8_.refs_12_), channel_id=1, source_target_pairs={{0,2},{2,0},{4,6},{6,4},{8,10},{10,8},{12,14},{14,12},{16,18},{18,... | collective-permute-start | bytes 3145736 | tf_op jit(solution)/shard_map/ppermute | solution.py:744
  177.6 35.5 %collective-permute-start.32 = (bf16[8,64,1024]{2,1,0:T(8,128)(2,1)}, bf16[8,64,1024]{2,1,0:T(8,128)(2,1)}, u32[]{:S(2)}, u32[]{:S(2)}) collective-permute-start(bf16[8,64,1024]{2,1,0:T(8,128)(2,1)} %get-tuple-element.193.refs_20_), channel_id=1, source_target_pairs={{0,1},{1,0},{2,3},{3,2},{4,5},{5,4},{6,7},{7,6},{8,9},{9,8},{10,11... | collective-permute-start | bytes 3145736 | tf_op jit(solution)/shard_map/ppermute | solution.py:1004
  287.6 16.3 %collective-permute-start.34 = (bf16[4,16,32,1024]{3,2,1,0:T(8,128)(2,1)}, bf16[4,16,32,1024]{3,2,1,0:T(8,128)(2,1)}, u32[]{:S(2)}, u32[]{:S(2)}) collective-permute-start(bf16[4,16,32,1024]{3,2,1,0:T(8,128)(2,1)} %get-tuple-element.201), channel_id=1, source_target_pairs={{0,1},{1,0},{2,3},{3,2},{4,5},{5,4},{6,7},{7,6},{8,9},{9,8},{10,11... | collective-permute-start | bytes 12582920 | tf_op jit(solution)/shard_map/ppermute | solution.py:1004
  288.0 15.9 %collective-permute-start.35 = (bf16[4,16,32,1024]{3,2,1,0:T(8,128)(2,1)}, bf16[4,16,32,1024]{3,2,1,0:T(8,128)(2,1)}, u32[]{:S(2)}, u32[]{:S(2)}) collective-permute-start(bf16[4,16,32,1024]{3,2,1,0:T(8,128)(2,1)} %get-tuple-element.203), channel_id=1, source_target_pairs={{0,1},{1,0},{2,3},{3,2},{4,5},{5,4},{6,7},{7,6},{8,9},{9,8},{10,11... | collective-permute-start | bytes 12582920 | tf_op jit(solution)/shard_map/ppermute | solution.py:1004
  309.3 48.1 %collective-permute-start.37 = (bf16[4,2,2,2,32,1024]{5,4,3,2,1,0:T(8,128)(2,1)}, bf16[4,2,2,2,32,1024]{5,4,3,2,1,0:T(8,128)(2,1)S(1)}, u32[]{:S(2)}, u32[]{:S(2)}) collective-permute-start(bf16[4,2,2,2,32,1024]{5,4,3,2,1,0:T(8,128)(2,1)} %get-tuple-element.213), channel_id=1, source_target_pairs={{0,4},{2,6},{4,0},{6,2},{8,12},{10,14},{12,8},{14,10},{16,20},{18,... | collective-permute-start | bytes 6291464 | tf_op jit(solution)/shard_map/ppermute | solution.py:744
  309.4 51.6 %collective-permute-start.36 = (bf16[4,2,2,2,32,1024]{5,4,3,2,1,0:T(8,128)(2,1)}, bf16[4,2,2,2,32,1024]{5,4,3,2,1,0:T(8,128)(2,1)}, u32[]{:S(2)}, u32[]{:S(2)}) collective-permute-start(bf16[4,2,2,2,32,1024]{5,4,3,2,1,0:T(8,128)(2,1)} %get-tuple-element.204), channel_id=1, source_target_pairs={{0,2},{2,0},{4,6},{6,4},{8,10},{10,8},{12,14},{14,12},{16,18},{18,... | collective-permute-start | bytes 6291464 | tf_op jit(solution)/shard_map/ppermute | solution.py:744
  351.3 16.5 %collective-permute-start.38 = (bf16[2,1024,256]{2,1,0:T(8,128)(2,1)}, bf16[2,1024,256]{2,1,0:T(8,128)(2,1)S(1)}, u32[]{:S(2)}, u32[]{:S(2)}) collective-permute-start(bf16[2,1024,256]{2,1,0:T(8,128)(2,1)} %get-tuple-element.218), channel_id=1, source_target_pairs={{0,1},{1,0},{2,3},{3,2},{4,5},{5,4},{6,7},{7,6},{8,9},{9,8},{10,11... | collective-permute-start | bytes 3145736 | tf_op jit(solution)/shard_map/ppermute | solution.py:1004
  365.7 29.6 %collective-permute-start.41 = (bf16[4,2,2,32,1024]{4,3,2,1,0:T(8,128)(2,1)}, bf16[4,2,2,32,1024]{4,3,2,1,0:T(8,128)(2,1)}, u32[]{:S(2)}, u32[]{:S(2)}) collective-permute-start(bf16[4,2,2,32,1024]{4,3,2,1,0:T(8,128)(2,1)} %get-tuple-element.229), channel_id=1, source_target_pairs={{0,2},{2,0},{4,6},{6,4},{8,10},{10,8},{12,14},{14,12},{16,18},{18,... | collective-permute-start | bytes 3145736 | tf_op jit(solution)/shard_map/ppermute | solution.py:744
  367.5 27.8 %collective-permute-start.40 = (bf16[4,2,2,32,1024]{4,3,2,1,0:T(8,128)(2,1)}, bf16[4,2,2,32,1024]{4,3,2,1,0:T(8,128)(2,1)}, u32[]{:S(2)}, u32[]{:S(2)}) collective-permute-start(bf16[4,2,2,32,1024]{4,3,2,1,0:T(8,128)(2,1)} %get-tuple-element.214), channel_id=1, source_target_pairs={{0,4},{2,6},{4,0},{6,2},{8,12},{10,14},{12,8},{14,10},{16,20},{18,... | collective-permute-start | bytes 3145736 | tf_op jit(solution)/shard_map/ppermute | solution.py:744
  367.8 33.6 %collective-permute-start.43 = (bf16[4,16,32,256]{3,2,1,0:T(8,128)(2,1)}, bf16[4,16,32,256]{3,2,1,0:T(8,128)(2,1)S(1)}, u32[]{:S(2)}, u32[]{:S(2)}) collective-permute-start(bf16[4,16,32,256]{3,2,1,0:T(8,128)(2,1)} %get-tuple-element.236), channel_id=1, source_target_pairs={{0,1},{1,0},{2,3},{3,2},{4,5},{5,4},{6,7},{7,6},{8,9},{9,8},{10,11... | collective-permute-start | bytes 3145736 | tf_op jit(solution)/shard_map/ppermute | solution.py:1004
  376.6 24.8 %collective-permute-start.42 = (bf16[3,16,32,256]{3,2,1,0:T(8,128)(2,1)}, bf16[3,16,32,256]{3,2,1,0:T(8,128)(2,1)}, u32[]{:S(2)}, u32[]{:S(2)}) collective-permute-start(bf16[3,16,32,256]{3,2,1,0:T(8,128)(2,1)} %get-tuple-element.233), channel_id=1, source_target_pairs={{0,1},{1,0},{2,3},{3,2},{4,5},{5,4},{6,7},{7,6},{8,9},{9,8},{10,11... | collective-permute-start | bytes 2359304 | tf_op jit(solution)/shard_map/ppermute | solution.py:1004
  377.1 24.3 %collective-permute-start.44 = (bf16[3,16,32,256]{3,2,1,0:T(8,128)(2,1)}, bf16[3,16,32,256]{3,2,1,0:T(8,128)(2,1)}, u32[]{:S(2)}, u32[]{:S(2)}) collective-permute-start(bf16[3,16,32,256]{3,2,1,0:T(8,128)(2,1)} %get-tuple-element.238), channel_id=1, source_target_pairs={{0,1},{1,0},{2,3},{3,2},{4,5},{5,4},{6,7},{7,6},{8,9},{9,8},{10,11... | collective-permute-start | bytes 2359304 | tf_op jit(solution)/shard_map/ppermute | solution.py:1004
  404.3 51.3 %collective-permute-start.49 = (bf16[5,2,2,2,32,256]{5,4,3,2,1,0:T(8,128)(2,1)}, bf16[5,2,2,2,32,256]{5,4,3,2,1,0:T(8,128)(2,1)S(1)}, u32[]{:S(2)}, u32[]{:S(2)}) collective-permute-start(bf16[5,2,2,2,32,256]{5,4,3,2,1,0:T(8,128)(2,1)} %get-tuple-element.247), channel_id=1, source_target_pairs={{0,4},{2,6},{4,0},{6,2},{8,12},{10,14},{12,8},{14,10},{16,20},{18,... | collective-permute-start | bytes 1966088 | tf_op jit(solution)/shard_map/ppermute | solution.py:744
  406.1 49.6 %collective-permute-start.48 = (bf16[5,2,2,2,32,256]{5,4,3,2,1,0:T(8,128)(2,1)}, bf16[5,2,2,2,32,256]{5,4,3,2,1,0:T(8,128)(2,1)S(1)}, u32[]{:S(2)}, u32[]{:S(2)}) collective-permute-start(bf16[5,2,2,2,32,256]{5,4,3,2,1,0:T(8,128)(2,1)} %get-tuple-element.239), channel_id=1, source_target_pairs={{0,2},{2,0},{4,6},{6,4},{8,10},{10,8},{12,14},{14,12},{16,18},{18,... | collective-permute-start | bytes 1966088 | tf_op jit(solution)/shard_map/ppermute | solution.py:744
  407.8 40.3 %collective-permute-start.46 = (bf16[8,32,1024]{2,1,0:T(8,128)(2,1)}, bf16[8,32,1024]{2,1,0:T(8,128)(2,1)S(1)}, u32[]{:S(2)}, u32[]{:S(2)}) collective-permute-start(bf16[8,32,1024]{2,1,0:T(8,128)(2,1)} %get-tuple-element.243), channel_id=1, source_target_pairs={{0,16},{2,18},{4,20},{6,22},{8,24},{10,26},{12,28},{14,30},{16,0},... | collective-permute-start | bytes 1572872 | tf_op jit(solution)/shard_map/ppermute | solution.py:744
  414.2 34.0 %collective-permute-start.47 = (bf16[8,32,1024]{2,1,0:T(8,128)(2,1)}, bf16[8,32,1024]{2,1,0:T(8,128)(2,1)}, u32[]{:S(2)}, u32[]{:S(2)}) collective-permute-start(bf16[8,32,1024]{2,1,0:T(8,128)(2,1)} %get-tuple-element.244), channel_id=1, source_target_pairs={{0,24},{2,26},{4,28},{6,30},{8,16},{10,18},{12,20},{14,22},{16,8},... | collective-permute-start | bytes 1572872 | tf_op jit(solution)/shard_map/ppermute | solution.py:744
  414.2 36.3 %collective-permute-start.45 = (bf16[8,32,1024]{2,1,0:T(8,128)(2,1)}, bf16[8,32,1024]{2,1,0:T(8,128)(2,1)}, u32[]{:S(2)}, u32[]{:S(2)}) collective-permute-start(bf16[8,32,1024]{2,1,0:T(8,128)(2,1)} %get-tuple-element.230), channel_id=1, source_target_pairs={{0,8},{2,10},{4,12},{6,14},{8,0},{10,2},{12,4},{14,6},{16,24},{18,... | collective-permute-start | bytes 1572872 | tf_op jit(solution)/shard_map/ppermute | solution.py:744
  475.4 34.5 %collective-permute-start.57 = (bf16[3,2,2,2,32,256]{5,4,3,2,1,0:T(8,128)(2,1)S(1)}, bf16[3,2,2,2,32,256]{5,4,3,2,1,0:T(8,128)(2,1)S(1)}, u32[]{:S(2)}, u32[]{:S(2)}) collective-permute-start(bf16[3,2,2,2,32,256]{5,4,3,2,1,0:T(8,128)(2,1)S(1)} %get-tuple-element.277), channel_id=1, source_target_pairs={{0,4},{2,6},{4,0},{6,2},{8,12},{10,14},{12,8},{14,10},{16,20},{18,... | collective-permute-start | bytes 1179656 | tf_op jit(solution)/shard_map/ppermute | solution.py:744
  476.2 33.7 %collective-permute-start.56 = (bf16[3,2,2,2,32,256]{5,4,3,2,1,0:T(8,128)(2,1)S(1)}, bf16[3,2,2,2,32,256]{5,4,3,2,1,0:T(8,128)(2,1)S(1)}, u32[]{:S(2)}, u32[]{:S(2)}) collective-permute-start(bf16[3,2,2,2,32,256]{5,4,3,2,1,0:T(8,128)(2,1)S(1)} %get-tuple-element.267), channel_id=1, source_target_pairs={{0,2},{2,0},{4,6},{6,4},{8,10},{10,8},{12,14},{14,12},{16,18},{18,... | collective-permute-start | bytes 1179656 | tf_op jit(solution)/shard_map/ppermute | solution.py:744
  477.2 35.9 %collective-permute-start.59 = (bf16[10,32,256]{2,1,0:T(8,128)(2,1)S(1)}, bf16[10,32,256]{2,1,0:T(8,128)(2,1)S(1)}, u32[]{:S(2)}, u32[]{:S(2)}) collective-permute-start(bf16[10,32,256]{2,1,0:T(8,128)(2,1)S(1)} %get-tuple-element.280), channel_id=1, source_target_pairs={{0,16},{2,18},{4,20},{6,22},{8,24},{10,26},{12,28},{14,30},{16,0},... | collective-permute-start | bytes 491528 | tf_op jit(solution)/shard_map/ppermute | solution.py:744
  486.8 26.4 %collective-permute-start.60 = (bf16[10,32,256]{2,1,0:T(8,128)(2,1)S(1)}, bf16[10,32,256]{2,1,0:T(8,128)(2,1)S(1)}, u32[]{:S(2)}, u32[]{:S(2)}) collective-permute-start(bf16[10,32,256]{2,1,0:T(8,128)(2,1)S(1)} %get-tuple-element.281), channel_id=1, source_target_pairs={{0,24},{2,26},{4,28},{6,30},{8,16},{10,18},{12,20},{14,22},{16,8},... | collective-permute-start | bytes 491528 | tf_op jit(solution)/shard_map/ppermute | solution.py:744
  489.8 23.4 %collective-permute-start.58 = (bf16[10,32,256]{2,1,0:T(8,128)(2,1)S(1)}, bf16[10,32,256]{2,1,0:T(8,128)(2,1)S(1)}, u32[]{:S(2)}, u32[]{:S(2)}) collective-permute-start(bf16[10,32,256]{2,1,0:T(8,128)(2,1)S(1)} %get-tuple-element.261), channel_id=1, source_target_pairs={{0,8},{2,10},{4,12},{6,14},{8,0},{10,2},{12,4},{14,6},{16,24},{18,... | collective-permute-start | bytes 491528 | tf_op jit(solution)/shard_map/ppermute | solution.py:744
  512.2 16.3 %collective-permute-start.61 = (bf16[3,2,2,32,256]{4,3,2,1,0:T(8,128)(2,1)}, bf16[3,2,2,32,256]{4,3,2,1,0:T(8,128)(2,1)S(1)}, u32[]{:S(2)}, u32[]{:S(2)}) collective-permute-start(bf16[3,2,2,32,256]{4,3,2,1,0:T(8,128)(2,1)} %get-tuple-element.278), channel_id=1, source_target_pairs={{0,4},{2,6},{4,0},{6,2},{8,12},{10,14},{12,8},{14,10},{16,20},{18,... | collective-permute-start | bytes 589832 | tf_op jit(solution)/shard_map/ppermute | solution.py:744
  (110 other events, 1531.1 us)

commit v5 on v4

--- a/solution.py
+++ b/solution.py
@@ -17,6 +17,7 @@
 BOTH = ("dp", "seq")
 ATT_Q = 256
 ATT_K = 512
+ROW_ALIGN = 16
 ROWS = 256
 FF_COLS = 512
 COST_SCALE = 100000
@@ -217,69 +218,80 @@
     return value[h * HEAD_DIM : (h + 1) * HEAD_DIM, :]
 
 
-def attend_kernel(bq, bk, tab, q_ref, ko_ref, vo_ref, kp_ref, vp_ref, sq_ref, so_ref, sp_ref, o_ref, lse_ref):
+def line_up(target, own_ref, other_ref, which, mine):
+    n = own_ref.shape[1]
+    target[pl.ds(pl.multiple_of(mine * n, n), n), :] = own_ref[which]
+    target[pl.ds(pl.multiple_of((1 - mine) * n, n), n), :] = other_ref[which]
+    target[2 * n :, :] = jnp.zeros((target.shape[0] - 2 * n, target.shape[1]), target.dtype)
+
+
+def attend_kernel(bq, bk, tab, q_ref, own_ref, other_ref, sq_ref, s_ref, o_ref, lse_ref, k_s, v_s):
     i = pl.program_id(1)
+
+    @pl.when(i == 0)
+    def _():
+        mine = tab[2 * pl.num_programs(1)]
+        line_up(k_s, own_ref, other_ref, 0, mine)
+        line_up(v_s, own_ref, other_ref, 1, mine)
+
     stacked = stack_heads(q_ref[...])
     seg_q = jnp.concatenate([sq_ref[0]] * GROUP, axis=1)
-
-    def over(k_ref, v_ref, s_ref, first, count, state):
-        def step(j, carry):
-            top, total, acc = carry
-            at = pl.multiple_of((first + j) * bk, bk)
-            scores = dot_nt(k_ref[0, pl.ds(at, bk), :], stacked)
-            scores = jnp.where(s_ref[pl.ds(at, bk), :] == seg_q, scores, NEG)
-            new_top = jnp.maximum(top, jnp.max(scores, axis=0, keepdims=True))
-            decay = jnp.exp(top - new_top)
-            probs = jnp.exp(scores - new_top)
-            total = total * decay + jnp.sum(probs, axis=0, keepdims=True)
-            low = probs.astype(BF16)
-            values = v_ref[0, pl.ds(at, bk), :].T
-            acc = tuple(
-                acc[h] * head_cols(decay, h, bq) + dot_nn(head_rows(values, h), head_cols(low, h, bq))
-                for h in range(GROUP)
-            )
-            return new_top, total, acc
-
-        return lax.fori_loop(0, count, step, state)
+    first = tab[2 * i]
+
+    def step(j, carry):
+        top, total, acc = carry
+        at = pl.multiple_of(first + j * bk, ROW_ALIGN)
+        scores = dot_nt(k_s[pl.ds(at, bk), :], stacked)
+        scores = jnp.where(s_ref[pl.ds(at, bk), :] == seg_q, scores, NEG)
+        new_top = jnp.maximum(top, jnp.max(scores, axis=0, keepdims=True))
+        decay = jnp.exp(top - new_top)
+        probs = jnp.exp(scores - new_top)
+        total = total * decay + jnp.sum(probs, axis=0, keepdims=True)
+        low = probs.astype(BF16)
+        values = v_s[pl.ds(at, bk), :].T
+        acc = tuple(
+            acc[h] * head_cols(decay, h, bq) + dot_nn(head_rows(values, h), head_cols(low, h, bq))
+            for h in range(GROUP)
+        )
+        return new_top, total, acc
 
     state = (
         jnp.full((1, GROUP * bq), -jnp.inf, F32),
         jnp.zeros((1, GROUP * bq), F32),
         tuple(jnp.zeros((HEAD_DIM, bq), F32) for _ in range(GROUP)),
     )
-    state = over(ko_ref, vo_ref, so_ref, tab[4 * i], tab[4 * i + 1], state)
-    top, total, acc = over(kp_ref, vp_ref, sp_ref, tab[4 * i + 2], tab[4 * i + 3], state)
+    top, total, acc = lax.fori_loop(0, tab[2 * i + 1], step, state)
     out = jnp.concatenate([acc[h] / head_cols(total, h, bq) for h in range(GROUP)], axis=0)
     o_ref[...] = out.T.astype(BF16)
     lse_ref[0, 0] = top + jnp.log(total)
 
 
-def attend_call(tab, q, own, other, seg_q, seg_own, seg_other, bq, bk, first, groups):
+def attend_specs(n, bq, padded, first):
+    def half(_):
+        return pl.BlockSpec((2, n, GROUP_WIDTH), lambda g, i, *_: (0, 0, g + first))
+
+    return [
+        half(0),
+        half(1),
+        pl.BlockSpec((1, 1, bq), lambda g, i, *_: (i, 0, 0)),
+        pl.BlockSpec((padded, 1), lambda *_: (0, 0)),
+    ]
+
+
+def attend_call(tab, q, own, other, seg_q, seg_col, bq, bk, first, groups):
     n, d = q.shape
     blocks = n // bq
-    query = pl.BlockSpec((bq, GROUP_WIDTH), lambda g, i, *_: (i, g + first))
-
-    def half(which):
-        return pl.BlockSpec((1, n, GROUP_WIDTH), lambda g, i, *_: (which, 0, g + first))
-
-    column = pl.BlockSpec((n, 1), lambda g, i, *_: (0, 0))
+    padded = seg_col.shape[0]
     spec = pltpu.PrefetchScalarGridSpec(
         num_scalar_prefetch=1,
         grid=(groups, blocks),
-        in_specs=[
-            query,
-            half(0),
-            half(1),
-            half(0),
-            half(1),
-            pl.BlockSpec((1, 1, bq), lambda g, i, *_: (i, 0, 0)),
-            column,
-            column,
-        ],
+        in_specs=[pl.BlockSpec((bq, GROUP_WIDTH), lambda g, i, *_: (i, g + first))]
+        + attend_specs(n, bq, padded, first),
         out_specs=[
             pl.BlockSpec((bq, GROUP_WIDTH), lambda g, i, *_: (i, g)),
             pl.BlockSpec((1, 1, 1, GROUP * bq), lambda g, i, *_: (g, i, 0, 0)),
         ],
+        scratch_shapes=[pltpu.VMEM((padded, GROUP_WIDTH), BF16)] * 2,
     )
     return pl.pallas_call(
         partial(attend_kernel, bq, bk),
@@ -291,19 +303,22 @@
         compiler_params=params(56),
         cost_estimate=cost(8_000_000_000 * groups, 3 * groups * n * d),
         name="attend",
-    )(tab, q, own, own, other, other, seg_q, seg_own, seg_other)
+    )(tab, q, own, other, seg_q, seg_col)
 
 
 def attend_back_kernel(
-    bq, bk, tab, q_ref, go_ref, o_ref, ko_ref, vo_ref, kp_ref, vp_ref, sq_ref, so_ref, sp_ref, lse_ref,
-    dq_ref, down_ref, dpart_ref, dko, dvo, dkp, dvp,
+    bq, bk, tab, q_ref, go_ref, o_ref, lse_ref, own_ref, other_ref, sq_ref, s_ref,
+    dq_ref, down_ref, dpart_ref, k_s, v_s, dk_s, dv_s,
 ):
     i = pl.program_id(1)
+    mine = tab[2 * pl.num_programs(1)]
 
     @pl.when(i == 0)
     def _():
-        for ref in (dko, dvo, dkp, dvp):
-            ref[...] = jnp.zeros_like(ref)
+        line_up(k_s, own_ref, other_ref, 0, mine)
+        line_up(v_s, own_ref, other_ref, 1, mine)
+        dk_s[...] = jnp.zeros_like(dk_s)
+        dv_s[...] = jnp.zeros_like(dv_s)
 
     stacked = stack_heads(q_ref[...])
     grad = go_ref[...]
@@ -314,47 +329,41 @@
     )
     seg_q = jnp.concatenate([sq_ref[0]] * GROUP, axis=1)
     lse = lse_ref[0, 0]
-
-    def over(k_ref, v_ref, s_ref, dk, dv, first, count, state):
-        def step(j, acc):
-            at = pl.multiple_of((first + j) * bk, bk)
-            keys = k_ref[0, pl.ds(at, bk), :]
-            scores = dot_nt(keys, stacked)
-            scores = jnp.where(s_ref[pl.ds(at, bk), :] == seg_q, scores, NEG)
-            probs = jnp.exp(scores - lse)
-            grad_probs = dot_nt(v_ref[0, pl.ds(at, bk), :], stacked_grad)
-            grad_scores = (probs * (grad_probs - inner)).astype(BF16)
-            dv[pl.ds(at, bk), :] += dot_nn(probs.astype(BF16), stacked_grad)
-            dk[pl.ds(at, bk), :] += dot_nn(grad_scores, stacked)
-            keys_t = keys.T
-            return tuple(
-                acc[h] + dot_nn(head_rows(keys_t, h), head_cols(grad_scores, h, bq)) for h in range(GROUP)
-            )
-
-        return lax.fori_loop(0, count, step, state)
+    first = tab[2 * i]
+
+    def step(j, acc):
+        at = pl.multiple_of(first + j * bk, ROW_ALIGN)
+        keys = k_s[pl.ds(at, bk), :]
+        scores = dot_nt(keys, stacked)
+        scores = jnp.where(s_ref[pl.ds(at, bk), :] == seg_q, scores, NEG)
+        probs = jnp.exp(scores - lse)
+        grad_probs = dot_nt(v_s[pl.ds(at, bk), :], stacked_grad)
+        grad_scores = (probs * (grad_probs - inner)).astype(BF16)
+        dv_s[pl.ds(at, bk), :] += dot_nn(probs.astype(BF16), stacked_grad)
+        dk_s[pl.ds(at, bk), :] += dot_nn(grad_scores, stacked)
+        keys_t = keys.T
+        return tuple(
+            acc[h] + dot_nn(head_rows(keys_t, h), head_cols(grad_scores, h, bq)) for h in range(GROUP)
+        )
 
     state = tuple(jnp.zeros((HEAD_DIM, bq), F32) for _ in range(GROUP))
-    state = over(ko_ref, vo_ref, so_ref, dko, dvo, tab[4 * i], tab[4 * i + 1], state)
-    state = over(kp_ref, vp_ref, sp_ref, dkp, dvp, tab[4 * i + 2], tab[4 * i + 3], state)
+    state = lax.fori_loop(0, tab[2 * i + 1], step, state)
     dq_ref[...] = (jnp.concatenate(state, axis=0).T * 0.125).astype(BF16)
 
     @pl.when(i == pl.num_programs(1) - 1)
     def _():
-        down_ref[0] = dko[...].astype(BF16)
-        down_ref[1] = dvo[...].astype(BF16)
-        dpart_ref[0] = dkp[...].astype(BF16)
-        dpart_ref[1] = dvp[...].astype(BF16)
-
-
-def attend_back_call(tab, q, grad, out, own, other, seg_q, seg_own, seg_other, lse, bq, bk, first, groups, out_first):
+        n = down_ref.shape[1]
+        for ref, half in ((down_ref, mine), (dpart_ref, 1 - mine)):
+            rows = pl.ds(pl.multiple_of(half * n, n), n)
+            ref[0] = dk_s[rows, :].astype(BF16)
+            ref[1] = dv_s[rows, :].astype(BF16)
+
+
+def attend_back_call(tab, q, grad, out, own, other, seg_q, seg_col, lse, bq, bk, first, groups, out_first):
     n, d = q.shape
     blocks = n // bq
+    padded = seg_col.shape[0]
     query = pl.BlockSpec((bq, GROUP_WIDTH), lambda g, i, *_: (i, g + first))
-
-    def half(which):
-        return pl.BlockSpec((1, n, GROUP_WIDTH), lambda g, i, *_: (which, 0, g + first))
-
-    column = pl.BlockSpec((n, 1), lambda *_: (0, 0))
     pair = pl.BlockSpec((2, n, GROUP_WIDTH), lambda g, i, *_: (0, 0, g))
     spec = pltpu.PrefetchScalarGridSpec(
         num_scalar_prefetch=1,
@@ -363,17 +372,12 @@
             query,
             query,
             pl.BlockSpec((bq, GROUP_WIDTH), lambda g, i, *_: (i, g + out_first)),
-            half(0),
-            half(1),
-            half(0),
-            half(1),
-            pl.BlockSpec((1, 1, bq), lambda g, i, *_: (i, 0, 0)),
-            column,
-            column,
             pl.BlockSpec((1, 1, 1, GROUP * bq), lambda g, i, *_: (g + out_first, i, 0, 0)),
-        ],
+        ]
+        + attend_specs(n, bq, padded, first),
         out_specs=[pl.BlockSpec((bq, GROUP_WIDTH), lambda g, i, *_: (i, g)), pair, pair],
-        scratch_shapes=[pltpu.VMEM((n, GROUP_WIDTH), F32)] * 4,
+        scratch_shapes=[pltpu.VMEM((padded, GROUP_WIDTH), BF16)] * 2
+        + [pltpu.VMEM((padded, GROUP_WIDTH), F32)] * 2,
     )
     width = groups * GROUP_WIDTH
     return pl.pallas_call(
@@ -387,7 +391,7 @@
         compiler_params=params(56),
         cost_estimate=cost(12_000_000_000 * groups, 6 * groups * n * d),
         name="attend_back",
-    )(tab, q, grad, out, own, own, other, other, seg_q, seg_own, seg_other, lse)
+    )(tab, q, grad, out, lse, own, other, seg_q, seg_col)
 
 
 def mid_kernel(weights, count, place, x_ref, gain_ref, bias_ref, *refs):
@@ -877,11 +881,18 @@
         held = self.order.run(lambda first, *rest: merge((first, *rest), outputs, *awaited), *arrays)
         for s, array in zip(self.sides, held, strict=True):
             s.hold(array, s.order[1])
-            s.other = self.exchange(s.held)
+
+    def cross(self):
+        for s in self.sides:
+            s.other = self.exchange(self.order.after(s.held))
 
     def finish(self):
         for s in self.sides:
-            s.buffers = [s.held, s.got, s.other, self.exchange(self.order.after(s.got))]
+            s.rest = self.exchange(self.order.after(s.got))
+
+    def ready(self):
+        for s in self.sides:
+            s.buffers = [s.held, s.got, s.other, s.rest]
             s.parts = s.parts_of()
 
 
@@ -904,8 +915,8 @@
 
 
 class Scatter:
-    def __init__(self, cube, one, two):
-        self.cube, self.sides, self.step = cube, (one, two), 0
+    def __init__(self, cube, one, two, direct):
+        self.cube, self.sides, self.step, self.direct = cube, (one, two), 0, direct
         self.sent, self.last = [], []
 
     def advance(self):
@@ -927,19 +938,23 @@
                     at += stream[0].count
         else:
             streams = [stream for side in self.sides for stream in side]
-            done = list(range(cube.bits))
-            self.sent = cube.add([[(stream, done, f) for stream in streams] for f in cube.far()], BF16)
-            self.last = [cube.send(sent, f) for sent, f in zip(self.sent, cube.far(), strict=True)]
+            if self.direct:
+                done, flips = list(range(cube.bits)), cube.far()
+            else:
+                done, flips = list(range(step)), [1 << step]
+            self.sent = cube.add([[(stream, done, f) for stream in streams] for f in flips], BF16)
+            self.last = [cube.send(sent, f) for sent, f in zip(self.sent, flips, strict=True)]
+            axes = [] if self.direct else list(range(step + 1, cube.bits))[::-1]
             for got in self.last:
                 at = 0
                 for stream in streams:
-                    stream.append(Term(got, [], at, stream[0].count))
+                    stream.append(Term(got, axes, at, stream[0].count))
                     at += stream[0].count
         self.step += 1
         return self
 
     def finish(self):
-        while self.step < 3:
+        while self.step < (3 if self.direct else self.cube.bits):
             self.advance()
         done = list(range(self.cube.bits))
         return self.cube.add([[(stream, done, 0)] for side in self.sides for stream in side], F32)
@@ -949,17 +964,13 @@
     return lax.optimization_barrier((value, others))[0]
 
 
-def block_table(seg_full, seg_local, my_index, n, bq, bk):
+def block_table(seg_full, seg_local, my_index, bq, bk):
     first, last = seg_local[::bq], seg_local[bq - 1 :: bq]
     low = jnp.sum((seg_full[None, :] < first[:, None]).astype(jnp.int32), axis=1)
     high = jnp.sum((seg_full[None, :] <= last[:, None]).astype(jnp.int32), axis=1)
-    columns = []
-    for index in (my_index, 1 - my_index):
-        start = jnp.clip(low - index * n, 0, n)
-        stop = jnp.clip(high - index * n, 0, n)
-        block = start // bk
-        columns += [block, jnp.where(stop > start, (stop + bk - 1) // bk - block, 0)]
-    return jnp.stack(columns, axis=1).reshape(-1).astype(jnp.int32)
+    start = low // ROW_ALIGN * ROW_ALIGN
+    table = jnp.stack([start, (high - start + bk - 1) // bk], axis=1).reshape(-1)
+    return jnp.concatenate([table, my_index[None]]).astype(jnp.int32)
 
 
 def body(
@@ -987,10 +998,9 @@
     my_index = lax.axis_index("seq")
     seg_full = segments[0]
     seg_local = lax.dynamic_slice_in_dim(seg_full, my_index * n, n)
-    seg_other = lax.dynamic_slice_in_dim(seg_full, (1 - my_index) * n, n)
-    tab = block_table(seg_full, seg_local, my_index, n, ATT_Q, ATT_K)
+    tab = block_table(seg_full, seg_local, my_index, ATT_Q, ATT_K)
     seg_q = seg_local.reshape(n // ATT_Q, 1, ATT_Q)
-    seg_own_col, seg_other_col = seg_local[:, None], seg_other[:, None]
+    seg_col = jnp.pad(seg_full, (0, ATT_K), constant_values=-1)[:, None]
 
     dp = devices // 2
     dp_index = lax.axis_index("dp")
@@ -1033,10 +1043,10 @@
         head.near(vectors)
         low.far()
         head.last()
+        head.cross()
         order.note(*[side.got for side in head.sides])
         head.finish()
-        low.near()
-        high.far()
+        head.ready()
         key_w = Spread(rows, [(head.sides[0], 0, rows, 0)])
         value_w = Spread(rows, [(head.sides[1], 0, rows, 0)])
         query_w = Spread(rows, [(head.sides[0], rows, cut_row, 0), (head.sides[1], rows, cut_row, cut_row)])
@@ -1050,29 +1060,36 @@
 
     h1, own = order.run(kv_call, place, x, ln[0], ln[1], [key_w, value_w])
     if aligned:
-        low.last()
+        low.near()
     other = exchange(order.after(own))
     q = order.run(q_call, place, h1, [query_w])
+    if aligned:
+        low.last()
+        high.far()
     outs, lses = [], []
-    plan = [(0, 1), (1, 1), (2, 2)] if groups == 4 else [(g, 1) for g in range(groups)]
+    plan = [(0, 2), (2, 1), (3, 1)] if groups == 4 else [(g, 1) for g in range(groups)]
     for i, (start, count) in enumerate(plan):
         if aligned and i == 1:
-            high.near(*[side.other for side in low.sides])
+            high.near()
+            low.finish()
         if aligned and i == 2:
-            high.last()
-            low.finish()
+            high.last(*[side.rest for side in low.sides])
+            low.cross()
         out, lse = order.run(
-            attend_call, tab, q, own, other, seg_q, seg_own_col, seg_other_col, ATT_Q, ATT_K, start, count
+            attend_call, tab, q, own, other, seg_q, seg_col, ATT_Q, ATT_K, start, count
         )
         outs.append(out)
         lses.append(lse)
     if aligned:
+        low.ready()
+        high.cross()
         out_w = Spread(
             rows, [(low.sides[0], half_up, cut_row, 0), (low.sides[1], half_down, cut_row, cut_row)]
         )
     mid, h2 = order.run(mid_call, place, x, outs, [out_w], ln[2], ln[3])
     if aligned:
         high.finish()
+        high.ready()
 
     up_rows = tiles * rows
     if aligned:
@@ -1104,7 +1121,7 @@
         grads = [*halves(dwu, 2), *halves(dwd, 2)]
     keep_up, send_up, keep_down, send_down = grads
     got_up, got_down = exchange(send_up), exchange(send_down)
-    big = Scatter(cube, [cube.terms([keep_up, got_up])], [cube.terms([keep_down, got_down])])
+    big = Scatter(cube, [cube.terms([keep_up, got_up])], [cube.terms([keep_down, got_down])], False)
 
     grad_mid, grad_att, keep_out, send_out, dln2 = order.run(
         mid_back_call, place, gmid, mid, cot, outs, [out_w], ln[2], dp
@@ -1116,7 +1133,7 @@
     def attend_back(g):
         which = [i for i, (start, _) in enumerate(plan) if start <= g][-1]
         return order.run(
-            attend_back_call, tab, q, grad_att, outs[which], own, other, seg_q, seg_own_col, seg_other_col,
+            attend_back_call, tab, q, grad_att, outs[which], own, other, seg_q, seg_col,
             lses[which], ATT_Q, ATT_K, g, 1, g - plan[which][0],
         )
 
@@ -1140,28 +1157,31 @@
         cube,
         [cube.terms(terms_0), cube.terms([keep_out, got_out], 0, 2)],
         [cube.terms(terms_1), cube.terms([keep_out, got_out], 2, 2)],
+        False,
     )
     tail_one.advance()
     got_2 = exchange(order.after(sent_2))
     dq_3, dkv_3, sent_3 = attend_back(3)
-    up_share, down_share = big.finish()
+    big.advance()
     tail_one.advance()
     got_3 = exchange(order.after(sent_3))
     keep_2, send_2 = finish_group(dq_2, dkv_2, got_2)
     keep_3, send_3 = finish_group(dq_3, dkv_3, got_3)
     tail_one.advance()
     terms_2, terms_3 = [keep_2, exchange(order.after(send_2))], [keep_3, exchange(order.after(send_3))]
-    tail_two = Scatter(cube, [cube.terms(terms_2)], [cube.terms(terms_3)])
+    tail_two = Scatter(cube, [cube.terms(terms_2)], [cube.terms(terms_3)], True)
     tail_two.advance()
     token_grad, dln1 = order.run(
         head_back_call, place, dqs, dkvs, x, grad_mid, [query_w, key_w, value_w], ln[0]
     )
     tail_two.advance()
-    one_a, out_a, one_b, out_b = tail_one.finish()
+    tail_one.advance()
+    up_share, down_share = big.finish()
     dln = jnp.concatenate([dln1, order.after(dln2)], axis=0).reshape(4, devices, rows).transpose(1, 0, 2)
     dln = lax.all_to_all(dln.reshape(devices, 4 * rows), BOTH, 0, 0, tiled=True)
     dln = jnp.sum(dln.reshape(devices, 4, rows), axis=0)
     tail_two.advance()
+    one_a, out_a, one_b, out_b = tail_one.finish()
     two_a, two_b = tail_two.finish()
 
     up_share = up_share.transpose(1, 0, 2).reshape(rows, hidden)

time: 558 us -> 520 us (0.932)
  waiting for transfers between devices: 111 us -> 71.5 us
    ppermute x42 -> x40, waiting for transfers between devices: 92.3 us -> 58.4 us  [send(): return lax.ppermute(array, 'dp', [(i, i ^ flip) for i in range(self.dp)])]
    ppermute x42 -> x40, starting transfers between devices: 65 us -> 56 us  [send(): return lax.ppermute(array, 'dp', [(i, i ^ flip) for i in range(self.dp)])]
    pallas_call x12 -> x14, Pallas kernels: 30.6 us -> 38.2 us  [run(): out = call(self.after(first), *rest)]
    ppermute x24, starting transfers between devices: 4.5 us -> 11.6 us  [exchange(): return lax.ppermute(value, 'seq', swap)]
    unnamed x183 -> x185, local copies, waits for them, and re-layouts: 36 us -> 33.4 us
  transfers between devices with their start and end apart: 68 -> 66, of which waited for: 22 -> 17; matrix products, arithmetic and copies ran while one was open for 3% -> 4% of each run, Pallas kernels for 39% -> 42%
where the time goes in v5:
time: 520 us; the launch traced here: 510 us
  Pallas kernels  303 us (58%)
  starting transfers between devices  79.3 us (15%)
  waiting for transfers between devices  71.5 us (14%)
  local copies, waits for them, and re-layouts  50.3 us (10%)
    pallas_call x4, Pallas kernels, attend_back_call(): pl.pallas_call(partial(attend_back_kernel, bq, bk), grid_spec=spec, out_s...  73.7 us
    pallas_call x1, Pallas kernels, ffn_call(): pl.pallas_call(partial(ffn_kernel, ups, downs, aligned), grid_spec=spec,...  69.4 us
    ppermute x40, waiting for transfers between devices, send(): return lax.ppermute(array, 'dp', [(i, i ^ flip) for i in range(self.dp)])  58.4 us
    ppermute x40, starting transfers between devices, send(): return lax.ppermute(array, 'dp', [(i, i ^ flip) for i in range(self.dp)])  56 us
    pallas_call x3, Pallas kernels, attend_call(): pl.pallas_call(partial(attend_kernel, bq, bk), grid_spec=spec, out_shape=...  49.4 us
    pallas_call x14, Pallas kernels, run(): out = call(self.after(first), *rest)  38.2 us
    unnamed x185, local copies, waits for them, and re-layouts  33.4 us
    pallas_call x1, Pallas kernels, head_back_call(): pl.pallas_call(partial(head_back_kernel, weights, len(dqs)), grid_spec=sp...  16.1 us
  transfers between devices with their start and end apart: 66, of which 17 were waited for; matrix products, arithmetic and copies ran while one was open for 4% of the time, Pallas kernels for 42%

profile of v5, /device:TPU:0, one launch (start us, length us, event | category | flops | bytes accessed | tf_op | source)
XLA Modules:
  0.0 510.3 jit_solution(5274611169368659267)
XLA Ops:
  2.4 5.1 %collective-permute-start.2 = (bf16[1,96,1024]{2,1,0:T(8,128)(2,1)S(1)}, bf16[1,96,1024]{2,1,0:T(8,128)(2,1)S(1)}, u32[]{:S(2)}, u32[]{:S(2)}) collective-permute-start(bf16[1,96,1024]{2,1,0:T(8,128)(2,1)S(1)} %maximum_bitcast_fusion.2.refs_0_), channel_id=1, source_target_pairs={{0,24},{2,26},{4,28},{6,30},{8,16},{10,18},{12,20},{14,22},{16,8},... | collective-permute-start | bytes 589832 | tf_op jit(solution)/shard_map/ppermute | solution.py:748
  9.5 6.0 %all-to-all-start = ((f32[32,1,128]{2,1,0:T(1,128)}), f32[32,1,128]{2,1,0:T(1,128)S(1)}, u32[]{:S(2)}, u32[]{:S(2)}) async-start(f32[32,1,128]{2,1,0:T(1,128)} %broadcast_in_dim.30), calls=%async_computation | async-start | bytes 32768 | tf_op jit(solution)/shard_map/all_to_all | solution.py:1023
  17.2 9.2 %all-to-all-done = f32[32,1,128]{2,1,0:T(1,128)S(1)} async-done(((f32[32,1,128]{2,1,0:T(1,128)}), f32[32,1,128]{2,1,0:T(1,128)S(1)}, u32[]{:S(2)}, u32[]{:S(2)}) %all-to-all-start) | async-done | bytes 16416 | tf_op jit(solution)/shard_map/all_to_all | solution.py:1023
  29.4 7.9 %collective-permute-done.4.refs_3_ = bf16[4,48,1024]{2,1,0:T(8,128)(2,1)S(1)} collective-permute-done((bf16[4,48,1024]{2,1,0:T(8,128)(2,1)S(1)}, bf16[4,48,1024]{2,1,0:T(8,128)(2,1)S(1)}, u32[]{:S(2)}, u32[]{:S(2)}) %collective-permute-start.4) | collective-permute-done | bytes 393248 | tf_op jit(solution)/shard_map/ppermute | solution.py:748
  41.1 15.9 %collective-permute-done.6.refs_5_.refs_16_.refs_24_ = bf16[8,48,1024]{2,1,0:T(8,128)(2,1)} collective-permute-done((bf16[8,48,1024]{2,1,0:T(8,128)(2,1)}, bf16[8,48,1024]{2,1,0:T(8,128)(2,1)}, u32[]{:S(2)}, u32[]{:S(2)}) %collective-permute-start.6) | collective-permute-done | bytes 786464 | tf_op jit(solution)/shard_map/ppermute | solution.py:748
  58.0 2.5 collective-permute-start.13
  70.0 10.8 %kv_proj.1 = (bf16[1024,1024]{1,0:T(8,128)(2,1)S(1)}, bf16[2,1024,1024]{2,1,0:T(8,128)(2,1)}) custom-call(s32[2]{0:T(128)S(1)} %copy-done.72, bf16[1024,1024]{1,0:T(8,128)(2,1)S(1)} %bitcast.138, f32[1,1024]{1,0:T(1,128)S(1)} %squeeze.35.gain_ref.refs_10_, f32[1,1024]{1,0:T(1,128)S(1)} %squeeze.36.bias_ref, ...), custom_call_target="tpu_custom_call" | custom-call | flops 42949 | bytes 125 | tf_op jit(solution)/shard_map/kv_proj/pallas_call | solution.py:169
  80.8 7.7 %collective-permute-done.12.refs_2_ = bf16[1,160,1024]{2,1,0:T(8,128)(2,1)} collective-permute-done((bf16[1,160,1024]{2,1,0:T(8,128)(2,1)S(1)}, bf16[1,160,1024]{2,1,0:T(8,128)(2,1)}, u32[]{:S(2)}, u32[]{:S(2)}) %collective-permute-start.12) | collective-permute-done | bytes 327712 | tf_op jit(solution)/shard_map/ppermute | solution.py:748
  92.5 5.4 %q_proj.1.q_ref = bf16[1024,1024]{1,0:T(8,128)(2,1)S(1)} custom-call(s32[2]{0:T(128)S(1)} %copy-done.72, bf16[1024,1024]{1,0:T(8,128)(2,1)S(1)} %get-tuple-element.168.h_ref, bf16[8,48,1024]{2,1,0:T(8,128)(2,1)S(1)} %get-tuple-element.164.refs_0_.refs_11_.refs_19_, bf16[8,48,1024]{2,1,0:T(8,128)(2,1)} %collective-permute-done.5.refs_1_.refs_12_.refs_20_, ...), custom_call_target="tpu_custom_call" | custom-call | flops 21474 | bytes 62 | tf_op jit(solution)/shard_map/q_proj/pallas_call | solution.py:197
  99.2 7.7 %collective-permute-done.15.refs_3_ = bf16[4,80,1024]{2,1,0:T(8,128)(2,1)S(1)} collective-permute-done((bf16[4,80,1024]{2,1,0:T(8,128)(2,1)S(1)}, bf16[4,80,1024]{2,1,0:T(8,128)(2,1)S(1)}, u32[]{:S(2)}, u32[]{:S(2)}) %collective-permute-start.15) | collective-permute-done | bytes 655392 | tf_op jit(solution)/shard_map/ppermute | solution.py:748
  112.1 2.6 collective-permute-start.19
  119.4 22.8 %attend.3 = (bf16[1024,512]{1,0:T(8,128)(2,1)}, f32[2,4,1,1024]{3,2,1,0:T(1,128)}) custom-call(s32[9]{0:T(128)} %pad_add_fusion.2.tab, bf16[1024,1024]{1,0:T(8,128)(2,1)} %copy-done, bf16[2,1024,1024]{2,1,0:T(8,128)(2,1)} %get-tuple-element.178.own_ref, bf16[2,1024,1024]{2,1,0:T(8,128)(2,1)} %collective-permute-done.16.other_ref, s32[4,1,256]{2,1,0:T(1,128)} %bitcast.163, ...), custom_call_target="tpu_custom_call" | custom-call | flops 160000 | bytes 62 | tf_op jit(solution)/shard_map/attend/pallas_call | solution.py:296
  142.9 3.5 collective-permute-start.21
  146.4 13.1 %attend.4 = (bf16[1024,256]{1,0:T(8,128)(2,1)}, f32[1,4,1,1024]{3,2,1,0:T(1,128)}) custom-call(s32[9]{0:T(128)} %pad_add_fusion.2.tab, bf16[1024,1024]{1,0:T(8,128)(2,1)} %copy-done, bf16[2,1024,1024]{2,1,0:T(8,128)(2,1)} %get-tuple-element.178.own_ref, bf16[2,1024,1024]{2,1,0:T(8,128)(2,1)} %collective-permute-done.16.other_ref, s32[4,1,256]{2,1,0:T(1,128)} %bitcast.164, ...), custom_call_target="tpu_custom_call" | custom-call | flops 80000 | bytes 31 | tf_op jit(solution)/shard_map/attend/pallas_call | solution.py:296
  166.3 13.5 %attend.5 = (bf16[1024,256]{1,0:T(8,128)(2,1)}, f32[1,4,1,1024]{3,2,1,0:T(1,128)}) custom-call(s32[9]{0:T(128)} %pad_add_fusion.2.tab, bf16[1024,1024]{1,0:T(8,128)(2,1)} %copy-done, bf16[2,1024,1024]{2,1,0:T(8,128)(2,1)} %get-tuple-element.178.own_ref, bf16[2,1024,1024]{2,1,0:T(8,128)(2,1)} %collective-permute-done.16.other_ref, s32[4,1,256]{2,1,0:T(1,128)} %bitcast.165, ...), custom_call_target="tpu_custom_call" | custom-call | flops 80000 | bytes 31 | tf_op jit(solution)/shard_map/attend/pallas_call | solution.py:296
  183.2 6.9 %out_proj.1 = (f32[1024,1024]{1,0:T(8,128)S(1)}, bf16[1024,1024]{1,0:T(8,128)(2,1)S(1)}) custom-call(s32[2]{0:T(128)S(1)} %copy-done.73, bf16[1024,1024]{1,0:T(8,128)(2,1)S(1)} %bitcast.139, f32[1,1024]{1,0:T(1,128)S(1)} %squeeze.37.gain_ref, f32[1,1024]{1,0:T(1,128)S(1)} %squeeze.38.bias_ref, bf16[1024,512]{1,0:T(8,128)(2,1)S(1)} %copy-done.39, ...), custom_call_target="tpu_custom_call" | custom-call | flops 21474 | bytes 125 | tf_op jit(solution)/shard_map/out_proj/pallas_call | solution.py:421
  190.2 2.0 copy-done.38
  194.1 2.4 collective-permute-done.30.refs_11_.refs_15_
  199.0 69.4 %ffn.1 = (bf16[1024,1024]{1,0:T(8,128)(2,1)}, f32[1024,1024]{1,0:T(8,128)}, bf16[4,16,32,1024]{3,2,1,0:T(8,128)(2,1)}, bf16[4,16,32,1024]{3,2,1,0:T(8,128)(2,1)}...) custom-call(s32[2]{0:T(128)} %pad_add_fusion.1.place, bf16[1024,1024]{1,0:T(8,128)(2,1)} %copy-done.51, ...), custom_call_target="tpu_custom_call" | custom-call | flops 515396 | bytes 482 | tf_op jit(solution)/shard_map/ffn/pallas_call | solution.py:616
  269.0 15.7 %out_proj_back.1 = (f32[1024,1024]{1,0:T(8,128)}, bf16[1024,1024]{1,0:T(8,128)(2,1)}, bf16[4,16,32,256]{3,2,1,0:T(8,128)(2,1)S(1)}, bf16[4,16,32,256]{3,2,1,0:T(8,128)(2,1)}, f32[2,1024]{1,0:T(2,128)S(1)}) custom-call(s32[2]{0:T(128)S(1)} %copy-done.74, f32[1024,1024]{1,0:T(8,128)} %get-tuple-element.205.gh_ref, f32[1024,1024]{1,0:T(8,128)} %copy-done.38, ...), custom_call_target="tpu_custom_call" | custom-call | flops 42949 | bytes 230 | tf_op jit(solution)/shard_map/out_proj_back/pallas_call | solution.py:493
  284.7 2.0 copy-done.77
  286.7 5.5 %add_terms.14 = (bf16[4,2,2,2,32,1024]{5,4,3,2,1,0:T(8,128)(2,1)}, bf16[4,2,2,2,32,1024]{5,4,3,2,1,0:T(8,128)(2,1)}) custom-call(s32[4]{0:T(128)S(1)} %shift-right-arithmetic_and_fusion.mine, bf16[4,2,2,2,2,32,1024]{6,5,4,3,2,1,0:T(8,128)(2,1)S(1)} %bitcast.98, bf16[4,2,2,2,2,32,1024]{6,5,4,3,2,1,0:T(8,128)(2,1)} %bitcast.19.refs_1_, ...), custom_call_target="tpu_custom_call" | custom-call | flops 83 | bytes 167 | tf_op jit(solution)/shard_map/add_terms/pallas_call | solution.py:912
  294.8 18.4 %attend_back.4 = (bf16[1024,256]{1,0:T(8,128)(2,1)}, bf16[2,1024,256]{2,1,0:T(8,128)(2,1)}, bf16[2,1024,256]{2,1,0:T(8,128)(2,1)}) custom-call(s32[9]{0:T(128)} %pad_add_fusion.2.tab, bf16[1024,1024]{1,0:T(8,128)(2,1)} %copy-done, bf16[1024,1024]{1,0:T(8,128)(2,1)} %get-tuple-element.214.go_ref, bf16[1024,512]{1,0:T(8,128)(2,1)} %get-tuple-element.179.refs_0_.o_ref, ...), custom_call_target="tpu_custom_call" | custom-call | flops 120000 | bytes 62 | tf_op jit(solution)/shard_map/attend_back/pallas_call | solution.py:383
  313.2 18.4 %attend_back.5 = (bf16[1024,256]{1,0:T(8,128)(2,1)}, bf16[2,1024,256]{2,1,0:T(8,128)(2,1)}, bf16[2,1024,256]{2,1,0:T(8,128)(2,1)}) custom-call(s32[9]{0:T(128)} %pad_add_fusion.2.tab, bf16[1024,1024]{1,0:T(8,128)(2,1)} %copy-done, bf16[1024,1024]{1,0:T(8,128)(2,1)} %get-tuple-element.214.go_ref, bf16[1024,512]{1,0:T(8,128)(2,1)} %get-tuple-element.179.refs_0_.o_ref, ...), custom_call_target="tpu_custom_call" | custom-call | flops 120000 | bytes 62 | tf_op jit(solution)/shard_map/attend_back/pallas_call | solution.py:383
  331.6 3.3 collective-permute-start.38
  334.9 5.5 %collective-permute-done.37.refs_5_.refs_6_.refs_7_.refs_8_ = bf16[4,2,2,2,32,1024]{5,4,3,2,1,0:T(8,128)(2,1)S(1)} collective-permute-done((bf16[4,2,2,2,32,1024]{5,4,3,2,1,0:T(8,128)(2,1)}, bf16[4,2,2,2,32,1024]{5,4,3,2,1,0:T(8,128)(2,1)S(1)}, u32[]{:S(2)}, u32[]{:S(2)}) %collective-permute-start.37) | collective-permute-done | bytes 2097184 | tf_op jit(solution)/shard_map/ppermute | solution.py:748
  341.0 4.2 add_terms.15
  348.9 3.3 qkv_grad.4
  353.3 3.3 qkv_grad.5
  359.0 18.6 %attend_back.6 = (bf16[1024,256]{1,0:T(8,128)(2,1)}, bf16[2,1024,256]{2,1,0:T(8,128)(2,1)}, bf16[2,1024,256]{2,1,0:T(8,128)(2,1)}) custom-call(s32[9]{0:T(128)} %pad_add_fusion.2.tab, bf16[1024,1024]{1,0:T(8,128)(2,1)} %copy-done, bf16[1024,1024]{1,0:T(8,128)(2,1)} %get-tuple-element.214.go_ref, bf16[1024,256]{1,0:T(8,128)(2,1)} %get-tuple-element.183.refs_1_.o_ref, ...), custom_call_target="tpu_custom_call" | custom-call | flops 120000 | bytes 62 | tf_op jit(solution)/shard_map/attend_back/pallas_call | solution.py:383
  379.2 3.6 add_terms.16
  382.8 2.9 add_terms.17
  387.7 18.4 %attend_back.7 = (bf16[1024,256]{1,0:T(8,128)(2,1)}, bf16[2,1024,256]{2,1,0:T(8,128)(2,1)}, bf16[2,1024,256]{2,1,0:T(8,128)(2,1)}) custom-call(s32[9]{0:T(128)} %pad_add_fusion.2.tab, bf16[1024,1024]{1,0:T(8,128)(2,1)} %copy-done, bf16[1024,1024]{1,0:T(8,128)(2,1)} %get-tuple-element.214.go_ref, bf16[1024,256]{1,0:T(8,128)(2,1)} %get-tuple-element.191.refs_2_.o_ref, ...), custom_call_target="tpu_custom_call" | custom-call | flops 120000 | bytes 62 | tf_op jit(solution)/shard_map/attend_back/pallas_call | solution.py:383
  406.0 2.1 collective-permute-start.48
  409.7 3.2 add_terms.18
  413.0 2.6 add_terms.19
  417.7 2.4 qkv_grad.6
  421.1 2.4 qkv_grad.7
  423.6 2.6 collective-permute-done.51.refs_11_.refs_15_.refs_13_.refs_18_.refs_21_
  426.3 2.6 add_terms.20
  429.6 6.6 %collective-permute-start.57 = (bf16[8,32,1024]{2,1,0:T(8,128)(2,1)}, bf16[8,32,1024]{2,1,0:T(8,128)(2,1)}, u32[]{:S(2)}, u32[]{:S(2)}) collective-permute-start(bf16[8,32,1024]{2,1,0:T(8,128)(2,1)} %add_terms.18), channel_id=1, source_target_pairs={{0,16},{2,18},{4,20},{6,22},{8,24},{10,26},{12,28},{14,30},{16,0},... | collective-permute-start | bytes 1572872 | tf_op jit(solution)/shard_map/ppermute | solution.py:748
  441.1 16.1 %qkv_back.1 = (bf16[1024,1024]{1,0:T(8,128)(2,1)}, f32[2,1024]{1,0:T(2,128)S(1)}) custom-call(s32[2]{0:T(128)S(1)} %copy-done.74, bf16[1024,256]{1,0:T(8,128)(2,1)S(1)} %copy-done.53, bf16[1024,256]{1,0:T(8,128)(2,1)S(1)} %copy-done.55, bf16[1024,256]{1,0:T(8,128)(2,1)S(1)} %copy-done.57, bf16[1024,256]{1,0:T(8,128)(2,1)S(1)} %copy-done.59, ...), custom_call_target="tpu_custom_call" | custom-call | flops 64424 | bytes 209 | tf_op jit(solution)/shard_map/qkv_back/pallas_call | solution.py:702
  467.3 3.2 add_terms.24
  472.2 5.6 %all-to-all-start.1 = ((f32[32,1,128]{2,1,0:T(1,128)}), f32[32,1,128]{2,1,0:T(1,128)S(1)}, u32[]{:S(2)}, u32[]{:S(2)}) async-start(f32[32,1,128]{2,1,0:T(1,128)} %bitcast.34), calls=%async_computation.1 | async-start | bytes 32768 | tf_op jit(solution)/shard_map/all_to_all | solution.py:1181
  477.9 2.7 collective-permute-start.60
  486.1 2.7 collective-permute-done.59.refs_7_.refs_15_.refs_23_.refs_10_
  499.3 2.4 collective-permute-start.63
  502.4 5.1 %collective-permute-done.62.refs_5_.refs_12_ = bf16[6,32,256]{2,1,0:T(8,128)(2,1)S(1)} collective-permute-done((bf16[6,32,256]{2,1,0:T(8,128)(2,1)S(1)}, bf16[6,32,256]{2,1,0:T(8,128)(2,1)S(1)}, u32[]{:S(2)}, u32[]{:S(2)}) %collective-permute-start.62) | collective-permute-done | bytes 98336 | tf_op jit(solution)/shard_map/ppermute | solution.py:748
  (349 shorter events, 108.4 us)
Async XLA Ops:
  2.4 24.0 %collective-permute-start.2 = (bf16[1,96,1024]{2,1,0:T(8,128)(2,1)S(1)}, bf16[1,96,1024]{2,1,0:T(8,128)(2,1)S(1)}, u32[]{:S(2)}, u32[]{:S(2)}) collective-permute-start(bf16[1,96,1024]{2,1,0:T(8,128)(2,1)S(1)} %maximum_bitcast_fusion.2.refs_0_), channel_id=1, source_target_pairs={{0,24},{2,26},{4,28},{6,30},{8,16},{10,18},{12,20},{14,22},{16,8},... | collective-permute-start | bytes 589832 | tf_op jit(solution)/shard_map/ppermute | solution.py:748
  7.5 18.9 %collective-permute-start.1 = (bf16[1,96,1024]{2,1,0:T(8,128)(2,1)S(1)}, bf16[1,96,1024]{2,1,0:T(8,128)(2,1)S(1)}, u32[]{:S(2)}, u32[]{:S(2)}) collective-permute-start(bf16[1,96,1024]{2,1,0:T(8,128)(2,1)S(1)} %maximum_bitcast_fusion.2.refs_0_), channel_id=1, source_target_pairs={{0,16},{2,18},{4,20},{6,22},{8,24},{10,26},{12,28},{14,30},{16,0},... | collective-permute-start | bytes 589832 | tf_op jit(solution)/shard_map/ppermute | solution.py:748
  7.5 18.9 %collective-permute-start = (bf16[1,96,1024]{2,1,0:T(8,128)(2,1)S(1)}, bf16[1,96,1024]{2,1,0:T(8,128)(2,1)S(1)}, u32[]{:S(2)}, u32[]{:S(2)}) collective-permute-start(bf16[1,96,1024]{2,1,0:T(8,128)(2,1)S(1)} %maximum_bitcast_fusion.2.refs_0_), channel_id=1, source_target_pairs={{0,8},{2,10},{4,12},{6,14},{8,0},{10,2},{12,4},{14,6},{16,24},{18,... | collective-permute-start | bytes 589832 | tf_op jit(solution)/shard_map/ppermute | solution.py:748
  9.5 16.8 %all-to-all-start = ((f32[32,1,128]{2,1,0:T(1,128)}), f32[32,1,128]{2,1,0:T(1,128)S(1)}, u32[]{:S(2)}, u32[]{:S(2)}) async-start(f32[32,1,128]{2,1,0:T(1,128)} %broadcast_in_dim.30), calls=%async_computation | async-start | bytes 32768 | tf_op jit(solution)/shard_map/all_to_all | solution.py:1023
  38.6 18.4 %collective-permute-start.6 = (bf16[8,48,1024]{2,1,0:T(8,128)(2,1)}, bf16[8,48,1024]{2,1,0:T(8,128)(2,1)}, u32[]{:S(2)}, u32[]{:S(2)}) collective-permute-start(bf16[8,48,1024]{2,1,0:T(8,128)(2,1)} %get-tuple-element.166.refs_4_.refs_15_.refs_23_), channel_id=1, source_target_pairs={{0,4},{2,6},{4,0},{6,2},{8,12},{10,14},{12,8},{14,10},{16,20},{18,... | collective-permute-start | bytes 2359304 | tf_op jit(solution)/shard_map/ppermute | solution.py:748
  39.4 18.1 %collective-permute-start.5 = (bf16[8,48,1024]{2,1,0:T(8,128)(2,1)S(1)}, bf16[8,48,1024]{2,1,0:T(8,128)(2,1)}, u32[]{:S(2)}, u32[]{:S(2)}) collective-permute-start(bf16[8,48,1024]{2,1,0:T(8,128)(2,1)S(1)} %get-tuple-element.164.refs_0_.refs_11_.refs_19_), channel_id=1, source_target_pairs={{0,2},{2,0},{4,6},{6,4},{8,10},{10,8},{12,14},{14,12},{16,18},{18,... | collective-permute-start | bytes 2359304 | tf_op jit(solution)/shard_map/ppermute | solution.py:748
  40.6 19.9 %collective-permute-start.7 = (bf16[8,48,1024]{2,1,0:T(8,128)(2,1)S(1)}, bf16[8,48,1024]{2,1,0:T(8,128)(2,1)}, u32[]{:S(2)}, u32[]{:S(2)}) collective-permute-start(bf16[8,48,1024]{2,1,0:T(8,128)(2,1)S(1)} %get-tuple-element.164.refs_0_.refs_11_.refs_19_), channel_id=1, source_target_pairs={{0,1},{1,0},{2,3},{3,2},{4,5},{5,4},{6,7},{7,6},{8,9},{9,8},{10,11... | collective-permute-start | bytes 2359304 | tf_op jit(solution)/shard_map/ppermute | solution.py:1014
  40.6 19.9 %collective-permute-start.9 = (bf16[8,48,1024]{2,1,0:T(8,128)(2,1)}, bf16[8,48,1024]{2,1,0:T(8,128)(2,1)}, u32[]{:S(2)}, u32[]{:S(2)}) collective-permute-start(bf16[8,48,1024]{2,1,0:T(8,128)(2,1)} %get-tuple-element.166.refs_4_.refs_15_.refs_23_), channel_id=1, source_target_pairs={{0,1},{1,0},{2,3},{3,2},{4,5},{5,4},{6,7},{7,6},{8,9},{9,8},{10,11... | collective-permute-start | bytes 2359304 | tf_op jit(solution)/shard_map/ppermute | solution.py:1014
  58.0 22.8 %collective-permute-start.13 = (bf16[1,160,1024]{2,1,0:T(8,128)(2,1)S(1)}, bf16[1,160,1024]{2,1,0:T(8,128)(2,1)S(1)}, u32[]{:S(2)}, u32[]{:S(2)}) collective-permute-start(bf16[1,160,1024]{2,1,0:T(8,128)(2,1)S(1)} %maximum_bitcast_fusion.refs_0_), channel_id=1, source_target_pairs={{0,24},{2,26},{4,28},{6,30},{8,16},{10,18},{12,20},{14,22},{16,8},... | collective-permute-start | bytes 983048 | tf_op jit(solution)/shard_map/ppermute | solution.py:748
  60.5 28.0 %collective-permute-start.12 = (bf16[1,160,1024]{2,1,0:T(8,128)(2,1)S(1)}, bf16[1,160,1024]{2,1,0:T(8,128)(2,1)}, u32[]{:S(2)}, u32[]{:S(2)}) collective-permute-start(bf16[1,160,1024]{2,1,0:T(8,128)(2,1)S(1)} %maximum_bitcast_fusion.refs_0_), channel_id=1, source_target_pairs={{0,16},{2,18},{4,20},{6,22},{8,24},{10,26},{12,28},{14,30},{16,0},... | collective-permute-start | bytes 983048 | tf_op jit(solution)/shard_map/ppermute | solution.py:748
  60.5 28.0 %collective-permute-start.11 = (bf16[1,160,1024]{2,1,0:T(8,128)(2,1)S(1)}, bf16[1,160,1024]{2,1,0:T(8,128)(2,1)}, u32[]{:S(2)}, u32[]{:S(2)}) collective-permute-start(bf16[1,160,1024]{2,1,0:T(8,128)(2,1)S(1)} %maximum_bitcast_fusion.refs_0_), channel_id=1, source_target_pairs={{0,8},{2,10},{4,12},{6,14},{8,0},{10,2},{12,4},{14,6},{16,24},{18,... | collective-permute-start | bytes 983048 | tf_op jit(solution)/shard_map/ppermute | solution.py:748
  89.6 25.1 %collective-permute-start.16 = (bf16[2,1024,1024]{2,1,0:T(8,128)(2,1)}, bf16[2,1024,1024]{2,1,0:T(8,128)(2,1)}, u32[]{:S(2)}, u32[]{:S(2)}) collective-permute-start(bf16[2,1024,1024]{2,1,0:T(8,128)(2,1)} %get-tuple-element.178.own_ref), channel_id=1, source_target_pairs={{0,1},{1,0},{2,3},{3,2},{4,5},{5,4},{6,7},{7,6},{8,9},{9,8},{10,11... | collective-permute-start | bytes 12582920 | tf_op jit(solution)/shard_map/ppermute | solution.py:1014
  89.7 17.1 %collective-permute-start.15 = (bf16[4,80,1024]{2,1,0:T(8,128)(2,1)S(1)}, bf16[4,80,1024]{2,1,0:T(8,128)(2,1)S(1)}, u32[]{:S(2)}, u32[]{:S(2)}) collective-permute-start(bf16[4,80,1024]{2,1,0:T(8,128)(2,1)S(1)} %get-tuple-element.173.refs_2_), channel_id=1, source_target_pairs={{0,2},{2,0},{4,6},{6,4},{8,10},{10,8},{12,14},{14,12},{16,18},{18,... | collective-permute-start | bytes 1966088 | tf_op jit(solution)/shard_map/ppermute | solution.py:748
  91.2 16.8 %collective-permute-start.14 = (bf16[4,80,1024]{2,1,0:T(8,128)(2,1)S(1)}, bf16[4,80,1024]{2,1,0:T(8,128)(2,1)S(1)}, u32[]{:S(2)}, u32[]{:S(2)}) collective-permute-start(bf16[4,80,1024]{2,1,0:T(8,128)(2,1)S(1)} %get-tuple-element.172.refs_0_), channel_id=1, source_target_pairs={{0,4},{2,6},{4,0},{6,2},{8,12},{10,14},{12,8},{14,10},{16,20},{18,... | collective-permute-start | bytes 1966088 | tf_op jit(solution)/shard_map/ppermute | solution.py:748
  109.6 32.6 %collective-permute-start.24 = (bf16[8,80,1024]{2,1,0:T(8,128)(2,1)}, bf16[8,80,1024]{2,1,0:T(8,128)(2,1)S(1)}, u32[]{:S(2)}, u32[]{:S(2)}) collective-permute-start(bf16[8,80,1024]{2,1,0:T(8,128)(2,1)} %get-tuple-element.194.refs_7_.refs_16_), channel_id=1, source_target_pairs={{0,4},{2,6},{4,0},{6,2},{8,12},{10,14},{12,8},{14,10},{16,20},{18,... | collective-permute-start | bytes 3932168 | tf_op jit(solution)/shard_map/ppermute | solution.py:748
  111.0 31.3 %collective-permute-start.22 = (bf16[8,80,1024]{2,1,0:T(8,128)(2,1)}, bf16[8,80,1024]{2,1,0:T(8,128)(2,1)}, u32[]{:S(2)}, u32[]{:S(2)}) collective-permute-start(bf16[8,80,1024]{2,1,0:T(8,128)(2,1)} %get-tuple-element.193.refs_3_.refs_0_.refs_4_), channel_id=1, source_target_pairs={{0,2},{2,0},{4,6},{6,4},{8,10},{10,8},{12,14},{14,12},{16,18},{18,... | collective-permute-start | bytes 3932168 | tf_op jit(solution)/shard_map/ppermute | solution.py:748
  112.1 30.0 %collective-permute-start.19 = (bf16[1,128,1024]{2,1,0:T(8,128)(2,1)S(1)}, bf16[1,128,1024]{2,1,0:T(8,128)(2,1)S(1)}, u32[]{:S(2)}, u32[]{:S(2)}) collective-permute-start(bf16[1,128,1024]{2,1,0:T(8,128)(2,1)S(1)} %maximum_bitcast_fusion.1.refs_0_), channel_id=1, source_target_pairs={{0,24},{2,26},{4,28},{6,30},{8,16},{10,18},{12,20},{14,22},{16,8},... | collective-permute-start | bytes 786440 | tf_op jit(solution)/shard_map/ppermute | solution.py:748
  114.7 27.4 %collective-permute-start.18 = (bf16[1,128,1024]{2,1,0:T(8,128)(2,1)S(1)}, bf16[1,128,1024]{2,1,0:T(8,128)(2,1)S(1)}, u32[]{:S(2)}, u32[]{:S(2)}) collective-permute-start(bf16[1,128,1024]{2,1,0:T(8,128)(2,1)S(1)} %maximum_bitcast_fusion.1.refs_0_), channel_id=1, source_target_pairs={{0,16},{2,18},{4,20},{6,22},{8,24},{10,26},{12,28},{14,30},{16,0},... | collective-permute-start | bytes 786440 | tf_op jit(solution)/shard_map/ppermute | solution.py:748
  114.7 27.4 %collective-permute-start.17 = (bf16[1,128,1024]{2,1,0:T(8,128)(2,1)S(1)}, bf16[1,128,1024]{2,1,0:T(8,128)(2,1)S(1)}, u32[]{:S(2)}, u32[]{:S(2)}) collective-permute-start(bf16[1,128,1024]{2,1,0:T(8,128)(2,1)S(1)} %maximum_bitcast_fusion.1.refs_0_), channel_id=1, source_target_pairs={{0,8},{2,10},{4,12},{6,14},{8,0},{10,2},{12,4},{14,6},{16,24},{18,... | collective-permute-start | bytes 786440 | tf_op jit(solution)/shard_map/ppermute | solution.py:748
  142.3 18.5 %collective-permute-start.23 = (bf16[8,80,1024]{2,1,0:T(8,128)(2,1)}, bf16[8,80,1024]{2,1,0:T(8,128)(2,1)S(1)}, u32[]{:S(2)}, u32[]{:S(2)}) collective-permute-start(bf16[8,80,1024]{2,1,0:T(8,128)(2,1)} %collective-permute-done.22.refs_4_.refs_1_.refs_5_), channel_id=1, source_target_pairs={{0,1},{1,0},{2,3},{3,2},{4,5},{5,4},{6,7},{7,6},{8,9},{9,8},{10,11... | collective-permute-start | bytes 3932168 | tf_op jit(solution)/shard_map/ppermute | solution.py:1014
  142.6 18.2 %collective-permute-start.25 = (bf16[8,80,1024]{2,1,0:T(8,128)(2,1)S(1)}, bf16[8,80,1024]{2,1,0:T(8,128)(2,1)S(1)}, u32[]{:S(2)}, u32[]{:S(2)}) collective-permute-start(bf16[8,80,1024]{2,1,0:T(8,128)(2,1)S(1)} %collective-permute-done.24.refs_8_.refs_17_), channel_id=1, source_target_pairs={{0,1},{1,0},{2,3},{3,2},{4,5},{5,4},{6,7},{7,6},{8,9},{9,8},{10,11... | collective-permute-start | bytes 3932168 | tf_op jit(solution)/shard_map/ppermute | solution.py:1014
  142.9 16.7 %collective-permute-start.21 = (bf16[4,64,1024]{2,1,0:T(8,128)(2,1)S(1)}, bf16[4,64,1024]{2,1,0:T(8,128)(2,1)S(1)}, u32[]{:S(2)}, u32[]{:S(2)}) collective-permute-start(bf16[4,64,1024]{2,1,0:T(8,128)(2,1)S(1)} %get-tuple-element.185.refs_2_), channel_id=1, source_target_pairs={{0,2},{2,0},{4,6},{6,4},{8,10},{10,8},{12,14},{14,12},{16,18},{18,... | collective-permute-start | bytes 1572872 | tf_op jit(solution)/shard_map/ppermute | solution.py:748
  146.4 13.6 %collective-permute-start.20 = (bf16[4,64,1024]{2,1,0:T(8,128)(2,1)S(1)}, bf16[4,64,1024]{2,1,0:T(8,128)(2,1)S(1)}, u32[]{:S(2)}, u32[]{:S(2)}) collective-permute-start(bf16[4,64,1024]{2,1,0:T(8,128)(2,1)S(1)} %get-tuple-element.184.refs_0_), channel_id=1, source_target_pairs={{0,4},{2,6},{4,0},{6,2},{8,12},{10,14},{12,8},{14,10},{16,20},{18,... | collective-permute-start | bytes 1572872 | tf_op jit(solution)/shard_map/ppermute | solution.py:748
  164.0 16.7 %collective-permute-start.26 = (bf16[8,80,1024]{2,1,0:T(8,128)(2,1)}, bf16[8,80,1024]{2,1,0:T(8,128)(2,1)}, u32[]{:S(2)}, u32[]{:S(2)}) collective-permute-start(bf16[8,80,1024]{2,1,0:T(8,128)(2,1)} %get-tuple-element.193.refs_3_.refs_0_.refs_4_), channel_id=1, source_target_pairs={{0,1},{1,0},{2,3},{3,2},{4,5},{5,4},{6,7},{7,6},{8,9},{9,8},{10,11... | collective-permute-start | bytes 3932168 | tf_op jit(solution)/shard_map/ppermute | solution.py:1014
  164.5 16.3 %collective-permute-start.27 = (bf16[8,80,1024]{2,1,0:T(8,128)(2,1)}, bf16[8,80,1024]{2,1,0:T(8,128)(2,1)}, u32[]{:S(2)}, u32[]{:S(2)}) collective-permute-start(bf16[8,80,1024]{2,1,0:T(8,128)(2,1)} %get-tuple-element.194.refs_7_.refs_16_), channel_id=1, source_target_pairs={{0,1},{1,0},{2,3},{3,2},{4,5},{5,4},{6,7},{7,6},{8,9},{9,8},{10,11... | collective-permute-start | bytes 3932168 | tf_op jit(solution)/shard_map/ppermute | solution.py:1014
  164.5 29.1 %collective-permute-start.31 = (bf16[8,64,1024]{2,1,0:T(8,128)(2,1)}, bf16[8,64,1024]{2,1,0:T(8,128)(2,1)}, u32[]{:S(2)}, u32[]{:S(2)}) collective-permute-start(bf16[8,64,1024]{2,1,0:T(8,128)(2,1)} %get-tuple-element.201.refs_20_), channel_id=1, source_target_pairs={{0,4},{2,6},{4,0},{6,2},{8,12},{10,14},{12,8},{14,10},{16,20},{18,... | collective-permute-start | bytes 3145736 | tf_op jit(solution)/shard_map/ppermute | solution.py:748
  166.1 27.5 %collective-permute-start.28 = (bf16[8,64,1024]{2,1,0:T(8,128)(2,1)}, bf16[8,64,1024]{2,1,0:T(8,128)(2,1)}, u32[]{:S(2)}, u32[]{:S(2)}) collective-permute-start(bf16[8,64,1024]{2,1,0:T(8,128)(2,1)} %get-tuple-element.198.refs_8_.refs_12_), channel_id=1, source_target_pairs={{0,2},{2,0},{4,6},{6,4},{8,10},{10,8},{12,14},{14,12},{16,18},{18,... | collective-permute-start | bytes 3145736 | tf_op jit(solution)/shard_map/ppermute | solution.py:748
  179.8 14.3 %collective-permute-start.29 = (bf16[8,64,1024]{2,1,0:T(8,128)(2,1)}, bf16[8,64,1024]{2,1,0:T(8,128)(2,1)S(1)}, u32[]{:S(2)}, u32[]{:S(2)}) collective-permute-start(bf16[8,64,1024]{2,1,0:T(8,128)(2,1)} %get-tuple-element.198.refs_8_.refs_12_), channel_id=1, source_target_pairs={{0,1},{1,0},{2,3},{3,2},{4,5},{5,4},{6,7},{7,6},{8,9},{9,8},{10,11... | collective-permute-start | bytes 3145736 | tf_op jit(solution)/shard_map/ppermute | solution.py:1014
  180.7 13.4 %collective-permute-start.32 = (bf16[8,64,1024]{2,1,0:T(8,128)(2,1)}, bf16[8,64,1024]{2,1,0:T(8,128)(2,1)S(1)}, u32[]{:S(2)}, u32[]{:S(2)}) collective-permute-start(bf16[8,64,1024]{2,1,0:T(8,128)(2,1)} %get-tuple-element.201.refs_20_), channel_id=1, source_target_pairs={{0,1},{1,0},{2,3},{3,2},{4,5},{5,4},{6,7},{7,6},{8,9},{9,8},{10,11... | collective-permute-start | bytes 3145736 | tf_op jit(solution)/shard_map/ppermute | solution.py:1014
  268.4 16.3 %collective-permute-start.34 = (bf16[4,16,32,1024]{3,2,1,0:T(8,128)(2,1)}, bf16[4,16,32,1024]{3,2,1,0:T(8,128)(2,1)}, u32[]{:S(2)}, u32[]{:S(2)}) collective-permute-start(bf16[4,16,32,1024]{3,2,1,0:T(8,128)(2,1)} %get-tuple-element.209), channel_id=1, source_target_pairs={{0,1},{1,0},{2,3},{3,2},{4,5},{5,4},{6,7},{7,6},{8,9},{9,8},{10,11... | collective-permute-start | bytes 12582920 | tf_op jit(solution)/shard_map/ppermute | solution.py:1014
  268.8 15.9 %collective-permute-start.35 = (bf16[4,16,32,1024]{3,2,1,0:T(8,128)(2,1)}, bf16[4,16,32,1024]{3,2,1,0:T(8,128)(2,1)S(1)}, u32[]{:S(2)}, u32[]{:S(2)}) collective-permute-start(bf16[4,16,32,1024]{3,2,1,0:T(8,128)(2,1)} %get-tuple-element.211), channel_id=1, source_target_pairs={{0,1},{1,0},{2,3},{3,2},{4,5},{5,4},{6,7},{7,6},{8,9},{9,8},{10,11... | collective-permute-start | bytes 12582920 | tf_op jit(solution)/shard_map/ppermute | solution.py:1014
  292.2 48.1 %collective-permute-start.37 = (bf16[4,2,2,2,32,1024]{5,4,3,2,1,0:T(8,128)(2,1)}, bf16[4,2,2,2,32,1024]{5,4,3,2,1,0:T(8,128)(2,1)S(1)}, u32[]{:S(2)}, u32[]{:S(2)}) collective-permute-start(bf16[4,2,2,2,32,1024]{5,4,3,2,1,0:T(8,128)(2,1)} %get-tuple-element.220), channel_id=1, source_target_pairs={{0,4},{2,6},{4,0},{6,2},{8,12},{10,14},{12,8},{14,10},{16,20},{18,... | collective-permute-start | bytes 6291464 | tf_op jit(solution)/shard_map/ppermute | solution.py:748
  292.8 48.2 %collective-permute-start.36 = (bf16[4,2,2,2,32,1024]{5,4,3,2,1,0:T(8,128)(2,1)}, bf16[4,2,2,2,32,1024]{5,4,3,2,1,0:T(8,128)(2,1)}, u32[]{:S(2)}, u32[]{:S(2)}) collective-permute-start(bf16[4,2,2,2,32,1024]{5,4,3,2,1,0:T(8,128)(2,1)} %get-tuple-element.212), channel_id=1, source_target_pairs={{0,2},{2,0},{4,6},{6,4},{8,10},{10,8},{12,14},{14,12},{16,18},{18,... | collective-permute-start | bytes 6291464 | tf_op jit(solution)/shard_map/ppermute | solution.py:748
  331.6 17.3 %collective-permute-start.38 = (bf16[2,1024,256]{2,1,0:T(8,128)(2,1)}, bf16[2,1024,256]{2,1,0:T(8,128)(2,1)S(1)}, u32[]{:S(2)}, u32[]{:S(2)}) collective-permute-start(bf16[2,1024,256]{2,1,0:T(8,128)(2,1)} %get-tuple-element.225), channel_id=1, source_target_pairs={{0,1},{1,0},{2,3},{3,2},{4,5},{5,4},{6,7},{7,6},{8,9},{9,8},{10,11... | collective-permute-start | bytes 3145736 | tf_op jit(solution)/shard_map/ppermute | solution.py:1014
  345.3 32.3 %collective-permute-start.41 = (bf16[4,2,2,32,1024]{4,3,2,1,0:T(8,128)(2,1)}, bf16[4,2,2,32,1024]{4,3,2,1,0:T(8,128)(2,1)}, u32[]{:S(2)}, u32[]{:S(2)}) collective-permute-start(bf16[4,2,2,32,1024]{4,3,2,1,0:T(8,128)(2,1)} %get-tuple-element.236), channel_id=1, source_target_pairs={{0,2},{2,0},{4,6},{6,4},{8,10},{10,8},{12,14},{14,12},{16,18},{18,... | collective-permute-start | bytes 3145736 | tf_op jit(solution)/shard_map/ppermute | solution.py:748
  347.2 30.4 %collective-permute-start.40 = (bf16[4,2,2,32,1024]{4,3,2,1,0:T(8,128)(2,1)}, bf16[4,2,2,32,1024]{4,3,2,1,0:T(8,128)(2,1)}, u32[]{:S(2)}, u32[]{:S(2)}) collective-permute-start(bf16[4,2,2,32,1024]{4,3,2,1,0:T(8,128)(2,1)} %get-tuple-element.221), channel_id=1, source_target_pairs={{0,4},{2,6},{4,0},{6,2},{8,12},{10,14},{12,8},{14,10},{16,20},{18,... | collective-permute-start | bytes 3145736 | tf_op jit(solution)/shard_map/ppermute | solution.py:748
  348.9 33.9 %collective-permute-start.43 = (bf16[4,16,32,256]{3,2,1,0:T(8,128)(2,1)}, bf16[4,16,32,256]{3,2,1,0:T(8,128)(2,1)S(1)}, u32[]{:S(2)}, u32[]{:S(2)}) collective-permute-start(bf16[4,16,32,256]{3,2,1,0:T(8,128)(2,1)} %get-tuple-element.242), channel_id=1, source_target_pairs={{0,1},{1,0},{2,3},{3,2},{4,5},{5,4},{6,7},{7,6},{8,9},{9,8},{10,11... | collective-permute-start | bytes 3145736 | tf_op jit(solution)/shard_map/ppermute | solution.py:1014
  358.5 24.3 %collective-permute-start.42 = (bf16[3,16,32,256]{3,2,1,0:T(8,128)(2,1)}, bf16[3,16,32,256]{3,2,1,0:T(8,128)(2,1)}, u32[]{:S(2)}, u32[]{:S(2)}) collective-permute-start(bf16[3,16,32,256]{3,2,1,0:T(8,128)(2,1)} %get-tuple-element.239), channel_id=1, source_target_pairs={{0,1},{1,0},{2,3},{3,2},{4,5},{5,4},{6,7},{7,6},{8,9},{9,8},{10,11... | collective-permute-start | bytes 2359304 | tf_op jit(solution)/shard_map/ppermute | solution.py:1014
  359.0 23.8 %collective-permute-start.44 = (bf16[3,16,32,256]{3,2,1,0:T(8,128)(2,1)}, bf16[3,16,32,256]{3,2,1,0:T(8,128)(2,1)}, u32[]{:S(2)}, u32[]{:S(2)}) collective-permute-start(bf16[3,16,32,256]{3,2,1,0:T(8,128)(2,1)} %get-tuple-element.244), channel_id=1, source_target_pairs={{0,1},{1,0},{2,3},{3,2},{4,5},{5,4},{6,7},{7,6},{8,9},{9,8},{10,11... | collective-permute-start | bytes 2359304 | tf_op jit(solution)/shard_map/ppermute | solution.py:1014
  382.8 25.3 %collective-permute-start.45 = (bf16[8,2,32,1024]{3,2,1,0:T(8,128)(2,1)}, bf16[8,2,32,1024]{3,2,1,0:T(8,128)(2,1)}, u32[]{:S(2)}, u32[]{:S(2)}) collective-permute-start(bf16[8,2,32,1024]{3,2,1,0:T(8,128)(2,1)} %add_terms.16), channel_id=1, source_target_pairs={{0,8},{2,10},{4,12},{6,14},{8,0},{10,2},{12,4},{14,6},{16,24},{18,... | collective-permute-start | bytes 3145736 | tf_op jit(solution)/shard_map/ppermute | solution.py:748
  385.8 27.2 %collective-permute-start.47 = (bf16[5,2,2,2,32,256]{5,4,3,2,1,0:T(8,128)(2,1)}, bf16[5,2,2,2,32,256]{5,4,3,2,1,0:T(8,128)(2,1)S(1)}, u32[]{:S(2)}, u32[]{:S(2)}) collective-permute-start(bf16[5,2,2,2,32,256]{5,4,3,2,1,0:T(8,128)(2,1)} %get-tuple-element.251), channel_id=1, source_target_pairs={{0,4},{2,6},{4,0},{6,2},{8,12},{10,14},{12,8},{14,10},{16,20},{18,... | collective-permute-start | bytes 1966088 | tf_op jit(solution)/shard_map/ppermute | solution.py:748
  386.1 26.9 %collective-permute-start.46 = (bf16[5,2,2,2,32,256]{5,4,3,2,1,0:T(8,128)(2,1)}, bf16[5,2,2,2,32,256]{5,4,3,2,1,0:T(8,128)(2,1)S(1)}, u32[]{:S(2)}, u32[]{:S(2)}) collective-permute-start(bf16[5,2,2,2,32,256]{5,4,3,2,1,0:T(8,128)(2,1)} %get-tuple-element.245), channel_id=1, source_target_pairs={{0,2},{2,0},{4,6},{6,4},{8,10},{10,8},{12,14},{14,12},{16,18},{18,... | collective-permute-start | bytes 1966088 | tf_op jit(solution)/shard_map/ppermute | solution.py:748
  429.6 37.7 %collective-permute-start.57 = (bf16[8,32,1024]{2,1,0:T(8,128)(2,1)}, bf16[8,32,1024]{2,1,0:T(8,128)(2,1)}, u32[]{:S(2)}, u32[]{:S(2)}) collective-permute-start(bf16[8,32,1024]{2,1,0:T(8,128)(2,1)} %add_terms.18), channel_id=1, source_target_pairs={{0,16},{2,18},{4,20},{6,22},{8,24},{10,26},{12,28},{14,30},{16,0},... | collective-permute-start | bytes 1572872 | tf_op jit(solution)/shard_map/ppermute | solution.py:748
  438.9 18.3 %collective-permute-start.55 = (bf16[3,2,2,2,32,256]{5,4,3,2,1,0:T(8,128)(2,1)}, bf16[3,2,2,2,32,256]{5,4,3,2,1,0:T(8,128)(2,1)}, u32[]{:S(2)}, u32[]{:S(2)}) collective-permute-start(bf16[3,2,2,2,32,256]{5,4,3,2,1,0:T(8,128)(2,1)} %get-tuple-element.280), channel_id=1, source_target_pairs={{0,4},{2,6},{4,0},{6,2},{8,12},{10,14},{12,8},{14,10},{16,20},{18,... | collective-permute-start | bytes 1179656 | tf_op jit(solution)/shard_map/ppermute | solution.py:748
  439.2 18.0 %collective-permute-start.54 = (bf16[3,2,2,2,32,256]{5,4,3,2,1,0:T(8,128)(2,1)}, bf16[3,2,2,2,32,256]{5,4,3,2,1,0:T(8,128)(2,1)}, u32[]{:S(2)}, u32[]{:S(2)}) collective-permute-start(bf16[3,2,2,2,32,256]{5,4,3,2,1,0:T(8,128)(2,1)} %get-tuple-element.270), channel_id=1, source_target_pairs={{0,2},{2,0},{4,6},{6,4},{8,10},{10,8},{12,14},{14,12},{16,18},{18,... | collective-permute-start | bytes 1179656 | tf_op jit(solution)/shard_map/ppermute | solution.py:748
  440.8 21.8 %collective-permute-start.56 = (bf16[10,2,32,256]{3,2,1,0:T(8,128)(2,1)}, bf16[10,2,32,256]{3,2,1,0:T(8,128)(2,1)S(1)}, u32[]{:S(2)}, u32[]{:S(2)}) collective-permute-start(bf16[10,2,32,256]{3,2,1,0:T(8,128)(2,1)} %add_terms.20), channel_id=1, source_target_pairs={{0,8},{2,10},{4,12},{6,14},{8,0},{10,2},{12,4},{14,6},{16,24},{18,... | collective-permute-start | bytes 983048 | tf_op jit(solution)/shard_map/ppermute | solution.py:748
  472.2 13.2 %all-to-all-start.1 = ((f32[32,1,128]{2,1,0:T(1,128)}), f32[32,1,128]{2,1,0:T(1,128)S(1)}, u32[]{:S(2)}, u32[]{:S(2)}) async-start(f32[32,1,128]{2,1,0:T(1,128)} %bitcast.34), calls=%async_computation.1 | async-start | bytes 32768 | tf_op jit(solution)/shard_map/all_to_all | solution.py:1181
  477.9 19.1 %collective-permute-start.60 = (bf16[10,32,256]{2,1,0:T(8,128)(2,1)}, bf16[10,32,256]{2,1,0:T(8,128)(2,1)}, u32[]{:S(2)}, u32[]{:S(2)}) collective-permute-start(bf16[10,32,256]{2,1,0:T(8,128)(2,1)} %copy-done.71), channel_id=1, source_target_pairs={{0,16},{2,18},{4,20},{6,22},{8,24},{10,26},{12,28},{14,30},{16,0},... | collective-permute-start | bytes 491528 | tf_op jit(solution)/shard_map/ppermute | solution.py:748
  (109 other events, 1121.7 us)
